TPU v7x, 32 devices: a whole 2x2x4 slice. The times are simulated.
32 devices in a mesh: dp: 8 (over z, y), seq: 4 (over x, core).
Axes of the slice: x: 2, y: 2, z: 4, core: 2. Of those that a mesh axis runs over, the one named last changes fastest.
Arguments:
- tokens: bfloat16 [24, 1024, 768], P('dp', 'seq'), may hold values from -6 to 6
- cotangent: bfloat16 [24, 1024, 768], P('dp', 'seq'), may hold values from -6 to 6
- lengths: int32 [24], P('dp'), may hold values from 128 to 1024, as said below
- block_perm: int32 [24, 2], P('dp'), may hold values from 0 to 1, each once within a row
- w_qkv: bfloat16 [768, 2304], replicated, may hold values from -0.21875 to 0.21875
- b_query: bfloat16 [768], replicated, may hold values from -1.75 to 1.75
- b_value: bfloat16 [768], replicated, may hold values from -0.3125 to 0.3125
- w_out: bfloat16 [768, 768], replicated, may hold values from -1.75 to 1.75
- b_out: bfloat16 [768], replicated, may hold values from -1.75 to 1.75
- ln1_gain: bfloat16 [768], replicated, may hold values from 0.099609375 to 1.8984375
- ln1_shift: bfloat16 [768], replicated, may hold values from -1.75 to 1.75
- w_up: bfloat16 [768, 3072], replicated, may hold values from -0.21875 to 0.21875
- b_up: bfloat16 [3072], replicated, may hold values from -1.75 to 1.75
- w_down: bfloat16 [3072, 768], replicated, may hold values from -0.109375 to 0.109375
- b_down: bfloat16 [768], replicated, may hold values from -1.75 to 1.75
- ln2_gain: bfloat16 [768], replicated, may hold values from 0.099609375 to 1.8984375
- ln2_shift: bfloat16 [768], replicated, may hold values from -1.75 to 1.75
Outputs:
- out_tokens: bfloat16 [24, 1024, 768], P('dp', 'seq')
- grad_tokens: float32 [24, 1024, 768], P('dp', 'seq')
- grad_w_qkv: float32 [768, 2304], replicated
- grad_b_query: float32 [768], replicated
- grad_b_value: float32 [768], replicated
- grad_w_out: float32 [768, 768], replicated
- grad_b_out: float32 [768], replicated
- grad_ln1_gain: float32 [768], replicated
- grad_ln1_shift: float32 [768], replicated
- grad_w_up: float32 [768, 3072], replicated
- grad_b_up: float32 [3072], replicated
- grad_w_down: float32 [3072, 768], replicated
- grad_b_down: float32 [768], replicated
- grad_ln2_gain: float32 [768], replicated
- grad_ln2_shift: float32 [768], replicated
Inputs may be any that keep to these rules, and one draw needn't show every extreme that they name: `lengths`: every length is even; in each aligned group of 3 consecutive sequences, one has length 1024. `block_perm`: each row is 0, 1 or 1, 0.
All inputs are finite; a program needn't handle non-finite values.
Results may differ from a plain program's by a relative error of at most 0.017.
Values may be sent and summed in bfloat16 or wider, within the bound.
No kernel may reach another device: no remote copies, remote signals or barrier semaphores. Data moves between devices by JAX's collectives and lax.ppermute only.
A program may use at most 320 MiB of HBM per device.

v0:
```python
import functools
import jax
import jax.numpy as jnp
from jax import lax
from jax.experimental import pallas as pl
from jax.experimental.pallas import tpu as pltpu
from jax.sharding import PartitionSpec as P

HEAD_DIM = 64
SOFT = HEAD_DIM ** -0.5 * 1.4426950408889634
NN = (((1,), (0,)), ((), ()))
NT = (((1,), (1,)), ((), ()))
TN = (((0,), (0,)), ((), ()))
VMEM_LIMIT = 50 * 1024 * 1024
HEADS = 12
EPSILON = 1e-06
BITS = {"c": ("seq", 0), "x": ("seq", 1), "y": ("dp", 0), "l": ("dp", 1), "h": ("dp", 2)}


def own_number(order):
    number = jnp.int32(0)
    for letter in order:
        axis, shift = BITS[letter]
        number = number * 2 + ((lax.axis_index(axis) >> shift) & 1)
    return number


def exchange(array_in, axis, flip):
    return lax.ppermute(array_in, axis, [(i, i ^ flip) for i in range(lax.axis_size(axis))])


def exchange_bit(array_in, letter):
    axis, shift = BITS[letter]
    return exchange(array_in, axis, 1 << shift)


def extra_flips(axis, used):
    return [1 << shift for shift in range(used, lax.axis_size(axis).bit_length() - 1)]


def add_extra(array_in):
    for flip in extra_flips("dp", 3):
        array_in = array_in + exchange(array_in, "dp", flip)
    return array_in


def halve(array_in, order):
    for letter in order:
        half = array_in.shape[0] // 2
        array_in = array_in[:half] + exchange_bit(array_in[half:], letter)
    return array_in


def double(array_in, order):
    for letter in reversed(order):
        array_in = jnp.concatenate([array_in, exchange_bit(array_in, letter)])
    return array_in


def spread(pieces, order):
    for letter in reversed(order):
        pieces = pieces + [exchange_bit(piece, letter) for piece in pieces]
    return pieces


def sum_all(array_in, axes):
    for axis in axes:
        for flip in extra_flips(axis, 0):
            array_in = array_in + exchange(array_in, axis, flip)
    return array_in


def sum_low(*parts):
    total = parts[0].astype(jnp.float32)
    for part in parts[1:]:
        total = total + part.astype(jnp.float32)
    return total.astype(jnp.bfloat16)


def dot_f32(left, right, dims):
    return lax.dot_general(left, right, dims, preferred_element_type=jnp.float32)


def shift_matrix(half, block, whole):
    row = lax.broadcasted_iota(jnp.int32, (block, whole), 0)
    col = lax.broadcasted_iota(jnp.int32, (block, whole), 1)
    return jnp.where((col == row + half) & (row < half), 1.0, 0.0).astype(jnp.bfloat16)


def mask_tiles(half, block):
    row = lax.broadcasted_iota(jnp.int32, (16, block), 0)
    col = lax.broadcasted_iota(jnp.int32, (16, block), 1)
    key_tile = jnp.where((row == 0) & (col >= half), -1e30, 0.0).astype(jnp.bfloat16)
    query_tile = jnp.where(row == 0, 1.0, 0.0).astype(jnp.bfloat16)
    return key_tile, query_tile


def attend_forward(
    heads, info, x0, x1, x2, x3, w_t, bias, c0, c1, c2, c3, qkv, ctx_blk, lse, x_t, x_seq, qkv_s, c_tok
):
    half, mine = info[0], info[3]
    whole = x_seq.shape[0]
    quarter = whole // 4
    block = whole // 2
    wide = heads * HEAD_DIM
    for r, piece in enumerate((x0, x1, x2, x3)):
        x_seq[pl.ds(pl.multiple_of((r ^ mine) * quarter, quarter), quarter), :] = piece[...]
    row = lax.broadcasted_iota(jnp.int32, (block, 1), 0)
    shift = shift_matrix(half, block, whole)
    first = jnp.where(row < half, x_seq[0:block, :], jnp.zeros((), jnp.bfloat16))
    second = dot_f32(shift, x_seq[...], NN).astype(jnp.bfloat16)
    for b, rows in enumerate((first, second)):
        turned = rows.T
        x_t[b] = turned
        projected = dot_f32(w_t[...], turned, NN) + bias[...]
        qkv_s[b] = projected.astype(jnp.bfloat16)
    qkv[...] = qkv_s[...]
    key_tile, query_tile = mask_tiles(half, block)

    def one_block(b, carry):
        target = info[1 + b]
        for h in range(heads):
            rows = slice(h * HEAD_DIM, (h + 1) * HEAD_DIM)
            q_t = jnp.concatenate([qkv_s[b, rows, :], query_tile])
            k_t = jnp.concatenate(
                [qkv_s[target, wide + h * HEAD_DIM : wide + (h + 1) * HEAD_DIM, :], key_tile]
            )
            v_t = qkv_s[target, 2 * wide + h * HEAD_DIM : 2 * wide + (h + 1) * HEAD_DIM, :]
            scores = dot_f32(k_t, q_t, TN) * SOFT
            top = jnp.max(scores, axis=0, keepdims=True)
            expo = jnp.exp2(scores - top)
            total = jnp.sum(expo, axis=0, keepdims=True)
            context = dot_f32(v_t, expo.astype(jnp.bfloat16), NN) / total
            ctx_blk[b, rows, :] = context
            lse[b, h : h + 1, :] = top + jnp.log2(total)
        return carry

    lax.fori_loop(0, 2, one_block, 0)
    lane = lax.broadcasted_iota(jnp.int32, (1, block), 1)
    early = jnp.where(lane < half, ctx_blk[0], 0.0)
    late = dot_f32(ctx_blk[1].astype(jnp.bfloat16), shift, NN)
    for j in range(4):
        part = late[:, j * quarter : (j + 1) * quarter]
        if j < 2:
            part = part + early[:, j * quarter : (j + 1) * quarter]
        c_tok[j] = part.astype(jnp.bfloat16)
    for r, piece in enumerate((c0, c1, c2, c3)):
        piece[...] = c_tok[r ^ mine]


def attend_backward(
    heads, last, info, g0, g1, g2, g3, w_t, qkv, ctx_blk, lse, x_t, acc, dx0, dx1, dx2, dx3, grad_w, grad_b,
    g_tok, g_blk, d_qkv, dx_s,
):
    half, mine = info[0], info[3]
    quarter = g0.shape[1]
    block = 2 * quarter
    whole = 4 * quarter
    wide = heads * HEAD_DIM
    for r, piece in enumerate((g0, g1, g2, g3)):
        g_tok[r ^ mine] = piece[...]
    shift = shift_matrix(half, block, whole)
    lane = lax.broadcasted_iota(jnp.int32, (1, block), 1)
    g_all = jnp.concatenate([g_tok[j] for j in range(4)], axis=1)
    g_blk[0] = jnp.where(lane < half, g_all[:, :block], jnp.zeros((), jnp.bfloat16))
    g_blk[1] = dot_f32(g_all, shift, NT).astype(jnp.bfloat16)
    key_tile, query_tile = mask_tiles(half, block)

    def one_block(b, carry):
        target = info[1 + b]
        for h in range(heads):
            rows = slice(h * HEAD_DIM, (h + 1) * HEAD_DIM)
            k_rows = slice(wide + h * HEAD_DIM, wide + (h + 1) * HEAD_DIM)
            v_rows = slice(2 * wide + h * HEAD_DIM, 2 * wide + (h + 1) * HEAD_DIM)
            q_t = qkv[b, rows, :]
            k_t = qkv[target, k_rows, :]
            v_t = qkv[target, v_rows, :]
            g_t = g_blk[b, rows, :]
            scores = dot_f32(
                jnp.concatenate([k_t, key_tile]), jnp.concatenate([q_t, query_tile]), TN
            )
            probs = jnp.exp2(scores * SOFT - lse[b, h : h + 1, :])
            d_probs = dot_f32(v_t, g_t, TN)
            delta = jnp.sum(ctx_blk[b, rows, :] * g_t.astype(jnp.float32), axis=0, keepdims=True)
            d_scores = (probs * (d_probs - delta)).astype(jnp.bfloat16)
            scaling = HEAD_DIM ** -0.5
            d_qkv[b, rows, :] = (dot_f32(k_t, d_scores, NN) * scaling).astype(jnp.bfloat16)
            d_qkv[target, k_rows, :] = (dot_f32(q_t, d_scores, NT) * scaling).astype(jnp.bfloat16)
            d_qkv[target, v_rows, :] = dot_f32(g_t, probs.astype(jnp.bfloat16), NT).astype(
                jnp.bfloat16
            )
        return carry

    lax.fori_loop(0, 2, one_block, 0)
    early, late = d_qkv[0], d_qkv[1]
    total = acc[...] + dot_f32(x_t[0], early, NT) + dot_f32(x_t[1], late, NT)
    if last:
        tile = grad_w.shape[1]
        for q in range(8):
            grad_w[q ^ info[4]] = total[q * tile : (q + 1) * tile].astype(jnp.bfloat16)
    else:
        grad_w[...] = total
    grad_b[...] = jnp.sum(early.astype(jnp.float32), axis=1, keepdims=True) + jnp.sum(
        late.astype(jnp.float32), axis=1, keepdims=True
    )
    back = dot_f32(late, shift, NN)
    front = jnp.where(lane < half, early.astype(jnp.float32), 0.0)
    for j in range(4):
        part = back[:, j * quarter : (j + 1) * quarter]
        if j < 2:
            part = part + front[:, j * quarter : (j + 1) * quarter]
        dx_s[j] = dot_f32(part.astype(jnp.bfloat16), w_t[...], TN).astype(jnp.bfloat16)
    for r, piece in enumerate((dx0, dx1, dx2, dx3)):
        piece[...] = dx_s[r ^ mine]


def kernel_call(body, scalars, arrays, outs, scratch, aliases={}):
    return pl.pallas_call(
        body,
        out_shape=outs,
        in_specs=[pl.BlockSpec(memory_space=pltpu.SMEM)]
        + [pl.BlockSpec(memory_space=pltpu.VMEM)] * len(arrays),
        out_specs=[pl.BlockSpec(memory_space=pltpu.VMEM)] * len(outs),
        scratch_shapes=scratch,
        input_output_aliases=aliases,
        compiler_params=pltpu.CompilerParams(vmem_limit_bytes=VMEM_LIMIT),
        cost_estimate=pl.CostEstimate(
            flops=6 * 10**9, transcendentals=0, bytes_accessed=20 * 1024 * 1024
        ),
    )(scalars, *arrays)


def attention_forward(info, pieces, w_t, bias, heads):
    quarter, features = pieces[0].shape
    whole, block, wide = 4 * quarter, 2 * quarter, heads * HEAD_DIM
    out = jax.ShapeDtypeStruct
    outs = [out((wide, quarter), jnp.bfloat16)] * 4 + [
        out((2, 3 * wide, block), jnp.bfloat16),
        out((2, wide, block), jnp.float32),
        out((2, 8, block), jnp.float32),
        out((2, features, block), jnp.bfloat16),
    ]
    scratch = [
        pltpu.VMEM((whole, features), jnp.bfloat16),
        pltpu.VMEM((2, 3 * wide, block), jnp.bfloat16),
        pltpu.VMEM((4, wide, quarter), jnp.bfloat16),
    ]
    found = kernel_call(
        functools.partial(attend_forward, heads), info, [*pieces, w_t, bias], outs, scratch
    )
    return found[:4], found[4:]


def attention_backward(info, pieces, w_t, kept, acc, heads, last):
    wide, quarter = pieces[0].shape
    features = w_t.shape[1]
    block = 2 * quarter
    out = jax.ShapeDtypeStruct
    outs = [out((quarter, features), jnp.bfloat16)] * 4 + [
        out((8, features // 8, 3 * wide), jnp.bfloat16)
        if last
        else out((features, 3 * wide), jnp.float32),
        out((3 * wide, 1), jnp.float32),
    ]
    scratch = [
        pltpu.VMEM((4, wide, quarter), jnp.bfloat16),
        pltpu.VMEM((2, wide, block), jnp.bfloat16),
        pltpu.VMEM((2, 3 * wide, block), jnp.bfloat16),
        pltpu.VMEM((4, quarter, features), jnp.bfloat16),
    ]
    found = kernel_call(
        functools.partial(attend_backward, heads, last),
        info,
        [*pieces, w_t, *kept, acc],
        outs,
        scratch,
    )
    return found[:4], found[4], found[5]

def live_rows(places, rows, mine, local_rows, offset):
    row = lax.broadcasted_iota(jnp.int32, (rows, 1), 0)
    length = jnp.zeros((rows, 1), jnp.int32)
    for s in range(rows // local_rows):
        length = jnp.where(row >= s * local_rows, places[offset + s], length)
    position = mine * local_rows + lax.rem(row, local_rows)
    return jnp.where(position < length, 1.0, 0.0)


def normal_parts(array_in):
    centered = array_in - jnp.mean(array_in, axis=1, keepdims=True)
    spread = jnp.mean(centered * centered, axis=1, keepdims=True)
    inverse = lax.rsqrt(spread + EPSILON)
    return centered * inverse, inverse


def normal_back(hat, inverse, gain, d_out):
    scaled = d_out * gain
    mean_scaled = jnp.mean(scaled, axis=1, keepdims=True)
    mean_product = jnp.mean(scaled * hat, axis=1, keepdims=True)
    return inverse * (scaled - mean_scaled - hat * mean_product)


def column_sum(array_in):
    return jnp.sum(array_in, axis=0, keepdims=True)


def feed_forward(shape, places, *refs):
    seq_count, seq_parts, steps = shape
    pieces, refs = refs[: seq_count * seq_parts], refs[seq_count * seq_parts :]
    tokens, cot, w_out, vectors, w_up, b_up, w_down = refs[:7]
    out, context, first_in, first_low, active, slope, d_second, d_lowered, sums = refs[7:16]
    first_norm, lowered = refs[16:]
    rows, features = tokens.shape
    local_rows = rows // seq_count
    wide = features // seq_parts
    mine = places[9]
    step = pl.program_id(0)
    f32 = jnp.float32

    @pl.when(step == 0)
    def start():
        for s in range(seq_count):
            for r in range(seq_parts):
                context[
                    pl.ds(pl.multiple_of((r ^ mine) * wide, wide), wide),
                    s * local_rows : (s + 1) * local_rows,
                ] = pieces[s * seq_parts + r][...]
        live = live_rows(places, rows, mine, local_rows, 11)
        attended = dot_f32(context[...], w_out[...], TN) + vectors[0:1, :]
        total = jnp.where(live > 0, tokens[...].astype(f32), 0.0) + attended
        first_in[...] = total
        hat, _ = normal_parts(total)
        normed = hat * vectors[1:2, :] + vectors[2:3, :]
        first_norm[...] = normed
        first_low[...] = normed.astype(jnp.bfloat16)

    lifted = dot_f32(first_low[...], w_up[...], NN) + b_up[...]
    cdf = 0.5 * (1.0 + lax.erf(lifted * 0.7071067811865476))
    density = jnp.exp(lifted * lifted * -0.5) * 0.3989422804014327
    gelu = (lifted * cdf).astype(jnp.bfloat16)
    active[0] = gelu
    slope[0] = (cdf + lifted * density).astype(jnp.bfloat16)
    part = dot_f32(gelu, w_down[...], NN)

    @pl.when(step == 0)
    def first():
        lowered[...] = part

    @pl.when(step > 0)
    def later():
        lowered[...] += part

    @pl.when(step == steps - 1)
    def finish():
        live = live_rows(places, rows, mine, local_rows, 11)
        hat, inverse = normal_parts(first_norm[...] + (lowered[...] + vectors[3:4, :]))
        gain = vectors[4:5, :]
        out[...] = ((hat * gain + vectors[5:6, :]) * live).astype(jnp.bfloat16)
        incoming = cot[...].astype(f32) * live
        back = normal_back(hat, inverse, gain, incoming)
        d_second[...] = back
        low = back.astype(jnp.bfloat16)
        d_lowered[...] = low
        sums[0:1, :] = column_sum(low.astype(f32))
        sums[1:2, :] = column_sum(incoming * hat)
        sums[2:3, :] = column_sum(incoming)


def hidden_back(places, active, slope, w_up, w_down, first_t, d_lowered, grad_down, grad_up, grad_b):
    inner = places[8]
    f32 = jnp.float32
    down = dot_f32(active[0], d_lowered[...], TN).astype(jnp.bfloat16)
    tile = down.shape[0] // 4
    for q in range(4):
        grad_down[0, pl.ds(pl.multiple_of((q ^ inner) * tile, tile), tile), :] = down[
            q * tile : (q + 1) * tile
        ]
    d_active = dot_f32(d_lowered[...], w_down[...], NT)
    d_lifted = (d_active * slope[0].astype(f32)).astype(jnp.bfloat16)
    grad_b[...] = column_sum(d_lifted.astype(f32))
    grad_up[0] = dot_f32(first_t[...], d_lifted, NN).astype(jnp.bfloat16)
    return dot_f32(d_lifted, w_up[...], NT)


def turn_rows(places, source, target):
    inner = places[8]
    tile = target.shape[0] // 4
    turned = source[...].T
    for q in range(4):
        target[pl.ds(pl.multiple_of((q ^ inner) * tile, tile), tile), :] = turned[
            q * tile : (q + 1) * tile
        ]


def back_send(
    places, active, slope, w_up, w_down, first_low, d_lowered, d_second,
    grad_down, grad_up, grad_b, d_first, first_t,
):
    step = pl.program_id(0)

    @pl.when(step == 0)
    def start():
        turn_rows(places, first_low, first_t)
        d_first[...] = d_second[...]

    d_first[...] += hidden_back(
        places, active, slope, w_up, w_down, first_t, d_lowered, grad_down, grad_up, grad_b
    )


def back_keep(shape, places, *refs):
    seq_count, seq_parts, steps = shape
    active, slope, w_up, w_down, first_low, d_lowered, d_part = refs[:7]
    first_in, context, w_out, vectors = refs[7:11]
    grad_down, grad_up, grad_b, d_first_in, sums, grad_out = refs[11:17]
    pieces = refs[17 : 17 + seq_count * seq_parts]
    first_t, d_first, turned = refs[17 + seq_count * seq_parts :]
    step = pl.program_id(0)
    f32 = jnp.float32

    @pl.when(step == 0)
    def start():
        turn_rows(places, first_low, first_t)
        d_first[...] = d_part[...]

    d_first[...] += hidden_back(
        places, active, slope, w_up, w_down, first_t, d_lowered, grad_down, grad_up, grad_b
    )

    @pl.when(step == steps - 1)
    def finish():
        rows, features = first_in.shape
        local_rows = rows // seq_count
        wide = features // seq_parts
        mine = places[9]
        hat, inverse = normal_parts(first_in[...])
        incoming = d_first[...]
        back = normal_back(hat, inverse, vectors[1:2, :], incoming)
        d_first_in[...] = back
        low = back.astype(jnp.bfloat16)
        sums[0:1, :] = column_sum(low.astype(f32))
        sums[1:2, :] = column_sum(incoming * hat)
        sums[2:3, :] = column_sum(incoming)
        turned[...] = dot_f32(w_out[...], low, NT).astype(jnp.bfloat16)
        for r in range(seq_parts):
            own = turned[pl.ds(pl.multiple_of((r ^ mine) * wide, wide), wide), :]
            for s in range(seq_count):
                pieces[s * seq_parts + r][...] = own[:, s * local_rows : (s + 1) * local_rows]
        product = dot_f32(context[...], low, NN).astype(jnp.bfloat16)
        block_rows, block_cols = grad_out.shape[2:]
        across = features // block_cols
        for j in range(seq_parts):
            for q in range(wide // block_rows * across):
                row, col = j * wide + q // across * block_rows, q % across * block_cols
                grad_out[j ^ mine, q ^ places[10]] = product[
                    row : row + block_rows, col : col + block_cols
                ]


def whole_spec(shape):
    return pl.BlockSpec(shape, lambda p, places: (0,) * len(shape))


def step_call(body, places, steps, ins, in_specs, outs, out_specs, scratch, flops):
    return pl.pallas_call(
        body,
        out_shape=outs,
        grid_spec=pltpu.PrefetchScalarGridSpec(
            num_scalar_prefetch=1,
            grid=(steps,),
            in_specs=in_specs,
            out_specs=out_specs,
            scratch_shapes=scratch,
        ),
        compiler_params=pltpu.CompilerParams(vmem_limit_bytes=VMEM_LIMIT),
        cost_estimate=pl.CostEstimate(
            flops=flops, transcendentals=0, bytes_accessed=20 * 1024 * 1024
        ),
    )(places, *ins)


def run_feed_forward(places, pieces, tokens, cot, w_out, vectors, w_up, b_up, w_down, dims):
    seq_count, seq_parts = dims
    rows, features = tokens.shape
    hidden = w_up.shape[1]
    steps = 8
    tile = hidden // steps
    out, bf16, f32 = jax.ShapeDtypeStruct, jnp.bfloat16, jnp.float32
    square = (rows, features)
    up_spec = pl.BlockSpec((features, tile), lambda p, places: (0, places[p]))
    down_spec = pl.BlockSpec((tile, features), lambda p, places: (places[p], 0))
    bias_spec = pl.BlockSpec((1, tile), lambda p, places: (0, places[p]))
    kept_spec = pl.BlockSpec((1, rows, tile), lambda p, places: (p, 0, 0))
    return step_call(
        functools.partial(feed_forward, (seq_count, seq_parts, steps)),
        places,
        steps,
        [*pieces, tokens, cot, w_out, vectors, w_up, b_up, w_down],
        [whole_spec(p.shape) for p in pieces]
        + [whole_spec(square), whole_spec(square), whole_spec(w_out.shape), whole_spec(vectors.shape)]
        + [up_spec, bias_spec, down_spec],
        [
            out(square, bf16),
            out((features, rows), bf16),
            out(square, f32),
            out(square, bf16),
            out((steps, rows, tile), bf16),
            out((steps, rows, tile), bf16),
            out(square, f32),
            out(square, bf16),
            out((8, features), f32),
        ],
        [
            whole_spec(square),
            whole_spec((features, rows)),
            whole_spec(square),
            whole_spec(square),
            kept_spec,
            kept_spec,
            whole_spec(square),
            whole_spec(square),
            whole_spec((8, features)),
        ],
        [pltpu.VMEM(square, f32), pltpu.VMEM(square, f32)],
        2 * rows * features * (2 * hidden + features),
    )


def back_specs(first, rows, features, tile):
    kept = pl.BlockSpec((1, rows, tile), lambda p, places: (p + first, 0, 0))
    up = pl.BlockSpec((features, tile), lambda p, places: (0, places[p + first]))
    down = pl.BlockSpec((tile, features), lambda p, places: (places[p + first], 0))
    bias = pl.BlockSpec((1, tile), lambda p, places: (0, places[p + first] % 4))
    grad_down = pl.BlockSpec((1, tile, features), lambda p, places: (p, 0, 0))
    grad_up = pl.BlockSpec((1, features, tile), lambda p, places: (p, 0, 0))
    return [kept, kept, up, down], [grad_down, grad_up, bias]


def run_back_send(places, active, slope, w_up, w_down, first_low, d_lowered, d_second):
    steps_all, rows, tile = active.shape
    features = first_low.shape[1]
    steps = steps_all // 2
    out, bf16, f32 = jax.ShapeDtypeStruct, jnp.bfloat16, jnp.float32
    square = (rows, features)
    ins, outs = back_specs(steps, rows, features, tile)
    return step_call(
        back_send,
        places,
        steps,
        [active, slope, w_up, w_down, first_low, d_lowered, d_second],
        ins + [whole_spec(square)] * 3,
        [
            out((steps, tile, features), bf16),
            out((steps, features, tile), bf16),
            out((1, steps * tile), f32),
            out(square, f32),
        ],
        outs + [whole_spec(square)],
        [pltpu.VMEM((features, rows), bf16)],
        8 * rows * features * steps * tile,
    )


def run_back_keep(
    places, active, slope, w_up, w_down, first_low, d_lowered, d_part, first_in, context, w_out,
    vectors, dims,
):
    seq_count, seq_parts = dims
    steps_all, rows, tile = active.shape
    features = first_low.shape[1]
    steps = steps_all // 2
    out, bf16, f32 = jax.ShapeDtypeStruct, jnp.bfloat16, jnp.float32
    square = (rows, features)
    turned = (features, rows)
    piece = (features // seq_parts, rows // seq_count)
    count = seq_count * seq_parts
    out_blocks = (seq_parts, 8, features // seq_parts // 4, features // 2)
    ins, outs = back_specs(0, rows, features, tile)
    return step_call(
        functools.partial(back_keep, (seq_count, seq_parts, steps)),
        places,
        steps,
        [active, slope, w_up, w_down, first_low, d_lowered, d_part, first_in, context, w_out, vectors],
        ins
        + [whole_spec(square)] * 4
        + [whole_spec(turned), whole_spec(w_out.shape), whole_spec(vectors.shape)],
        [
            out((steps, tile, features), bf16),
            out((steps, features, tile), bf16),
            out((1, steps * tile), f32),
            out(square, f32),
            out((8, features), f32),
            out(out_blocks, bf16),
        ]
        + [out(piece, bf16)] * count,
        outs
        + [whole_spec(square), whole_spec((8, features)), whole_spec(out_blocks)]
        + [whole_spec(piece)] * count,
        [pltpu.VMEM(turned, bf16), pltpu.VMEM(square, f32), pltpu.VMEM(turned, bf16)],
        8 * rows * features * steps * tile,
    )


def place_rows(places, *refs):
    pieces, out = refs[:8], refs[8]
    step = pl.program_id(0)
    for k, piece in enumerate(pieces):

        @pl.when(step == k)
        def copy():
            tile = piece.shape[1]
            for q in range(4):
                out[pl.ds(pl.multiple_of((q ^ places[8]) * tile, tile), tile), :] = piece[q].astype(
                    jnp.float32
                )


def gather_hidden(places, pieces, shape):
    _, rows, cols = pieces[0].shape
    by_rows = shape[1] == cols
    block = (4 * rows, cols)
    index = (lambda p, places: (places[p], 0)) if by_rows else (lambda p, places: (0, places[p]))
    return step_call(
        place_rows,
        places,
        8,
        pieces,
        [whole_spec(p.shape) for p in pieces],
        jax.ShapeDtypeStruct(shape, jnp.float32),
        pl.BlockSpec(block, index),
        [],
        8 * rows * cols,
    )


def place_blocks(places, *refs):
    pieces, out = refs[:-1], refs[-1]
    mine, inner = places[9], places[10]
    step = pl.program_id(0)
    block_rows, block_cols = pieces[0].shape[1:]
    across = out.shape[1] // block_cols
    for k, piece in enumerate(pieces):

        @pl.when(step == k)
        def copy():
            for q in range(piece.shape[0]):
                row, col = q // across * block_rows, q % across * block_cols
                out[row : row + block_rows, col : col + block_cols] = piece[q ^ inner].astype(
                    jnp.float32
                )


def gather_out(places, pieces, shape):
    wide = shape[0] // len(pieces)
    return step_call(
        place_blocks,
        places,
        len(pieces),
        pieces,
        [whole_spec(p.shape) for p in pieces],
        jax.ShapeDtypeStruct(shape, jnp.float32),
        pl.BlockSpec((wide, shape[1]), lambda p, places: (p ^ places[9], 0)),
        [],
        1000,
    )


def place_heads(places, *refs):
    pieces, out = refs[:-1], refs[-1]
    mine, inner = places[9], places[10]
    seq_parts = len(pieces)
    step = pl.program_id(0)
    wide = pieces[0].shape[2] // 3
    for r, piece in enumerate(pieces):
        for j in range(seq_parts):

            @pl.when((r ^ mine) == j)
            def copy():
                rows = piece[step ^ inner].astype(jnp.float32)
                for k in range(3):
                    start = (k * seq_parts + j) * wide
                    out[:, start : start + wide] = rows[:, k * wide : (k + 1) * wide]


def gather_heads(places, pieces, shape):
    rows = pieces[0].shape[1]
    return step_call(
        place_heads,
        places,
        8,
        pieces,
        [whole_spec(p.shape) for p in pieces],
        jax.ShapeDtypeStruct(shape, jnp.float32),
        pl.BlockSpec((rows, shape[1]), lambda p, places: (p, 0)),
        [],
        1000,
    )


def per_device(
    tokens,
    cotangent,
    lengths,
    block_perm,
    w_qkv,
    b_query,
    b_value,
    w_out,
    b_out,
    ln1_gain,
    ln1_shift,
    w_up,
    b_up,
    w_down,
    b_down,
    ln2_gain,
    ln2_shift,
):
    seq_parts = lax.axis_size("seq")
    mine = lax.axis_index("seq")
    seq_count, local_rows, features = tokens.shape
    flat_rows = seq_count * local_rows
    hidden = w_up.shape[1]
    heads = HEADS // seq_parts
    wide = heads * HEAD_DIM
    dims = (seq_count, seq_parts)
    f32 = jnp.float32

    w_heads = jnp.concatenate(
        [
            lax.dynamic_slice_in_dim(w_qkv, k * features + mine * wide, wide, axis=1)
            for k in range(3)
        ],
        axis=1,
    )
    w_t = w_heads.T
    bias = jnp.concatenate(
        [
            lax.dynamic_slice_in_dim(b_query, mine * wide, wide),
            jnp.zeros((wide,), b_query.dtype),
            lax.dynamic_slice_in_dim(b_value, mine * wide, wide),
        ]
    ).astype(f32)[:, None]
    outer = own_number("cyl")
    places = jnp.concatenate(
        [
            jnp.arange(8, dtype=jnp.int32) ^ outer,
            jnp.stack([own_number("hx"), mine, own_number("ylh")]),
            lengths,
        ]
    )
    infos = [
        jnp.stack([lengths[s] // 2, block_perm[s, 0], block_perm[s, 1], mine, own_number("ylh")])
        for s in range(seq_count)
    ]
    vectors = jnp.stack(
        [v.astype(f32) for v in (b_out, ln1_gain, ln1_shift, b_down, ln2_gain, ln2_shift, b_out, b_out)]
    )

    arrived, kept = [], []
    for s in range(seq_count):
        near = tokens[s]
        across = exchange_bit(near, "x")
        pieces = [near, exchange_bit(near, "c"), across, exchange_bit(across, "c")]
        contexts, saved = attention_forward(infos[s], pieces, w_t, bias, heads)
        kept.append(saved)
        arrived += [contexts[0]] + [exchange(contexts[r], "seq", r) for r in range(1, seq_parts)]

    (
        out_rows,
        context,
        first_in,
        first_low,
        active,
        slope,
        d_second,
        d_lowered,
        sums_two,
    ) = run_feed_forward(
        places,
        arrived,
        tokens.reshape(flat_rows, features),
        cotangent.reshape(flat_rows, features),
        w_out,
        vectors,
        w_up,
        b_up.astype(f32).reshape(1, hidden),
        w_down,
        dims,
    )
    out_tokens = out_rows.reshape(seq_count, local_rows, features)
    send_down, send_up, b_up_send, d_part = run_back_send(
        places, active, slope, w_up, w_down, first_low, d_lowered, d_second
    )
    came_down = exchange_bit(send_down, "c")
    came_up = exchange_bit(send_up, "c")
    keep_down, keep_up, b_up_keep, d_first_in, sums_one, grad_out, *d_contexts = run_back_keep(
        places, active, slope, w_up, w_down, first_low, d_lowered, d_part, first_in, context, w_out,
        vectors, dims,
    )

    down_y = exchange_bit(sum_low(keep_down[2:], came_down[2:]), "y")
    down_l = exchange_bit(sum_low(keep_down[1], came_down[1], down_y[1]), "l")
    down_own = sum_low(keep_down[0], came_down[0], down_y[0], down_l)
    down_own = add_extra(halve(down_own.reshape(4, hidden // 32, features), "hx"))
    up_l3 = exchange_bit(sum_low(keep_up[3], came_up[3]), "l")
    up_l1 = exchange_bit(sum_low(keep_up[1], came_up[1]), "l")
    up_y = exchange_bit(sum_low(keep_up[2], came_up[2], up_l3), "y")
    up_own = sum_low(keep_up[0], came_up[0], up_l1, up_y)
    up_own = add_extra(halve(up_own.reshape(4, features // 4, hidden // 8), "hx"))
    out_x = exchange_bit(grad_out[2:], "x")
    out_c = exchange_bit(sum_low(grad_out[1], out_x[1]), "c")
    out_own = add_extra(halve(sum_low(grad_out[0], out_x[0], out_c), "ylh"))

    down_pieces = spread([double(down_own, "hx")], "cyl")
    up_first = double(up_own, "hx")
    up_two = exchange_bit(up_first, "y")
    up_four = [up_first, exchange_bit(up_first, "l"), up_two, exchange_bit(up_two, "l")]
    up_pieces = spread(up_four, "c")
    out_pieces = spread([double(out_own, "ylh")], "xc")
    full_down = gather_hidden(places, down_pieces, (hidden, features))
    full_up = gather_hidden(places, up_pieces, (features, hidden))
    full_out = gather_out(places, out_pieces, (features, features))

    half_hidden = jnp.where(
        (outer >= 4), jnp.concatenate([b_up_send, b_up_keep], axis=1),
        jnp.concatenate([b_up_keep, b_up_send], axis=1),
    )
    packed = jnp.concatenate(
        [sums_one[:3].reshape(-1), sums_two[:3].reshape(-1), half_hidden.reshape(-1)]
    )
    packed = sum_all(packed.reshape(-1, 128), ("seq", "dp")).reshape(-1)
    (
        full_b_out,
        full_gain_one,
        full_shift_one,
        full_b_down,
        full_gain_two,
        full_shift_two,
    ) = [packed[i * features : (i + 1) * features] for i in range(6)]
    full_b_up = packed[6 * features :]

    total_w = jnp.zeros((features, 3 * wide), f32)
    total_b = jnp.zeros((3 * wide, 1), f32)
    d_inputs = []
    for s in range(seq_count):
        pieces = d_contexts[s * seq_parts : (s + 1) * seq_parts]
        pieces = pieces[:1] + [exchange(pieces[r], "seq", r) for r in range(1, seq_parts)]
        parts, total_w, part_b = attention_backward(
            infos[s], pieces, w_t, kept[s], total_w, heads, s == seq_count - 1
        )
        total_b = total_b + part_b
        near = parts[0].astype(f32) + exchange_bit(parts[1], "c")
        far = (parts[2].astype(f32) + exchange_bit(parts[3], "c")).astype(jnp.bfloat16)
        d_inputs.append(near + exchange_bit(far, "x"))
    own_pos = mine * local_rows + jnp.arange(local_rows, dtype=jnp.int32)
    live = (own_pos[None, :] < lengths[:, None]).astype(f32)
    grad_tokens = (
        jnp.stack(d_inputs) + d_first_in.reshape(seq_count, local_rows, features)
    ) * live[:, :, None]

    qkv_own = add_extra(halve(total_w, "ylh"))
    full_qkv = gather_heads(
        places, spread([double(qkv_own, "ylh")], "xc"), (features, 3 * features)
    )
    b_all = double(sum_all(total_b.reshape(1, 3 * wide), ("dp",)), "xc")
    b_rows = [
        lax.dynamic_slice_in_dim(b_all, j ^ mine, 1, axis=0).reshape(3 * wide)
        for j in range(seq_parts)
    ]
    full_b_query = jnp.concatenate([row[:wide] for row in b_rows])
    full_b_value = jnp.concatenate([row[2 * wide :] for row in b_rows])
    return (
        out_tokens,
        grad_tokens,
        full_qkv,
        full_b_query,
        full_b_value,
        full_out,
        full_b_out,
        full_gain_one,
        full_shift_one,
        full_up,
        full_b_up,
        full_down,
        full_b_down,
        full_gain_two,
        full_shift_two,
    )


def solution(mesh):
    in_specs = (
        P("dp", "seq", None),
        P("dp", "seq", None),
        P("dp"),
        P("dp", None),
        P(),
        P(),
        P(),
        P(),
        P(),
        P(),
        P(),
        P(),
        P(),
        P(),
        P(),
        P(),
        P(),
    )
    out_specs = (
        P("dp", "seq", None),
        P("dp", "seq", None),
        P(),
        P(),
        P(),
        P(),
        P(),
        P(),
        P(),
        P(),
        P(),
        P(),
        P(),
        P(),
        P(),
    )
    return jax.shard_map(
        per_device, mesh=mesh, in_specs=in_specs, out_specs=out_specs, check_vma=False
    )
```

profile of v0, /device:TPU:0, one launch (start us, length us, event | category | flops | bytes accessed | tf_op | source)
XLA Modules:
  0.0 470.9 jit_solution(1952514121166267092)
XLA Ops:
  9.3 5.7 %collective-permute-done.13.x2 = bf16[256,768]{1,0:T(8,128)(2,1)} collective-permute-done((bf16[256,768]{1,0:T(8,128)(2,1)S(1)}, bf16[256,768]{1,0:T(8,128)(2,1)}, u32[]{:S(2)}, u32[]{:S(2)}) %collective-permute-start.13) | collective-permute-done | bytes 393248 | tf_op jit(solution)/shard_map/ppermute | solution.py:29
  34.4 7.9 %shard_map.282 = (bf16[192,256]{1,0:T(8,128)(2,1)S(1)}, bf16[192,256]{1,0:T(8,128)(2,1)S(1)}, bf16[192,256]{1,0:T(8,128)(2,1)S(1)}, bf16[192,256]{1,0:T(8,128)(2...) custom-call(s32[5]{0:T(128)S(1)} %stack.84.info, ...), custom_call_target="tpu_custom_call" | custom-call | flops 6000000000 | bytes 20971520 | tf_op jit(solution)/shard_map/pallas_call | solution.py:218
  46.1 8.1 %shard_map.281 = (bf16[192,256]{1,0:T(8,128)(2,1)S(1)}, bf16[192,256]{1,0:T(8,128)(2,1)}, bf16[192,256]{1,0:T(8,128)(2,1)S(1)}, bf16[192,256]{1,0:T(8,128)(2,1)}...) custom-call(s32[5]{0:T(128)S(1)} %stack.82.info, ...), custom_call_target="tpu_custom_call" | custom-call | flops 6000000000 | bytes 20971520 | tf_op jit(solution)/shard_map/pallas_call | solution.py:218
  56.6 7.6 %shard_map.280 = (bf16[192,256]{1,0:T(8,128)(2,1)S(1)}, bf16[192,256]{1,0:T(8,128)(2,1)}, bf16[192,256]{1,0:T(8,128)(2,1)}, bf16[192,256]{1,0:T(8,128)(2,1)S(1)}...) custom-call(s32[5]{0:T(128)S(1)} %stack.80.info, ...), custom_call_target="tpu_custom_call" | custom-call | flops 6000000000 | bytes 20971520 | tf_op jit(solution)/shard_map/pallas_call | solution.py:218
  75.6 25.7 %shard_map.283 = (bf16[768,768]{1,0:T(8,128)(2,1)}, bf16[768,768]{1,0:T(8,128)(2,1)S(1)}, f32[768,768]{1,0:T(8,128)}, bf16[768,768]{1,0:T(8,128)(2,1)S(1)}, bf16...) custom-call(s32[14]{0:T(128)S(1)} %concatenate.88.places, ...), custom_call_target="tpu_custom_call" | custom-call | flops 8153726976 | bytes 20971520 | tf_op jit(solution)/shard_map/pallas_call | solution.py:465
  103.6 15.5 %shard_map.284 = (bf16[4,384,768]{2,1,0:T(8,128)(2,1)}, bf16[4,768,384]{2,1,0:T(8,128)(2,1)}, f32[1,1536]{1,0:T(1,128)S(1)}, f32[768,768]{1,0:T(8,128)}) custom-call(s32[14]{0:T(128)S(1)} %concatenate.88.places, bf16[8,768,384]{2,1,0:T(8,128)(2,1)} %get-tuple-element.101.active.refs_0_, bf16[8,768,384]{2,1,0:T(8,128)(2,1)} %get-tuple-element.102.slope.refs_1_, ...), custom_call_target="tpu_custom_call" | custom-call | flops 7247757312 | bytes 20971520 | tf_op jit(solution)/shard_map/pallas_call | solution.py:465
  119.7 21.2 %shard_map.285 = (bf16[4,384,768]{2,1,0:T(8,128)(2,1)}, bf16[4,768,384]{2,1,0:T(8,128)(2,1)}, f32[1,1536]{1,0:T(1,128)S(1)}, f32[768,768]{1,0:T(8,128)}, f32[8,7...) custom-call(s32[14]{0:T(128)S(1)} %concatenate.88.places, ...), custom_call_target="tpu_custom_call" | custom-call | flops 7247757312 | bytes 20971520 | tf_op jit(solution)/shard_map/pallas_call | solution.py:465
  151.0 12.4 %shard_map.286 = (bf16[256,768]{1,0:T(8,128)(2,1)S(1)}, bf16[256,768]{1,0:T(8,128)(2,1)S(1)}, bf16[256,768]{1,0:T(8,128)(2,1)S(1)}, bf16[256,768]{1,0:T(8,128)(2...) custom-call(s32[5]{0:T(128)S(1)} %stack.80.info, bf16[192,256]{1,0:T(8,128)(2,1)S(1)} %get-tuple-element.109.g0, ...), custom_call_target="tpu_custom_call" | custom-call | flops 6000000000 | bytes 20971520 | tf_op jit(solution)/shard_map/pallas_call | solution.py:218
  166.1 12.5 %shard_map.287 = (bf16[256,768]{1,0:T(8,128)(2,1)S(1)}, bf16[256,768]{1,0:T(8,128)(2,1)S(1)}, bf16[256,768]{1,0:T(8,128)(2,1)S(1)}, bf16[256,768]{1,0:T(8,128)(2...) custom-call(s32[5]{0:T(128)S(1)} %stack.82.info, bf16[192,256]{1,0:T(8,128)(2,1)S(1)} %get-tuple-element.121.g0, ...), custom_call_target="tpu_custom_call" | custom-call | flops 6000000000 | bytes 20971520 | tf_op jit(solution)/shard_map/pallas_call | solution.py:218
  179.7 12.1 %shard_map.288 = (bf16[256,768]{1,0:T(8,128)(2,1)S(1)}, bf16[256,768]{1,0:T(8,128)(2,1)S(1)}, bf16[256,768]{1,0:T(8,128)(2,1)S(1)}, bf16[256,768]{1,0:T(8,128)(2...) custom-call(s32[5]{0:T(128)S(1)} %stack.84.info, bf16[192,256]{1,0:T(8,128)(2,1)S(1)} %get-tuple-element.134.g0, ...), custom_call_target="tpu_custom_call" | custom-call | flops 6000000000 | bytes 20971520 | tf_op jit(solution)/shard_map/pallas_call | solution.py:218
  217.2 6.0 %collective-permute-done.37 = bf16[2,96,576]{2,1,0:T(8,128)(2,1)S(1)} collective-permute-done((bf16[2,96,576]{2,1,0:T(8,128)(2,1)S(1)}, bf16[2,96,576]{2,1,0:T(8,128)(2,1)S(1)}, u32[]{:S(2)}, u32[]{:S(2)}) %collective-permute-start.37) | collective-permute-done | bytes 221216 | tf_op jit(solution)/shard_map/ppermute | solution.py:29
  236.4 11.5 %collective-permute-done.39 = bf16[1,96,576]{2,1,0:T(8,128)(2,1)S(1)} collective-permute-done((bf16[1,96,576]{2,1,0:T(8,128)(2,1)S(1)}, bf16[1,96,576]{2,1,0:T(8,128)(2,1)S(1)}, u32[]{:S(2)}, u32[]{:S(2)}) %collective-permute-start.39) | collective-permute-done | bytes 110624 | tf_op jit(solution)/shard_map/ppermute | solution.py:29
  265.4 9.9 %collective-permute-done.40 = bf16[2,96,576]{2,1,0:T(8,128)(2,1)S(1)} collective-permute-done((bf16[2,96,576]{2,1,0:T(8,128)(2,1)S(1)}, bf16[2,96,576]{2,1,0:T(8,128)(2,1)S(1)}, u32[]{:S(2)}, u32[]{:S(2)}) %collective-permute-start.40) | collective-permute-done | bytes 221216 | tf_op jit(solution)/shard_map/ppermute | solution.py:29
  282.4 6.4 %collective-permute-done.83 = bf16[384,768]{1,0:T(8,128)(2,1)S(1)} collective-permute-done((bf16[384,768]{1,0:T(8,128)(2,1)S(1)}, bf16[384,768]{1,0:T(8,128)(2,1)S(1)}, u32[]{:S(2)}, u32[]{:S(2)}) %collective-permute-start.83) | collective-permute-done | bytes 589856 | tf_op jit(solution)/shard_map/ppermute | solution.py:29
  295.2 13.2 %collective-permute-done.70 = bf16[2,192,384]{2,1,0:T(8,128)(2,1)S(1)} collective-permute-done((bf16[2,192,384]{2,1,0:T(8,128)(2,1)S(1)}, bf16[2,192,384]{2,1,0:T(8,128)(2,1)S(1)}, u32[]{:S(2)}, u32[]{:S(2)}) %collective-permute-start.70) | collective-permute-done | bytes 294944 | tf_op jit(solution)/shard_map/ppermute | solution.py:29
  330.1 17.4 %collective-permute-done.72 = bf16[1,192,384]{2,1,0:T(8,128)(2,1)S(1)} collective-permute-done((bf16[1,192,384]{2,1,0:T(8,128)(2,1)S(1)}, bf16[1,192,384]{2,1,0:T(8,128)(2,1)S(1)}, u32[]{:S(2)}, u32[]{:S(2)}) %collective-permute-start.72) | collective-permute-done | bytes 147488 | tf_op jit(solution)/shard_map/ppermute | solution.py:29
  357.3 14.6 %collective-permute-done.73 = bf16[2,192,384]{2,1,0:T(8,128)(2,1)} collective-permute-done((bf16[2,192,384]{2,1,0:T(8,128)(2,1)}, bf16[2,192,384]{2,1,0:T(8,128)(2,1)}, u32[]{:S(2)}, u32[]{:S(2)}) %collective-permute-start.73) | collective-permute-done | bytes 294944 | tf_op jit(solution)/shard_map/ppermute | solution.py:29
  387.7 5.6 %collective-permute-done.60.refs_3_ = bf16[8,48,384]{2,1,0:T(8,128)(2,1)S(1)} collective-permute-done((bf16[8,48,384]{2,1,0:T(8,128)(2,1)}, bf16[8,48,384]{2,1,0:T(8,128)(2,1)S(1)}, u32[]{:S(2)}, u32[]{:S(2)}) %collective-permute-start.60) | collective-permute-done | bytes 294944 | tf_op jit(solution)/shard_map/ppermute | solution.py:29
  397.6 14.6 %collective-permute-done.44.refs_3_ = bf16[8,96,576]{2,1,0:T(8,128)(2,1)} collective-permute-done((bf16[8,96,576]{2,1,0:T(8,128)(2,1)S(1)}, bf16[8,96,576]{2,1,0:T(8,128)(2,1)}, u32[]{:S(2)}, u32[]{:S(2)}) %collective-permute-start.44) | collective-permute-done | bytes 884768 | tf_op jit(solution)/shard_map/ppermute | solution.py:29
  417.1 6.6 %collective-permute-done.76.refs_3_ = bf16[4,192,384]{2,1,0:T(8,128)(2,1)S(1)} collective-permute-done((bf16[4,192,384]{2,1,0:T(8,128)(2,1)}, bf16[4,192,384]{2,1,0:T(8,128)(2,1)S(1)}, u32[]{:S(2)}, u32[]{:S(2)}) %collective-permute-start.76) | collective-permute-done | bytes 589856 | tf_op jit(solution)/shard_map/ppermute | solution.py:29
  428.8 12.0 %collective-permute-done.90.refs_3_ = bf16[4,96,768]{2,1,0:T(8,128)(2,1)S(1)} collective-permute-done((bf16[4,96,768]{2,1,0:T(8,128)(2,1)}, bf16[4,96,768]{2,1,0:T(8,128)(2,1)S(1)}, u32[]{:S(2)}, u32[]{:S(2)}) %collective-permute-start.90) | collective-permute-done | bytes 589856 | tf_op jit(solution)/shard_map/ppermute | solution.py:29
  447.1 7.8 %shard_map.289 = f32[768,2304]{1,0:T(8,128)} custom-call(s32[14]{0:T(128)S(1)} %concatenate.88.places, bf16[8,96,576]{2,1,0:T(8,128)(2,1)S(1)} %pad_maximum_fusion.refs_0_, bf16[8,96,576]{2,1,0:T(8,128)(2,1)S(1)} %collective-permute-done.42.refs_1_, bf16[8,96,576]{2,1,0:T(8,128)(2,1)} %collective-permute-done.43.refs_2_, ...), custom_call_target="tpu_custom_call" | custom-call | flops 1000 | bytes 20971520 | tf_op jit(solution)/shard_map/pallas_call | solution.py:465
  455.0 7.2 %shard_map.291 = f32[768,3072]{1,0:T(8,128)} custom-call(s32[14]{0:T(128)S(1)} %concatenate.88.places, bf16[4,192,384]{2,1,0:T(8,128)(2,1)S(1)} %pad_maximum_fusion.1.refs_0_, bf16[4,192,384]{2,1,0:T(8,128)(2,1)} %collective-permute-done.74.refs_1_, bf16[4,192,384]{2,1,0:T(8,128)(2,1)} %collective-permute-done.75.refs_2_, ...), custom_call_target="tpu_custom_call" | custom-call | flops 589824 | bytes 20971520 | tf_op jit(solution)/shard_map/pallas_call | solution.py:465
  463.8 6.8 %shard_map.292 = f32[3072,768]{1,0:T(8,128)} custom-call(s32[14]{0:T(128)S(1)} %concatenate.88.places, bf16[4,96,768]{2,1,0:T(8,128)(2,1)S(1)} %pad_maximum_fusion.2.refs_0_, bf16[4,96,768]{2,1,0:T(8,128)(2,1)} %collective-permute-done.88.refs_1_, bf16[4,96,768]{2,1,0:T(8,128)(2,1)S(1)} %collective-permute-done.89.refs_2_, ...), custom_call_target="tpu_custom_call" | custom-call | flops 589824 | bytes 20971520 | tf_op jit(solution)/shard_map/pallas_call | solution.py:465
  (387 shorter events, 192.8 us)
Async XLA Ops:
  5.0 28.3 %collective-permute-start.12 = (bf16[256,768]{1,0:T(8,128)(2,1)S(1)}, bf16[256,768]{1,0:T(8,128)(2,1)}, u32[]{:S(2)}, u32[]{:S(2)}) collective-permute-start(bf16[256,768]{1,0:T(8,128)(2,1)S(1)} %get-tuple-element.166.x0), channel_id=1, source_target_pairs={{0,1},{1,0},{2,3},{3,2},{4,5},{5,4},{6,7},{7,6},{8,9},{9,8},{10,11... | collective-permute-start | bytes 1179656 | tf_op jit(solution)/shard_map/ppermute | solution.py:29
  5.0 28.9 %collective-permute-start.7 = (bf16[256,768]{1,0:T(8,128)(2,1)S(1)}, bf16[256,768]{1,0:T(8,128)(2,1)S(1)}, u32[]{:S(2)}, u32[]{:S(2)}) collective-permute-start(bf16[256,768]{1,0:T(8,128)(2,1)S(1)} %get-tuple-element.167.x0), channel_id=1, source_target_pairs={{0,2},{1,3},{2,0},{3,1},{4,6},{5,7},{6,4},{7,5},{8,10},{9,11},{10,... | collective-permute-start | bytes 1179656 | tf_op jit(solution)/shard_map/ppermute | solution.py:29
  5.1 38.8 %collective-permute-start.6 = (bf16[256,768]{1,0:T(8,128)(2,1)S(1)}, bf16[256,768]{1,0:T(8,128)(2,1)}, u32[]{:S(2)}, u32[]{:S(2)}) collective-permute-start(bf16[256,768]{1,0:T(8,128)(2,1)S(1)} %get-tuple-element.167.x0), channel_id=1, source_target_pairs={{0,1},{1,0},{2,3},{3,2},{4,5},{5,4},{6,7},{7,6},{8,9},{9,8},{10,11... | collective-permute-start | bytes 1179656 | tf_op jit(solution)/shard_map/ppermute | solution.py:29
  5.5 28.5 %collective-permute-start.1 = (bf16[256,768]{1,0:T(8,128)(2,1)S(1)}, bf16[256,768]{1,0:T(8,128)(2,1)S(1)}, u32[]{:S(2)}, u32[]{:S(2)}) collective-permute-start(bf16[256,768]{1,0:T(8,128)(2,1)S(1)} %get-tuple-element.168.x0), channel_id=1, source_target_pairs={{0,2},{1,3},{2,0},{3,1},{4,6},{5,7},{6,4},{7,5},{8,10},{9,11},{10,... | collective-permute-start | bytes 1179656 | tf_op jit(solution)/shard_map/ppermute | solution.py:29
  119.2 108.1 %collective-permute-start.81 = (bf16[4,384,768]{2,1,0:T(8,128)(2,1)}, bf16[4,384,768]{2,1,0:T(8,128)(2,1)}, u32[]{:S(2)}, u32[]{:S(2)}) collective-permute-start(bf16[4,384,768]{2,1,0:T(8,128)(2,1)} %get-tuple-element.160), channel_id=1, source_target_pairs={{0,1},{1,0},{2,3},{3,2},{4,5},{5,4},{6,7},{7,6},{8,9},{9,8},{10,11... | collective-permute-start | bytes 7077896 | tf_op jit(solution)/shard_map/ppermute | solution.py:29
  119.5 111.1 %collective-permute-start.66 = (bf16[4,768,384]{2,1,0:T(8,128)(2,1)}, bf16[4,768,384]{2,1,0:T(8,128)(2,1)}, u32[]{:S(2)}, u32[]{:S(2)}) collective-permute-start(bf16[4,768,384]{2,1,0:T(8,128)(2,1)} %get-tuple-element.158), channel_id=1, source_target_pairs={{0,1},{1,0},{2,3},{3,2},{4,5},{5,4},{6,7},{7,6},{8,9},{9,8},{10,11... | collective-permute-start | bytes 7077896 | tf_op jit(solution)/shard_map/ppermute | solution.py:29
  214.6 78.8 %collective-permute-start.28 = (bf16[256,768]{1,0:T(8,128)(2,1)S(1)}, bf16[256,768]{1,0:T(8,128)(2,1)S(1)}, u32[]{:S(2)}, u32[]{:S(2)}) collective-permute-start(bf16[256,768]{1,0:T(8,128)(2,1)S(1)} %get-tuple-element.133), channel_id=1, source_target_pairs={{0,1},{1,0},{2,3},{3,2},{4,5},{5,4},{6,7},{7,6},{8,9},{9,8},{10,11... | collective-permute-start | bytes 1179656 | tf_op jit(solution)/shard_map/ppermute | solution.py:29
  223.2 70.0 %collective-permute-start.49 = (f32[2,576]{1,0:T(2,128)S(1)}, f32[2,576]{1,0:T(2,128)S(1)}, u32[]{:S(2)}, u32[]{:S(2)}) collective-permute-start(f32[2,576]{1,0:T(2,128)S(1)} %pad_maximum_fusion.11), channel_id=1, source_target_pairs={{0,2},{1,3},{2,0},{3,1},{4,6},{5,7},{6,4},{7,5},{8,10},{9,11},{10,... | collective-permute-start | bytes 13832 | tf_op jit(solution)/shard_map/ppermute | solution.py:29
  230.7 30.7 %collective-permute-start.82 = (bf16[2,384,768]{2,1,0:T(8,128)(2,1)S(1)}, bf16[2,384,768]{2,1,0:T(8,128)(2,1)S(1)}, u32[]{:S(2)}, u32[]{:S(2)}) collective-permute-start(bf16[2,384,768]{2,1,0:T(8,128)(2,1)S(1)} %add_convert_fusion), channel_id=1, source_target_pairs={{0,4},{4,0},{8,12},{12,8},{16,20},{20,16},{24,28},{28,24},{1,5},{5... | collective-permute-start | bytes 3538952 | tf_op jit(solution)/shard_map/ppermute | solution.py:29
  279.4 35.0 %collective-permute-start.41 = (bf16[4,96,576]{2,1,0:T(8,128)(2,1)S(1)}, bf16[4,96,576]{2,1,0:T(8,128)(2,1)S(1)}, u32[]{:S(2)}, u32[]{:S(2)}) collective-permute-start(bf16[4,96,576]{2,1,0:T(8,128)(2,1)S(1)} %pad_maximum_fusion.3), channel_id=1, source_target_pairs={{0,4},{4,0},{8,12},{12,8},{16,20},{20,16},{24,28},{28,24},{1,5},{5... | collective-permute-start | bytes 1327112 | tf_op jit(solution)/shard_map/ppermute | solution.py:29
  316.5 40.1 %collective-permute-start.42 = (bf16[8,96,576]{2,1,0:T(8,128)(2,1)S(1)}, bf16[8,96,576]{2,1,0:T(8,128)(2,1)S(1)}, u32[]{:S(2)}, u32[]{:S(2)}) collective-permute-start(bf16[8,96,576]{2,1,0:T(8,128)(2,1)S(1)} %pad_maximum_fusion.refs_0_), channel_id=1, source_target_pairs={{0,1},{1,0},{2,3},{3,2},{4,5},{5,4},{6,7},{7,6},{8,9},{9,8},{10,11... | collective-permute-start | bytes 2654216 | tf_op jit(solution)/shard_map/ppermute | solution.py:29
  322.0 27.5 %collective-permute-start.23 = (bf16[256,768]{1,0:T(8,128)(2,1)S(1)}, bf16[256,768]{1,0:T(8,128)(2,1)S(1)}, u32[]{:S(2)}, u32[]{:S(2)}) collective-permute-start(bf16[256,768]{1,0:T(8,128)(2,1)S(1)} %add_convert_fusion.6), channel_id=1, source_target_pairs={{0,2},{1,3},{2,0},{3,1},{4,6},{5,7},{6,4},{7,5},{8,10},{9,11},{10,... | collective-permute-start | bytes 1179656 | tf_op jit(solution)/shard_map/ppermute | solution.py:29
  322.8 28.6 %collective-permute-start.29 = (bf16[256,768]{1,0:T(8,128)(2,1)S(1)}, bf16[256,768]{1,0:T(8,128)(2,1)S(1)}, u32[]{:S(2)}, u32[]{:S(2)}) collective-permute-start(bf16[256,768]{1,0:T(8,128)(2,1)S(1)} %add_convert_fusion.5), channel_id=1, source_target_pairs={{0,2},{1,3},{2,0},{3,1},{4,6},{5,7},{6,4},{7,5},{8,10},{9,11},{10,... | collective-permute-start | bytes 1179656 | tf_op jit(solution)/shard_map/ppermute | solution.py:29
  347.5 46.5 %collective-permute-start.43 = (bf16[8,96,576]{2,1,0:T(8,128)(2,1)S(1)}, bf16[8,96,576]{2,1,0:T(8,128)(2,1)}, u32[]{:S(2)}, u32[]{:S(2)}) collective-permute-start(bf16[8,96,576]{2,1,0:T(8,128)(2,1)S(1)} %pad_maximum_fusion.refs_0_), channel_id=1, source_target_pairs={{0,2},{1,3},{2,0},{3,1},{4,6},{5,7},{6,4},{7,5},{8,10},{9,11},{10,... | collective-permute-start | bytes 2654216 | tf_op jit(solution)/shard_map/ppermute | solution.py:29
  351.4 26.7 %collective-permute-start.87 = (bf16[2,96,768]{2,1,0:T(8,128)(2,1)}, bf16[2,96,768]{2,1,0:T(8,128)(2,1)}, u32[]{:S(2)}, u32[]{:S(2)}) collective-permute-start(bf16[2,96,768]{2,1,0:T(8,128)(2,1)} %pad_maximum_fusion.6), channel_id=1, source_target_pairs={{0,16},{4,20},{8,24},{12,28},{16,0},{20,4},{24,8},{28,12},{1,17},{... | collective-permute-start | bytes 884744 | tf_op jit(solution)/shard_map/ppermute | solution.py:29
  355.2 25.5 %collective-permute-start.35 = (bf16[256,768]{1,0:T(8,128)(2,1)}, bf16[256,768]{1,0:T(8,128)(2,1)}, u32[]{:S(2)}, u32[]{:S(2)}) collective-permute-start(bf16[256,768]{1,0:T(8,128)(2,1)} %add_convert_fusion.4), channel_id=1, source_target_pairs={{0,2},{1,3},{2,0},{3,1},{4,6},{5,7},{6,4},{7,5},{8,10},{9,11},{10,... | collective-permute-start | bytes 1179656 | tf_op jit(solution)/shard_map/ppermute | solution.py:29
  356.5 30.4 %collective-permute-start.59 = (bf16[8,48,384]{2,1,0:T(8,128)(2,1)S(1)}, bf16[8,48,384]{2,1,0:T(8,128)(2,1)S(1)}, u32[]{:S(2)}, u32[]{:S(2)}) collective-permute-start(bf16[8,48,384]{2,1,0:T(8,128)(2,1)S(1)} %pad_maximum_fusion.4.refs_0_), channel_id=1, source_target_pairs={{0,2},{1,3},{2,0},{3,1},{4,6},{5,7},{6,4},{7,5},{8,10},{9,11},{10,... | collective-permute-start | bytes 884744 | tf_op jit(solution)/shard_map/ppermute | solution.py:29
  378.1 34.0 %collective-permute-start.44 = (bf16[8,96,576]{2,1,0:T(8,128)(2,1)S(1)}, bf16[8,96,576]{2,1,0:T(8,128)(2,1)}, u32[]{:S(2)}, u32[]{:S(2)}) collective-permute-start(bf16[8,96,576]{2,1,0:T(8,128)(2,1)S(1)} %collective-permute-done.42.refs_1_), channel_id=1, source_target_pairs={{0,2},{1,3},{2,0},{3,1},{4,6},{5,7},{6,4},{7,5},{8,10},{9,11},{10,... | collective-permute-start | bytes 2654216 | tf_op jit(solution)/shard_map/ppermute | solution.py:29
  395.5 28.2 %collective-permute-start.76 = (bf16[4,192,384]{2,1,0:T(8,128)(2,1)}, bf16[4,192,384]{2,1,0:T(8,128)(2,1)S(1)}, u32[]{:S(2)}, u32[]{:S(2)}) collective-permute-start(bf16[4,192,384]{2,1,0:T(8,128)(2,1)} %collective-permute-done.75.refs_2_), channel_id=1, source_target_pairs={{0,8},{4,12},{8,0},{12,4},{16,24},{20,28},{24,16},{28,20},{1,9},{5... | collective-permute-start | bytes 1769480 | tf_op jit(solution)/shard_map/ppermute | solution.py:29
  414.6 26.2 %collective-permute-start.90 = (bf16[4,96,768]{2,1,0:T(8,128)(2,1)}, bf16[4,96,768]{2,1,0:T(8,128)(2,1)S(1)}, u32[]{:S(2)}, u32[]{:S(2)}) collective-permute-start(bf16[4,96,768]{2,1,0:T(8,128)(2,1)} %collective-permute-done.88.refs_1_), channel_id=1, source_target_pairs={{0,4},{4,0},{8,12},{12,8},{16,20},{20,16},{24,28},{28,24},{1,5},{5... | collective-permute-start | bytes 1769480 | tf_op jit(solution)/shard_map/ppermute | solution.py:29
  423.7 38.4 %collective-permute-start.91 = (bf16[4,96,768]{2,1,0:T(8,128)(2,1)S(1)}, bf16[4,96,768]{2,1,0:T(8,128)(2,1)S(1)}, u32[]{:S(2)}, u32[]{:S(2)}) collective-permute-start(bf16[4,96,768]{2,1,0:T(8,128)(2,1)S(1)} %pad_maximum_fusion.2.refs_0_), channel_id=1, source_target_pairs={{0,1},{1,0},{2,3},{3,2},{4,5},{5,4},{6,7},{7,6},{8,9},{9,8},{10,11... | collective-permute-start | bytes 1769480 | tf_op jit(solution)/shard_map/ppermute | solution.py:29
  423.7 31.2 %collective-permute-start.80 = (bf16[4,192,384]{2,1,0:T(8,128)(2,1)S(1)}, bf16[4,192,384]{2,1,0:T(8,128)(2,1)}, u32[]{:S(2)}, u32[]{:S(2)}) collective-permute-start(bf16[4,192,384]{2,1,0:T(8,128)(2,1)S(1)} %collective-permute-done.76.refs_3_), channel_id=1, source_target_pairs={{0,1},{1,0},{2,3},{3,2},{4,5},{5,4},{6,7},{7,6},{8,9},{9,8},{10,11... | collective-permute-start | bytes 1769480 | tf_op jit(solution)/shard_map/ppermute | solution.py:29
  424.3 37.9 %collective-permute-start.92 = (bf16[4,96,768]{2,1,0:T(8,128)(2,1)}, bf16[4,96,768]{2,1,0:T(8,128)(2,1)S(1)}, u32[]{:S(2)}, u32[]{:S(2)}) collective-permute-start(bf16[4,96,768]{2,1,0:T(8,128)(2,1)} %collective-permute-done.88.refs_1_), channel_id=1, source_target_pairs={{0,1},{1,0},{2,3},{3,2},{4,5},{5,4},{6,7},{7,6},{8,9},{9,8},{10,11... | collective-permute-start | bytes 1769480 | tf_op jit(solution)/shard_map/ppermute | solution.py:29
  428.8 33.3 %collective-permute-start.93 = (bf16[4,96,768]{2,1,0:T(8,128)(2,1)S(1)}, bf16[4,96,768]{2,1,0:T(8,128)(2,1)S(1)}, u32[]{:S(2)}, u32[]{:S(2)}) collective-permute-start(bf16[4,96,768]{2,1,0:T(8,128)(2,1)S(1)} %collective-permute-done.89.refs_2_), channel_id=1, source_target_pairs={{0,1},{1,0},{2,3},{3,2},{4,5},{5,4},{6,7},{7,6},{8,9},{9,8},{10,11... | collective-permute-start | bytes 1769480 | tf_op jit(solution)/shard_map/ppermute | solution.py:29
  (123 other events, 1580.4 us)
where the time goes:
time: 476 us; the launch traced here: 471 us
  waiting for transfers between devices  172 us (36%)
  Pallas kernels  148 us (31%)
  starting transfers between devices  90.2 us (19%)
  local copies, waits for them, and re-layouts  29.6 us (6%)
  other arithmetic  21.1 us (4%)
  between operations  9.7 us (2%)
    ppermute x95, waiting for transfers between devices, exchange(): lax.ppermute(array_in, axis, [(i, i ^ flip) for i in range(lax.axis_size(...  172 us
    ppermute x95, starting transfers between devices, exchange(): lax.ppermute(array_in, axis, [(i, i ^ flip) for i in range(lax.axis_size(...  90.2 us
    pallas_call x7, Pallas kernels, step_call(): pl.pallas_call(body, out_shape=outs, grid_spec=pltpu.PrefetchScalarGridSp...  87.7 us
    pallas_call x6, Pallas kernels, kernel_call(): pl.pallas_call(body, out_shape=outs, in_specs=[pl.BlockSpec(memory_space=...  60.6 us
    unnamed x107, local copies, waits for them, and re-layouts  15 us
  transfers between devices with their start and end apart: 95, of which 32 were waited for; matrix products, arithmetic and copies ran while one was open for 8% of the time, Pallas kernels for 21%

commit v1 on v0

--- a/solution.py
+++ b/solution.py
@@ -41,32 +41,6 @@
 def add_extra(array_in):
     for flip in extra_flips("dp", 3):
         array_in = array_in + exchange(array_in, "dp", flip)
-    return array_in
-
-
-def halve(array_in, order):
-    for letter in order:
-        half = array_in.shape[0] // 2
-        array_in = array_in[:half] + exchange_bit(array_in[half:], letter)
-    return array_in
-
-
-def double(array_in, order):
-    for letter in reversed(order):
-        array_in = jnp.concatenate([array_in, exchange_bit(array_in, letter)])
-    return array_in
-
-
-def spread(pieces, order):
-    for letter in reversed(order):
-        pieces = pieces + [exchange_bit(piece, letter) for piece in pieces]
-    return pieces
-
-
-def sum_all(array_in, axes):
-    for axis in axes:
-        for flip in extra_flips(axis, 0):
-            array_in = array_in + exchange(array_in, axis, flip)
     return array_in
 
 
@@ -149,16 +123,17 @@
 
 
 def attend_backward(
-    heads, last, info, g0, g1, g2, g3, w_t, qkv, ctx_blk, lse, x_t, acc, dx0, dx1, dx2, dx3, grad_w, grad_b,
-    g_tok, g_blk, d_qkv, dx_s,
+    heads, index, info, g0, g1, g2, g3, w_t, qkv, ctx_blk, lse, x_t, acc, *refs
 ):
+    last = len(refs) == 11
+    (dx0, dx1, dx2, dx3, grad_w, grad_b, g_tok, g_blk, d_qkv, dx_s) = refs[-10:]
     half, mine = info[0], info[3]
-    quarter = g0.shape[1]
+    quarter = g0.shape[2]
     block = 2 * quarter
     whole = 4 * quarter
     wide = heads * HEAD_DIM
-    for r, piece in enumerate((g0, g1, g2, g3)):
-        g_tok[r ^ mine] = piece[...]
+    for r, piece in enumerate((g0[index], g1[index], g2[0, index], g3[index])):
+        g_tok[r ^ mine] = piece
     shift = shift_matrix(half, block, whole)
     lane = lax.broadcasted_iota(jnp.int32, (1, block), 1)
     g_all = jnp.concatenate([g_tok[j] for j in range(4)], axis=1)
@@ -197,7 +172,8 @@
     if last:
         tile = grad_w.shape[1]
         for q in range(8):
-            grad_w[q ^ info[4]] = total[q * tile : (q + 1) * tile].astype(jnp.bfloat16)
+            grad_w[q ^ info[4], :, : 3 * wide] = total[q * tile : (q + 1) * tile].astype(jnp.bfloat16)
+        grad_w[:, :, 3 * wide :] = refs[0][...]
     else:
         grad_w[...] = total
     grad_b[...] = jnp.sum(early.astype(jnp.float32), axis=1, keepdims=True) + jnp.sum(
@@ -251,15 +227,15 @@
     return found[:4], found[4:]
 
 
-def attention_backward(info, pieces, w_t, kept, acc, heads, last):
-    wide, quarter = pieces[0].shape
+def attention_backward(info, pieces, index, w_t, kept, acc, heads, out_own=None):
+    _, wide, quarter = pieces[0].shape
     features = w_t.shape[1]
     block = 2 * quarter
     out = jax.ShapeDtypeStruct
     outs = [out((quarter, features), jnp.bfloat16)] * 4 + [
-        out((8, features // 8, 3 * wide), jnp.bfloat16)
-        if last
-        else out((features, 3 * wide), jnp.float32),
+        out((features, 3 * wide), jnp.float32)
+        if out_own is None
+        else out((8, features // 8, 4 * wide), jnp.bfloat16),
         out((3 * wide, 1), jnp.float32),
     ]
     scratch = [
@@ -269,9 +245,9 @@
         pltpu.VMEM((4, quarter, features), jnp.bfloat16),
     ]
     found = kernel_call(
-        functools.partial(attend_backward, heads, last),
+        functools.partial(attend_backward, heads, index),
         info,
-        [*pieces, w_t, *kept, acc],
+        [*pieces, w_t, *kept, acc] + ([] if out_own is None else [out_own]),
         outs,
         scratch,
     )
@@ -413,8 +389,8 @@
     active, slope, w_up, w_down, first_low, d_lowered, d_part = refs[:7]
     first_in, context, w_out, vectors = refs[7:11]
     grad_down, grad_up, grad_b, d_first_in, sums, grad_out = refs[11:17]
-    pieces = refs[17 : 17 + seq_count * seq_parts]
-    first_t, d_first, turned = refs[17 + seq_count * seq_parts :]
+    pieces = refs[17:-3]
+    first_t, d_first, turned = refs[-3:]
     step = pl.program_id(0)
     f32 = jnp.float32
 
@@ -445,7 +421,12 @@
         for r in range(seq_parts):
             own = turned[pl.ds(pl.multiple_of((r ^ mine) * wide, wide), wide), :]
             for s in range(seq_count):
-                pieces[s * seq_parts + r][...] = own[:, s * local_rows : (s + 1) * local_rows]
+                target, place = pieces[3 * min(s, 1) + min(r, 2)], max(s - 1, 0)
+                columns = own[:, s * local_rows : (s + 1) * local_rows]
+                if r < 2:
+                    target[place] = columns
+                else:
+                    target[r - 2, place] = columns
         product = dot_f32(context[...], low, NN).astype(jnp.bfloat16)
         block_rows, block_cols = grad_out.shape[2:]
         across = features // block_cols
@@ -573,8 +554,10 @@
     square = (rows, features)
     turned = (features, rows)
     piece = (features // seq_parts, rows // seq_count)
-    count = seq_count * seq_parts
-    out_blocks = (seq_parts, 8, features // seq_parts // 4, features // 2)
+    pieces = []
+    for n in (1, seq_count - 1):
+        pieces += [(n, *piece), (n, *piece), (2, n, *piece)]
+    out_blocks = (seq_parts, 8, features // seq_parts // 2, features // 4)
     ins, outs = back_specs(0, rows, features, tile)
     return step_call(
         functools.partial(back_keep, (seq_count, seq_parts, steps)),
@@ -592,36 +575,38 @@
             out((8, features), f32),
             out(out_blocks, bf16),
         ]
-        + [out(piece, bf16)] * count,
+        + [out(p, bf16) for p in pieces],
         outs
         + [whole_spec(square), whole_spec((8, features)), whole_spec(out_blocks)]
-        + [whole_spec(piece)] * count,
+        + [whole_spec(p) for p in pieces],
         [pltpu.VMEM(turned, bf16), pltpu.VMEM(square, f32), pltpu.VMEM(turned, bf16)],
         8 * rows * features * steps * tile,
     )
 
 
-def place_rows(places, *refs):
-    pieces, out = refs[:8], refs[8]
+def place_rows(by_rows, places, *refs):
+    pieces, out = refs[:4], refs[4]
     step = pl.program_id(0)
-    for k, piece in enumerate(pieces):
+    tile = pieces[0].shape[1]
+    for k in range(8):
+        c, y, l = k >> 2, (k >> 1) & 1, k & 1
 
         @pl.when(step == k)
         def copy():
-            tile = piece.shape[1]
             for q in range(4):
-                out[pl.ds(pl.multiple_of((q ^ places[8]) * tile, tile), tile), :] = piece[q].astype(
-                    jnp.float32
-                )
-
-
-def gather_hidden(places, pieces, shape):
+                h, x = q >> 1, q & 1
+                piece, sub = (c * 2 + y, l * 4 + x * 2 + h) if by_rows else (c * 2 + l, x * 4 + y * 2 + h)
+                out[pl.ds(pl.multiple_of((q ^ places[8]) * tile, tile), tile), :] = pieces[piece][
+                    sub
+                ].astype(jnp.float32)
+
+
+def gather_hidden(places, pieces, shape, by_rows):
     _, rows, cols = pieces[0].shape
-    by_rows = shape[1] == cols
     block = (4 * rows, cols)
     index = (lambda p, places: (places[p], 0)) if by_rows else (lambda p, places: (0, places[p]))
     return step_call(
-        place_rows,
+        functools.partial(place_rows, by_rows),
         places,
         8,
         pieces,
@@ -633,65 +618,44 @@
     )
 
 
-def place_blocks(places, *refs):
-    pieces, out = refs[:-1], refs[-1]
-    mine, inner = places[9], places[10]
-    step = pl.program_id(0)
-    block_rows, block_cols = pieces[0].shape[1:]
-    across = out.shape[1] // block_cols
-    for k, piece in enumerate(pieces):
-
-        @pl.when(step == k)
-        def copy():
-            for q in range(piece.shape[0]):
-                row, col = q // across * block_rows, q % across * block_cols
-                out[row : row + block_rows, col : col + block_cols] = piece[q ^ inner].astype(
-                    jnp.float32
-                )
-
-
-def gather_out(places, pieces, shape):
-    wide = shape[0] // len(pieces)
-    return step_call(
-        place_blocks,
-        places,
-        len(pieces),
-        pieces,
-        [whole_spec(p.shape) for p in pieces],
-        jax.ShapeDtypeStruct(shape, jnp.float32),
-        pl.BlockSpec((wide, shape[1]), lambda p, places: (p ^ places[9], 0)),
-        [],
-        1000,
-    )
-
-
 def place_heads(places, *refs):
-    pieces, out = refs[:-1], refs[-1]
+    pieces, out, out_w = refs[:-2], refs[-2], refs[-1]
     mine, inner = places[9], places[10]
     seq_parts = len(pieces)
     step = pl.program_id(0)
-    wide = pieces[0].shape[2] // 3
+    wide = out_w.shape[0] // seq_parts
     for r, piece in enumerate(pieces):
         for j in range(seq_parts):
 
             @pl.when((r ^ mine) == j)
             def copy():
-                rows = piece[step ^ inner].astype(jnp.float32)
+                rows = piece[step ^ inner, :, : 3 * wide].astype(jnp.float32)
                 for k in range(3):
                     start = (k * seq_parts + j) * wide
                     out[:, start : start + wide] = rows[:, k * wide : (k + 1) * wide]
 
+        @pl.when(step == r)
+        def copy_out():
+            tile, width = wide // 2, out_w.shape[1] // 4
+            for q in range(8):
+                row = pl.multiple_of((r ^ mine) * wide + q // 4 * tile, tile)
+                col = q % 4 * width
+                out_w[pl.ds(row, tile), col : col + width] = piece[
+                    q ^ inner, :, 3 * wide :
+                ].astype(jnp.float32)
+
 
 def gather_heads(places, pieces, shape):
     rows = pieces[0].shape[1]
+    square = (shape[0], shape[0])
     return step_call(
         place_heads,
         places,
         8,
         pieces,
         [whole_spec(p.shape) for p in pieces],
-        jax.ShapeDtypeStruct(shape, jnp.float32),
-        pl.BlockSpec((rows, shape[1]), lambda p, places: (p, 0)),
+        [jax.ShapeDtypeStruct(shape, jnp.float32), jax.ShapeDtypeStruct(square, jnp.float32)],
+        [pl.BlockSpec((rows, shape[1]), lambda p, places: (p, 0)), whole_spec(square)],
         [],
         1000,
     )
@@ -799,37 +763,111 @@
         vectors, dims,
     )
 
-    down_y = exchange_bit(sum_low(keep_down[2:], came_down[2:]), "y")
-    down_l = exchange_bit(sum_low(keep_down[1], came_down[1], down_y[1]), "l")
+    half_hidden = jnp.where(
+        (outer >= 4),
+        jnp.concatenate([b_up_send, b_up_keep], axis=1),
+        jnp.concatenate([b_up_keep, b_up_send], axis=1),
+    )
+    sums = jnp.concatenate(
+        [sums_one[:3].reshape(-1), sums_two[:3].reshape(-1), half_hidden.reshape(-1)]
+    ).reshape(-1, 128)
+    first_group, second_group = [
+        [own, exchange_bit(near, "c"), exchange_bit(pair, "x")]
+        for own, near, pair in (d_contexts[:3], d_contexts[3:])
+    ]
+    for group in (first_group, second_group):
+        group.append(exchange_bit(group[2][1], "c"))
+    total_w = jnp.zeros((features, 3 * wide), f32)
+    total_b = jnp.zeros((3 * wide, 1), f32)
+    parts = []
+
+    def attend(s, group, total_w, total_b, out_own=None):
+        found, total_w, part_b = attention_backward(
+            infos[s], group, max(s - 1, 0), w_t, kept[s], total_w, heads, out_own
+        )
+        parts.append(found)
+        return total_w, total_b + part_b
+
+    sends = [
+        sum_low(keep_down[2:], came_down[2:]),
+        sum_low(keep_up[1::2], came_up[1::2]),
+        grad_out[2:],
+    ]
+    sends, first_group = lax.optimization_barrier((sends, first_group))
+    down_y, up_l, out_x = [exchange_bit(v, bit) for v, bit in zip(sends, "ylx")]
+    out_c = exchange_bit(sum_low(grad_out[1], out_x[1]), "c")
+    sums = sums + exchange_bit(sums, "c")
+    total_w, total_b = attend(0, first_group, total_w, total_b)
+    for s in range(1, seq_count - 1):
+        total_w, total_b = attend(s, second_group, total_w, total_b)
+
+    out_own = sum_low(grad_out[0], out_x[0], out_c)
+    sends = [
+        sum_low(keep_down[1], came_down[1], down_y[1]),
+        sum_low(keep_up[2], came_up[2], up_l[1]),
+        sums,
+    ]
+    (sends, total_w, parts, out_own) = lax.optimization_barrier((sends, total_w, parts, out_own))
+    down_l, up_y, more = [exchange_bit(v, bit) for v, bit in zip(sends, "lyx")]
+    sums = sends[2] + more
+    near, far = [], []
+
+    def cross(s):
+        near.append(parts[s][0].astype(f32) + exchange_bit(parts[s][1], "c"))
+        far.append(sum_low(parts[s][2], exchange_bit(parts[s][3], "c")))
+
+    for s in range(seq_count - 1):
+        cross(s)
+    total_w, total_b = attend(seq_count - 1, second_group, total_w, total_b, out_own)
+    (down_l, up_y, far, total_w, total_b, parts[-1], sums) = lax.optimization_barrier(
+        (down_l, up_y, far, total_w, total_b, parts[-1], sums)
+    )
+    small = jnp.concatenate(
+        [sums.reshape(-1), total_b.reshape(-1), jnp.zeros((-total_b.shape[0] % 128,), f32)]
+    ).reshape(-1, 128)
+
     down_own = sum_low(keep_down[0], came_down[0], down_y[0], down_l)
-    down_own = add_extra(halve(down_own.reshape(4, hidden // 32, features), "hx"))
-    up_l3 = exchange_bit(sum_low(keep_up[3], came_up[3]), "l")
-    up_l1 = exchange_bit(sum_low(keep_up[1], came_up[1]), "l")
-    up_y = exchange_bit(sum_low(keep_up[2], came_up[2], up_l3), "y")
-    up_own = sum_low(keep_up[0], came_up[0], up_l1, up_y)
-    up_own = add_extra(halve(up_own.reshape(4, features // 4, hidden // 8), "hx"))
-    out_x = exchange_bit(grad_out[2:], "x")
-    out_c = exchange_bit(sum_low(grad_out[1], out_x[1]), "c")
-    out_own = add_extra(halve(sum_low(grad_out[0], out_x[0], out_c), "ylh"))
-
-    down_pieces = spread([double(down_own, "hx")], "cyl")
-    up_first = double(up_own, "hx")
-    up_two = exchange_bit(up_first, "y")
-    up_four = [up_first, exchange_bit(up_first, "l"), up_two, exchange_bit(up_two, "l")]
-    up_pieces = spread(up_four, "c")
-    out_pieces = spread([double(out_own, "ylh")], "xc")
-    full_down = gather_hidden(places, down_pieces, (hidden, features))
-    full_up = gather_hidden(places, up_pieces, (features, hidden))
-    full_out = gather_out(places, out_pieces, (features, features))
-
-    half_hidden = jnp.where(
-        (outer >= 4), jnp.concatenate([b_up_send, b_up_keep], axis=1),
-        jnp.concatenate([b_up_keep, b_up_send], axis=1),
-    )
-    packed = jnp.concatenate(
-        [sums_one[:3].reshape(-1), sums_two[:3].reshape(-1), half_hidden.reshape(-1)]
-    )
-    packed = sum_all(packed.reshape(-1, 128), ("seq", "dp")).reshape(-1)
+    down_own = down_own.reshape(4, hidden // 32, features)
+    up_own = sum_low(keep_up[0], came_up[0], up_l[0], up_y)
+    up_own = up_own.reshape(2, 2, features // 4, hidden // 8)
+    keeps = [down_own[:2], up_own[:, 0], total_w[:4], small]
+    sends = [down_own[2:], up_own[:, 1], total_w[4:], small]
+    (keeps, sends) = lax.optimization_barrier((keeps, sends))
+    got = [exchange_bit(v, bit) for v, bit in zip(sends, "hxyy")]
+    far_came = [exchange_bit(v, "x") for v in far]
+    down_own, up_own, qkv_own, small = [k + g for k, g in zip(keeps, got)]
+    qkv_own = qkv_own[:2] + exchange_bit(qkv_own[2:], "l")
+    small = small + exchange_bit(small, "l")
+    far = []
+    cross(seq_count - 1)
+
+    keeps = [down_own[:1], up_own[:1], qkv_own[:1], small]
+    sends = [down_own[1:], up_own[1:], qkv_own[1:], small]
+    (keeps, sends, far, far_came) = lax.optimization_barrier((keeps, sends, far, far_came))
+    got = [exchange_bit(v, bit) for v, bit in zip(sends, "xhhh")]
+    far_came += [exchange_bit(v, "x") for v in far]
+    *shards, small = [add_extra(k + g) for k, g in zip(keeps, got)]
+
+    packed = small.reshape(-1)
+    row_b = packed[sums.size : sums.size + 3 * wide].reshape(1, 3 * wide)
+    for bits in ("hhhc", "xylx", "lxy"):
+        (shards, row_b, far_came) = lax.optimization_barrier((shards, row_b, far_came))
+        shards = [
+            jnp.concatenate([shard, exchange_bit(shard, bit)]) for shard, bit in zip(shards, bits)
+        ]
+        if len(bits) > 3:
+            row_b = jnp.concatenate([row_b, exchange_bit(row_b, bits[3])])
+    shards = lax.optimization_barrier(shards)
+    last = [exchange_bit(shard, bit) for shard, bit in zip(shards, "ylx")]
+    near_c = [exchange_bit(shard, "c") for shard in shards]
+    far_c = [exchange_bit(shard, "c") for shard in last]
+    full_down, full_up = [
+        gather_hidden(places, [shards[i], last[i], near_c[i], far_c[i]], shape, i == 0)
+        for i, shape in ((0, (hidden, features)), (1, (features, hidden)))
+    ]
+    full_qkv, full_out = gather_heads(
+        places, [shards[2], near_c[2], last[2], far_c[2]], (features, 3 * features)
+    )
     (
         full_b_out,
         full_gain_one,
@@ -838,38 +876,18 @@
         full_gain_two,
         full_shift_two,
     ) = [packed[i * features : (i + 1) * features] for i in range(6)]
-    full_b_up = packed[6 * features :]
-
-    total_w = jnp.zeros((features, 3 * wide), f32)
-    total_b = jnp.zeros((3 * wide, 1), f32)
-    d_inputs = []
-    for s in range(seq_count):
-        pieces = d_contexts[s * seq_parts : (s + 1) * seq_parts]
-        pieces = pieces[:1] + [exchange(pieces[r], "seq", r) for r in range(1, seq_parts)]
-        parts, total_w, part_b = attention_backward(
-            infos[s], pieces, w_t, kept[s], total_w, heads, s == seq_count - 1
-        )
-        total_b = total_b + part_b
-        near = parts[0].astype(f32) + exchange_bit(parts[1], "c")
-        far = (parts[2].astype(f32) + exchange_bit(parts[3], "c")).astype(jnp.bfloat16)
-        d_inputs.append(near + exchange_bit(far, "x"))
-    own_pos = mine * local_rows + jnp.arange(local_rows, dtype=jnp.int32)
-    live = (own_pos[None, :] < lengths[:, None]).astype(f32)
-    grad_tokens = (
-        jnp.stack(d_inputs) + d_first_in.reshape(seq_count, local_rows, features)
-    ) * live[:, :, None]
-
-    qkv_own = add_extra(halve(total_w, "ylh"))
-    full_qkv = gather_heads(
-        places, spread([double(qkv_own, "ylh")], "xc"), (features, 3 * features)
-    )
-    b_all = double(sum_all(total_b.reshape(1, 3 * wide), ("dp",)), "xc")
+    full_b_up = packed[6 * features : 6 * features + hidden]
     b_rows = [
-        lax.dynamic_slice_in_dim(b_all, j ^ mine, 1, axis=0).reshape(3 * wide)
+        lax.dynamic_slice_in_dim(row_b, j ^ mine, 1, axis=0).reshape(3 * wide)
         for j in range(seq_parts)
     ]
     full_b_query = jnp.concatenate([row[:wide] for row in b_rows])
     full_b_value = jnp.concatenate([row[2 * wide :] for row in b_rows])
+
+    own_pos = mine * local_rows + jnp.arange(local_rows, dtype=jnp.int32)
+    live = (own_pos[None, :] < lengths[:, None]).astype(f32)
+    d_inputs = jnp.stack([n + f for n, f in zip(near, far_came)])
+    grad_tokens = (d_inputs + d_first_in.reshape(seq_count, local_rows, features)) * live[:, :, None]
     return (
         out_tokens,
         grad_tokens,

time: 476 us -> 398 us (0.84)
  waiting for transfers between devices: 172 us -> 112 us
  starting transfers between devices: 90.2 us -> 57.3 us
  local copies, waits for them, and re-layouts: 29.6 us -> 40.7 us
    ppermute x95 -> x73, waiting for transfers between devices: 172 us -> 112 us  [exchange(): lax.ppermute(array_in, axis, [(i, i ^ flip) for i in range(lax.axis_size(...]
    ppermute x95 -> x73, starting transfers between devices: 90.2 us -> 57.3 us  [exchange(): lax.ppermute(array_in, axis, [(i, i ^ flip) for i in range(lax.axis_size(...]
    convert_element_type x8 -> x11, other arithmetic: 8.84 us -> 16 us  [sum_low(): return total.astype(jnp.bfloat16)]
    unnamed x107 -> x133, local copies, waits for them, and re-layouts: 15 us -> 22 us
    pallas_call x7 -> x6, Pallas kernels: 87.7 us -> 86.2 us  [step_call(): pl.pallas_call(body, out_shape=outs, grid_spec=pltpu.PrefetchScalarGridSp...]
  transfers between devices with their start and end apart: 95 -> 73, of which waited for: 32 -> 26; matrix products, arithmetic and copies ran while one was open for 8% -> 9% of each run, Pallas kernels for 21% -> 25%
where the time goes in v1:
time: 398 us; the launch traced here: 393 us
  Pallas kernels  148 us (37%)
  waiting for transfers between devices  112 us (28%)
  starting transfers between devices  57.3 us (14%)
  local copies, waits for them, and re-layouts  40.7 us (10%)
  other arithmetic  25.3 us (6%)
  between operations  9.73 us (2%)
    ppermute x73, waiting for transfers between devices, exchange(): lax.ppermute(array_in, axis, [(i, i ^ flip) for i in range(lax.axis_size(...  112 us
    pallas_call x6, Pallas kernels, step_call(): pl.pallas_call(body, out_shape=outs, grid_spec=pltpu.PrefetchScalarGridSp...  86.2 us
    pallas_call x6, Pallas kernels, kernel_call(): pl.pallas_call(body, out_shape=outs, in_specs=[pl.BlockSpec(memory_space=...  61.7 us
    ppermute x73, starting transfers between devices, exchange(): lax.ppermute(array_in, axis, [(i, i ^ flip) for i in range(lax.axis_size(...  57.3 us
    unnamed x133, local copies, waits for them, and re-layouts  22 us
    convert_element_type x11, other arithmetic, sum_low(): return total.astype(jnp.bfloat16)  16 us
  transfers between devices with their start and end apart: 73, of which 26 were waited for; matrix products, arithmetic and copies ran while one was open for 9% of the time, Pallas kernels for 25%

profile of v1, /device:TPU:0, one launch (start us, length us, event | category | flops | bytes accessed | tf_op | source)
XLA Modules:
  0.0 393.1 jit_solution(4524277233437910969)
XLA Ops:
  9.2 5.8 %collective-permute-done.13.x2 = bf16[256,768]{1,0:T(8,128)(2,1)} collective-permute-done((bf16[256,768]{1,0:T(8,128)(2,1)S(1)}, bf16[256,768]{1,0:T(8,128)(2,1)}, u32[]{:S(2)}, u32[]{:S(2)}) %collective-permute-start.13) | collective-permute-done | bytes 393248 | tf_op jit(solution)/shard_map/ppermute | solution.py:29
  35.3 7.9 %shard_map.282 = (bf16[192,256]{1,0:T(8,128)(2,1)S(1)}, bf16[192,256]{1,0:T(8,128)(2,1)S(1)}, bf16[192,256]{1,0:T(8,128)(2,1)S(1)}, bf16[192,256]{1,0:T(8,128)(2...) custom-call(s32[5]{0:T(128)S(1)} %stack.84.info, ...), custom_call_target="tpu_custom_call" | custom-call | flops 6000000000 | bytes 20971520 | tf_op jit(solution)/shard_map/pallas_call | solution.py:194
  47.0 8.1 %shard_map.281 = (bf16[192,256]{1,0:T(8,128)(2,1)S(1)}, bf16[192,256]{1,0:T(8,128)(2,1)}, bf16[192,256]{1,0:T(8,128)(2,1)S(1)}, bf16[192,256]{1,0:T(8,128)(2,1)}...) custom-call(s32[5]{0:T(128)S(1)} %stack.82.info, ...), custom_call_target="tpu_custom_call" | custom-call | flops 6000000000 | bytes 20971520 | tf_op jit(solution)/shard_map/pallas_call | solution.py:194
  56.9 7.7 %shard_map.280 = (bf16[192,256]{1,0:T(8,128)(2,1)S(1)}, bf16[192,256]{1,0:T(8,128)(2,1)}, bf16[192,256]{1,0:T(8,128)(2,1)}, bf16[192,256]{1,0:T(8,128)(2,1)S(1)}...) custom-call(s32[5]{0:T(128)S(1)} %stack.80.info, ...), custom_call_target="tpu_custom_call" | custom-call | flops 6000000000 | bytes 20971520 | tf_op jit(solution)/shard_map/pallas_call | solution.py:194
  69.8 3.9 collective-permute-done.4.refs_2_
  78.4 25.7 %shard_map.283 = (bf16[768,768]{1,0:T(8,128)(2,1)}, bf16[768,768]{1,0:T(8,128)(2,1)S(1)}, f32[768,768]{1,0:T(8,128)}, bf16[768,768]{1,0:T(8,128)(2,1)S(1)}, bf16...) custom-call(s32[14]{0:T(128)S(1)} %concatenate.81.places, ...), custom_call_target="tpu_custom_call" | custom-call | flops 8153726976 | bytes 20971520 | tf_op jit(solution)/shard_map/pallas_call | solution.py:446
  106.4 15.5 %shard_map.284 = (bf16[4,384,768]{2,1,0:T(8,128)(2,1)}, bf16[4,768,384]{2,1,0:T(8,128)(2,1)}, f32[1,1536]{1,0:T(1,128)S(1)}, f32[768,768]{1,0:T(8,128)}) custom-call(s32[14]{0:T(128)S(1)} %concatenate.81.places, bf16[8,768,384]{2,1,0:T(8,128)(2,1)} %get-tuple-element.171.active.refs_0_, bf16[8,768,384]{2,1,0:T(8,128)(2,1)} %get-tuple-element.172.slope.refs_1_, ...), custom_call_target="tpu_custom_call" | custom-call | flops 7247757312 | bytes 20971520 | tf_op jit(solution)/shard_map/pallas_call | solution.py:446
  122.5 21.5 %shard_map.285 = (bf16[4,384,768]{2,1,0:T(8,128)(2,1)}, bf16[4,768,384]{2,1,0:T(8,128)(2,1)}, f32[1,1536]{1,0:T(1,128)S(1)}, f32[768,768]{1,0:T(8,128)}, f32[8,7...) custom-call(s32[14]{0:T(128)S(1)} %concatenate.81.places, ...), custom_call_target="tpu_custom_call" | custom-call | flops 7247757312 | bytes 20971520 | tf_op jit(solution)/shard_map/pallas_call | solution.py:446
  151.3 5.6 %collective-permute-done.21.g2 = bf16[2,1,192,256]{3,2,1,0:T(8,128)(2,1)S(1)} collective-permute-done((bf16[2,1,192,256]{3,2,1,0:T(8,128)(2,1)S(1)}, bf16[2,1,192,256]{3,2,1,0:T(8,128)(2,1)S(1)}, u32[]{:S(2)}, u32[]{:S(2)}) %collective-permute-start.21) | collective-permute-done | bytes 196640 | tf_op jit(solution)/shard_map/ppermute | solution.py:29
  169.5 12.3 %shard_map.286 = (bf16[256,768]{1,0:T(8,128)(2,1)S(1)}, bf16[256,768]{1,0:T(8,128)(2,1)}, bf16[256,768]{1,0:T(8,128)(2,1)S(1)}, bf16[256,768]{1,0:T(8,128)(2,1)S...) custom-call(s32[5]{0:T(128)S(1)} %stack.80.info, bf16[1,192,256]{2,1,0:T(8,128)(2,1)S(1)} %get-tuple-element.200.g0, ...), custom_call_target="tpu_custom_call" | custom-call | flops 6000000000 | bytes 20971520 | tf_op jit(solution)/shard_map/pallas_call | solution.py:194
  183.5 13.0 %shard_map.287 = (bf16[256,768]{1,0:T(8,128)(2,1)S(1)}, bf16[256,768]{1,0:T(8,128)(2,1)}, bf16[256,768]{1,0:T(8,128)(2,1)S(1)}, bf16[256,768]{1,0:T(8,128)(2,1)S...) custom-call(s32[5]{0:T(128)S(1)} %stack.82.info, bf16[2,192,256]{2,1,0:T(8,128)(2,1)S(1)} %copy-done.13, ...), custom_call_target="tpu_custom_call" | custom-call | flops 6000000000 | bytes 20971520 | tf_op jit(solution)/shard_map/pallas_call | solution.py:194
  206.4 12.6 %shard_map.288 = (bf16[256,768]{1,0:T(8,128)(2,1)S(1)}, bf16[256,768]{1,0:T(8,128)(2,1)S(1)}, bf16[256,768]{1,0:T(8,128)(2,1)S(1)}, bf16[256,768]{1,0:T(8,128)(2...) custom-call(s32[5]{0:T(128)S(1)} %stack.84.info, bf16[2,192,256]{2,1,0:T(8,128)(2,1)S(1)} %copy-done.13, ...), custom_call_target="tpu_custom_call" | custom-call | flops 6000000000 | bytes 20971520 | tf_op jit(solution)/shard_map/pallas_call | solution.py:194
  235.9 10.7 %collective-permute-done.41 = f32[65,128]{1,0:T(8,128)S(1)} collective-permute-done((f32[65,128]{1,0:T(8,128)S(1)}, f32[65,128]{1,0:T(8,128)S(1)}, u32[]{:S(2)}, u32[]{:S(2)}) %collective-permute-start.41) | collective-permute-done | bytes 33312 | tf_op jit(solution)/shard_map/ppermute | solution.py:29
  247.1 3.5 collective-permute-done.42
  253.8 6.1 %collective-permute-done.40 = bf16[2,96,768]{2,1,0:T(8,128)(2,1)S(1)} collective-permute-done((bf16[2,96,768]{2,1,0:T(8,128)(2,1)S(1)}, bf16[2,96,768]{2,1,0:T(8,128)(2,1)S(1)}, u32[]{:S(2)}, u32[]{:S(2)}) %collective-permute-start.40) | collective-permute-done | bytes 294944 | tf_op jit(solution)/shard_map/ppermute | solution.py:29
  262.9 5.6 %collective-permute-done.45 = bf16[256,768]{1,0:T(8,128)(2,1)S(1)} collective-permute-done((bf16[256,768]{1,0:T(8,128)(2,1)}, bf16[256,768]{1,0:T(8,128)(2,1)S(1)}, u32[]{:S(2)}, u32[]{:S(2)}) %collective-permute-start.45) | collective-permute-done | bytes 393248 | tf_op jit(solution)/shard_map/ppermute | solution.py:29
  276.1 6.6 %collective-permute-done.49 = f32[65,128]{1,0:T(8,128)S(1)} collective-permute-done((f32[65,128]{1,0:T(8,128)S(1)}, f32[65,128]{1,0:T(8,128)S(1)}, u32[]{:S(2)}, u32[]{:S(2)}) %collective-permute-start.49) | collective-permute-done | bytes 33312 | tf_op jit(solution)/shard_map/ppermute | solution.py:29
  286.1 13.1 %collective-permute-done.53 = bf16[1,96,768]{2,1,0:T(8,128)(2,1)S(1)} collective-permute-done((bf16[1,96,768]{2,1,0:T(8,128)(2,1)S(1)}, bf16[1,96,768]{2,1,0:T(8,128)(2,1)S(1)}, u32[]{:S(2)}, u32[]{:S(2)}) %collective-permute-start.53) | collective-permute-done | bytes 147488 | tf_op jit(solution)/shard_map/ppermute | solution.py:29
  318.3 11.3 %collective-permute-done.63 = bf16[4,96,768]{2,1,0:T(8,128)(2,1)S(1)} collective-permute-done((bf16[4,96,768]{2,1,0:T(8,128)(2,1)S(1)}, bf16[4,96,768]{2,1,0:T(8,128)(2,1)S(1)}, u32[]{:S(2)}, u32[]{:S(2)}) %collective-permute-start.63) | collective-permute-done | bytes 589856 | tf_op jit(solution)/shard_map/ppermute | solution.py:29
  340.2 15.7 %collective-permute-done.70.refs_1_ = bf16[8,96,768]{2,1,0:T(8,128)(2,1)} collective-permute-done((bf16[8,96,768]{2,1,0:T(8,128)(2,1)S(1)}, bf16[8,96,768]{2,1,0:T(8,128)(2,1)}, u32[]{:S(2)}, u32[]{:S(2)}) %collective-permute-start.70) | collective-permute-done | bytes 1179680 | tf_op jit(solution)/shard_map/ppermute | solution.py:29
  356.4 3.9 collective-permute-done.67.refs_1_
  367.3 7.4 %shard_map.291 = f32[3072,768]{1,0:T(8,128)} custom-call(s32[14]{0:T(128)S(1)} %concatenate.81.places, bf16[8,96,768]{2,1,0:T(8,128)(2,1)S(1)} %pad_maximum_fusion.refs_0_, bf16[8,96,768]{2,1,0:T(8,128)(2,1)} %collective-permute-done.70.refs_1_, bf16[8,96,768]{2,1,0:T(8,128)(2,1)} %collective-permute-done.71.refs_2_, ...), custom_call_target="tpu_custom_call" | custom-call | flops 589824 | bytes 20971520 | tf_op jit(solution)/shard_map/pallas_call | solution.py:446
  375.7 7.0 %shard_map.290 = f32[768,3072]{1,0:T(8,128)} custom-call(s32[14]{0:T(128)S(1)} %concatenate.81.places, bf16[8,192,384]{2,1,0:T(8,128)(2,1)S(1)} %pad_maximum_fusion.1.refs_0_, bf16[8,192,384]{2,1,0:T(8,128)(2,1)} %collective-permute-done.67.refs_1_, bf16[8,192,384]{2,1,0:T(8,128)(2,1)S(1)} %collective-permute-done.68.refs_2_, bf16[8,192,384]{2,1,0:T(8,128)(2,1)} %copy-done.44), custom_call_target="tpu_custom_call" | custom-call | flops 589824 | bytes 20971520 | tf_op jit(solution)/shard_map/pallas_call | solution.py:446
  383.8 9.1 %shard_map.289 = (f32[768,2304]{1,0:T(8,128)}, f32[768,768]{1,0:T(8,128)}) custom-call(s32[14]{0:T(128)S(1)} %concatenate.81.places, bf16[8,96,768]{2,1,0:T(8,128)(2,1)S(1)} %pad_maximum_fusion.2.refs_0_, bf16[8,96,768]{2,1,0:T(8,128)(2,1)S(1)} %collective-permute-done.64.refs_1_, bf16[8,96,768]{2,1,0:T(8,128)(2,1)} %collective-permute-done.65.refs_2_, ...), custom_call_target="tpu_custom_call" | custom-call | flops 1000 | bytes 20971520 | tf_op jit(solution)/shard_map/pallas_call | solution.py:446
  (364 shorter events, 143.6 us)
Async XLA Ops:
  5.0 29.2 %collective-permute-start.12 = (bf16[256,768]{1,0:T(8,128)(2,1)S(1)}, bf16[256,768]{1,0:T(8,128)(2,1)}, u32[]{:S(2)}, u32[]{:S(2)}) collective-permute-start(bf16[256,768]{1,0:T(8,128)(2,1)S(1)} %get-tuple-element.306.x0), channel_id=1, source_target_pairs={{0,1},{1,0},{2,3},{3,2},{4,5},{5,4},{6,7},{7,6},{8,9},{9,8},{10,11... | collective-permute-start | bytes 1179656 | tf_op jit(solution)/shard_map/ppermute | solution.py:29
  5.0 29.8 %collective-permute-start.7 = (bf16[256,768]{1,0:T(8,128)(2,1)S(1)}, bf16[256,768]{1,0:T(8,128)(2,1)S(1)}, u32[]{:S(2)}, u32[]{:S(2)}) collective-permute-start(bf16[256,768]{1,0:T(8,128)(2,1)S(1)} %get-tuple-element.307.x0), channel_id=1, source_target_pairs={{0,2},{1,3},{2,0},{3,1},{4,6},{5,7},{6,4},{7,5},{8,10},{9,11},{10,... | collective-permute-start | bytes 1179656 | tf_op jit(solution)/shard_map/ppermute | solution.py:29
  5.1 39.7 %collective-permute-start.6 = (bf16[256,768]{1,0:T(8,128)(2,1)S(1)}, bf16[256,768]{1,0:T(8,128)(2,1)}, u32[]{:S(2)}, u32[]{:S(2)}) collective-permute-start(bf16[256,768]{1,0:T(8,128)(2,1)S(1)} %get-tuple-element.307.x0), channel_id=1, source_target_pairs={{0,1},{1,0},{2,3},{3,2},{4,5},{5,4},{6,7},{7,6},{8,9},{9,8},{10,11... | collective-permute-start | bytes 1179656 | tf_op jit(solution)/shard_map/ppermute | solution.py:29
  5.5 29.4 %collective-permute-start.1 = (bf16[256,768]{1,0:T(8,128)(2,1)S(1)}, bf16[256,768]{1,0:T(8,128)(2,1)S(1)}, u32[]{:S(2)}, u32[]{:S(2)}) collective-permute-start(bf16[256,768]{1,0:T(8,128)(2,1)S(1)} %get-tuple-element.308.x0), channel_id=1, source_target_pairs={{0,2},{1,3},{2,0},{3,1},{4,6},{5,7},{6,4},{7,5},{8,10},{9,11},{10,... | collective-permute-start | bytes 1179656 | tf_op jit(solution)/shard_map/ppermute | solution.py:29
  15.0 20.2 %collective-permute-start.14 = (bf16[256,768]{1,0:T(8,128)(2,1)}, bf16[256,768]{1,0:T(8,128)(2,1)}, u32[]{:S(2)}, u32[]{:S(2)}) collective-permute-start(bf16[256,768]{1,0:T(8,128)(2,1)} %collective-permute-done.13.x2), channel_id=1, source_target_pairs={{0,1},{1,0},{2,3},{3,2},{4,5},{5,4},{6,7},{7,6},{8,9},{9,8},{10,11... | collective-permute-start | bytes 1179656 | tf_op jit(solution)/shard_map/ppermute | solution.py:29
  34.2 20.9 %collective-permute-start = (bf16[256,768]{1,0:T(8,128)(2,1)S(1)}, bf16[256,768]{1,0:T(8,128)(2,1)S(1)}, u32[]{:S(2)}, u32[]{:S(2)}) collective-permute-start(bf16[256,768]{1,0:T(8,128)(2,1)S(1)} %get-tuple-element.308.x0), channel_id=1, source_target_pairs={{0,1},{1,0},{2,3},{3,2},{4,5},{5,4},{6,7},{7,6},{8,9},{9,8},{10,11... | collective-permute-start | bytes 1179656 | tf_op jit(solution)/shard_map/ppermute | solution.py:29
  34.8 22.0 %collective-permute-start.2 = (bf16[256,768]{1,0:T(8,128)(2,1)S(1)}, bf16[256,768]{1,0:T(8,128)(2,1)S(1)}, u32[]{:S(2)}, u32[]{:S(2)}) collective-permute-start(bf16[256,768]{1,0:T(8,128)(2,1)S(1)} %collective-permute-done.1.x2), channel_id=1, source_target_pairs={{0,1},{1,0},{2,3},{3,2},{4,5},{5,4},{6,7},{7,6},{8,9},{9,8},{10,11... | collective-permute-start | bytes 1179656 | tf_op jit(solution)/shard_map/ppermute | solution.py:29
  44.7 22.0 %collective-permute-start.15 = (bf16[192,256]{1,0:T(8,128)(2,1)S(1)}, bf16[192,256]{1,0:T(8,128)(2,1)S(1)}, u32[]{:S(2)}, u32[]{:S(2)}) collective-permute-start(bf16[192,256]{1,0:T(8,128)(2,1)S(1)} %get-tuple-element.167), channel_id=1, source_target_pairs={{0,1},{1,0},{2,3},{3,2},{4,5},{5,4},{6,7},{7,6},{8,9},{9,8},{10,11... | collective-permute-start | bytes 294920 | tf_op jit(solution)/shard_map/ppermute | solution.py:29
  44.8 22.3 %collective-permute-start.16 = (bf16[192,256]{1,0:T(8,128)(2,1)S(1)}, bf16[192,256]{1,0:T(8,128)(2,1)S(1)}, u32[]{:S(2)}, u32[]{:S(2)}) collective-permute-start(bf16[192,256]{1,0:T(8,128)(2,1)S(1)} %get-tuple-element.168), channel_id=1, source_target_pairs={{0,2},{1,3},{2,0},{3,1},{4,6},{5,7},{6,4},{7,5},{8,10},{9,11},{10,... | collective-permute-start | bytes 294920 | tf_op jit(solution)/shard_map/ppermute | solution.py:29
  46.9 20.4 %collective-permute-start.17 = (bf16[192,256]{1,0:T(8,128)(2,1)S(1)}, bf16[192,256]{1,0:T(8,128)(2,1)S(1)}, u32[]{:S(2)}, u32[]{:S(2)}) collective-permute-start(bf16[192,256]{1,0:T(8,128)(2,1)S(1)} %get-tuple-element.169), channel_id=1, source_target_pairs={{0,3},{1,2},{2,1},{3,0},{4,7},{5,6},{6,5},{7,4},{8,11},{9,10},{10,... | collective-permute-start | bytes 294920 | tf_op jit(solution)/shard_map/ppermute | solution.py:29
  121.9 35.0 %collective-permute-start.19 = (bf16[4,768,384]{2,1,0:T(8,128)(2,1)}, bf16[4,768,384]{2,1,0:T(8,128)(2,1)}, u32[]{:S(2)}, u32[]{:S(2)}) collective-permute-start(bf16[4,768,384]{2,1,0:T(8,128)(2,1)} %get-tuple-element.182), channel_id=1, source_target_pairs={{0,1},{1,0},{2,3},{3,2},{4,5},{5,4},{6,7},{7,6},{8,9},{9,8},{10,11... | collective-permute-start | bytes 7077896 | tf_op jit(solution)/shard_map/ppermute | solution.py:29
  122.3 37.3 %collective-permute-start.18 = (bf16[4,384,768]{2,1,0:T(8,128)(2,1)}, bf16[4,384,768]{2,1,0:T(8,128)(2,1)}, u32[]{:S(2)}, u32[]{:S(2)}) collective-permute-start(bf16[4,384,768]{2,1,0:T(8,128)(2,1)} %get-tuple-element.180), channel_id=1, source_target_pairs={{0,1},{1,0},{2,3},{3,2},{4,5},{5,4},{6,7},{7,6},{8,9},{9,8},{10,11... | collective-permute-start | bytes 7077896 | tf_op jit(solution)/shard_map/ppermute | solution.py:29
  156.9 26.6 %collective-permute-start.26 = (bf16[2,192,256]{2,1,0:T(8,128)(2,1)S(1)}, bf16[2,192,256]{2,1,0:T(8,128)(2,1)S(1)}, u32[]{:S(2)}, u32[]{:S(2)}) collective-permute-start(bf16[2,192,256]{2,1,0:T(8,128)(2,1)S(1)} %copy-done.15), channel_id=1, source_target_pairs={{0,1},{1,0},{2,3},{3,2},{4,5},{5,4},{6,7},{7,6},{8,9},{9,8},{10,11... | collective-permute-start | bytes 589832 | tf_op jit(solution)/shard_map/ppermute | solution.py:29
  164.7 33.1 %collective-permute-start.24 = (bf16[2,768,384]{2,1,0:T(8,128)(2,1)S(1)}, bf16[2,768,384]{2,1,0:T(8,128)(2,1)}, u32[]{:S(2)}, u32[]{:S(2)}) collective-permute-start(bf16[2,768,384]{2,1,0:T(8,128)(2,1)S(1)} %add_convert_fusion), channel_id=1, source_target_pairs={{0,8},{4,12},{8,0},{12,4},{16,24},{20,28},{24,16},{28,20},{1,9},{5... | collective-permute-start | bytes 3538952 | tf_op jit(solution)/shard_map/ppermute | solution.py:29
  166.5 32.9 %collective-permute-start.23 = (bf16[2,384,768]{2,1,0:T(8,128)(2,1)}, bf16[2,384,768]{2,1,0:T(8,128)(2,1)S(1)}, u32[]{:S(2)}, u32[]{:S(2)}) collective-permute-start(bf16[2,384,768]{2,1,0:T(8,128)(2,1)} %add_convert_fusion.1), channel_id=1, source_target_pairs={{0,4},{4,0},{8,12},{12,8},{16,20},{20,16},{24,28},{28,24},{1,5},{5... | collective-permute-start | bytes 3538952 | tf_op jit(solution)/shard_map/ppermute | solution.py:29
  230.8 22.2 %collective-permute-start.39 = (bf16[4,96,768]{2,1,0:T(8,128)(2,1)}, bf16[4,96,768]{2,1,0:T(8,128)(2,1)S(1)}, u32[]{:S(2)}, u32[]{:S(2)}) collective-permute-start(bf16[4,96,768]{2,1,0:T(8,128)(2,1)} %get-tuple-element.252), channel_id=1, source_target_pairs={{0,4},{4,0},{8,12},{12,8},{16,20},{20,16},{24,28},{28,24},{1,5},{5... | collective-permute-start | bytes 1769480 | tf_op jit(solution)/shard_map/ppermute | solution.py:29
  231.8 21.0 %collective-permute-start.37 = (bf16[2,96,768]{2,1,0:T(8,128)(2,1)}, bf16[2,96,768]{2,1,0:T(8,128)(2,1)S(1)}, u32[]{:S(2)}, u32[]{:S(2)}) collective-permute-start(bf16[2,96,768]{2,1,0:T(8,128)(2,1)} %bitcast.37), channel_id=1, source_target_pairs={{0,16},{4,20},{8,24},{12,28},{16,0},{20,4},{24,8},{28,12},{1,17},{... | collective-permute-start | bytes 884744 | tf_op jit(solution)/shard_map/ppermute | solution.py:29
  330.5 25.5 %collective-permute-start.70 = (bf16[8,96,768]{2,1,0:T(8,128)(2,1)S(1)}, bf16[8,96,768]{2,1,0:T(8,128)(2,1)}, u32[]{:S(2)}, u32[]{:S(2)}) collective-permute-start(bf16[8,96,768]{2,1,0:T(8,128)(2,1)S(1)} %pad_maximum_fusion.refs_0_), channel_id=1, source_target_pairs={{0,4},{4,0},{8,12},{12,8},{16,20},{20,16},{24,28},{28,24},{1,5},{5... | collective-permute-start | bytes 3538952 | tf_op jit(solution)/shard_map/ppermute | solution.py:29
  331.9 24.1 %collective-permute-start.71 = (bf16[8,96,768]{2,1,0:T(8,128)(2,1)S(1)}, bf16[8,96,768]{2,1,0:T(8,128)(2,1)}, u32[]{:S(2)}, u32[]{:S(2)}) collective-permute-start(bf16[8,96,768]{2,1,0:T(8,128)(2,1)S(1)} %pad_maximum_fusion.refs_0_), channel_id=1, source_target_pairs={{0,1},{1,0},{2,3},{3,2},{4,5},{5,4},{6,7},{7,6},{8,9},{9,8},{10,11... | collective-permute-start | bytes 3538952 | tf_op jit(solution)/shard_map/ppermute | solution.py:29
  331.9 28.5 %collective-permute-start.67 = (bf16[8,192,384]{2,1,0:T(8,128)(2,1)S(1)}, bf16[8,192,384]{2,1,0:T(8,128)(2,1)}, u32[]{:S(2)}, u32[]{:S(2)}) collective-permute-start(bf16[8,192,384]{2,1,0:T(8,128)(2,1)S(1)} %pad_maximum_fusion.1.refs_0_), channel_id=1, source_target_pairs={{0,8},{4,12},{8,0},{12,4},{16,24},{20,28},{24,16},{28,20},{1,9},{5... | collective-permute-start | bytes 3538952 | tf_op jit(solution)/shard_map/ppermute | solution.py:29
  333.3 28.2 %collective-permute-start.65 = (bf16[8,96,768]{2,1,0:T(8,128)(2,1)S(1)}, bf16[8,96,768]{2,1,0:T(8,128)(2,1)}, u32[]{:S(2)}, u32[]{:S(2)}) collective-permute-start(bf16[8,96,768]{2,1,0:T(8,128)(2,1)S(1)} %pad_maximum_fusion.2.refs_0_), channel_id=1, source_target_pairs={{0,2},{1,3},{2,0},{3,1},{4,6},{5,7},{6,4},{7,5},{8,10},{9,11},{10,... | collective-permute-start | bytes 3538952 | tf_op jit(solution)/shard_map/ppermute | solution.py:29
  339.8 34.9 %collective-permute-start.68 = (bf16[8,192,384]{2,1,0:T(8,128)(2,1)S(1)}, bf16[8,192,384]{2,1,0:T(8,128)(2,1)S(1)}, u32[]{:S(2)}, u32[]{:S(2)}) collective-permute-start(bf16[8,192,384]{2,1,0:T(8,128)(2,1)S(1)} %pad_maximum_fusion.1.refs_0_), channel_id=1, source_target_pairs={{0,1},{1,0},{2,3},{3,2},{4,5},{5,4},{6,7},{7,6},{8,9},{9,8},{10,11... | collective-permute-start | bytes 3538952 | tf_op jit(solution)/shard_map/ppermute | solution.py:29
  355.9 26.8 %collective-permute-start.64 = (bf16[8,96,768]{2,1,0:T(8,128)(2,1)S(1)}, bf16[8,96,768]{2,1,0:T(8,128)(2,1)S(1)}, u32[]{:S(2)}, u32[]{:S(2)}) collective-permute-start(bf16[8,96,768]{2,1,0:T(8,128)(2,1)S(1)} %pad_maximum_fusion.2.refs_0_), channel_id=1, source_target_pairs={{0,1},{1,0},{2,3},{3,2},{4,5},{5,4},{6,7},{7,6},{8,9},{9,8},{10,11... | collective-permute-start | bytes 3538952 | tf_op jit(solution)/shard_map/ppermute | solution.py:29
  361.5 21.2 %collective-permute-start.66 = (bf16[8,96,768]{2,1,0:T(8,128)(2,1)}, bf16[8,96,768]{2,1,0:T(8,128)(2,1)S(1)}, u32[]{:S(2)}, u32[]{:S(2)}) collective-permute-start(bf16[8,96,768]{2,1,0:T(8,128)(2,1)} %collective-permute-done.65.refs_2_), channel_id=1, source_target_pairs={{0,1},{1,0},{2,3},{3,2},{4,5},{5,4},{6,7},{7,6},{8,9},{9,8},{10,11... | collective-permute-start | bytes 3538952 | tf_op jit(solution)/shard_map/ppermute | solution.py:29
  (114 other events, 1045.5 us)

commit v2 on v1

--- a/solution.py
+++ b/solution.py
@@ -55,6 +55,11 @@
     return lax.dot_general(left, right, dims, preferred_element_type=jnp.float32)
 
 
+def sequence_scalars(places, index):
+    seq_count = (places.shape[0] - 11) // 3
+    return places[11 + index] >> 1, places[9], 11 + seq_count + 2 * index
+
+
 def shift_matrix(half, block, whole):
     row = lax.broadcasted_iota(jnp.int32, (block, whole), 0)
     col = lax.broadcasted_iota(jnp.int32, (block, whole), 1)
@@ -70,36 +75,36 @@
 
 
 def attend_forward(
-    heads, info, x0, x1, x2, x3, w_t, bias, c0, c1, c2, c3, qkv, ctx_blk, lse, x_t, x_seq, qkv_s, c_tok
+    heads, index, places, x0, x1, x2, x3, w_t, bias, c0, c1, c2, c3,
+    x_out, qkv_out, ctx_blk, lse, tok, c_tok, x_seq, qkv, sems,
 ):
-    half, mine = info[0], info[3]
+    half, mine, perm = sequence_scalars(places, index)
     whole = x_seq.shape[0]
     quarter = whole // 4
     block = whole // 2
     wide = heads * HEAD_DIM
     for r, piece in enumerate((x0, x1, x2, x3)):
         x_seq[pl.ds(pl.multiple_of((r ^ mine) * quarter, quarter), quarter), :] = piece[...]
-    row = lax.broadcasted_iota(jnp.int32, (block, 1), 0)
+    keep_x = pltpu.make_async_copy(x_seq, x_out, sems.at[0])
+    keep_x.start()
+    lane = lax.broadcasted_iota(jnp.int32, (1, block), 1)
+    tok[...] = (dot_f32(w_t[...], x_seq[...], NT) + bias[...]).astype(jnp.bfloat16)
     shift = shift_matrix(half, block, whole)
-    first = jnp.where(row < half, x_seq[0:block, :], jnp.zeros((), jnp.bfloat16))
-    second = dot_f32(shift, x_seq[...], NN).astype(jnp.bfloat16)
-    for b, rows in enumerate((first, second)):
-        turned = rows.T
-        x_t[b] = turned
-        projected = dot_f32(w_t[...], turned, NN) + bias[...]
-        qkv_s[b] = projected.astype(jnp.bfloat16)
-    qkv[...] = qkv_s[...]
+    qkv[0] = jnp.where(lane < half, tok[:, :block], jnp.zeros((), jnp.bfloat16))
+    qkv[1] = dot_f32(tok[...], shift, NT).astype(jnp.bfloat16)
+    keep_qkv = pltpu.make_async_copy(qkv, qkv_out, sems.at[1])
+    keep_qkv.start()
     key_tile, query_tile = mask_tiles(half, block)
 
     def one_block(b, carry):
-        target = info[1 + b]
+        target = places[perm + b]
         for h in range(heads):
             rows = slice(h * HEAD_DIM, (h + 1) * HEAD_DIM)
-            q_t = jnp.concatenate([qkv_s[b, rows, :], query_tile])
+            q_t = jnp.concatenate([qkv[b, rows, :], query_tile])
             k_t = jnp.concatenate(
-                [qkv_s[target, wide + h * HEAD_DIM : wide + (h + 1) * HEAD_DIM, :], key_tile]
+                [qkv[target, wide + h * HEAD_DIM : wide + (h + 1) * HEAD_DIM, :], key_tile]
             )
-            v_t = qkv_s[target, 2 * wide + h * HEAD_DIM : 2 * wide + (h + 1) * HEAD_DIM, :]
+            v_t = qkv[target, 2 * wide + h * HEAD_DIM : 2 * wide + (h + 1) * HEAD_DIM, :]
             scores = dot_f32(k_t, q_t, TN) * SOFT
             top = jnp.max(scores, axis=0, keepdims=True)
             expo = jnp.exp2(scores - top)
@@ -110,7 +115,6 @@
         return carry
 
     lax.fori_loop(0, 2, one_block, 0)
-    lane = lax.broadcasted_iota(jnp.int32, (1, block), 1)
     early = jnp.where(lane < half, ctx_blk[0], 0.0)
     late = dot_f32(ctx_blk[1].astype(jnp.bfloat16), shift, NN)
     for j in range(4):
@@ -120,14 +124,21 @@
         c_tok[j] = part.astype(jnp.bfloat16)
     for r, piece in enumerate((c0, c1, c2, c3)):
         piece[...] = c_tok[r ^ mine]
+    keep_x.wait()
+    keep_qkv.wait()
 
 
 def attend_backward(
-    heads, index, info, g0, g1, g2, g3, w_t, qkv, ctx_blk, lse, x_t, acc, *refs
+    heads, index, places, g0, g1, g2, g3, w_t, x_in, qkv, ctx_blk, lse, acc_in, acc_b, *refs
 ):
-    last = len(refs) == 11
-    (dx0, dx1, dx2, dx3, grad_w, grad_b, g_tok, g_blk, d_qkv, dx_s) = refs[-10:]
-    half, mine = info[0], info[3]
+    last = len(refs) == 16
+    (dx0, dx1, dx2, dx3, grad_w, grad_b, g_tok, g_blk, d_qkv, tok, x_seq, acc, dx_s, sems) = refs[-14:]
+    bring_x = pltpu.make_async_copy(x_in, x_seq, sems.at[0])
+    bring_acc = pltpu.make_async_copy(acc_in, acc, sems.at[1])
+    bring_x.start()
+    bring_acc.start()
+    half, mine, perm = sequence_scalars(places, index)
+    index = max(index - 1, 0)
     quarter = g0.shape[2]
     block = 2 * quarter
     whole = 4 * quarter
@@ -142,7 +153,7 @@
     key_tile, query_tile = mask_tiles(half, block)
 
     def one_block(b, carry):
-        target = info[1 + b]
+        target = places[perm + b]
         for h in range(heads):
             rows = slice(h * HEAD_DIM, (h + 1) * HEAD_DIM)
             k_rows = slice(wide + h * HEAD_DIM, wide + (h + 1) * HEAD_DIM)
@@ -167,89 +178,119 @@
         return carry
 
     lax.fori_loop(0, 2, one_block, 0)
-    early, late = d_qkv[0], d_qkv[1]
-    total = acc[...] + dot_f32(x_t[0], early, NT) + dot_f32(x_t[1], late, NT)
+    late = dot_f32(d_qkv[1], shift, NN)
+    front = jnp.where(lane < half, d_qkv[0].astype(jnp.float32), 0.0)
+    tok[:, block:] = late[:, block:].astype(jnp.bfloat16)
+    tok[:, :block] = (late[:, :block] + front).astype(jnp.bfloat16)
+    sent = []
+    for r, piece in enumerate((dx0, dx1, dx2, dx3)):
+        columns = tok[:, pl.ds(pl.multiple_of((r ^ mine) * quarter, quarter), quarter)]
+        dx_s[r] = dot_f32(columns, w_t[...], TN).astype(jnp.bfloat16)
+        sent.append(pltpu.make_async_copy(dx_s.at[r], piece, sems.at[2 + r]))
+        sent[-1].start()
+    bring_acc.wait()
+    bring_x.wait()
+    total = acc[...] + dot_f32(tok[...], x_seq[...], NN)
+    ones = jnp.ones((8, whole), jnp.bfloat16)
+    sums = acc_b[...] + dot_f32(ones, tok[...], NT)
     if last:
-        tile = grad_w.shape[1]
+        out_own, vectors = refs[:2]
+        inner = places[10]
+        turned = total.T
+        tile = out_own.shape[1]
+        extra = grad_w.shape[1] - tile
+        grad_w[:, tile:, :] = jnp.zeros((8, extra, 4 * wide), jnp.bfloat16)
         for q in range(8):
-            grad_w[q ^ info[4], :, : 3 * wide] = total[q * tile : (q + 1) * tile].astype(jnp.bfloat16)
-        grad_w[:, :, 3 * wide :] = refs[0][...]
+            grad_w[q ^ inner, :tile, : 3 * wide] = turned[q * tile : (q + 1) * tile].astype(
+                jnp.bfloat16
+            )
+        grad_w[:, :tile, 3 * wide :] = out_own[...]
+        row = lax.broadcasted_iota(jnp.int32, (extra, 1), 0)
+        own_row = jnp.concatenate([sums[0:1, :], jnp.zeros((1, wide), jnp.float32)], axis=1)
+        grad_w[inner, tile:, :] = jnp.where(row == 10, own_row, vectors[...]).astype(jnp.bfloat16)
+        grad_b[...] = sums
     else:
         grad_w[...] = total
-    grad_b[...] = jnp.sum(early.astype(jnp.float32), axis=1, keepdims=True) + jnp.sum(
-        late.astype(jnp.float32), axis=1, keepdims=True
-    )
-    back = dot_f32(late, shift, NN)
-    front = jnp.where(lane < half, early.astype(jnp.float32), 0.0)
-    for j in range(4):
-        part = back[:, j * quarter : (j + 1) * quarter]
-        if j < 2:
-            part = part + front[:, j * quarter : (j + 1) * quarter]
-        dx_s[j] = dot_f32(part.astype(jnp.bfloat16), w_t[...], TN).astype(jnp.bfloat16)
-    for r, piece in enumerate((dx0, dx1, dx2, dx3)):
-        piece[...] = dx_s[r ^ mine]
-
-
-def kernel_call(body, scalars, arrays, outs, scratch, aliases={}):
+        grad_b[...] = sums
+    for copy in sent:
+        copy.wait()
+
+
+def kernel_call(body, scalars, arrays, outs, scratch, left_in=(), left_out=()):
+    def spec(away):
+        return pl.BlockSpec(memory_space=pl.ANY if away else pltpu.VMEM)
+
     return pl.pallas_call(
         body,
         out_shape=outs,
         in_specs=[pl.BlockSpec(memory_space=pltpu.SMEM)]
-        + [pl.BlockSpec(memory_space=pltpu.VMEM)] * len(arrays),
-        out_specs=[pl.BlockSpec(memory_space=pltpu.VMEM)] * len(outs),
+        + [spec(i in left_in) for i in range(len(arrays))],
+        out_specs=[spec(i in left_out) for i in range(len(outs))],
         scratch_shapes=scratch,
-        input_output_aliases=aliases,
         compiler_params=pltpu.CompilerParams(vmem_limit_bytes=VMEM_LIMIT),
         cost_estimate=pl.CostEstimate(
-            flops=6 * 10**9, transcendentals=0, bytes_accessed=20 * 1024 * 1024
+            flops=10**8, transcendentals=0, bytes_accessed=1024 * 1024
         ),
     )(scalars, *arrays)
 
 
-def attention_forward(info, pieces, w_t, bias, heads):
+def attention_forward(places, pieces, index, w_t, bias, heads):
     quarter, features = pieces[0].shape
     whole, block, wide = 4 * quarter, 2 * quarter, heads * HEAD_DIM
     out = jax.ShapeDtypeStruct
     outs = [out((wide, quarter), jnp.bfloat16)] * 4 + [
+        out((whole, features), jnp.bfloat16),
         out((2, 3 * wide, block), jnp.bfloat16),
         out((2, wide, block), jnp.float32),
         out((2, 8, block), jnp.float32),
-        out((2, features, block), jnp.bfloat16),
     ]
     scratch = [
+        pltpu.VMEM((3 * wide, whole), jnp.bfloat16),
+        pltpu.VMEM((4, wide, quarter), jnp.bfloat16),
         pltpu.VMEM((whole, features), jnp.bfloat16),
         pltpu.VMEM((2, 3 * wide, block), jnp.bfloat16),
-        pltpu.VMEM((4, wide, quarter), jnp.bfloat16),
+        pltpu.SemaphoreType.DMA((2,)),
     ]
     found = kernel_call(
-        functools.partial(attend_forward, heads), info, [*pieces, w_t, bias], outs, scratch
+        functools.partial(attend_forward, heads, index),
+        places,
+        [*pieces, w_t, bias],
+        outs,
+        scratch,
+        left_out=(4, 5),
     )
     return found[:4], found[4:]
 
 
-def attention_backward(info, pieces, index, w_t, kept, acc, heads, out_own=None):
+def attention_backward(places, pieces, index, w_t, kept, acc, acc_b, heads, late=()):
     _, wide, quarter = pieces[0].shape
     features = w_t.shape[1]
     block = 2 * quarter
     out = jax.ShapeDtypeStruct
-    outs = [out((quarter, features), jnp.bfloat16)] * 4 + [
-        out((features, 3 * wide), jnp.float32)
-        if out_own is None
-        else out((8, features // 8, 4 * wide), jnp.bfloat16),
-        out((3 * wide, 1), jnp.float32),
-    ]
+    grad = (
+        out((8, features // 8 + 16, 4 * wide), jnp.bfloat16)
+        if late
+        else out((3 * wide, features), jnp.float32)
+    )
+    outs = [out((quarter, features), jnp.bfloat16)] * 4 + [grad, out((8, 3 * wide), jnp.float32)]
     scratch = [
         pltpu.VMEM((4, wide, quarter), jnp.bfloat16),
         pltpu.VMEM((2, wide, block), jnp.bfloat16),
         pltpu.VMEM((2, 3 * wide, block), jnp.bfloat16),
+        pltpu.VMEM((3 * wide, 4 * quarter), jnp.bfloat16),
+        pltpu.VMEM((4 * quarter, features), jnp.bfloat16),
+        pltpu.VMEM((3 * wide, features), jnp.float32),
         pltpu.VMEM((4, quarter, features), jnp.bfloat16),
+        pltpu.SemaphoreType.DMA((6,)),
     ]
     found = kernel_call(
         functools.partial(attend_backward, heads, index),
-        info,
-        [*pieces, w_t, *kept, acc] + ([] if out_own is None else [out_own]),
+        places,
+        [*pieces, w_t, *kept, acc, acc_b, *late],
         outs,
         scratch,
+        left_in=(5, 9),
+        left_out=(0, 1, 2, 3),
     )
     return found[:4], found[4], found[5]
 
@@ -442,7 +483,7 @@
     return pl.BlockSpec(shape, lambda p, places: (0,) * len(shape))
 
 
-def step_call(body, places, steps, ins, in_specs, outs, out_specs, scratch, flops):
+def step_call(body, places, steps, ins, in_specs, outs, out_specs, scratch, flops, aliases={}):
     return pl.pallas_call(
         body,
         out_shape=outs,
@@ -453,6 +494,7 @@
             out_specs=out_specs,
             scratch_shapes=scratch,
         ),
+        input_output_aliases=aliases,
         compiler_params=pltpu.CompilerParams(vmem_limit_bytes=VMEM_LIMIT),
         cost_estimate=pl.CostEstimate(
             flops=flops, transcendentals=0, bytes_accessed=20 * 1024 * 1024
@@ -584,55 +626,72 @@
     )
 
 
-def place_rows(by_rows, places, *refs):
-    pieces, out = refs[:4], refs[4]
+def place_rows(by_rows, late, places, *refs):
+    pieces, out = refs[:2], refs[-1]
     step = pl.program_id(0)
     tile = pieces[0].shape[1]
-    for k in range(8):
-        c, y, l = k >> 2, (k >> 1) & 1, k & 1
+    for k in range(4):
+        c, other = k >> 1, k & 1
 
         @pl.when(step == k)
         def copy():
             for q in range(4):
                 h, x = q >> 1, q & 1
-                piece, sub = (c * 2 + y, l * 4 + x * 2 + h) if by_rows else (c * 2 + l, x * 4 + y * 2 + h)
-                out[pl.ds(pl.multiple_of((q ^ places[8]) * tile, tile), tile), :] = pieces[piece][
+                sub = other * 4 + x * 2 + h if by_rows else x * 4 + other * 2 + h
+                out[pl.ds(pl.multiple_of((q ^ places[8]) * tile, tile), tile), :] = pieces[c][
                     sub
                 ].astype(jnp.float32)
 
 
-def gather_hidden(places, pieces, shape, by_rows):
-    _, rows, cols = pieces[0].shape
+def gather_hidden(places, early, late, shape, by_rows):
+    _, rows, cols = early[0].shape
     block = (4 * rows, cols)
-    index = (lambda p, places: (places[p], 0)) if by_rows else (lambda p, places: (0, places[p]))
-    return step_call(
-        functools.partial(place_rows, by_rows),
-        places,
-        8,
-        pieces,
-        [whole_spec(p.shape) for p in pieces],
-        jax.ShapeDtypeStruct(shape, jnp.float32),
-        pl.BlockSpec(block, index),
-        [],
-        8 * rows * cols,
-    )
+    total = []
+    for bit, pieces in enumerate((early, late)):
+
+        def number(p):
+            return (p >> 1) * 4 + bit * 2 + (p & 1) if by_rows else p * 2 + bit
+
+        if by_rows:
+            index = lambda p, places, number=number: (places[number(p)], 0)
+        else:
+            index = lambda p, places, number=number: (0, places[number(p)])
+        total = [
+            step_call(
+                functools.partial(place_rows, by_rows, bit),
+                places,
+                4,
+                pieces + total,
+                [whole_spec(p.shape) for p in pieces]
+                + [pl.BlockSpec(memory_space=pl.ANY)] * len(total),
+                jax.ShapeDtypeStruct(shape, jnp.float32),
+                pl.BlockSpec(block, index),
+                [],
+                8 * rows * cols,
+                {3: 0} if total else {},
+            )
+        ]
+    return total[0]
 
 
 def place_heads(places, *refs):
-    pieces, out, out_w = refs[:-2], refs[-2], refs[-1]
+    pieces = refs[:-5]
+    out, out_w, vector_rows, head_rows, held = refs[-5:]
     mine, inner = places[9], places[10]
     seq_parts = len(pieces)
     step = pl.program_id(0)
     wide = out_w.shape[0] // seq_parts
+    rows = out.shape[0]
+    f32 = jnp.float32
     for r, piece in enumerate(pieces):
         for j in range(seq_parts):
 
             @pl.when((r ^ mine) == j)
             def copy():
-                rows = piece[step ^ inner, :, : 3 * wide].astype(jnp.float32)
+                block = piece[step ^ inner, :rows, : 3 * wide].astype(f32)
                 for k in range(3):
                     start = (k * seq_parts + j) * wide
-                    out[:, start : start + wide] = rows[:, k * wide : (k + 1) * wide]
+                    out[:, start : start + wide] = block[:, k * wide : (k + 1) * wide]
 
         @pl.when(step == r)
         def copy_out():
@@ -641,22 +700,39 @@
                 row = pl.multiple_of((r ^ mine) * wide + q // 4 * tile, tile)
                 col = q % 4 * width
                 out_w[pl.ds(row, tile), col : col + width] = piece[
-                    q ^ inner, :, 3 * wide :
-                ].astype(jnp.float32)
+                    q ^ inner, :rows, 3 * wide :
+                ].astype(f32)
+
+        @pl.when(step == seq_parts)
+        def copy_vectors():
+            held[r ^ mine] = piece[inner, rows:, :].astype(f32)
+
+    @pl.when(step == seq_parts)
+    def sum_vectors():
+        total = held[0]
+        for j in range(1, seq_parts):
+            total = total + held[j]
+        vector_rows[...] = total
+        for j in range(seq_parts):
+            head_rows[j : j + 1, :] = held[j, 10:11, :]
 
 
 def gather_heads(places, pieces, shape):
-    rows = pieces[0].shape[1]
-    square = (shape[0], shape[0])
+    out, f32 = jax.ShapeDtypeStruct, jnp.float32
+    features = shape[0]
+    rows = features // 8
+    square = (features, features)
+    extra = (pieces[0].shape[1] - rows, features)
     return step_call(
         place_heads,
         places,
         8,
         pieces,
         [whole_spec(p.shape) for p in pieces],
-        [jax.ShapeDtypeStruct(shape, jnp.float32), jax.ShapeDtypeStruct(square, jnp.float32)],
-        [pl.BlockSpec((rows, shape[1]), lambda p, places: (p, 0)), whole_spec(square)],
-        [],
+        [out(shape, f32), out(square, f32), out(extra, f32), out((8, features), f32)],
+        [pl.BlockSpec((rows, shape[1]), lambda p, places: (p, 0))]
+        + [whole_spec(square), whole_spec(extra), whole_spec((8, features))],
+        [pltpu.VMEM((len(pieces), *extra), f32)],
         1000,
     )
 
@@ -711,22 +787,26 @@
             jnp.arange(8, dtype=jnp.int32) ^ outer,
             jnp.stack([own_number("hx"), mine, own_number("ylh")]),
             lengths,
+            block_perm.reshape(-1),
         ]
     )
-    infos = [
-        jnp.stack([lengths[s] // 2, block_perm[s, 0], block_perm[s, 1], mine, own_number("ylh")])
-        for s in range(seq_count)
-    ]
     vectors = jnp.stack(
         [v.astype(f32) for v in (b_out, ln1_gain, ln1_shift, b_down, ln2_gain, ln2_shift, b_out, b_out)]
     )
 
-    arrived, kept = [], []
+    arrived, kept, crossed = [], [], []
     for s in range(seq_count):
         near = tokens[s]
-        across = exchange_bit(near, "x")
+        start = near
+        if s > 0:
+            after = [crossed[-1]] + arrived[(s - 2) * seq_parts : (s - 2) * seq_parts + 1] * (s > 1)
+            start, _ = lax.optimization_barrier((near, after))
+        across = exchange_bit(start, "x")
+        crossed.append(across)
+        if s > 0:
+            across, _ = lax.optimization_barrier((across, arrived[-seq_parts]))
         pieces = [near, exchange_bit(near, "c"), across, exchange_bit(across, "c")]
-        contexts, saved = attention_forward(infos[s], pieces, w_t, bias, heads)
+        contexts, saved = attention_forward(places, pieces, s, w_t, bias, heads)
         kept.append(saved)
         arrived += [contexts[0]] + [exchange(contexts[r], "seq", r) for r in range(1, seq_parts)]
 
@@ -767,105 +847,108 @@
         (outer >= 4),
         jnp.concatenate([b_up_send, b_up_keep], axis=1),
         jnp.concatenate([b_up_keep, b_up_send], axis=1),
-    )
-    sums = jnp.concatenate(
-        [sums_one[:3].reshape(-1), sums_two[:3].reshape(-1), half_hidden.reshape(-1)]
-    ).reshape(-1, 128)
-    first_group, second_group = [
-        [own, exchange_bit(near, "c"), exchange_bit(pair, "x")]
-        for own, near, pair in (d_contexts[:3], d_contexts[3:])
-    ]
-    for group in (first_group, second_group):
-        group.append(exchange_bit(group[2][1], "c"))
-    total_w = jnp.zeros((features, 3 * wide), f32)
-    total_b = jnp.zeros((3 * wide, 1), f32)
-    parts = []
-
-    def attend(s, group, total_w, total_b, out_own=None):
-        found, total_w, part_b = attention_backward(
-            infos[s], group, max(s - 1, 0), w_t, kept[s], total_w, heads, out_own
+    ).reshape(-1, features)
+    filler = jnp.zeros((10 - half_hidden.shape[0], features), f32)
+    sums = jnp.concatenate([sums_one[:3], sums_two[:3], half_hidden, filler])
+
+    def hand_on(own, near, came):
+        return [own, exchange_bit(near, "c"), came, exchange_bit(came[1], "c")]
+
+    first_came = exchange_bit(d_contexts[2], "x")
+    second_pair, first_came = lax.optimization_barrier((d_contexts[5], first_came))
+    second_came = exchange_bit(second_pair, "x")
+    total_w = jnp.zeros((3 * wide, features), f32)
+    total_b = jnp.zeros((8, 3 * wide), f32)
+    parts, near, far = [], [], []
+
+    def attend(s, group, total_w, total_b, late=()):
+        found, total_w, total_b = attention_backward(
+            places, group, s, w_t, kept[s], total_w, total_b, heads, late
         )
         parts.append(found)
-        return total_w, total_b + part_b
-
-    sends = [
-        sum_low(keep_down[2:], came_down[2:]),
-        sum_low(keep_up[1::2], came_up[1::2]),
-        grad_out[2:],
-    ]
-    sends, first_group = lax.optimization_barrier((sends, first_group))
-    down_y, up_l, out_x = [exchange_bit(v, bit) for v, bit in zip(sends, "ylx")]
-    out_c = exchange_bit(sum_low(grad_out[1], out_x[1]), "c")
-    sums = sums + exchange_bit(sums, "c")
-    total_w, total_b = attend(0, first_group, total_w, total_b)
-    for s in range(1, seq_count - 1):
-        total_w, total_b = attend(s, second_group, total_w, total_b)
-
-    out_own = sum_low(grad_out[0], out_x[0], out_c)
-    sends = [
-        sum_low(keep_down[1], came_down[1], down_y[1]),
-        sum_low(keep_up[2], came_up[2], up_l[1]),
-        sums,
-    ]
-    (sends, total_w, parts, out_own) = lax.optimization_barrier((sends, total_w, parts, out_own))
-    down_l, up_y, more = [exchange_bit(v, bit) for v, bit in zip(sends, "lyx")]
-    sums = sends[2] + more
-    near, far = [], []
+        return total_w, total_b
 
     def cross(s):
         near.append(parts[s][0].astype(f32) + exchange_bit(parts[s][1], "c"))
         far.append(sum_low(parts[s][2], exchange_bit(parts[s][3], "c")))
 
-    for s in range(seq_count - 1):
+    sends = [
+        sum_low(keep_down[3], came_down[3]),
+        sum_low(keep_up[3], came_up[3]),
+        grad_out[2:],
+    ]
+    sends, first_came = lax.optimization_barrier((sends, first_came))
+    down_y1, up_l3, out_x = [exchange_bit(v, bit) for v, bit in zip(sends, "ylx")]
+    total_w, total_b = attend(0, hand_on(d_contexts[0], d_contexts[1], first_came), total_w, total_b)
+    (down_y1, up_l3, out_x, total_w, parts[0], second_came, near_pair) = lax.optimization_barrier(
+        (down_y1, up_l3, out_x, total_w, parts[0], second_came, d_contexts[3:5])
+    )
+
+    sends = [
+        sum_low(keep_down[2], came_down[2]),
+        sum_low(keep_up[1], came_up[1]),
+        sum_low(grad_out[1], out_x[1]),
+    ]
+    (sends, total_w) = lax.optimization_barrier((sends, total_w))
+    down_y0, up_l1, out_c = [exchange_bit(v, bit) for v, bit in zip(sends, "ylc")]
+    cross(0)
+    second_group = hand_on(*near_pair, second_came)
+    for s in range(1, seq_count - 1):
+        total_w, total_b = attend(s, second_group, total_w, total_b)
+    out_own = sum_low(grad_out[0], out_x[0], out_c)
+    (down_y0, up_l1, total_w, parts[1:], near, far, out_own) = lax.optimization_barrier(
+        (down_y0, up_l1, total_w, parts[1:], near, far, out_own)
+    )
+
+    sends = [
+        sum_low(keep_down[1], came_down[1], down_y1),
+        sum_low(keep_up[2], came_up[2], up_l3),
+    ]
+    (sends, total_w) = lax.optimization_barrier((sends, total_w))
+    down_l, up_y = [exchange_bit(v, bit) for v, bit in zip(sends, "ly")]
+    far_came = [exchange_bit(far[0], "x")]
+    for s in range(1, seq_count - 1):
         cross(s)
-    total_w, total_b = attend(seq_count - 1, second_group, total_w, total_b, out_own)
-    (down_l, up_y, far, total_w, total_b, parts[-1], sums) = lax.optimization_barrier(
-        (down_l, up_y, far, total_w, total_b, parts[-1], sums)
-    )
-    small = jnp.concatenate(
-        [sums.reshape(-1), total_b.reshape(-1), jnp.zeros((-total_b.shape[0] % 128,), f32)]
-    ).reshape(-1, 128)
-
-    down_own = sum_low(keep_down[0], came_down[0], down_y[0], down_l)
+    total_w, total_b = attend(seq_count - 1, second_group, total_w, total_b, (out_own, sums))
+
+    (down_l, up_y, far, far_came, total_w, parts[-1]) = lax.optimization_barrier(
+        (down_l, up_y, far, far_came, total_w, parts[-1])
+    )
+    down_own = sum_low(keep_down[0], came_down[0], down_y0, down_l)
     down_own = down_own.reshape(4, hidden // 32, features)
-    up_own = sum_low(keep_up[0], came_up[0], up_l[0], up_y)
+    up_own = sum_low(keep_up[0], came_up[0], up_l1, up_y)
     up_own = up_own.reshape(2, 2, features // 4, hidden // 8)
-    keeps = [down_own[:2], up_own[:, 0], total_w[:4], small]
-    sends = [down_own[2:], up_own[:, 1], total_w[4:], small]
+    keeps = [down_own[:2], up_own[:, 0], total_w[:4]]
+    sends = [down_own[2:], up_own[:, 1], total_w[4:]]
     (keeps, sends) = lax.optimization_barrier((keeps, sends))
-    got = [exchange_bit(v, bit) for v, bit in zip(sends, "hxyy")]
-    far_came = [exchange_bit(v, "x") for v in far]
-    down_own, up_own, qkv_own, small = [k + g for k, g in zip(keeps, got)]
+    got = [exchange_bit(v, bit) for v, bit in zip(sends, "hxy")]
+    far_came += [exchange_bit(v, "x") for v in far[1:]]
+    down_own, up_own, qkv_own = [k + g for k, g in zip(keeps, got)]
     qkv_own = qkv_own[:2] + exchange_bit(qkv_own[2:], "l")
-    small = small + exchange_bit(small, "l")
     far = []
     cross(seq_count - 1)
 
-    keeps = [down_own[:1], up_own[:1], qkv_own[:1], small]
-    sends = [down_own[1:], up_own[1:], qkv_own[1:], small]
+    keeps = [down_own[:1], up_own[:1], qkv_own[:1]]
+    sends = [down_own[1:], up_own[1:], qkv_own[1:]]
     (keeps, sends, far, far_came) = lax.optimization_barrier((keeps, sends, far, far_came))
-    got = [exchange_bit(v, bit) for v, bit in zip(sends, "xhhh")]
+    got = [exchange_bit(v, bit) for v, bit in zip(sends, "xhh")]
     far_came += [exchange_bit(v, "x") for v in far]
-    *shards, small = [add_extra(k + g) for k, g in zip(keeps, got)]
-
-    packed = small.reshape(-1)
-    row_b = packed[sums.size : sums.size + 3 * wide].reshape(1, 3 * wide)
-    for bits in ("hhhc", "xylx", "lxy"):
-        (shards, row_b, far_came) = lax.optimization_barrier((shards, row_b, far_came))
+    shards = [add_extra(k + g) for k, g in zip(keeps, got)]
+
+    for bits in ("hhh", "xyl", "lxy"):
+        (shards, far_came) = lax.optimization_barrier((shards, far_came))
         shards = [
             jnp.concatenate([shard, exchange_bit(shard, bit)]) for shard, bit in zip(shards, bits)
         ]
-        if len(bits) > 3:
-            row_b = jnp.concatenate([row_b, exchange_bit(row_b, bits[3])])
     shards = lax.optimization_barrier(shards)
     last = [exchange_bit(shard, bit) for shard, bit in zip(shards, "ylx")]
     near_c = [exchange_bit(shard, "c") for shard in shards]
     far_c = [exchange_bit(shard, "c") for shard in last]
     full_down, full_up = [
-        gather_hidden(places, [shards[i], last[i], near_c[i], far_c[i]], shape, i == 0)
+        gather_hidden(places, [shards[i], near_c[i]], [last[i], far_c[i]], shape, i == 0)
         for i, shape in ((0, (hidden, features)), (1, (features, hidden)))
     ]
-    full_qkv, full_out = gather_heads(
+    full_qkv, full_out, vector_rows, head_rows = gather_heads(
         places, [shards[2], near_c[2], last[2], far_c[2]], (features, 3 * features)
     )
     (
@@ -875,14 +958,10 @@
         full_b_down,
         full_gain_two,
         full_shift_two,
-    ) = [packed[i * features : (i + 1) * features] for i in range(6)]
-    full_b_up = packed[6 * features : 6 * features + hidden]
-    b_rows = [
-        lax.dynamic_slice_in_dim(row_b, j ^ mine, 1, axis=0).reshape(3 * wide)
-        for j in range(seq_parts)
-    ]
-    full_b_query = jnp.concatenate([row[:wide] for row in b_rows])
-    full_b_value = jnp.concatenate([row[2 * wide :] for row in b_rows])
+    ) = [vector_rows[i] for i in range(6)]
+    full_b_up = vector_rows[6 : 6 + hidden // features].reshape(hidden)
+    full_b_query = head_rows[:seq_parts, :wide].reshape(features)
+    full_b_value = head_rows[:seq_parts, 2 * wide : 3 * wide].reshape(features)
 
     own_pos = mine * local_rows + jnp.arange(local_rows, dtype=jnp.int32)
     live = (own_pos[None, :] < lengths[:, None]).astype(f32)

time: 398 us -> 391 us (0.982)
  local copies, waits for them, and re-layouts: 40.7 us -> 28.7 us
  waiting for transfers between devices: 112 us -> 124 us
  between operations: 9.73 us -> 2.15 us
  starting transfers between devices: 57.3 us -> 50.3 us
  other arithmetic: 25.3 us -> 30.1 us
    ppermute x73 -> x68, waiting for transfers between devices: 112 us -> 124 us  [exchange(): lax.ppermute(array_in, axis, [(i, i ^ flip) for i in range(lax.axis_size(...]
    ppermute x73 -> x68, starting transfers between devices: 57.3 us -> 50.3 us  [exchange(): lax.ppermute(array_in, axis, [(i, i ^ flip) for i in range(lax.axis_size(...]
    unnamed x133 -> x128, local copies, waits for them, and re-layouts: 22 us -> 16.2 us
    slice x13 -> x10, local copies, waits for them, and re-layouts: 5.81 us -> 0.87 us  [the longest x1 0.64 us: per_device(): vector_rows[i]]
    convert_element_type x11, other arithmetic: 16 us -> 20.3 us  [sum_low(): return total.astype(jnp.bfloat16)]
    another operation x3 -> x0, local copies, waits for them, and re-layouts: 4.13 us -> none  [per_device(): jnp.stack([lengths[s] // 2, block_perm[s, 0], block_perm[s, 1], mine, own...]
    pallas_call x6 -> x8, Pallas kernels: 86.2 us -> 89.4 us  [step_call(): pl.pallas_call(body, out_shape=outs, grid_spec=pltpu.PrefetchScalarGridSp...]
  transfers between devices with their start and end apart: 73 -> 68, of which waited for: 26 -> 25; matrix products, arithmetic and copies ran while one was open for 9% -> 9% of each run, Pallas kernels for 25% -> 26%
where the time goes in v2:
time: 391 us; the launch traced here: 386 us
  Pallas kernels  151 us (39%)
  waiting for transfers between devices  124 us (32%)
  starting transfers between devices  50.3 us (13%)
  other arithmetic  30.1 us (8%)
  local copies, waits for them, and re-layouts  28.7 us (7%)
    ppermute x68, waiting for transfers between devices, exchange(): lax.ppermute(array_in, axis, [(i, i ^ flip) for i in range(lax.axis_size(...  124 us
    pallas_call x8, Pallas kernels, step_call(): pl.pallas_call(body, out_shape=outs, grid_spec=pltpu.PrefetchScalarGridSp...  89.4 us
    pallas_call x6, Pallas kernels, kernel_call(): pl.pallas_call(body, out_shape=outs, in_specs=[pl.BlockSpec(memory_space=...  61.7 us
    ppermute x68, starting transfers between devices, exchange(): lax.ppermute(array_in, axis, [(i, i ^ flip) for i in range(lax.axis_size(...  50.3 us
    convert_element_type x11, other arithmetic, sum_low(): return total.astype(jnp.bfloat16)  20.3 us
    unnamed x128, local copies, waits for them, and re-layouts  16.2 us
  transfers between devices with their start and end apart: 68, of which 25 were waited for; matrix products, arithmetic and copies ran while one was open for 9% of the time, Pallas kernels for 26%

profile of v2, /device:TPU:0, one launch (start us, length us, event | category | flops | bytes accessed | tf_op | source)
XLA Modules:
  0.0 386.0 jit_solution(9712029021767936848)
XLA Ops:
  5.5 8.6 %collective-permute-done.1.x2 = bf16[256,768]{1,0:T(8,128)(2,1)S(1)} collective-permute-done((bf16[256,768]{1,0:T(8,128)(2,1)S(1)}, bf16[256,768]{1,0:T(8,128)(2,1)S(1)}, u32[]{:S(2)}, u32[]{:S(2)}) %collective-permute-start.1) | collective-permute-done | bytes 393248 | tf_op jit(solution)/shard_map/ppermute | solution.py:29
  25.5 7.1 %shard_map.280 = (bf16[192,256]{1,0:T(8,128)(2,1)S(1)}, bf16[192,256]{1,0:T(8,128)(2,1)S(1)}, bf16[192,256]{1,0:T(8,128)(2,1)S(1)}, bf16[192,256]{1,0:T(8,128)(2...) custom-call(s32[20]{0:T(128)S(1)} %concatenate.60.places, ...), custom_call_target="tpu_custom_call" | custom-call | flops 100000000 | bytes 1048576 | tf_op jit(solution)/shard_map/pallas_call | solution.py:223
  35.4 7.2 %shard_map.281 = (bf16[192,256]{1,0:T(8,128)(2,1)S(1)}, bf16[192,256]{1,0:T(8,128)(2,1)}, bf16[192,256]{1,0:T(8,128)(2,1)S(1)}, bf16[192,256]{1,0:T(8,128)(2,1)}...) custom-call(s32[20]{0:T(128)S(1)} %concatenate.60.places, ...), custom_call_target="tpu_custom_call" | custom-call | flops 100000000 | bytes 1048576 | tf_op jit(solution)/shard_map/pallas_call | solution.py:223
  49.1 6.8 %shard_map.282 = (bf16[192,256]{1,0:T(8,128)(2,1)S(1)}, bf16[192,256]{1,0:T(8,128)(2,1)}, bf16[192,256]{1,0:T(8,128)(2,1)}, bf16[192,256]{1,0:T(8,128)(2,1)}, bf...) custom-call(s32[20]{0:T(128)S(1)} %concatenate.60.places, ...), custom_call_target="tpu_custom_call" | custom-call | flops 100000000 | bytes 1048576 | tf_op jit(solution)/shard_map/pallas_call | solution.py:223
  67.5 26.3 %shard_map.283 = (bf16[768,768]{1,0:T(8,128)(2,1)}, bf16[768,768]{1,0:T(8,128)(2,1)S(1)}, f32[768,768]{1,0:T(8,128)}, bf16[768,768]{1,0:T(8,128)(2,1)S(1)}, bf16...) custom-call(s32[20]{0:T(128)S(1)} %concatenate.60.places, ...), custom_call_target="tpu_custom_call" | custom-call | flops 8153726976 | bytes 20971520 | tf_op jit(solution)/shard_map/pallas_call | solution.py:487
  96.8 15.6 %shard_map.284 = (bf16[4,384,768]{2,1,0:T(8,128)(2,1)}, bf16[4,768,384]{2,1,0:T(8,128)(2,1)}, f32[1,1536]{1,0:T(1,128)S(1)}, f32[768,768]{1,0:T(8,128)}) custom-call(s32[20]{0:T(128)S(1)} %concatenate.60.places, bf16[8,768,384]{2,1,0:T(8,128)(2,1)} %get-tuple-element.185.active.refs_0_, bf16[8,768,384]{2,1,0:T(8,128)(2,1)} %get-tuple-element.186.slope.refs_1_, ...), custom_call_target="tpu_custom_call" | custom-call | flops 7247757312 | bytes 20971520 | tf_op jit(solution)/shard_map/pallas_call | solution.py:487
  113.2 21.2 %shard_map.285 = (bf16[4,384,768]{2,1,0:T(8,128)(2,1)}, bf16[4,768,384]{2,1,0:T(8,128)(2,1)}, f32[1,1536]{1,0:T(1,128)S(1)}, f32[768,768]{1,0:T(8,128)}, f32[8,7...) custom-call(s32[20]{0:T(128)S(1)} %concatenate.60.places, ...), custom_call_target="tpu_custom_call" | custom-call | flops 7247757312 | bytes 20971520 | tf_op jit(solution)/shard_map/pallas_call | solution.py:487
  138.1 3.7 collective-permute-done.20.g2
  156.0 13.7 %shard_map.286 = (bf16[256,768]{1,0:T(8,128)(2,1)S(1)}, bf16[256,768]{1,0:T(8,128)(2,1)S(1)}, bf16[256,768]{1,0:T(8,128)(2,1)S(1)}, bf16[256,768]{1,0:T(8,128)(2...) custom-call(s32[20]{0:T(128)S(1)} %concatenate.60.places, bf16[1,192,256]{2,1,0:T(8,128)(2,1)S(1)} %get-tuple-element.204.g0, ...), custom_call_target="tpu_custom_call" | custom-call | flops 100000000 | bytes 1048576 | tf_op jit(solution)/shard_map/pallas_call | solution.py:223
  169.7 5.0 %collective-permute-done.26.g2 = bf16[2,2,192,256]{3,2,1,0:T(8,128)(2,1)S(1)} collective-permute-done((bf16[2,2,192,256]{3,2,1,0:T(8,128)(2,1)S(1)}, bf16[2,2,192,256]{3,2,1,0:T(8,128)(2,1)S(1)}, u32[]{:S(2)}, u32[]{:S(2)}) %collective-permute-start.26) | collective-permute-done | bytes 393248 | tf_op jit(solution)/shard_map/ppermute | solution.py:29
  183.3 13.5 %shard_map.287 = (bf16[256,768]{1,0:T(8,128)(2,1)S(1)}, bf16[256,768]{1,0:T(8,128)(2,1)S(1)}, bf16[256,768]{1,0:T(8,128)(2,1)S(1)}, bf16[256,768]{1,0:T(8,128)(2...) custom-call(s32[20]{0:T(128)S(1)} %concatenate.60.places, bf16[2,192,256]{2,1,0:T(8,128)(2,1)S(1)} %get-tuple-element.223.g0, ...), custom_call_target="tpu_custom_call" | custom-call | flops 100000000 | bytes 1048576 | tf_op jit(solution)/shard_map/pallas_call | solution.py:223
  207.0 13.4 %shard_map.288 = (bf16[256,768]{1,0:T(8,128)(2,1)S(1)}, bf16[256,768]{1,0:T(8,128)(2,1)}, bf16[256,768]{1,0:T(8,128)(2,1)S(1)}, bf16[256,768]{1,0:T(8,128)(2,1)S...) custom-call(s32[20]{0:T(128)S(1)} %concatenate.60.places, bf16[2,192,256]{2,1,0:T(8,128)(2,1)S(1)} %get-tuple-element.223.g0, ...), custom_call_target="tpu_custom_call" | custom-call | flops 100000000 | bytes 1048576 | tf_op jit(solution)/shard_map/pallas_call | solution.py:223
  233.5 4.3 %collective-permute-done.39 = bf16[2,192,384]{2,1,0:T(8,128)(2,1)S(1)} collective-permute-done((bf16[2,192,384]{2,1,0:T(8,128)(2,1)S(1)}, bf16[2,192,384]{2,1,0:T(8,128)(2,1)S(1)}, u32[]{:S(2)}, u32[]{:S(2)}) %collective-permute-start.39) | collective-permute-done | bytes 294944 | tf_op jit(solution)/shard_map/ppermute | solution.py:29
  237.8 7.2 %collective-permute-done.38 = bf16[2,96,768]{2,1,0:T(8,128)(2,1)S(1)} collective-permute-done((bf16[2,96,768]{2,1,0:T(8,128)(2,1)S(1)}, bf16[2,96,768]{2,1,0:T(8,128)(2,1)S(1)}, u32[]{:S(2)}, u32[]{:S(2)}) %collective-permute-start.38) | collective-permute-done | bytes 294944 | tf_op jit(solution)/shard_map/ppermute | solution.py:29
  246.2 8.1 %collective-permute-done.41 = bf16[2,112,768]{2,1,0:T(8,128)(2,1)S(1)} collective-permute-done((bf16[2,112,768]{2,1,0:T(8,128)(2,1)S(1)}, bf16[2,112,768]{2,1,0:T(8,128)(2,1)S(1)}, u32[]{:S(2)}, u32[]{:S(2)}) %collective-permute-start.41) | collective-permute-done | bytes 344096 | tf_op jit(solution)/shard_map/ppermute | solution.py:29
  260.0 12.4 %collective-permute-done.45 = bf16[1,192,384]{2,1,0:T(8,128)(2,1)S(1)} collective-permute-done((bf16[1,192,384]{2,1,0:T(8,128)(2,1)S(1)}, bf16[1,192,384]{2,1,0:T(8,128)(2,1)S(1)}, u32[]{:S(2)}, u32[]{:S(2)}) %collective-permute-start.45) | collective-permute-done | bytes 147488 | tf_op jit(solution)/shard_map/ppermute | solution.py:29
  275.6 14.7 %collective-permute-done.49 = bf16[1,192,384]{2,1,0:T(8,128)(2,1)S(1)} collective-permute-done((bf16[1,192,384]{2,1,0:T(8,128)(2,1)S(1)}, bf16[1,192,384]{2,1,0:T(8,128)(2,1)S(1)}, u32[]{:S(2)}, u32[]{:S(2)}) %collective-permute-start.49) | collective-permute-done | bytes 147488 | tf_op jit(solution)/shard_map/ppermute | solution.py:29
  296.7 5.7 %collective-permute-done.52 = bf16[2,192,384]{2,1,0:T(8,128)(2,1)S(1)} collective-permute-done((bf16[2,192,384]{2,1,0:T(8,128)(2,1)S(1)}, bf16[2,192,384]{2,1,0:T(8,128)(2,1)S(1)}, u32[]{:S(2)}, u32[]{:S(2)}) %collective-permute-start.52) | collective-permute-done | bytes 294944 | tf_op jit(solution)/shard_map/ppermute | solution.py:29
  307.4 9.5 %collective-permute-done.57 = bf16[4,192,384]{2,1,0:T(8,128)(2,1)S(1)} collective-permute-done((bf16[4,192,384]{2,1,0:T(8,128)(2,1)S(1)}, bf16[4,192,384]{2,1,0:T(8,128)(2,1)S(1)}, u32[]{:S(2)}, u32[]{:S(2)}) %collective-permute-start.57) | collective-permute-done | bytes 589856 | tf_op jit(solution)/shard_map/ppermute | solution.py:29
  329.2 20.8 %collective-permute-done.65.refs_0_ = bf16[8,96,768]{2,1,0:T(8,128)(2,1)} collective-permute-done((bf16[8,96,768]{2,1,0:T(8,128)(2,1)}, bf16[8,96,768]{2,1,0:T(8,128)(2,1)}, u32[]{:S(2)}, u32[]{:S(2)}) %collective-permute-start.65) | collective-permute-done | bytes 1179680 | tf_op jit(solution)/shard_map/ppermute | solution.py:29
  356.6 4.8 %shard_map.292.refs_2_ = f32[3072,768]{1,0:T(8,128)} custom-call(s32[20]{0:T(128)S(1)} %concatenate.60.places, bf16[8,96,768]{2,1,0:T(8,128)(2,1)} %pad_maximum_fusion.1.refs_0_, bf16[8,96,768]{2,1,0:T(8,128)(2,1)} %collective-permute-done.67.refs_1_), custom_call_target="tpu_custom_call" | custom-call | flops 589824 | bytes 20971520 | tf_op jit(solution)/shard_map/pallas_call | solution.py:487
  364.6 4.4 %shard_map.293 = f32[3072,768]{1,0:T(8,128)} custom-call(s32[20]{0:T(128)S(1)} %concatenate.60.places, bf16[8,96,768]{2,1,0:T(8,128)(2,1)} %collective-permute-done.65.refs_0_, bf16[8,96,768]{2,1,0:T(8,128)(2,1)S(1)} %collective-permute-done.66.refs_1_, f32[3072,768]{1,0:T(8,128)} %shard_map.292.refs_2_), custom_call_target="tpu_custom_call", output_to_operand_aliasing={{}: (3, {})} | custom-call | flops 589824 | bytes 20971520 | tf_op jit(solution)/shard_map/pallas_call | solution.py:487
  369.0 4.4 %shard_map.291 = f32[768,3072]{1,0:T(8,128)} custom-call(s32[20]{0:T(128)S(1)} %concatenate.60.places, bf16[8,192,384]{2,1,0:T(8,128)(2,1)} %collective-permute-done.62.refs_0_, bf16[8,192,384]{2,1,0:T(8,128)(2,1)S(1)} %collective-permute-done.63.refs_1_, f32[768,3072]{1,0:T(8,128)} %shard_map.290.refs_2_), custom_call_target="tpu_custom_call", output_to_operand_aliasing={{}: (3, {})} | custom-call | flops 589824 | bytes 20971520 | tf_op jit(solution)/shard_map/pallas_call | solution.py:487
  373.5 9.4 %shard_map.289 = (f32[768,2304]{1,0:T(8,128)}, f32[768,768]{1,0:T(8,128)}, f32[16,768]{1,0:T(8,128)S(1)}, f32[8,768]{1,0:T(8,128)S(1)}) custom-call(s32[20]{0:T(128)S(1)} %concatenate.60.places, bf16[8,112,768]{2,1,0:T(8,128)(2,1)S(1)} %pad_maximum_fusion.refs_0_, bf16[8,112,768]{2,1,0:T(8,128)(2,1)S(1)} %collective-permute-done.59.refs_1_, ...), custom_call_target="tpu_custom_call" | custom-call | flops 1000 | bytes 20971520 | tf_op jit(solution)/shard_map/pallas_call | solution.py:487
  (337 shorter events, 135.8 us)
Async XLA Ops:
  5.0 20.6 %collective-permute-start = (bf16[256,768]{1,0:T(8,128)(2,1)S(1)}, bf16[256,768]{1,0:T(8,128)(2,1)S(1)}, u32[]{:S(2)}, u32[]{:S(2)}) collective-permute-start(bf16[256,768]{1,0:T(8,128)(2,1)S(1)} %get-tuple-element.338.x0), channel_id=1, source_target_pairs={{0,1},{1,0},{2,3},{3,2},{4,5},{5,4},{6,7},{7,6},{8,9},{9,8},{10,11... | collective-permute-start | bytes 1179656 | tf_op jit(solution)/shard_map/ppermute | solution.py:29
  5.0 29.1 %collective-permute-start.6 = (bf16[256,768]{1,0:T(8,128)(2,1)S(1)}, bf16[256,768]{1,0:T(8,128)(2,1)S(1)}, u32[]{:S(2)}, u32[]{:S(2)}) collective-permute-start(bf16[256,768]{1,0:T(8,128)(2,1)S(1)} %get-tuple-element.172.x0), channel_id=1, source_target_pairs={{0,1},{1,0},{2,3},{3,2},{4,5},{5,4},{6,7},{7,6},{8,9},{9,8},{10,11... | collective-permute-start | bytes 1179656 | tf_op jit(solution)/shard_map/ppermute | solution.py:29
  14.1 19.3 %collective-permute-start.7 = (bf16[256,768]{1,0:T(8,128)(2,1)S(1)}, bf16[256,768]{1,0:T(8,128)(2,1)}, u32[]{:S(2)}, u32[]{:S(2)}) collective-permute-start(bf16[256,768]{1,0:T(8,128)(2,1)S(1)} %get-tuple-element.172.x0), channel_id=1, source_target_pairs={{0,2},{1,3},{2,0},{3,1},{4,6},{5,7},{6,4},{7,5},{8,10},{9,11},{10,... | collective-permute-start | bytes 1179656 | tf_op jit(solution)/shard_map/ppermute | solution.py:29
  112.4 29.4 %collective-permute-start.19 = (bf16[4,768,384]{2,1,0:T(8,128)(2,1)}, bf16[4,768,384]{2,1,0:T(8,128)(2,1)S(1)}, u32[]{:S(2)}, u32[]{:S(2)}) collective-permute-start(bf16[4,768,384]{2,1,0:T(8,128)(2,1)} %get-tuple-element.196), channel_id=1, source_target_pairs={{0,1},{1,0},{2,3},{3,2},{4,5},{5,4},{6,7},{7,6},{8,9},{9,8},{10,11... | collective-permute-start | bytes 7077896 | tf_op jit(solution)/shard_map/ppermute | solution.py:29
  113.1 32.2 %collective-permute-start.18 = (bf16[4,384,768]{2,1,0:T(8,128)(2,1)}, bf16[4,384,768]{2,1,0:T(8,128)(2,1)S(1)}, u32[]{:S(2)}, u32[]{:S(2)}) collective-permute-start(bf16[4,384,768]{2,1,0:T(8,128)(2,1)} %get-tuple-element.194), channel_id=1, source_target_pairs={{0,1},{1,0},{2,3},{3,2},{4,5},{5,4},{6,7},{7,6},{8,9},{9,8},{10,11... | collective-permute-start | bytes 7077896 | tf_op jit(solution)/shard_map/ppermute | solution.py:29
  146.9 27.7 %collective-permute-start.23 = (bf16[2,8,96,192]{3,2,1,0:T(8,128)(2,1)}, bf16[2,8,96,192]{3,2,1,0:T(8,128)(2,1)}, u32[]{:S(2)}, u32[]{:S(2)}) collective-permute-start(bf16[2,8,96,192]{3,2,1,0:T(8,128)(2,1)} %slice.171), channel_id=1, source_target_pairs={{0,2},{1,3},{2,0},{3,1},{4,6},{5,7},{6,4},{7,5},{8,10},{9,11},{10,... | collective-permute-start | bytes 1769480 | tf_op jit(solution)/shard_map/ppermute | solution.py:29
  148.1 26.6 %collective-permute-start.21 = (bf16[384,768]{1,0:T(8,128)(2,1)}, bf16[384,768]{1,0:T(8,128)(2,1)}, u32[]{:S(2)}, u32[]{:S(2)}) collective-permute-start(bf16[384,768]{1,0:T(8,128)(2,1)} %get-tuple-element.201), channel_id=1, source_target_pairs={{0,4},{4,0},{8,12},{12,8},{16,20},{20,16},{24,28},{28,24},{1,5},{5... | collective-permute-start | bytes 1769480 | tf_op jit(solution)/shard_map/ppermute | solution.py:29
  149.6 25.1 %collective-permute-start.22 = (bf16[768,384]{1,0:T(8,128)(2,1)}, bf16[768,384]{1,0:T(8,128)(2,1)}, u32[]{:S(2)}, u32[]{:S(2)}) collective-permute-start(bf16[768,384]{1,0:T(8,128)(2,1)} %get-tuple-element.202), channel_id=1, source_target_pairs={{0,8},{4,12},{8,0},{12,4},{16,24},{20,28},{24,16},{28,20},{1,9},{5... | collective-permute-start | bytes 1769480 | tf_op jit(solution)/shard_map/ppermute | solution.py:29
  151.2 23.5 %collective-permute-start.26 = (bf16[2,2,192,256]{3,2,1,0:T(8,128)(2,1)S(1)}, bf16[2,2,192,256]{3,2,1,0:T(8,128)(2,1)S(1)}, u32[]{:S(2)}, u32[]{:S(2)}) collective-permute-start(bf16[2,2,192,256]{3,2,1,0:T(8,128)(2,1)S(1)} %get-tuple-element.216), channel_id=1, source_target_pairs={{0,2},{1,3},{2,0},{3,1},{4,6},{5,7},{6,4},{7,5},{8,10},{9,11},{10,... | collective-permute-start | bytes 1179656 | tf_op jit(solution)/shard_map/ppermute | solution.py:29
  176.7 20.2 %collective-permute-start.33 = (bf16[8,96,192]{2,1,0:T(8,128)(2,1)}, bf16[8,96,192]{2,1,0:T(8,128)(2,1)}, u32[]{:S(2)}, u32[]{:S(2)}) collective-permute-start(bf16[8,96,192]{2,1,0:T(8,128)(2,1)} %fusion.12), channel_id=1, source_target_pairs={{0,1},{1,0},{2,3},{3,2},{4,5},{5,4},{6,7},{7,6},{8,9},{9,8},{10,11... | collective-permute-start | bytes 884744 | tf_op jit(solution)/shard_map/ppermute | solution.py:29
  176.7 21.9 %collective-permute-start.32 = (bf16[256,768]{1,0:T(8,128)(2,1)S(1)}, bf16[256,768]{1,0:T(8,128)(2,1)}, u32[]{:S(2)}, u32[]{:S(2)}) collective-permute-start(bf16[256,768]{1,0:T(8,128)(2,1)S(1)} %get-tuple-element.240), channel_id=1, source_target_pairs={{0,1},{1,0},{2,3},{3,2},{4,5},{5,4},{6,7},{7,6},{8,9},{9,8},{10,11... | collective-permute-start | bytes 1179656 | tf_op jit(solution)/shard_map/ppermute | solution.py:29
  177.2 23.2 %collective-permute-start.31 = (bf16[256,768]{1,0:T(8,128)(2,1)S(1)}, bf16[256,768]{1,0:T(8,128)(2,1)}, u32[]{:S(2)}, u32[]{:S(2)}) collective-permute-start(bf16[256,768]{1,0:T(8,128)(2,1)S(1)} %get-tuple-element.238), channel_id=1, source_target_pairs={{0,1},{1,0},{2,3},{3,2},{4,5},{5,4},{6,7},{7,6},{8,9},{9,8},{10,11... | collective-permute-start | bytes 1179656 | tf_op jit(solution)/shard_map/ppermute | solution.py:29
  180.2 22.2 %collective-permute-start.27 = (bf16[384,768]{1,0:T(8,128)(2,1)S(1)}, bf16[384,768]{1,0:T(8,128)(2,1)S(1)}, u32[]{:S(2)}, u32[]{:S(2)}) collective-permute-start(bf16[384,768]{1,0:T(8,128)(2,1)S(1)} %copy-done.40), channel_id=1, source_target_pairs={{0,4},{4,0},{8,12},{12,8},{16,20},{20,16},{24,28},{28,24},{1,5},{5... | collective-permute-start | bytes 1769480 | tf_op jit(solution)/shard_map/ppermute | solution.py:29
  181.7 20.7 %collective-permute-start.28 = (bf16[768,384]{1,0:T(8,128)(2,1)S(1)}, bf16[768,384]{1,0:T(8,128)(2,1)S(1)}, u32[]{:S(2)}, u32[]{:S(2)}) collective-permute-start(bf16[768,384]{1,0:T(8,128)(2,1)S(1)} %copy-done.39), channel_id=1, source_target_pairs={{0,8},{4,12},{8,0},{12,4},{16,24},{20,28},{24,16},{28,20},{1,9},{5... | collective-permute-start | bytes 1769480 | tf_op jit(solution)/shard_map/ppermute | solution.py:29
  232.7 21.7 %collective-permute-start.43 = (bf16[256,768]{1,0:T(8,128)(2,1)S(1)}, bf16[256,768]{1,0:T(8,128)(2,1)S(1)}, u32[]{:S(2)}, u32[]{:S(2)}) collective-permute-start(bf16[256,768]{1,0:T(8,128)(2,1)S(1)} %add_convert_fusion.5), channel_id=1, source_target_pairs={{0,2},{1,3},{2,0},{3,1},{4,6},{5,7},{6,4},{7,5},{8,10},{9,11},{10,... | collective-permute-start | bytes 1179656 | tf_op jit(solution)/shard_map/ppermute | solution.py:29
  272.7 20.7 %collective-permute-start.48 = (bf16[1,96,768]{2,1,0:T(8,128)(2,1)S(1)}, bf16[1,96,768]{2,1,0:T(8,128)(2,1)S(1)}, u32[]{:S(2)}, u32[]{:S(2)}) collective-permute-start(bf16[1,96,768]{2,1,0:T(8,128)(2,1)S(1)} %add.204), channel_id=1, source_target_pairs={{0,16},{4,20},{8,24},{12,28},{16,0},{20,4},{24,8},{28,12},{1,17},{... | collective-permute-start | bytes 442376 | tf_op jit(solution)/shard_map/ppermute | solution.py:29
  275.6 19.7 %collective-permute-start.50 = (bf16[1,112,768]{2,1,0:T(8,128)(2,1)S(1)}, bf16[1,112,768]{2,1,0:T(8,128)(2,1)S(1)}, u32[]{:S(2)}, u32[]{:S(2)}) collective-permute-start(bf16[1,112,768]{2,1,0:T(8,128)(2,1)S(1)} %add.206), channel_id=1, source_target_pairs={{0,16},{4,20},{8,24},{12,28},{16,0},{20,4},{24,8},{28,12},{1,17},{... | collective-permute-start | bytes 516104 | tf_op jit(solution)/shard_map/ppermute | solution.py:29
  320.3 30.6 %collective-permute-start.60 = (bf16[8,112,768]{2,1,0:T(8,128)(2,1)S(1)}, bf16[8,112,768]{2,1,0:T(8,128)(2,1)}, u32[]{:S(2)}, u32[]{:S(2)}) collective-permute-start(bf16[8,112,768]{2,1,0:T(8,128)(2,1)S(1)} %pad_maximum_fusion.refs_0_), channel_id=1, source_target_pairs={{0,2},{1,3},{2,0},{3,1},{4,6},{5,7},{6,4},{7,5},{8,10},{9,11},{10,... | collective-permute-start | bytes 4128776 | tf_op jit(solution)/shard_map/ppermute | solution.py:29
  321.3 28.7 %collective-permute-start.65 = (bf16[8,96,768]{2,1,0:T(8,128)(2,1)}, bf16[8,96,768]{2,1,0:T(8,128)(2,1)}, u32[]{:S(2)}, u32[]{:S(2)}) collective-permute-start(bf16[8,96,768]{2,1,0:T(8,128)(2,1)} %pad_maximum_fusion.1.refs_0_), channel_id=1, source_target_pairs={{0,4},{4,0},{8,12},{12,8},{16,20},{20,16},{24,28},{28,24},{1,5},{5... | collective-permute-start | bytes 3538952 | tf_op jit(solution)/shard_map/ppermute | solution.py:29
  322.7 28.2 %collective-permute-start.62 = (bf16[8,192,384]{2,1,0:T(8,128)(2,1)S(1)}, bf16[8,192,384]{2,1,0:T(8,128)(2,1)}, u32[]{:S(2)}, u32[]{:S(2)}) collective-permute-start(bf16[8,192,384]{2,1,0:T(8,128)(2,1)S(1)} %pad_maximum_fusion.2.refs_0_), channel_id=1, source_target_pairs={{0,8},{4,12},{8,0},{12,4},{16,24},{20,28},{24,16},{28,20},{1,9},{5... | collective-permute-start | bytes 3538952 | tf_op jit(solution)/shard_map/ppermute | solution.py:29
  328.7 32.7 %collective-permute-start.64 = (bf16[8,192,384]{2,1,0:T(8,128)(2,1)S(1)}, bf16[8,192,384]{2,1,0:T(8,128)(2,1)S(1)}, u32[]{:S(2)}, u32[]{:S(2)}) collective-permute-start(bf16[8,192,384]{2,1,0:T(8,128)(2,1)S(1)} %pad_maximum_fusion.2.refs_0_), channel_id=1, source_target_pairs={{0,1},{1,0},{2,3},{3,2},{4,5},{5,4},{6,7},{7,6},{8,9},{9,8},{10,11... | collective-permute-start | bytes 3538952 | tf_op jit(solution)/shard_map/ppermute | solution.py:29
  328.8 44.7 %collective-permute-start.59 = (bf16[8,112,768]{2,1,0:T(8,128)(2,1)S(1)}, bf16[8,112,768]{2,1,0:T(8,128)(2,1)S(1)}, u32[]{:S(2)}, u32[]{:S(2)}) collective-permute-start(bf16[8,112,768]{2,1,0:T(8,128)(2,1)S(1)} %pad_maximum_fusion.refs_0_), channel_id=1, source_target_pairs={{0,1},{1,0},{2,3},{3,2},{4,5},{5,4},{6,7},{7,6},{8,9},{9,8},{10,11... | collective-permute-start | bytes 4128776 | tf_op jit(solution)/shard_map/ppermute | solution.py:29
  350.9 18.2 %collective-permute-start.63 = (bf16[8,192,384]{2,1,0:T(8,128)(2,1)}, bf16[8,192,384]{2,1,0:T(8,128)(2,1)S(1)}, u32[]{:S(2)}, u32[]{:S(2)}) collective-permute-start(bf16[8,192,384]{2,1,0:T(8,128)(2,1)} %collective-permute-done.62.refs_0_), channel_id=1, source_target_pairs={{0,1},{1,0},{2,3},{3,2},{4,5},{5,4},{6,7},{7,6},{8,9},{9,8},{10,11... | collective-permute-start | bytes 3538952 | tf_op jit(solution)/shard_map/ppermute | solution.py:29
  350.9 22.6 %collective-permute-start.61 = (bf16[8,112,768]{2,1,0:T(8,128)(2,1)}, bf16[8,112,768]{2,1,0:T(8,128)(2,1)}, u32[]{:S(2)}, u32[]{:S(2)}) collective-permute-start(bf16[8,112,768]{2,1,0:T(8,128)(2,1)} %collective-permute-done.60.refs_2_), channel_id=1, source_target_pairs={{0,1},{1,0},{2,3},{3,2},{4,5},{5,4},{6,7},{7,6},{8,9},{9,8},{10,11... | collective-permute-start | bytes 4128776 | tf_op jit(solution)/shard_map/ppermute | solution.py:29
  (106 other events, 1185.8 us)

commit v3 on v2

--- a/solution.py
+++ b/solution.py
@@ -11,7 +11,7 @@
 NN = (((1,), (0,)), ((), ()))
 NT = (((1,), (1,)), ((), ()))
 TN = (((0,), (0,)), ((), ()))
-VMEM_LIMIT = 50 * 1024 * 1024
+VMEM_LIMIT = 60 * 1024 * 1024
 HEADS = 12
 EPSILON = 1e-06
 BITS = {"c": ("seq", 0), "x": ("seq", 1), "y": ("dp", 0), "l": ("dp", 1), "h": ("dp", 2)}
@@ -131,8 +131,8 @@
 def attend_backward(
     heads, index, places, g0, g1, g2, g3, w_t, x_in, qkv, ctx_blk, lse, acc_in, acc_b, *refs
 ):
-    last = len(refs) == 16
-    (dx0, dx1, dx2, dx3, grad_w, grad_b, g_tok, g_blk, d_qkv, tok, x_seq, acc, dx_s, sems) = refs[-14:]
+    last = len(refs) == 14
+    (dx_keep, dx_send, grad_w, grad_b, g_tok, g_blk, d_qkv, tok, x_seq, acc, dx_s, sems) = refs[-12:]
     bring_x = pltpu.make_async_copy(x_in, x_seq, sems.at[0])
     bring_acc = pltpu.make_async_copy(acc_in, acc, sems.at[1])
     bring_x.start()
@@ -183,7 +183,8 @@
     tok[:, block:] = late[:, block:].astype(jnp.bfloat16)
     tok[:, :block] = (late[:, :block] + front).astype(jnp.bfloat16)
     sent = []
-    for r, piece in enumerate((dx0, dx1, dx2, dx3)):
+    for r in range(4):
+        piece = (dx_send if r & 1 else dx_keep).at[r >> 1]
         columns = tok[:, pl.ds(pl.multiple_of((r ^ mine) * quarter, quarter), quarter)]
         dx_s[r] = dot_f32(columns, w_t[...], TN).astype(jnp.bfloat16)
         sent.append(pltpu.make_async_copy(dx_s.at[r], piece, sems.at[2 + r]))
@@ -272,7 +273,7 @@
         if late
         else out((3 * wide, features), jnp.float32)
     )
-    outs = [out((quarter, features), jnp.bfloat16)] * 4 + [grad, out((8, 3 * wide), jnp.float32)]
+    outs = [out((2, quarter, features), jnp.bfloat16)] * 2 + [grad, out((8, 3 * wide), jnp.float32)]
     scratch = [
         pltpu.VMEM((4, wide, quarter), jnp.bfloat16),
         pltpu.VMEM((2, wide, block), jnp.bfloat16),
@@ -290,9 +291,9 @@
         outs,
         scratch,
         left_in=(5, 9),
-        left_out=(0, 1, 2, 3),
-    )
-    return found[:4], found[4], found[5]
+        left_out=(0, 1),
+    )
+    return found[:2], found[2], found[3]
 
 def live_rows(places, rows, mine, local_rows, offset):
     row = lax.broadcasted_iota(jnp.int32, (rows, 1), 0)
@@ -321,21 +322,59 @@
     return jnp.sum(array_in, axis=0, keepdims=True)
 
 
-def feed_forward(shape, places, *refs):
-    seq_count, seq_parts, steps = shape
-    pieces, refs = refs[: seq_count * seq_parts], refs[seq_count * seq_parts :]
-    tokens, cot, w_out, vectors, w_up, b_up, w_down = refs[:7]
-    out, context, first_in, first_low, active, slope, d_second, d_lowered, sums = refs[7:16]
-    first_norm, lowered = refs[16:]
+def token_layer(shape, places, *refs):
+    seq_count, seq_parts = shape
+    count = seq_count * seq_parts
+    pieces, refs = refs[:count], refs[count:]
+    tokens, cot_in, w_out, vectors, b_up, w_up_in, w_down_in = refs[:7]
+    out, send_down1, send_up1, send_down0, send_up0, keep_down, keep_up = refs[7:14]
+    d_first_in, sums, grad_out = refs[14:17]
+    sent = refs[17:23]
+    (
+        w_up, w_down, active, slope, context, first_in, first_norm, lowered,
+        first_low, first_t, d_lowered, turned, out_s, cot, grad_down, grad_up, sems,
+    ) = refs[23:]
     rows, features = tokens.shape
     local_rows = rows // seq_count
     wide = features // seq_parts
-    mine = places[9]
+    mine, inner = places[9], places[8]
     step = pl.program_id(0)
-    f32 = jnp.float32
+    quarters = w_up.shape[0]
+    width = w_up.shape[2]
+    f32, bf16 = jnp.float32, jnp.bfloat16
+
+    def bring(j):
+        return (
+            pltpu.make_async_copy(
+                w_up_in.at[:, pl.ds(j * width, width)], w_up.at[j], sems.at[j]
+            ),
+            pltpu.make_async_copy(
+                w_down_in.at[pl.ds(j * width, width), :], w_down.at[j], sems.at[quarters + j]
+            ),
+        )
+
+    keep_out = pltpu.make_async_copy(out_s, out, sems.at[2 * quarters])
+    bring_cot = pltpu.make_async_copy(cot_in, cot, sems.at[2 * quarters + 1])
+
+    def leave(relative):
+        down_ref, up_ref = (
+            (keep_down.at[pl.ds(0, 2)], keep_up.at[pl.ds(0, 2)]),
+            (keep_down.at[pl.ds(2, 2)], keep_up.at[pl.ds(2, 2)]),
+            (send_down0, send_up0),
+            (send_down1, send_up1),
+        )[relative]
+        first = 2 * quarters + 2 + 2 * relative
+        return (
+            pltpu.make_async_copy(grad_down.at[relative & 1], down_ref, sems.at[first]),
+            pltpu.make_async_copy(grad_up.at[relative & 1], up_ref, sems.at[first + 1]),
+        )
 
     @pl.when(step == 0)
     def start():
+        for j in range(quarters):
+            for copy in bring(j):
+                copy.start()
+        bring_cot.start()
         for s in range(seq_count):
             for r in range(seq_parts):
                 context[
@@ -349,126 +388,107 @@
         hat, _ = normal_parts(total)
         normed = hat * vectors[1:2, :] + vectors[2:3, :]
         first_norm[...] = normed
-        first_low[...] = normed.astype(jnp.bfloat16)
-
-    lifted = dot_f32(first_low[...], w_up[...], NN) + b_up[...]
-    cdf = 0.5 * (1.0 + lax.erf(lifted * 0.7071067811865476))
-    density = jnp.exp(lifted * lifted * -0.5) * 0.3989422804014327
-    gelu = (lifted * cdf).astype(jnp.bfloat16)
-    active[0] = gelu
-    slope[0] = (cdf + lifted * density).astype(jnp.bfloat16)
-    part = dot_f32(gelu, w_down[...], NN)
-
-    @pl.when(step == 0)
-    def first():
-        lowered[...] = part
-
-    @pl.when(step > 0)
-    def later():
-        lowered[...] += part
-
-    @pl.when(step == steps - 1)
-    def finish():
+        low = normed.astype(bf16)
+        first_low[...] = low
+        tile = features // 4
+        low_t = low.T
+        for q in range(4):
+            first_t[pl.ds(pl.multiple_of((q ^ inner) * tile, tile), tile), :] = low_t[
+                q * tile : (q + 1) * tile
+            ]
+        lowered[...] = jnp.zeros_like(lowered)
+        sums[...] = jnp.zeros_like(sums)
+
+    @pl.when(step < quarters)
+    def forward():
+        for j in range(quarters):
+
+            @pl.when(step == j)
+            def arrive():
+                for copy in bring(j):
+                    copy.wait()
+
+        lifted = dot_f32(first_low[...], w_up[step], NN) + b_up[step]
+        cdf = 0.5 * (1.0 + lax.erf(lifted * 0.7071067811865476))
+        density = jnp.exp(lifted * lifted * -0.5) * 0.3989422804014327
+        gelu = (lifted * cdf).astype(bf16)
+        active[step] = gelu
+        slope[step] = (cdf + lifted * density).astype(bf16)
+        lowered[...] += dot_f32(gelu, w_down[step], NN)
+
+    @pl.when(step == quarters - 1)
+    def turn():
         live = live_rows(places, rows, mine, local_rows, 11)
         hat, inverse = normal_parts(first_norm[...] + (lowered[...] + vectors[3:4, :]))
         gain = vectors[4:5, :]
-        out[...] = ((hat * gain + vectors[5:6, :]) * live).astype(jnp.bfloat16)
+        bring_cot.wait()
+        out_s[...] = ((hat * gain + vectors[5:6, :]) * live).astype(bf16)
+        keep_out.start()
         incoming = cot[...].astype(f32) * live
         back = normal_back(hat, inverse, gain, incoming)
-        d_second[...] = back
-        low = back.astype(jnp.bfloat16)
+        lowered[...] = back
+        low = back.astype(bf16)
         d_lowered[...] = low
         sums[0:1, :] = column_sum(low.astype(f32))
         sums[1:2, :] = column_sum(incoming * hat)
         sums[2:3, :] = column_sum(incoming)
 
-
-def hidden_back(places, active, slope, w_up, w_down, first_t, d_lowered, grad_down, grad_up, grad_b):
-    inner = places[8]
-    f32 = jnp.float32
-    down = dot_f32(active[0], d_lowered[...], TN).astype(jnp.bfloat16)
-    tile = down.shape[0] // 4
-    for q in range(4):
-        grad_down[0, pl.ds(pl.multiple_of((q ^ inner) * tile, tile), tile), :] = down[
-            q * tile : (q + 1) * tile
-        ]
-    d_active = dot_f32(d_lowered[...], w_down[...], NT)
-    d_lifted = (d_active * slope[0].astype(f32)).astype(jnp.bfloat16)
-    grad_b[...] = column_sum(d_lifted.astype(f32))
-    grad_up[0] = dot_f32(first_t[...], d_lifted, NN).astype(jnp.bfloat16)
-    return dot_f32(d_lifted, w_up[...], NT)
-
-
-def turn_rows(places, source, target):
-    inner = places[8]
-    tile = target.shape[0] // 4
-    turned = source[...].T
-    for q in range(4):
-        target[pl.ds(pl.multiple_of((q ^ inner) * tile, tile), tile), :] = turned[
-            q * tile : (q + 1) * tile
-        ]
-
-
-def back_send(
-    places, active, slope, w_up, w_down, first_low, d_lowered, d_second,
-    grad_down, grad_up, grad_b, d_first, first_t,
-):
-    step = pl.program_id(0)
-
-    @pl.when(step == 0)
-    def start():
-        turn_rows(places, first_low, first_t)
-        d_first[...] = d_second[...]
-
-    d_first[...] += hidden_back(
-        places, active, slope, w_up, w_down, first_t, d_lowered, grad_down, grad_up, grad_b
-    )
-
-
-def back_keep(shape, places, *refs):
-    seq_count, seq_parts, steps = shape
-    active, slope, w_up, w_down, first_low, d_lowered, d_part = refs[:7]
-    first_in, context, w_out, vectors = refs[7:11]
-    grad_down, grad_up, grad_b, d_first_in, sums, grad_out = refs[11:17]
-    pieces = refs[17:-3]
-    first_t, d_first, turned = refs[-3:]
-    step = pl.program_id(0)
-    f32 = jnp.float32
-
-    @pl.when(step == 0)
-    def start():
-        turn_rows(places, first_low, first_t)
-        d_first[...] = d_part[...]
-
-    d_first[...] += hidden_back(
-        places, active, slope, w_up, w_down, first_t, d_lowered, grad_down, grad_up, grad_b
-    )
-
-    @pl.when(step == steps - 1)
+    @pl.when(step >= quarters)
+    def backward():
+        relative = 2 * quarters - 1 - step
+        quarter = relative ^ (places[0] >> 1)
+        low_bit = places[0] & 1
+        slot = relative & 1
+        half = width // 2
+        tile = half // 4
+        for k in range(2):
+
+            @pl.when(relative == k)
+            def free():
+                for copy in leave(k + 2):
+                    copy.wait()
+
+        down = dot_f32(active[quarter], d_lowered[...], TN).astype(bf16)
+        for j in range(2):
+            for q in range(4):
+                grad_down[
+                    slot, j ^ low_bit, pl.ds(pl.multiple_of((q ^ inner) * tile, tile), tile), :
+                ] = down[j * half + q * tile : j * half + (q + 1) * tile]
+        d_active = dot_f32(d_lowered[...], w_down[quarter], NT)
+        d_lifted = (d_active * slope[quarter].astype(f32)).astype(bf16)
+        up = dot_f32(first_t[...], d_lifted, NN).astype(bf16)
+        for j in range(2):
+            grad_up[slot, j ^ low_bit] = up[:, j * half : (j + 1) * half]
+        sums[pl.ds(6 + quarter, 1), :] = column_sum(d_lifted.astype(f32))
+        lowered[...] += dot_f32(d_lifted, w_up[quarter], NT)
+        for k in range(quarters):
+
+            @pl.when(relative == k)
+            def start_leaving():
+                for copy in leave(k):
+                    copy.start()
+
+    @pl.when(step == 2 * quarters - 1)
     def finish():
-        rows, features = first_in.shape
-        local_rows = rows // seq_count
-        wide = features // seq_parts
-        mine = places[9]
         hat, inverse = normal_parts(first_in[...])
-        incoming = d_first[...]
+        incoming = lowered[...]
         back = normal_back(hat, inverse, vectors[1:2, :], incoming)
         d_first_in[...] = back
-        low = back.astype(jnp.bfloat16)
-        sums[0:1, :] = column_sum(low.astype(f32))
-        sums[1:2, :] = column_sum(incoming * hat)
-        sums[2:3, :] = column_sum(incoming)
-        turned[...] = dot_f32(w_out[...], low, NT).astype(jnp.bfloat16)
+        low = back.astype(bf16)
+        sums[3:4, :] = column_sum(low.astype(f32))
+        sums[4:5, :] = column_sum(incoming * hat)
+        sums[5:6, :] = column_sum(incoming)
+        turned[...] = dot_f32(w_out[...], low, NT).astype(bf16)
         for r in range(seq_parts):
             own = turned[pl.ds(pl.multiple_of((r ^ mine) * wide, wide), wide), :]
             for s in range(seq_count):
-                target, place = pieces[3 * min(s, 1) + min(r, 2)], max(s - 1, 0)
+                target, place = sent[3 * min(s, 1) + min(r, 2)], max(s - 1, 0)
                 columns = own[:, s * local_rows : (s + 1) * local_rows]
                 if r < 2:
                     target[place] = columns
                 else:
                     target[r - 2, place] = columns
-        product = dot_f32(context[...], low, NN).astype(jnp.bfloat16)
+        product = dot_f32(context[...], low, NN).astype(bf16)
         block_rows, block_cols = grad_out.shape[2:]
         across = features // block_cols
         for j in range(seq_parts):
@@ -477,10 +497,16 @@
                 grad_out[j ^ mine, q ^ places[10]] = product[
                     row : row + block_rows, col : col + block_cols
                 ]
+        keep_out.wait()
+        for k in range(2):
+            for copy in leave(k):
+                copy.wait()
 
 
 def whole_spec(shape):
-    return pl.BlockSpec(shape, lambda p, places: (0,) * len(shape))
+    return pl.BlockSpec(
+        shape, lambda p, places: (0,) * len(shape), pipeline_mode=pl.Buffered(buffer_count=1)
+    )
 
 
 def step_call(body, places, steps, ins, in_specs, outs, out_specs, scratch, flops, aliases={}):
@@ -502,131 +528,71 @@
     )(places, *ins)
 
 
-def run_feed_forward(places, pieces, tokens, cot, w_out, vectors, w_up, b_up, w_down, dims):
+def run_token_layer(places, pieces, tokens, cot, w_out, vectors, w_up, b_up, w_down, dims):
     seq_count, seq_parts = dims
     rows, features = tokens.shape
     hidden = w_up.shape[1]
-    steps = 8
-    tile = hidden // steps
+    quarters = 4
+    width = hidden // quarters
+    half = width // 2
     out, bf16, f32 = jax.ShapeDtypeStruct, jnp.bfloat16, jnp.float32
-    square = (rows, features)
-    up_spec = pl.BlockSpec((features, tile), lambda p, places: (0, places[p]))
-    down_spec = pl.BlockSpec((tile, features), lambda p, places: (places[p], 0))
-    bias_spec = pl.BlockSpec((1, tile), lambda p, places: (0, places[p]))
-    kept_spec = pl.BlockSpec((1, rows, tile), lambda p, places: (p, 0, 0))
+    square, turned = (rows, features), (features, rows)
+    piece = (features // seq_parts, rows // seq_count)
+    sent = []
+    for n in (1, seq_count - 1):
+        sent += [(n, *piece), (n, *piece), (2, n, *piece)]
+    out_blocks = (seq_parts, 8, features // seq_parts // 2, features // 4)
+    away = pl.BlockSpec(memory_space=pl.ANY)
+    down, up = (2, half, features), (2, features, half)
+
     return step_call(
-        functools.partial(feed_forward, (seq_count, seq_parts, steps)),
+        functools.partial(token_layer, dims),
         places,
-        steps,
-        [*pieces, tokens, cot, w_out, vectors, w_up, b_up, w_down],
+        2 * quarters,
+        [*pieces, tokens, cot, w_out, vectors, b_up.reshape(quarters, 1, width), w_up, w_down],
         [whole_spec(p.shape) for p in pieces]
-        + [whole_spec(square), whole_spec(square), whole_spec(w_out.shape), whole_spec(vectors.shape)]
-        + [up_spec, bias_spec, down_spec],
+        + [whole_spec(square), away, whole_spec(w_out.shape), whole_spec(vectors.shape)]
+        + [whole_spec((quarters, 1, width)), away, away],
         [
             out(square, bf16),
-            out((features, rows), bf16),
+            out(down, bf16),
+            out(up, bf16),
+            out(down, bf16),
+            out(up, bf16),
+            out((4, half, features), bf16),
+            out((4, features, half), bf16),
             out(square, f32),
-            out(square, bf16),
-            out((steps, rows, tile), bf16),
-            out((steps, rows, tile), bf16),
-            out(square, f32),
-            out(square, bf16),
-            out((8, features), f32),
-        ],
-        [
-            whole_spec(square),
-            whole_spec((features, rows)),
-            whole_spec(square),
-            whole_spec(square),
-            kept_spec,
-            kept_spec,
-            whole_spec(square),
-            whole_spec(square),
-            whole_spec((8, features)),
-        ],
-        [pltpu.VMEM(square, f32), pltpu.VMEM(square, f32)],
-        2 * rows * features * (2 * hidden + features),
-    )
-
-
-def back_specs(first, rows, features, tile):
-    kept = pl.BlockSpec((1, rows, tile), lambda p, places: (p + first, 0, 0))
-    up = pl.BlockSpec((features, tile), lambda p, places: (0, places[p + first]))
-    down = pl.BlockSpec((tile, features), lambda p, places: (places[p + first], 0))
-    bias = pl.BlockSpec((1, tile), lambda p, places: (0, places[p + first] % 4))
-    grad_down = pl.BlockSpec((1, tile, features), lambda p, places: (p, 0, 0))
-    grad_up = pl.BlockSpec((1, features, tile), lambda p, places: (p, 0, 0))
-    return [kept, kept, up, down], [grad_down, grad_up, bias]
-
-
-def run_back_send(places, active, slope, w_up, w_down, first_low, d_lowered, d_second):
-    steps_all, rows, tile = active.shape
-    features = first_low.shape[1]
-    steps = steps_all // 2
-    out, bf16, f32 = jax.ShapeDtypeStruct, jnp.bfloat16, jnp.float32
-    square = (rows, features)
-    ins, outs = back_specs(steps, rows, features, tile)
-    return step_call(
-        back_send,
-        places,
-        steps,
-        [active, slope, w_up, w_down, first_low, d_lowered, d_second],
-        ins + [whole_spec(square)] * 3,
-        [
-            out((steps, tile, features), bf16),
-            out((steps, features, tile), bf16),
-            out((1, steps * tile), f32),
-            out(square, f32),
-        ],
-        outs + [whole_spec(square)],
-        [pltpu.VMEM((features, rows), bf16)],
-        8 * rows * features * steps * tile,
-    )
-
-
-def run_back_keep(
-    places, active, slope, w_up, w_down, first_low, d_lowered, d_part, first_in, context, w_out,
-    vectors, dims,
-):
-    seq_count, seq_parts = dims
-    steps_all, rows, tile = active.shape
-    features = first_low.shape[1]
-    steps = steps_all // 2
-    out, bf16, f32 = jax.ShapeDtypeStruct, jnp.bfloat16, jnp.float32
-    square = (rows, features)
-    turned = (features, rows)
-    piece = (features // seq_parts, rows // seq_count)
-    pieces = []
-    for n in (1, seq_count - 1):
-        pieces += [(n, *piece), (n, *piece), (2, n, *piece)]
-    out_blocks = (seq_parts, 8, features // seq_parts // 2, features // 4)
-    ins, outs = back_specs(0, rows, features, tile)
-    return step_call(
-        functools.partial(back_keep, (seq_count, seq_parts, steps)),
-        places,
-        steps,
-        [active, slope, w_up, w_down, first_low, d_lowered, d_part, first_in, context, w_out, vectors],
-        ins
-        + [whole_spec(square)] * 4
-        + [whole_spec(turned), whole_spec(w_out.shape), whole_spec(vectors.shape)],
-        [
-            out((steps, tile, features), bf16),
-            out((steps, features, tile), bf16),
-            out((1, steps * tile), f32),
-            out(square, f32),
-            out((8, features), f32),
+            out((16, features), f32),
             out(out_blocks, bf16),
         ]
-        + [out(p, bf16) for p in pieces],
-        outs
-        + [whole_spec(square), whole_spec((8, features)), whole_spec(out_blocks)]
-        + [whole_spec(p) for p in pieces],
-        [pltpu.VMEM(turned, bf16), pltpu.VMEM(square, f32), pltpu.VMEM(turned, bf16)],
-        8 * rows * features * steps * tile,
-    )
-
-
-def place_rows(by_rows, late, places, *refs):
+        + [out(p, bf16) for p in sent],
+        [away] * 7
+        + [whole_spec(square), whole_spec((16, features)), whole_spec(out_blocks)]
+        + [whole_spec(p) for p in sent],
+        [
+            pltpu.VMEM((quarters, features, width), bf16),
+            pltpu.VMEM((quarters, width, features), bf16),
+            pltpu.VMEM((quarters, rows, width), bf16),
+            pltpu.VMEM((quarters, rows, width), bf16),
+            pltpu.VMEM(turned, bf16),
+            pltpu.VMEM(square, f32),
+            pltpu.VMEM(square, f32),
+            pltpu.VMEM(square, f32),
+            pltpu.VMEM(square, bf16),
+            pltpu.VMEM(turned, bf16),
+            pltpu.VMEM(square, bf16),
+            pltpu.VMEM(turned, bf16),
+            pltpu.VMEM(square, bf16),
+            pltpu.VMEM(square, bf16),
+            pltpu.VMEM((2, *down), bf16),
+            pltpu.VMEM((2, *up), bf16),
+            pltpu.SemaphoreType.DMA((4 * quarters + 2,)),
+        ],
+        2 * rows * features * (6 * hidden + 3 * features),
+    )
+
+
+def place_rows(by_rows, places, *refs):
     pieces, out = refs[:2], refs[-1]
     step = pl.program_id(0)
     tile = pieces[0].shape[1]
@@ -643,35 +609,30 @@
                 ].astype(jnp.float32)
 
 
-def gather_hidden(places, early, late, shape, by_rows):
-    _, rows, cols = early[0].shape
-    block = (4 * rows, cols)
-    total = []
-    for bit, pieces in enumerate((early, late)):
-
-        def number(p):
-            return (p >> 1) * 4 + bit * 2 + (p & 1) if by_rows else p * 2 + bit
-
-        if by_rows:
-            index = lambda p, places, number=number: (places[number(p)], 0)
-        else:
-            index = lambda p, places, number=number: (0, places[number(p)])
-        total = [
-            step_call(
-                functools.partial(place_rows, by_rows, bit),
-                places,
-                4,
-                pieces + total,
-                [whole_spec(p.shape) for p in pieces]
-                + [pl.BlockSpec(memory_space=pl.ANY)] * len(total),
-                jax.ShapeDtypeStruct(shape, jnp.float32),
-                pl.BlockSpec(block, index),
-                [],
-                8 * rows * cols,
-                {3: 0} if total else {},
-            )
-        ]
-    return total[0]
+def gather_hidden(places, pieces, begun, shape, by_rows):
+    _, rows, cols = pieces[0].shape
+    bit = 0 if begun is None else 1
+
+    def number(p):
+        return (p >> 1) * 4 + bit * 2 + (p & 1) if by_rows else p * 2 + bit
+
+    def index(p, places):
+        place = places[number(p)]
+        return (place, 0) if by_rows else (0, place)
+
+    begun = [] if begun is None else [begun]
+    return step_call(
+        functools.partial(place_rows, by_rows),
+        places,
+        4,
+        pieces + begun,
+        [whole_spec(p.shape) for p in pieces] + [pl.BlockSpec(memory_space=pl.ANY)] * len(begun),
+        jax.ShapeDtypeStruct(shape, jnp.float32),
+        pl.BlockSpec((4 * rows, cols), index),
+        [],
+        8 * rows * cols,
+        {3: 0} if begun else {},
+    )
 
 
 def place_heads(places, *refs):
@@ -812,15 +773,17 @@
 
     (
         out_rows,
-        context,
-        first_in,
-        first_low,
-        active,
-        slope,
-        d_second,
-        d_lowered,
-        sums_two,
-    ) = run_feed_forward(
+        send_down1,
+        send_up1,
+        send_down0,
+        send_up0,
+        keep_down,
+        keep_up,
+        d_first_in,
+        sums,
+        grad_out,
+        *d_contexts,
+    ) = run_token_layer(
         places,
         arrived,
         tokens.reshape(flat_rows, features),
@@ -833,28 +796,14 @@
         dims,
     )
     out_tokens = out_rows.reshape(seq_count, local_rows, features)
-    send_down, send_up, b_up_send, d_part = run_back_send(
-        places, active, slope, w_up, w_down, first_low, d_lowered, d_second
-    )
-    came_down = exchange_bit(send_down, "c")
-    came_up = exchange_bit(send_up, "c")
-    keep_down, keep_up, b_up_keep, d_first_in, sums_one, grad_out, *d_contexts = run_back_keep(
-        places, active, slope, w_up, w_down, first_low, d_lowered, d_part, first_in, context, w_out,
-        vectors, dims,
-    )
-
-    half_hidden = jnp.where(
-        (outer >= 4),
-        jnp.concatenate([b_up_send, b_up_keep], axis=1),
-        jnp.concatenate([b_up_keep, b_up_send], axis=1),
-    ).reshape(-1, features)
-    filler = jnp.zeros((10 - half_hidden.shape[0], features), f32)
-    sums = jnp.concatenate([sums_one[:3], sums_two[:3], half_hidden, filler])
 
     def hand_on(own, near, came):
         return [own, exchange_bit(near, "c"), came, exchange_bit(came[1], "c")]
 
     first_came = exchange_bit(d_contexts[2], "x")
+    came_down1, came_up1 = exchange_bit(send_down1, "c"), exchange_bit(send_up1, "c")
+    send_up0, first_came = lax.optimization_barrier((send_up0, first_came))
+    came_up0 = exchange_bit(send_up0, "c")
     second_pair, first_came = lax.optimization_barrier((d_contexts[5], first_came))
     second_came = exchange_bit(second_pair, "x")
     total_w = jnp.zeros((3 * wide, features), f32)
@@ -869,24 +818,30 @@
         return total_w, total_b
 
     def cross(s):
-        near.append(parts[s][0].astype(f32) + exchange_bit(parts[s][1], "c"))
-        far.append(sum_low(parts[s][2], exchange_bit(parts[s][3], "c")))
+        held, sent = parts[s]
+        came = exchange_bit(sent, "c")
+        near.append(held[0].astype(f32) + came[0])
+        far.append(sum_low(held[1], came[1]))
 
     sends = [
-        sum_low(keep_down[3], came_down[3]),
-        sum_low(keep_up[3], came_up[3]),
+        sum_low(keep_down[3], came_down1[1]),
+        sum_low(keep_up[3], came_up1[1]),
         grad_out[2:],
     ]
     sends, first_came = lax.optimization_barrier((sends, first_came))
     down_y1, up_l3, out_x = [exchange_bit(v, bit) for v, bit in zip(sends, "ylx")]
     total_w, total_b = attend(0, hand_on(d_contexts[0], d_contexts[1], first_came), total_w, total_b)
-    (down_y1, up_l3, out_x, total_w, parts[0], second_came, near_pair) = lax.optimization_barrier(
-        (down_y1, up_l3, out_x, total_w, parts[0], second_came, d_contexts[3:5])
-    )
+    (down_y1, up_l3, out_x, total_w, parts[0], second_came, near_pair, came_up0, send_down0) = (
+        lax.optimization_barrier(
+            (down_y1, up_l3, out_x, total_w, parts[0], second_came, d_contexts[3:5])
+            + (came_up0, send_down0)
+        )
+    )
+    came_down0 = exchange_bit(send_down0, "c")
 
     sends = [
-        sum_low(keep_down[2], came_down[2]),
-        sum_low(keep_up[1], came_up[1]),
+        sum_low(keep_down[2], came_down1[0]),
+        sum_low(keep_up[1], came_up0[1]),
         sum_low(grad_out[1], out_x[1]),
     ]
     (sends, total_w) = lax.optimization_barrier((sends, total_w))
@@ -901,8 +856,8 @@
     )
 
     sends = [
-        sum_low(keep_down[1], came_down[1], down_y1),
-        sum_low(keep_up[2], came_up[2], up_l3),
+        sum_low(keep_down[1], came_down0[1], down_y1),
+        sum_low(keep_up[2], came_up1[0], up_l3),
     ]
     (sends, total_w) = lax.optimization_barrier((sends, total_w))
     down_l, up_y = [exchange_bit(v, bit) for v, bit in zip(sends, "ly")]
@@ -914,9 +869,9 @@
     (down_l, up_y, far, far_came, total_w, parts[-1]) = lax.optimization_barrier(
         (down_l, up_y, far, far_came, total_w, parts[-1])
     )
-    down_own = sum_low(keep_down[0], came_down[0], down_y0, down_l)
+    down_own = sum_low(keep_down[0], came_down0[0], down_y0, down_l)
     down_own = down_own.reshape(4, hidden // 32, features)
-    up_own = sum_low(keep_up[0], came_up[0], up_l1, up_y)
+    up_own = sum_low(keep_up[0], came_up0[0], up_l1, up_y)
     up_own = up_own.reshape(2, 2, features // 4, hidden // 8)
     keeps = [down_own[:2], up_own[:, 0], total_w[:4]]
     sends = [down_own[2:], up_own[:, 1], total_w[4:]]
@@ -930,43 +885,52 @@
 
     keeps = [down_own[:1], up_own[:1], qkv_own[:1]]
     sends = [down_own[1:], up_own[1:], qkv_own[1:]]
-    (keeps, sends, far, far_came) = lax.optimization_barrier((keeps, sends, far, far_came))
+    (keeps, sends, far, far_came, near) = lax.optimization_barrier(
+        (keeps, sends, far, far_came, near)
+    )
     got = [exchange_bit(v, bit) for v, bit in zip(sends, "xhh")]
     far_came += [exchange_bit(v, "x") for v in far]
     shards = [add_extra(k + g) for k, g in zip(keeps, got)]
 
+    own_pos = mine * local_rows + jnp.arange(local_rows, dtype=jnp.int32)
+    live = (own_pos[None, :] < lengths[:, None]).astype(f32)
+    d_inputs = jnp.stack([n + f for n, f in zip(near, far_came)])
+    grad_tokens = (d_inputs + d_first_in.reshape(seq_count, local_rows, features)) * live[:, :, None]
     for bits in ("hhh", "xyl", "lxy"):
-        (shards, far_came) = lax.optimization_barrier((shards, far_came))
+        if bits == "xyl":
+            (shards, grad_tokens) = lax.optimization_barrier((shards, grad_tokens))
+        else:
+            shards = lax.optimization_barrier(shards)
         shards = [
             jnp.concatenate([shard, exchange_bit(shard, bit)]) for shard, bit in zip(shards, bits)
         ]
     shards = lax.optimization_barrier(shards)
     last = [exchange_bit(shard, bit) for shard, bit in zip(shards, "ylx")]
     near_c = [exchange_bit(shard, "c") for shard in shards]
+    early = [
+        gather_hidden(places, [shards[i], near_c[i]], None, shape, i == 0)
+        for i, shape in ((0, (hidden, features)), (1, (features, hidden)))
+    ]
+    (last, early) = lax.optimization_barrier((last, early))
     far_c = [exchange_bit(shard, "c") for shard in last]
     full_down, full_up = [
-        gather_hidden(places, [shards[i], near_c[i]], [last[i], far_c[i]], shape, i == 0)
-        for i, shape in ((0, (hidden, features)), (1, (features, hidden)))
+        gather_hidden(places, [last[i], far_c[i]], early[i], early[i].shape, i == 0) for i in (0, 1)
     ]
     full_qkv, full_out, vector_rows, head_rows = gather_heads(
         places, [shards[2], near_c[2], last[2], far_c[2]], (features, 3 * features)
     )
     (
+        full_b_down,
+        full_gain_two,
+        full_shift_two,
         full_b_out,
         full_gain_one,
         full_shift_one,
-        full_b_down,
-        full_gain_two,
-        full_shift_two,
     ) = [vector_rows[i] for i in range(6)]
     full_b_up = vector_rows[6 : 6 + hidden // features].reshape(hidden)
     full_b_query = head_rows[:seq_parts, :wide].reshape(features)
     full_b_value = head_rows[:seq_parts, 2 * wide : 3 * wide].reshape(features)
 
-    own_pos = mine * local_rows + jnp.arange(local_rows, dtype=jnp.int32)
-    live = (own_pos[None, :] < lengths[:, None]).astype(f32)
-    d_inputs = jnp.stack([n + f for n, f in zip(near, far_came)])
-    grad_tokens = (d_inputs + d_first_in.reshape(seq_count, local_rows, features)) * live[:, :, None]
     return (
         out_tokens,
         grad_tokens,

time: 391 us -> 366 us (0.936)
  Pallas kernels: 151 us -> 133 us
  local copies, waits for them, and re-layouts: 28.7 us -> 22.3 us
  waiting for transfers between devices: 124 us -> 120 us
    pallas_call x8 -> x6, Pallas kernels: 89.4 us -> 70.5 us  [step_call(): pl.pallas_call(body, out_shape=outs, grid_spec=pltpu.PrefetchScalarGridSp...]
    unnamed x128 -> x112, local copies, waits for them, and re-layouts: 16.2 us -> 6.23 us
    ppermute x68 -> x67, waiting for transfers between devices: 124 us -> 120 us  [exchange(): lax.ppermute(array_in, axis, [(i, i ^ flip) for i in range(lax.axis_size(...]
    convert_element_type x11 -> x10, other arithmetic: 20.3 us -> 19.1 us  [sum_low(): return total.astype(jnp.bfloat16)]
    ppermute x68 -> x67, starting transfers between devices: 50.3 us -> 50.5 us  [exchange(): lax.ppermute(array_in, axis, [(i, i ^ flip) for i in range(lax.axis_size(...]
  transfers between devices with their start and end apart: 68 -> 67, of which waited for: 25 -> 25; matrix products, arithmetic and copies ran while one was open for 9% -> 9% of each run, Pallas kernels for 26% -> 23%
where the time goes in v3:
time: 366 us; the launch traced here: 361 us
  Pallas kernels  133 us (36%)
  waiting for transfers between devices  120 us (33%)
  starting transfers between devices  50.5 us (14%)
  other arithmetic  32.7 us (9%)
  local copies, waits for them, and re-layouts  22.3 us (6%)
    ppermute x67, waiting for transfers between devices, exchange(): lax.ppermute(array_in, axis, [(i, i ^ flip) for i in range(lax.axis_size(...  120 us
    pallas_call x6, Pallas kernels, step_call(): pl.pallas_call(body, out_shape=outs, grid_spec=pltpu.PrefetchScalarGridSp...  70.5 us
    pallas_call x6, Pallas kernels, kernel_call(): pl.pallas_call(body, out_shape=outs, in_specs=[pl.BlockSpec(memory_space=...  62.7 us
    ppermute x67, starting transfers between devices, exchange(): lax.ppermute(array_in, axis, [(i, i ^ flip) for i in range(lax.axis_size(...  50.5 us
    convert_element_type x10, other arithmetic, sum_low(): return total.astype(jnp.bfloat16)  19.1 us
  transfers between devices with their start and end apart: 67, of which 25 were waited for; matrix products, arithmetic and copies ran while one was open for 9% of the time, Pallas kernels for 23%

profile of v3, /device:TPU:0, one launch (start us, length us, event | category | flops | bytes accessed | tf_op | source)
XLA Modules:
  0.0 360.8 jit_solution(3178950967799415236)
XLA Ops:
  5.5 8.7 %collective-permute-done.1.x2 = bf16[256,768]{1,0:T(8,128)(2,1)} collective-permute-done((bf16[256,768]{1,0:T(8,128)(2,1)S(1)}, bf16[256,768]{1,0:T(8,128)(2,1)}, u32[]{:S(2)}, u32[]{:S(2)}) %collective-permute-start.1) | collective-permute-done | bytes 393248 | tf_op jit(solution)/shard_map/ppermute | solution.py:29
  22.8 8.4 %shard_map.280 = (bf16[192,256]{1,0:T(8,128)(2,1)}, bf16[192,256]{1,0:T(8,128)(2,1)}, bf16[192,256]{1,0:T(8,128)(2,1)}, bf16[192,256]{1,0:T(8,128)(2,1)}, bf16[1...) custom-call(s32[20]{0:T(128)} %concatenate.47.places, ...), custom_call_target="tpu_custom_call" | custom-call | flops 100000000 | bytes 1048576 | tf_op jit(solution)/shard_map/pallas_call | solution.py:224
  34.1 8.2 %shard_map.281 = (bf16[192,256]{1,0:T(8,128)(2,1)}, bf16[192,256]{1,0:T(8,128)(2,1)}, bf16[192,256]{1,0:T(8,128)(2,1)}, bf16[192,256]{1,0:T(8,128)(2,1)}, bf16[1...) custom-call(s32[20]{0:T(128)} %concatenate.47.places, ...), custom_call_target="tpu_custom_call" | custom-call | flops 100000000 | bytes 1048576 | tf_op jit(solution)/shard_map/pallas_call | solution.py:224
  47.1 8.2 %shard_map.282 = (bf16[192,256]{1,0:T(8,128)(2,1)}, bf16[192,256]{1,0:T(8,128)(2,1)}, bf16[192,256]{1,0:T(8,128)(2,1)}, bf16[192,256]{1,0:T(8,128)(2,1)}, bf16[1...) custom-call(s32[20]{0:T(128)} %concatenate.47.places, ...), custom_call_target="tpu_custom_call" | custom-call | flops 100000000 | bytes 1048576 | tf_op jit(solution)/shard_map/pallas_call | solution.py:224
  62.8 40.4 %shard_map.283 = (bf16[768,768]{1,0:T(8,128)(2,1)}, bf16[2,384,768]{2,1,0:T(8,128)(2,1)}, bf16[2,768,384]{2,1,0:T(8,128)(2,1)}, bf16[2,384,768]{2,1,0:T(8,128)(2...) custom-call(s32[20]{0:T(128)} %concatenate.47.places, ...), custom_call_target="tpu_custom_call" | custom-call | flops 24461180928 | bytes 20971520 | tf_op jit(solution)/shard_map/pallas_call | solution.py:513
  106.8 4.8 %collective-permute-done.20.g2 = bf16[2,1,192,256]{3,2,1,0:T(8,128)(2,1)S(1)} collective-permute-done((bf16[2,1,192,256]{3,2,1,0:T(8,128)(2,1)}, bf16[2,1,192,256]{3,2,1,0:T(8,128)(2,1)S(1)}, u32[]{:S(2)}, u32[]{:S(2)}) %collective-permute-start.20) | collective-permute-done | bytes 196640 | tf_op jit(solution)/shard_map/ppermute | solution.py:29
  123.9 12.4 %shard_map.284 = (bf16[2,256,768]{2,1,0:T(8,128)(2,1)}, bf16[2,256,768]{2,1,0:T(8,128)(2,1)}, f32[576,768]{1,0:T(8,128)}, f32[8,576]{1,0:T(8,128)}) custom-call(s32[20]{0:T(128)} %concatenate.47.places, bf16[1,192,256]{2,1,0:T(8,128)(2,1)} %get-tuple-element.181.g0, bf16[1,192,256]{2,1,0:T(8,128)(2,1)} %copy-done.28, bf16[2,1,192,256]{3,2,1,0:T(8,128)(2,1)} %copy-done.22, ...), custom_call_target="tpu_custom_call" | custom-call | flops 100000000 | bytes 1048576 | tf_op jit(solution)/shard_map/pallas_call | solution.py:224
  136.3 7.4 %collective-permute-done.26.g2 = bf16[2,2,192,256]{3,2,1,0:T(8,128)(2,1)S(1)} collective-permute-done((bf16[2,2,192,256]{3,2,1,0:T(8,128)(2,1)}, bf16[2,2,192,256]{3,2,1,0:T(8,128)(2,1)S(1)}, u32[]{:S(2)}, u32[]{:S(2)}) %collective-permute-start.26) | collective-permute-done | bytes 393248 | tf_op jit(solution)/shard_map/ppermute | solution.py:29
  154.4 12.6 %shard_map.285 = (bf16[2,256,768]{2,1,0:T(8,128)(2,1)}, bf16[2,256,768]{2,1,0:T(8,128)(2,1)}, f32[576,768]{1,0:T(8,128)}, f32[8,576]{1,0:T(8,128)}) custom-call(s32[20]{0:T(128)} %concatenate.47.places, bf16[2,192,256]{2,1,0:T(8,128)(2,1)} %get-tuple-element.202.g0, bf16[2,192,256]{2,1,0:T(8,128)(2,1)} %copy-done.19, bf16[2,2,192,256]{3,2,1,0:T(8,128)(2,1)} %copy-done.3, ...), custom_call_target="tpu_custom_call" | custom-call | flops 100000000 | bytes 1048576 | tf_op jit(solution)/shard_map/pallas_call | solution.py:224
  177.5 13.0 %shard_map.286 = (bf16[2,256,768]{2,1,0:T(8,128)(2,1)}, bf16[2,256,768]{2,1,0:T(8,128)(2,1)}, bf16[8,112,768]{2,1,0:T(8,128)(2,1)}, f32[8,576]{1,0:T(8,128)}) custom-call(s32[20]{0:T(128)} %concatenate.47.places, bf16[2,192,256]{2,1,0:T(8,128)(2,1)} %get-tuple-element.202.g0, bf16[2,192,256]{2,1,0:T(8,128)(2,1)} %copy-done.19, ...), custom_call_target="tpu_custom_call" | custom-call | flops 100000000 | bytes 1048576 | tf_op jit(solution)/shard_map/pallas_call | solution.py:224
  205.1 5.5 %collective-permute-done.40 = bf16[2,192,384]{2,1,0:T(8,128)(2,1)} collective-permute-done((bf16[2,192,384]{2,1,0:T(8,128)(2,1)}, bf16[2,192,384]{2,1,0:T(8,128)(2,1)}, u32[]{:S(2)}, u32[]{:S(2)}) %collective-permute-start.40) | collective-permute-done | bytes 294944 | tf_op jit(solution)/shard_map/ppermute | solution.py:29
  211.6 6.4 %collective-permute-done.39 = bf16[2,96,768]{2,1,0:T(8,128)(2,1)} collective-permute-done((bf16[2,96,768]{2,1,0:T(8,128)(2,1)}, bf16[2,96,768]{2,1,0:T(8,128)(2,1)}, u32[]{:S(2)}, u32[]{:S(2)}) %collective-permute-start.39) | collective-permute-done | bytes 294944 | tf_op jit(solution)/shard_map/ppermute | solution.py:29
  222.4 7.5 %collective-permute-done.42 = bf16[2,112,768]{2,1,0:T(8,128)(2,1)S(1)} collective-permute-done((bf16[2,112,768]{2,1,0:T(8,128)(2,1)S(1)}, bf16[2,112,768]{2,1,0:T(8,128)(2,1)S(1)}, u32[]{:S(2)}, u32[]{:S(2)}) %collective-permute-start.42) | collective-permute-done | bytes 344096 | tf_op jit(solution)/shard_map/ppermute | solution.py:29
  235.1 11.4 %collective-permute-done.46 = bf16[1,192,384]{2,1,0:T(8,128)(2,1)S(1)} collective-permute-done((bf16[1,192,384]{2,1,0:T(8,128)(2,1)S(1)}, bf16[1,192,384]{2,1,0:T(8,128)(2,1)S(1)}, u32[]{:S(2)}, u32[]{:S(2)}) %collective-permute-start.46) | collective-permute-done | bytes 147488 | tf_op jit(solution)/shard_map/ppermute | solution.py:29
  251.0 13.4 %collective-permute-done.49 = bf16[1,192,384]{2,1,0:T(8,128)(2,1)S(1)} collective-permute-done((bf16[1,192,384]{2,1,0:T(8,128)(2,1)S(1)}, bf16[1,192,384]{2,1,0:T(8,128)(2,1)S(1)}, u32[]{:S(2)}, u32[]{:S(2)}) %collective-permute-start.49) | collective-permute-done | bytes 147488 | tf_op jit(solution)/shard_map/ppermute | solution.py:29
  272.7 5.6 %collective-permute-done.53 = bf16[2,192,384]{2,1,0:T(8,128)(2,1)S(1)} collective-permute-done((bf16[2,192,384]{2,1,0:T(8,128)(2,1)S(1)}, bf16[2,192,384]{2,1,0:T(8,128)(2,1)S(1)}, u32[]{:S(2)}, u32[]{:S(2)}) %collective-permute-start.53) | collective-permute-done | bytes 294944 | tf_op jit(solution)/shard_map/ppermute | solution.py:29
  283.3 9.1 %collective-permute-done.56 = bf16[4,192,384]{2,1,0:T(8,128)(2,1)S(1)} collective-permute-done((bf16[4,192,384]{2,1,0:T(8,128)(2,1)S(1)}, bf16[4,192,384]{2,1,0:T(8,128)(2,1)S(1)}, u32[]{:S(2)}, u32[]{:S(2)}) %collective-permute-start.56) | collective-permute-done | bytes 589856 | tf_op jit(solution)/shard_map/ppermute | solution.py:29
  302.6 4.9 %shard_map.288.refs_2_ = f32[768,3072]{1,0:T(8,128)} custom-call(s32[20]{0:T(128)} %concatenate.47.places, bf16[8,192,384]{2,1,0:T(8,128)(2,1)} %copy-done.1, bf16[8,192,384]{2,1,0:T(8,128)(2,1)} %copy-done.11), custom_call_target="tpu_custom_call" | custom-call | flops 589824 | bytes 20971520 | tf_op jit(solution)/shard_map/pallas_call | solution.py:513
  307.5 4.9 %shard_map.287.refs_2_ = f32[3072,768]{1,0:T(8,128)} custom-call(s32[20]{0:T(128)} %concatenate.47.places, bf16[8,96,768]{2,1,0:T(8,128)(2,1)} %copy-done.2, bf16[8,96,768]{2,1,0:T(8,128)(2,1)} %collective-permute-done.62.refs_1_), custom_call_target="tpu_custom_call" | custom-call | flops 589824 | bytes 20971520 | tf_op jit(solution)/shard_map/pallas_call | solution.py:513
  312.5 13.0 %collective-permute-done.59.refs_0_ = bf16[8,96,768]{2,1,0:T(8,128)(2,1)} collective-permute-done((bf16[8,96,768]{2,1,0:T(8,128)(2,1)S(1)}, bf16[8,96,768]{2,1,0:T(8,128)(2,1)}, u32[]{:S(2)}, u32[]{:S(2)}) %collective-permute-start.59) | collective-permute-done | bytes 1179680 | tf_op jit(solution)/shard_map/ppermute | solution.py:29
  327.1 6.0 %collective-permute-done.66.refs_1_ = bf16[8,96,768]{2,1,0:T(8,128)(2,1)} collective-permute-done((bf16[8,96,768]{2,1,0:T(8,128)(2,1)}, bf16[8,96,768]{2,1,0:T(8,128)(2,1)}, u32[]{:S(2)}, u32[]{:S(2)}) %collective-permute-start.66) | collective-permute-done | bytes 1179680 | tf_op jit(solution)/shard_map/ppermute | solution.py:29
  333.0 4.9 %shard_map.291 = f32[3072,768]{1,0:T(8,128)} custom-call(s32[20]{0:T(128)} %concatenate.47.places, bf16[8,96,768]{2,1,0:T(8,128)(2,1)} %collective-permute-done.59.refs_0_, bf16[8,96,768]{2,1,0:T(8,128)(2,1)} %collective-permute-done.66.refs_1_, f32[3072,768]{1,0:T(8,128)} %shard_map.287.refs_2_), custom_call_target="tpu_custom_call", output_to_operand_aliasing={{}: (3, {})} | custom-call | flops 589824 | bytes 20971520 | tf_op jit(solution)/shard_map/pallas_call | solution.py:513
  339.0 4.9 %shard_map.290 = f32[768,3072]{1,0:T(8,128)} custom-call(s32[20]{0:T(128)} %concatenate.47.places, bf16[8,192,384]{2,1,0:T(8,128)(2,1)} %collective-permute-done.60.refs_0_, bf16[8,192,384]{2,1,0:T(8,128)(2,1)} %copy-done.12, f32[768,3072]{1,0:T(8,128)} %shard_map.288.refs_2_), custom_call_target="tpu_custom_call", output_to_operand_aliasing={{}: (3, {})} | custom-call | flops 589824 | bytes 20971520 | tf_op jit(solution)/shard_map/pallas_call | solution.py:513
  345.0 10.3 %shard_map.289 = (f32[768,2304]{1,0:T(8,128)}, f32[768,768]{1,0:T(8,128)}, f32[16,768]{1,0:T(8,128)}, f32[8,768]{1,0:T(8,128)}) custom-call(s32[20]{0:T(128)} %concatenate.47.places, bf16[8,112,768]{2,1,0:T(8,128)(2,1)} %copy-done, bf16[8,112,768]{2,1,0:T(8,128)(2,1)} %collective-permute-done.58.refs_1_, ...), custom_call_target="tpu_custom_call" | custom-call | flops 1000 | bytes 20971520 | tf_op jit(solution)/shard_map/pallas_call | solution.py:513
  (309 shorter events, 127.0 us)
Async XLA Ops:
  5.0 17.8 %collective-permute-start = (bf16[256,768]{1,0:T(8,128)(2,1)S(1)}, bf16[256,768]{1,0:T(8,128)(2,1)}, u32[]{:S(2)}, u32[]{:S(2)}) collective-permute-start(bf16[256,768]{1,0:T(8,128)(2,1)S(1)} %get-tuple-element.308.x0), channel_id=1, source_target_pairs={{0,1},{1,0},{2,3},{3,2},{4,5},{5,4},{6,7},{7,6},{8,9},{9,8},{10,11... | collective-permute-start | bytes 1179656 | tf_op jit(solution)/shard_map/ppermute | solution.py:29
  5.0 27.0 %collective-permute-start.6 = (bf16[256,768]{1,0:T(8,128)(2,1)S(1)}, bf16[256,768]{1,0:T(8,128)(2,1)S(1)}, u32[]{:S(2)}, u32[]{:S(2)}) collective-permute-start(bf16[256,768]{1,0:T(8,128)(2,1)S(1)} %get-tuple-element.155.x0), channel_id=1, source_target_pairs={{0,1},{1,0},{2,3},{3,2},{4,5},{5,4},{6,7},{7,6},{8,9},{9,8},{10,11... | collective-permute-start | bytes 1179656 | tf_op jit(solution)/shard_map/ppermute | solution.py:29
  111.5 32.2 %collective-permute-start.27 = (bf16[2,768,384]{2,1,0:T(8,128)(2,1)}, bf16[2,768,384]{2,1,0:T(8,128)(2,1)}, u32[]{:S(2)}, u32[]{:S(2)}) collective-permute-start(bf16[2,768,384]{2,1,0:T(8,128)(2,1)} %get-tuple-element.194), channel_id=1, source_target_pairs={{0,1},{1,0},{2,3},{3,2},{4,5},{5,4},{6,7},{7,6},{8,9},{9,8},{10,11... | collective-permute-start | bytes 3538952 | tf_op jit(solution)/shard_map/ppermute | solution.py:29
  115.4 28.3 %collective-permute-start.23 = (bf16[2,8,96,192]{3,2,1,0:T(8,128)(2,1)S(1)}, bf16[2,8,96,192]{3,2,1,0:T(8,128)(2,1)}, u32[]{:S(2)}, u32[]{:S(2)}) collective-permute-start(bf16[2,8,96,192]{3,2,1,0:T(8,128)(2,1)S(1)} %slice.197), channel_id=1, source_target_pairs={{0,2},{1,3},{2,0},{3,1},{4,6},{5,7},{6,4},{7,5},{8,10},{9,11},{10,... | collective-permute-start | bytes 1769480 | tf_op jit(solution)/shard_map/ppermute | solution.py:29
  116.5 27.2 %collective-permute-start.21 = (bf16[384,768]{1,0:T(8,128)(2,1)}, bf16[384,768]{1,0:T(8,128)(2,1)}, u32[]{:S(2)}, u32[]{:S(2)}) collective-permute-start(bf16[384,768]{1,0:T(8,128)(2,1)} %get-tuple-element.178), channel_id=1, source_target_pairs={{0,4},{4,0},{8,12},{12,8},{16,20},{20,16},{24,28},{28,24},{1,5},{5... | collective-permute-start | bytes 1769480 | tf_op jit(solution)/shard_map/ppermute | solution.py:29
  118.1 25.7 %collective-permute-start.22 = (bf16[768,384]{1,0:T(8,128)(2,1)}, bf16[768,384]{1,0:T(8,128)(2,1)}, u32[]{:S(2)}, u32[]{:S(2)}) collective-permute-start(bf16[768,384]{1,0:T(8,128)(2,1)} %fusion.9), channel_id=1, source_target_pairs={{0,8},{4,12},{8,0},{12,4},{16,24},{20,28},{24,16},{28,20},{1,9},{5... | collective-permute-start | bytes 1769480 | tf_op jit(solution)/shard_map/ppermute | solution.py:29
  121.0 22.7 %collective-permute-start.26 = (bf16[2,2,192,256]{3,2,1,0:T(8,128)(2,1)}, bf16[2,2,192,256]{3,2,1,0:T(8,128)(2,1)S(1)}, u32[]{:S(2)}, u32[]{:S(2)}) collective-permute-start(bf16[2,2,192,256]{3,2,1,0:T(8,128)(2,1)} %get-tuple-element.191), channel_id=1, source_target_pairs={{0,2},{1,3},{2,0},{3,1},{4,6},{5,7},{6,4},{7,5},{8,10},{9,11},{10,... | collective-permute-start | bytes 1179656 | tf_op jit(solution)/shard_map/ppermute | solution.py:29
  146.1 22.9 %collective-permute-start.33 = (bf16[2,256,768]{2,1,0:T(8,128)(2,1)}, bf16[2,256,768]{2,1,0:T(8,128)(2,1)}, u32[]{:S(2)}, u32[]{:S(2)}) collective-permute-start(bf16[2,256,768]{2,1,0:T(8,128)(2,1)} %get-tuple-element.215), channel_id=1, source_target_pairs={{0,1},{1,0},{2,3},{3,2},{4,5},{5,4},{6,7},{7,6},{8,9},{9,8},{10,11... | collective-permute-start | bytes 2359304 | tf_op jit(solution)/shard_map/ppermute | solution.py:29
  147.4 19.6 %collective-permute-start.34 = (bf16[8,96,192]{2,1,0:T(8,128)(2,1)S(1)}, bf16[8,96,192]{2,1,0:T(8,128)(2,1)S(1)}, u32[]{:S(2)}, u32[]{:S(2)}) collective-permute-start(bf16[8,96,192]{2,1,0:T(8,128)(2,1)S(1)} %fusion.12), channel_id=1, source_target_pairs={{0,1},{1,0},{2,3},{3,2},{4,5},{5,4},{6,7},{7,6},{8,9},{9,8},{10,11... | collective-permute-start | bytes 884744 | tf_op jit(solution)/shard_map/ppermute | solution.py:29
  147.9 24.9 %collective-permute-start.28 = (bf16[2,384,768]{2,1,0:T(8,128)(2,1)}, bf16[2,384,768]{2,1,0:T(8,128)(2,1)}, u32[]{:S(2)}, u32[]{:S(2)}) collective-permute-start(bf16[2,384,768]{2,1,0:T(8,128)(2,1)} %get-tuple-element.196), channel_id=1, source_target_pairs={{0,1},{1,0},{2,3},{3,2},{4,5},{5,4},{6,7},{7,6},{8,9},{9,8},{10,11... | collective-permute-start | bytes 3538952 | tf_op jit(solution)/shard_map/ppermute | solution.py:29
  151.2 19.2 %collective-permute-start.29 = (bf16[384,768]{1,0:T(8,128)(2,1)}, bf16[384,768]{1,0:T(8,128)(2,1)}, u32[]{:S(2)}, u32[]{:S(2)}) collective-permute-start(bf16[384,768]{1,0:T(8,128)(2,1)} %get-tuple-element.200), channel_id=1, source_target_pairs={{0,4},{4,0},{8,12},{12,8},{16,20},{20,16},{24,28},{28,24},{1,5},{5... | collective-permute-start | bytes 1769480 | tf_op jit(solution)/shard_map/ppermute | solution.py:29
  152.8 17.7 %collective-permute-start.30 = (bf16[768,384]{1,0:T(8,128)(2,1)}, bf16[768,384]{1,0:T(8,128)(2,1)}, u32[]{:S(2)}, u32[]{:S(2)}) collective-permute-start(bf16[768,384]{1,0:T(8,128)(2,1)} %fusion.11), channel_id=1, source_target_pairs={{0,8},{4,12},{8,0},{12,4},{16,24},{20,28},{24,16},{28,20},{1,9},{5... | collective-permute-start | bytes 1769480 | tf_op jit(solution)/shard_map/ppermute | solution.py:29
  170.5 20.0 %collective-permute-start.37 = (bf16[2,256,768]{2,1,0:T(8,128)(2,1)}, bf16[2,256,768]{2,1,0:T(8,128)(2,1)}, u32[]{:S(2)}, u32[]{:S(2)}) collective-permute-start(bf16[2,256,768]{2,1,0:T(8,128)(2,1)} %get-tuple-element.225), channel_id=1, source_target_pairs={{0,1},{1,0},{2,3},{3,2},{4,5},{5,4},{6,7},{7,6},{8,9},{9,8},{10,11... | collective-permute-start | bytes 2359304 | tf_op jit(solution)/shard_map/ppermute | solution.py:29
  198.9 20.2 %collective-permute-start.41 = (bf16[4,112,768]{2,1,0:T(8,128)(2,1)S(1)}, bf16[4,112,768]{2,1,0:T(8,128)(2,1)}, u32[]{:S(2)}, u32[]{:S(2)}) collective-permute-start(bf16[4,112,768]{2,1,0:T(8,128)(2,1)S(1)} %get-tuple-element.246), channel_id=1, source_target_pairs={{0,4},{4,0},{8,12},{12,8},{16,20},{20,16},{24,28},{28,24},{1,5},{5... | collective-permute-start | bytes 2064392 | tf_op jit(solution)/shard_map/ppermute | solution.py:29
  200.4 20.6 %collective-permute-start.43 = (bf16[2,256,768]{2,1,0:T(8,128)(2,1)}, bf16[2,256,768]{2,1,0:T(8,128)(2,1)}, u32[]{:S(2)}, u32[]{:S(2)}) collective-permute-start(bf16[2,256,768]{2,1,0:T(8,128)(2,1)} %get-tuple-element.248), channel_id=1, source_target_pairs={{0,1},{1,0},{2,3},{3,2},{4,5},{5,4},{6,7},{7,6},{8,9},{9,8},{10,11... | collective-permute-start | bytes 2359304 | tf_op jit(solution)/shard_map/ppermute | solution.py:29
  203.9 26.1 %collective-permute-start.44 = (bf16[256,768]{1,0:T(8,128)(2,1)}, bf16[256,768]{1,0:T(8,128)(2,1)S(1)}, u32[]{:S(2)}, u32[]{:S(2)}) collective-permute-start(bf16[256,768]{1,0:T(8,128)(2,1)} %get-tuple-element.250), channel_id=1, source_target_pairs={{0,2},{1,3},{2,0},{3,1},{4,6},{5,7},{6,4},{7,5},{8,10},{9,11},{10,... | collective-permute-start | bytes 1179656 | tf_op jit(solution)/shard_map/ppermute | solution.py:29
  234.2 35.2 %collective-permute-start.51 = (bf16[256,768]{1,0:T(8,128)(2,1)S(1)}, bf16[256,768]{1,0:T(8,128)(2,1)S(1)}, u32[]{:S(2)}, u32[]{:S(2)}) collective-permute-start(bf16[256,768]{1,0:T(8,128)(2,1)S(1)} %get-tuple-element.266), channel_id=1, source_target_pairs={{0,2},{1,3},{2,0},{3,1},{4,6},{5,7},{6,4},{7,5},{8,10},{9,11},{10,... | collective-permute-start | bytes 1179656 | tf_op jit(solution)/shard_map/ppermute | solution.py:29
  246.7 17.7 %collective-permute-start.49 = (bf16[1,192,384]{2,1,0:T(8,128)(2,1)S(1)}, bf16[1,192,384]{2,1,0:T(8,128)(2,1)S(1)}, u32[]{:S(2)}, u32[]{:S(2)}) collective-permute-start(bf16[1,192,384]{2,1,0:T(8,128)(2,1)S(1)} %add.222), channel_id=1, source_target_pairs={{0,16},{4,20},{8,24},{12,28},{16,0},{20,4},{24,8},{28,12},{1,17},{... | collective-permute-start | bytes 442376 | tf_op jit(solution)/shard_map/ppermute | solution.py:29
  246.7 20.7 %collective-permute-start.48 = (bf16[1,96,768]{2,1,0:T(8,128)(2,1)S(1)}, bf16[1,96,768]{2,1,0:T(8,128)(2,1)S(1)}, u32[]{:S(2)}, u32[]{:S(2)}) collective-permute-start(bf16[1,96,768]{2,1,0:T(8,128)(2,1)S(1)} %add.221), channel_id=1, source_target_pairs={{0,16},{4,20},{8,24},{12,28},{16,0},{20,4},{24,8},{28,12},{1,17},{... | collective-permute-start | bytes 442376 | tf_op jit(solution)/shard_map/ppermute | solution.py:29
  250.8 18.5 %collective-permute-start.50 = (bf16[1,112,768]{2,1,0:T(8,128)(2,1)S(1)}, bf16[1,112,768]{2,1,0:T(8,128)(2,1)S(1)}, u32[]{:S(2)}, u32[]{:S(2)}) collective-permute-start(bf16[1,112,768]{2,1,0:T(8,128)(2,1)S(1)} %add.223), channel_id=1, source_target_pairs={{0,16},{4,20},{8,24},{12,28},{16,0},{20,4},{24,8},{28,12},{1,17},{... | collective-permute-start | bytes 516104 | tf_op jit(solution)/shard_map/ppermute | solution.py:29
  296.0 30.6 %collective-permute-start.61 = (bf16[8,112,768]{2,1,0:T(8,128)(2,1)S(1)}, bf16[8,112,768]{2,1,0:T(8,128)(2,1)}, u32[]{:S(2)}, u32[]{:S(2)}) collective-permute-start(bf16[8,112,768]{2,1,0:T(8,128)(2,1)S(1)} %pad_maximum_fusion.refs_0_), channel_id=1, source_target_pairs={{0,2},{1,3},{2,0},{3,1},{4,6},{5,7},{6,4},{7,5},{8,10},{9,11},{10,... | collective-permute-start | bytes 4128776 | tf_op jit(solution)/shard_map/ppermute | solution.py:29
  297.5 28.0 %collective-permute-start.59 = (bf16[8,96,768]{2,1,0:T(8,128)(2,1)S(1)}, bf16[8,96,768]{2,1,0:T(8,128)(2,1)}, u32[]{:S(2)}, u32[]{:S(2)}) collective-permute-start(bf16[8,96,768]{2,1,0:T(8,128)(2,1)S(1)} %pad_maximum_fusion.1.refs_0_), channel_id=1, source_target_pairs={{0,4},{4,0},{8,12},{12,8},{16,20},{20,16},{24,28},{28,24},{1,5},{5... | collective-permute-start | bytes 3538952 | tf_op jit(solution)/shard_map/ppermute | solution.py:29
  298.8 27.7 %collective-permute-start.60 = (bf16[8,192,384]{2,1,0:T(8,128)(2,1)S(1)}, bf16[8,192,384]{2,1,0:T(8,128)(2,1)}, u32[]{:S(2)}, u32[]{:S(2)}) collective-permute-start(bf16[8,192,384]{2,1,0:T(8,128)(2,1)S(1)} %pad_maximum_fusion.2.refs_0_), channel_id=1, source_target_pairs={{0,8},{4,12},{8,0},{12,4},{16,24},{20,28},{24,16},{28,20},{1,9},{5... | collective-permute-start | bytes 3538952 | tf_op jit(solution)/shard_map/ppermute | solution.py:29
  302.5 41.4 %collective-permute-start.58 = (bf16[8,112,768]{2,1,0:T(8,128)(2,1)S(1)}, bf16[8,112,768]{2,1,0:T(8,128)(2,1)}, u32[]{:S(2)}, u32[]{:S(2)}) collective-permute-start(bf16[8,112,768]{2,1,0:T(8,128)(2,1)S(1)} %pad_maximum_fusion.refs_0_), channel_id=1, source_target_pairs={{0,1},{1,0},{2,3},{3,2},{4,5},{5,4},{6,7},{7,6},{8,9},{9,8},{10,11... | collective-permute-start | bytes 4128776 | tf_op jit(solution)/shard_map/ppermute | solution.py:29
  (97 other events, 763.5 us)

commit v4 on v3

--- a/solution.py
+++ b/solution.py
@@ -129,14 +129,16 @@
 
 
 def attend_backward(
-    heads, index, places, g0, g1, g2, g3, w_t, x_in, qkv, ctx_blk, lse, acc_in, acc_b, *refs
+    heads, index, places, g0, g1, g2, g3, w_t, x_in, qkv, ctx_blk, lse, *refs
 ):
-    last = len(refs) == 14
+    first, last = index == 0, len(refs) > 14
+    acc_in, acc_b = (None, None) if first else refs[:2]
     (dx_keep, dx_send, grad_w, grad_b, g_tok, g_blk, d_qkv, tok, x_seq, acc, dx_s, sems) = refs[-12:]
     bring_x = pltpu.make_async_copy(x_in, x_seq, sems.at[0])
-    bring_acc = pltpu.make_async_copy(acc_in, acc, sems.at[1])
     bring_x.start()
-    bring_acc.start()
+    if not first:
+        bring_acc = pltpu.make_async_copy(acc_in, acc, sems.at[1])
+        bring_acc.start()
     half, mine, perm = sequence_scalars(places, index)
     index = max(index - 1, 0)
     quarter = g0.shape[2]
@@ -189,13 +191,15 @@
         dx_s[r] = dot_f32(columns, w_t[...], TN).astype(jnp.bfloat16)
         sent.append(pltpu.make_async_copy(dx_s.at[r], piece, sems.at[2 + r]))
         sent[-1].start()
-    bring_acc.wait()
     bring_x.wait()
-    total = acc[...] + dot_f32(tok[...], x_seq[...], NN)
+    total = dot_f32(tok[...], x_seq[...], NN)
     ones = jnp.ones((8, whole), jnp.bfloat16)
-    sums = acc_b[...] + dot_f32(ones, tok[...], NT)
+    sums = dot_f32(ones, tok[...], NT)
+    if not first:
+        bring_acc.wait()
+        total, sums = total + acc[...], sums + acc_b[...]
     if last:
-        out_own, vectors = refs[:2]
+        out_own, vectors = refs[2:4]
         inner = places[10]
         turned = total.T
         tile = out_own.shape[1]
@@ -263,7 +267,7 @@
     return found[:4], found[4:]
 
 
-def attention_backward(places, pieces, index, w_t, kept, acc, acc_b, heads, late=()):
+def attention_backward(places, pieces, index, w_t, kept, before, heads, late=()):
     _, wide, quarter = pieces[0].shape
     features = w_t.shape[1]
     block = 2 * quarter
@@ -287,13 +291,13 @@
     found = kernel_call(
         functools.partial(attend_backward, heads, index),
         places,
-        [*pieces, w_t, *kept, acc, acc_b, *late],
+        [*pieces, w_t, *kept, *before, *late],
         outs,
         scratch,
-        left_in=(5, 9),
+        left_in=(5, 9) if before else (5,),
         left_out=(0, 1),
     )
-    return found[:2], found[2], found[3]
+    return found[:2], found[2:]
 
 def live_rows(places, rows, mine, local_rows, offset):
     row = lax.broadcasted_iota(jnp.int32, (rows, 1), 0)
@@ -328,12 +332,12 @@
     pieces, refs = refs[:count], refs[count:]
     tokens, cot_in, w_out, vectors, b_up, w_up_in, w_down_in = refs[:7]
     out, send_down1, send_up1, send_down0, send_up0, keep_down, keep_up = refs[7:14]
-    d_first_in, sums, grad_out = refs[14:17]
-    sent = refs[17:23]
+    d_first_in, sums, grad_out, send_out = refs[14:18]
+    sent = refs[18:24]
     (
         w_up, w_down, active, slope, context, first_in, first_norm, lowered,
         first_low, first_t, d_lowered, turned, out_s, cot, grad_down, grad_up, sems,
-    ) = refs[23:]
+    ) = refs[24:]
     rows, features = tokens.shape
     local_rows = rows // seq_count
     wide = features // seq_parts
@@ -494,9 +498,17 @@
         for j in range(seq_parts):
             for q in range(wide // block_rows * across):
                 row, col = j * wide + q // across * block_rows, q % across * block_cols
-                grad_out[j ^ mine, q ^ places[10]] = product[
-                    row : row + block_rows, col : col + block_cols
-                ]
+                block = product[row : row + block_rows, col : col + block_cols]
+                place, inner_place = j ^ mine, q ^ places[10]
+
+                @pl.when(place < 2)
+                def own():
+                    grad_out[place, inner_place] = block
+
+                @pl.when(place >= 2)
+                def across_x():
+                    send_out[place - 2, inner_place] = block
+
         keep_out.wait()
         for k in range(2):
             for copy in leave(k):
@@ -523,7 +535,7 @@
         input_output_aliases=aliases,
         compiler_params=pltpu.CompilerParams(vmem_limit_bytes=VMEM_LIMIT),
         cost_estimate=pl.CostEstimate(
-            flops=flops, transcendentals=0, bytes_accessed=20 * 1024 * 1024
+            flops=flops, transcendentals=0, bytes_accessed=1024 * 1024
         ),
     )(places, *ins)
 
@@ -541,7 +553,7 @@
     sent = []
     for n in (1, seq_count - 1):
         sent += [(n, *piece), (n, *piece), (2, n, *piece)]
-    out_blocks = (seq_parts, 8, features // seq_parts // 2, features // 4)
+    out_blocks = (seq_parts // 2, 8, features // seq_parts // 2, features // 4)
     away = pl.BlockSpec(memory_space=pl.ANY)
     down, up = (2, half, features), (2, features, half)
 
@@ -564,10 +576,12 @@
             out(square, f32),
             out((16, features), f32),
             out(out_blocks, bf16),
+            out(out_blocks, bf16),
         ]
         + [out(p, bf16) for p in sent],
         [away] * 7
-        + [whole_spec(square), whole_spec((16, features)), whole_spec(out_blocks)]
+        + [whole_spec(square), whole_spec((16, features))]
+        + [whole_spec(out_blocks)] * 2
         + [whole_spec(p) for p in sent],
         [
             pltpu.VMEM((quarters, features, width), bf16),
@@ -592,109 +606,113 @@
     )
 
 
-def place_rows(by_rows, places, *refs):
-    pieces, out = refs[:2], refs[-1]
-    step = pl.program_id(0)
-    tile = pieces[0].shape[1]
-    for k in range(4):
-        c, other = k >> 1, k & 1
-
-        @pl.when(step == k)
+def place_rows(count, by_rows, places, *refs):
+    pieces, out = refs[:count], refs[-1]
+    tile = pieces[0].shape[-2]
+    for k, piece in enumerate(pieces):
+
+        @pl.when(pl.program_id(0) >> 1 == k)
         def copy():
             for q in range(4):
                 h, x = q >> 1, q & 1
-                sub = other * 4 + x * 2 + h if by_rows else x * 4 + other * 2 + h
-                out[pl.ds(pl.multiple_of((q ^ places[8]) * tile, tile), tile), :] = pieces[c][
-                    sub
-                ].astype(jnp.float32)
-
-
-def gather_hidden(places, pieces, begun, shape, by_rows):
+                block = piece[x * 2 + h] if by_rows else piece[x, 0, h]
+                out[pl.ds(pl.multiple_of((q ^ places[8]) * tile, tile), tile), :] = block.astype(
+                    jnp.float32
+                )
+
+
+def gather_hidden(places, pieces, core, bit, begun, shape, by_rows):
     _, rows, cols = pieces[0].shape
-    bit = 0 if begun is None else 1
-
-    def number(p):
-        return (p >> 1) * 4 + bit * 2 + (p & 1) if by_rows else p * 2 + bit
+    if by_rows:
+        size = (4, rows, cols)
+    else:
+        pieces = [piece.reshape(2, 2, 2, rows, cols) for piece in pieces]
+        size = (2, 1, 2, rows, cols)
+
+    def source(k):
+        def index(p, places):
+            turn = jnp.clip(p - 2 * k, 0, 1)
+            return (turn, 0, 0) if by_rows else (0, turn, 0, 0, 0)
+
+        return pl.BlockSpec(size, index)
 
     def index(p, places):
-        place = places[number(p)]
+        turn = p & 1
+        place = places[(core + (p >> 1)) * 4 + (bit * 2 + turn if by_rows else turn * 2 + bit)]
         return (place, 0) if by_rows else (0, place)
 
     begun = [] if begun is None else [begun]
+    count = len(pieces)
     return step_call(
-        functools.partial(place_rows, by_rows),
+        functools.partial(place_rows, count, by_rows),
         places,
-        4,
+        2 * count,
         pieces + begun,
-        [whole_spec(p.shape) for p in pieces] + [pl.BlockSpec(memory_space=pl.ANY)] * len(begun),
+        [source(k) for k in range(count)] + [pl.BlockSpec(memory_space=pl.ANY)] * len(begun),
         jax.ShapeDtypeStruct(shape, jnp.float32),
         pl.BlockSpec((4 * rows, cols), index),
         [],
-        8 * rows * cols,
-        {3: 0} if begun else {},
-    )
-
-
-def place_heads(places, *refs):
-    pieces = refs[:-5]
-    out, out_w, vector_rows, head_rows, held = refs[-5:]
+        1000,
+        {count + 1: 0} if begun else {},
+    )
+
+
+def place_heads(late, places, *refs):
+    pieces, (out, out_w, vectors) = refs[:2], refs[-3:]
     mine, inner = places[9], places[10]
-    seq_parts = len(pieces)
     step = pl.program_id(0)
-    wide = out_w.shape[0] // seq_parts
-    rows = out.shape[0]
+    wide = out_w.shape[0]
+    rows, features = out.shape[0], out_w.shape[1]
+    seq_parts = features // wide
     f32 = jnp.float32
-    for r, piece in enumerate(pieces):
+    if late:
+        out[...] = refs[2][...]
+    for k, piece in enumerate(pieces):
+        r = k + 2 * late
+        block = piece[step ^ inner, :rows, : 3 * wide].astype(f32)
         for j in range(seq_parts):
 
             @pl.when((r ^ mine) == j)
             def copy():
-                block = piece[step ^ inner, :rows, : 3 * wide].astype(f32)
-                for k in range(3):
-                    start = (k * seq_parts + j) * wide
-                    out[:, start : start + wide] = block[:, k * wide : (k + 1) * wide]
-
-        @pl.when(step == r)
+                for section in range(3):
+                    start = section * features + j * wide
+                    out[:, start : start + wide] = block[:, section * wide : (section + 1) * wide]
+
+        @pl.when(step == k)
         def copy_out():
-            tile, width = wide // 2, out_w.shape[1] // 4
+            tile, width = wide // 2, features // 4
             for q in range(8):
-                row = pl.multiple_of((r ^ mine) * wide + q // 4 * tile, tile)
-                col = q % 4 * width
-                out_w[pl.ds(row, tile), col : col + width] = piece[
-                    q ^ inner, :rows, 3 * wide :
-                ].astype(f32)
-
-        @pl.when(step == seq_parts)
-        def copy_vectors():
-            held[r ^ mine] = piece[inner, rows:, :].astype(f32)
-
-    @pl.when(step == seq_parts)
-    def sum_vectors():
-        total = held[0]
-        for j in range(1, seq_parts):
-            total = total + held[j]
-        vector_rows[...] = total
-        for j in range(seq_parts):
-            head_rows[j : j + 1, :] = held[j, 10:11, :]
-
-
-def gather_heads(places, pieces, shape):
+                row, col = q // 4 * tile, q % 4 * width
+                out_w[row : row + tile, col : col + width] = piece[q ^ inner, :rows, 3 * wide :].astype(
+                    f32
+                )
+            vectors[k] = piece[inner, rows:, :].astype(f32)
+
+
+def gather_heads(places, pieces, begun, shape):
     out, f32 = jax.ShapeDtypeStruct, jnp.float32
     features = shape[0]
     rows = features // 8
-    square = (features, features)
-    extra = (pieces[0].shape[1] - rows, features)
+    wide = pieces[0].shape[2] // 4
+    late = begun is not None
+    extra = (2, pieces[0].shape[1] - rows, features)
+    main = pl.BlockSpec((rows, shape[1]), lambda p, places: (p, 0))
+
+    def own_rows(p, places):
+        return ((jnp.minimum(p, 1) + 2 * late) ^ places[9], 0)
+
     return step_call(
-        place_heads,
+        functools.partial(place_heads, int(late)),
         places,
         8,
-        pieces,
-        [whole_spec(p.shape) for p in pieces],
-        [out(shape, f32), out(square, f32), out(extra, f32), out((8, features), f32)],
-        [pl.BlockSpec((rows, shape[1]), lambda p, places: (p, 0))]
-        + [whole_spec(square), whole_spec(extra), whole_spec((8, features))],
-        [pltpu.VMEM((len(pieces), *extra), f32)],
+        pieces + (begun[:2] if late else []),
+        [whole_spec(p.shape) for p in pieces]
+        + ([main, pl.BlockSpec(memory_space=pl.ANY)] if late else []),
+        [out(shape, f32), out((features, features), f32), out(extra, f32)],
+        [main, pl.BlockSpec((wide, features), own_rows), whole_spec(extra)],
+        [],
         1000,
+        {3: 0, 4: 1} if late else {},
     )
 
 
@@ -764,6 +782,8 @@
             start, _ = lax.optimization_barrier((near, after))
         across = exchange_bit(start, "x")
         crossed.append(across)
+        if s == 0:
+            across, w_t, bias, places = lax.optimization_barrier((across, w_t, bias, places))
         if s > 0:
             across, _ = lax.optimization_barrier((across, arrived[-seq_parts]))
         pieces = [near, exchange_bit(near, "c"), across, exchange_bit(across, "c")]
@@ -782,6 +802,7 @@
         d_first_in,
         sums,
         grad_out,
+        send_out,
         *d_contexts,
     ) = run_token_layer(
         places,
@@ -806,16 +827,12 @@
     came_up0 = exchange_bit(send_up0, "c")
     second_pair, first_came = lax.optimization_barrier((d_contexts[5], first_came))
     second_came = exchange_bit(second_pair, "x")
-    total_w = jnp.zeros((3 * wide, features), f32)
-    total_b = jnp.zeros((8, 3 * wide), f32)
     parts, near, far = [], [], []
 
-    def attend(s, group, total_w, total_b, late=()):
-        found, total_w, total_b = attention_backward(
-            places, group, s, w_t, kept[s], total_w, total_b, heads, late
-        )
+    def attend(s, group, before, late=()):
+        found, total = attention_backward(places, group, s, w_t, kept[s], before, heads, late)
         parts.append(found)
-        return total_w, total_b
+        return total
 
     def cross(s):
         held, sent = parts[s]
@@ -826,14 +843,14 @@
     sends = [
         sum_low(keep_down[3], came_down1[1]),
         sum_low(keep_up[3], came_up1[1]),
-        grad_out[2:],
+        send_out,
     ]
     sends, first_came = lax.optimization_barrier((sends, first_came))
     down_y1, up_l3, out_x = [exchange_bit(v, bit) for v, bit in zip(sends, "ylx")]
-    total_w, total_b = attend(0, hand_on(d_contexts[0], d_contexts[1], first_came), total_w, total_b)
-    (down_y1, up_l3, out_x, total_w, parts[0], second_came, near_pair, came_up0, send_down0) = (
+    total = attend(0, hand_on(d_contexts[0], d_contexts[1], first_came), ())
+    (down_y1, up_l3, out_x, total, parts[0], second_came, near_pair, came_up0, send_down0) = (
         lax.optimization_barrier(
-            (down_y1, up_l3, out_x, total_w, parts[0], second_came, d_contexts[3:5])
+            (down_y1, up_l3, out_x, total, parts[0], second_came, d_contexts[3:5])
             + (came_up0, send_down0)
         )
     )
@@ -844,27 +861,27 @@
         sum_low(keep_up[1], came_up0[1]),
         sum_low(grad_out[1], out_x[1]),
     ]
-    (sends, total_w) = lax.optimization_barrier((sends, total_w))
+    (sends, total) = lax.optimization_barrier((sends, total))
     down_y0, up_l1, out_c = [exchange_bit(v, bit) for v, bit in zip(sends, "ylc")]
     cross(0)
     second_group = hand_on(*near_pair, second_came)
     for s in range(1, seq_count - 1):
-        total_w, total_b = attend(s, second_group, total_w, total_b)
+        total = attend(s, second_group, total)
     out_own = sum_low(grad_out[0], out_x[0], out_c)
-    (down_y0, up_l1, total_w, parts[1:], near, far, out_own) = lax.optimization_barrier(
-        (down_y0, up_l1, total_w, parts[1:], near, far, out_own)
+    (down_y0, up_l1, total, parts[1:], near, far, out_own) = lax.optimization_barrier(
+        (down_y0, up_l1, total, parts[1:], near, far, out_own)
     )
 
     sends = [
         sum_low(keep_down[1], came_down0[1], down_y1),
         sum_low(keep_up[2], came_up1[0], up_l3),
     ]
-    (sends, total_w) = lax.optimization_barrier((sends, total_w))
+    (sends, total) = lax.optimization_barrier((sends, total))
     down_l, up_y = [exchange_bit(v, bit) for v, bit in zip(sends, "ly")]
     far_came = [exchange_bit(far[0], "x")]
     for s in range(1, seq_count - 1):
         cross(s)
-    total_w, total_b = attend(seq_count - 1, second_group, total_w, total_b, (out_own, sums))
+    total_w, _ = attend(seq_count - 1, second_group, total, (out_own, sums))
 
     (down_l, up_y, far, far_came, total_w, parts[-1]) = lax.optimization_barrier(
         (down_l, up_y, far, far_came, total_w, parts[-1])
@@ -907,18 +924,29 @@
     shards = lax.optimization_barrier(shards)
     last = [exchange_bit(shard, bit) for shard, bit in zip(shards, "ylx")]
     near_c = [exchange_bit(shard, "c") for shard in shards]
+    shapes = ((hidden, features), (features, hidden))
     early = [
-        gather_hidden(places, [shards[i], near_c[i]], None, shape, i == 0)
-        for i, shape in ((0, (hidden, features)), (1, (features, hidden)))
+        gather_hidden(places, [shards[i], near_c[i]], 0, 0, None, shapes[i], i == 0) for i in (0, 1)
     ]
+    qkv_part, out_part, first_vectors = gather_heads(
+        places, [shards[2], near_c[2]], None, (features, 3 * features)
+    )
     (last, early) = lax.optimization_barrier((last, early))
     far_c = [exchange_bit(shard, "c") for shard in last]
+    early = [gather_hidden(places, [last[i]], 0, 1, early[i], shapes[i], i == 0) for i in (0, 1)]
+    (far_c, early, qkv_part) = lax.optimization_barrier((far_c, early, qkv_part))
     full_down, full_up = [
-        gather_hidden(places, [last[i], far_c[i]], early[i], early[i].shape, i == 0) for i in (0, 1)
+        gather_hidden(places, [far_c[i]], 1, 1, early[i], shapes[i], i == 0) for i in (0, 1)
     ]
-    full_qkv, full_out, vector_rows, head_rows = gather_heads(
-        places, [shards[2], near_c[2], last[2], far_c[2]], (features, 3 * features)
-    )
+    full_qkv, full_out, last_vectors = gather_heads(
+        places, [last[2], far_c[2]], [qkv_part, out_part], (features, 3 * features)
+    )
+    held = jnp.concatenate([first_vectors, last_vectors])
+    rows = [lax.dynamic_index_in_dim(held, j ^ mine, keepdims=False) for j in range(seq_parts)]
+    vector_rows = rows[0]
+    for row in rows[1:]:
+        vector_rows = vector_rows + row
+    head_rows = jnp.stack([row[10] for row in rows])
     (
         full_b_down,
         full_gain_two,

time: 366 us -> 369 us (level)
  Pallas kernels: 133 us -> 147 us
  waiting for transfers between devices: 120 us -> 108 us
    pallas_call x6 -> x9, Pallas kernels: 70.5 us -> 84.2 us  [step_call(): pl.pallas_call(body, out_shape=outs, grid_spec=pltpu.PrefetchScalarGridSp...]
    ppermute x67, waiting for transfers between devices: 120 us -> 108 us  [exchange(): lax.ppermute(array_in, axis, [(i, i ^ flip) for i in range(lax.axis_size(...]
    unnamed x112 -> x117, local copies, waits for them, and re-layouts: 6.23 us -> 7.57 us
  transfers between devices with their start and end apart: 67 -> 67, of which waited for: 25 -> 23; matrix products, arithmetic and copies ran while one was open for 9% -> 9% of each run, Pallas kernels for 23% -> 24%
where the time goes in v4:
time: 369 us; the launch traced here: 363 us
  Pallas kernels  147 us (40%)
  waiting for transfers between devices  108 us (29%)
  starting transfers between devices  51.3 us (14%)
  other arithmetic  35.4 us (10%)
  local copies, waits for them, and re-layouts  18.7 us (5%)
    ppermute x67, waiting for transfers between devices, exchange(): lax.ppermute(array_in, axis, [(i, i ^ flip) for i in range(lax.axis_size(...  108 us
    pallas_call x9, Pallas kernels, step_call(): pl.pallas_call(body, out_shape=outs, grid_spec=pltpu.PrefetchScalarGridSp...  84.2 us
    pallas_call x6, Pallas kernels, kernel_call(): pl.pallas_call(body, out_shape=outs, in_specs=[pl.BlockSpec(memory_space=...  63.2 us
    ppermute x67, starting transfers between devices, exchange(): lax.ppermute(array_in, axis, [(i, i ^ flip) for i in range(lax.axis_size(...  51.3 us
    convert_element_type x10, other arithmetic, sum_low(): return total.astype(jnp.bfloat16)  20.8 us
    unnamed x117, local copies, waits for them, and re-layouts  7.57 us
  transfers between devices with their start and end apart: 67, of which 23 were waited for; matrix products, arithmetic and copies ran while one was open for 9% of the time, Pallas kernels for 24%

profile of v4, /device:TPU:0, one launch (start us, length us, event | category | flops | bytes accessed | tf_op | source)
XLA Modules:
  0.0 362.8 jit_solution(17204878608076826427)
XLA Ops:
  16.9 8.4 %shard_map.280 = (bf16[192,256]{1,0:T(8,128)(2,1)}, bf16[192,256]{1,0:T(8,128)(2,1)}, bf16[192,256]{1,0:T(8,128)(2,1)}, bf16[192,256]{1,0:T(8,128)(2,1)}, bf16[1...) custom-call(s32[20]{0:T(128)} %concatenate.54.places, ...), custom_call_target="tpu_custom_call" | custom-call | flops 100000000 | bytes 1048576 | tf_op jit(solution)/shard_map/pallas_call | solution.py:228
  29.1 8.2 %shard_map.281 = (bf16[192,256]{1,0:T(8,128)(2,1)}, bf16[192,256]{1,0:T(8,128)(2,1)}, bf16[192,256]{1,0:T(8,128)(2,1)}, bf16[192,256]{1,0:T(8,128)(2,1)}, bf16[1...) custom-call(s32[20]{0:T(128)} %concatenate.54.places, ...), custom_call_target="tpu_custom_call" | custom-call | flops 100000000 | bytes 1048576 | tf_op jit(solution)/shard_map/pallas_call | solution.py:228
  41.6 8.2 %shard_map.282 = (bf16[192,256]{1,0:T(8,128)(2,1)}, bf16[192,256]{1,0:T(8,128)(2,1)}, bf16[192,256]{1,0:T(8,128)(2,1)}, bf16[192,256]{1,0:T(8,128)(2,1)}, bf16[1...) custom-call(s32[20]{0:T(128)} %concatenate.54.places, ...), custom_call_target="tpu_custom_call" | custom-call | flops 100000000 | bytes 1048576 | tf_op jit(solution)/shard_map/pallas_call | solution.py:228
  58.1 41.8 %shard_map.283 = (bf16[768,768]{1,0:T(8,128)(2,1)}, bf16[2,384,768]{2,1,0:T(8,128)(2,1)}, bf16[2,768,384]{2,1,0:T(8,128)(2,1)}, bf16[2,384,768]{2,1,0:T(8,128)(2...) custom-call(s32[20]{0:T(128)} %concatenate.54.places, ...), custom_call_target="tpu_custom_call" | custom-call | flops 24461180928 | bytes 1048576 | tf_op jit(solution)/shard_map/pallas_call | solution.py:525
  101.7 6.2 %collective-permute-done.20.g2 = bf16[2,1,192,256]{3,2,1,0:T(8,128)(2,1)S(1)} collective-permute-done((bf16[2,1,192,256]{3,2,1,0:T(8,128)(2,1)}, bf16[2,1,192,256]{3,2,1,0:T(8,128)(2,1)S(1)}, u32[]{:S(2)}, u32[]{:S(2)}) %collective-permute-start.20) | collective-permute-done | bytes 196640 | tf_op jit(solution)/shard_map/ppermute | solution.py:29
  119.5 12.5 %shard_map.284 = (bf16[2,256,768]{2,1,0:T(8,128)(2,1)}, bf16[2,256,768]{2,1,0:T(8,128)(2,1)}, f32[576,768]{1,0:T(8,128)}, f32[8,576]{1,0:T(8,128)}) custom-call(s32[20]{0:T(128)} %concatenate.54.places, bf16[1,192,256]{2,1,0:T(8,128)(2,1)} %get-tuple-element.202.g0, bf16[1,192,256]{2,1,0:T(8,128)(2,1)} %copy-done.30, bf16[2,1,192,256]{3,2,1,0:T(8,128)(2,1)} %copy-done.21, ...), custom_call_target="tpu_custom_call" | custom-call | flops 100000000 | bytes 1048576 | tf_op jit(solution)/shard_map/pallas_call | solution.py:228
  132.1 9.5 %collective-permute-done.26.g2 = bf16[2,2,192,256]{3,2,1,0:T(8,128)(2,1)S(1)} collective-permute-done((bf16[2,2,192,256]{3,2,1,0:T(8,128)(2,1)S(1)}, bf16[2,2,192,256]{3,2,1,0:T(8,128)(2,1)S(1)}, u32[]{:S(2)}, u32[]{:S(2)}) %collective-permute-start.26) | collective-permute-done | bytes 393248 | tf_op jit(solution)/shard_map/ppermute | solution.py:29
  152.3 12.7 %shard_map.285 = (bf16[2,256,768]{2,1,0:T(8,128)(2,1)}, bf16[2,256,768]{2,1,0:T(8,128)(2,1)}, f32[576,768]{1,0:T(8,128)}, f32[8,576]{1,0:T(8,128)}) custom-call(s32[20]{0:T(128)} %concatenate.54.places, bf16[2,192,256]{2,1,0:T(8,128)(2,1)} %get-tuple-element.226.g0, bf16[2,192,256]{2,1,0:T(8,128)(2,1)} %copy-done.18, bf16[2,2,192,256]{3,2,1,0:T(8,128)(2,1)} %copy-done.2, ...), custom_call_target="tpu_custom_call" | custom-call | flops 100000000 | bytes 1048576 | tf_op jit(solution)/shard_map/pallas_call | solution.py:228
  175.5 13.2 %shard_map.286 = (bf16[2,256,768]{2,1,0:T(8,128)(2,1)}, bf16[2,256,768]{2,1,0:T(8,128)(2,1)}, bf16[8,112,768]{2,1,0:T(8,128)(2,1)}, f32[8,576]{1,0:T(8,128)}) custom-call(s32[20]{0:T(128)} %concatenate.54.places, bf16[2,192,256]{2,1,0:T(8,128)(2,1)} %get-tuple-element.226.g0, bf16[2,192,256]{2,1,0:T(8,128)(2,1)} %copy-done.18, ...), custom_call_target="tpu_custom_call" | custom-call | flops 100000000 | bytes 1048576 | tf_op jit(solution)/shard_map/pallas_call | solution.py:228
  203.1 5.5 %collective-permute-done.40 = bf16[2,192,384]{2,1,0:T(8,128)(2,1)} collective-permute-done((bf16[2,192,384]{2,1,0:T(8,128)(2,1)}, bf16[2,192,384]{2,1,0:T(8,128)(2,1)}, u32[]{:S(2)}, u32[]{:S(2)}) %collective-permute-start.40) | collective-permute-done | bytes 294944 | tf_op jit(solution)/shard_map/ppermute | solution.py:29
  209.7 6.4 %collective-permute-done.39 = bf16[2,96,768]{2,1,0:T(8,128)(2,1)} collective-permute-done((bf16[2,96,768]{2,1,0:T(8,128)(2,1)}, bf16[2,96,768]{2,1,0:T(8,128)(2,1)}, u32[]{:S(2)}, u32[]{:S(2)}) %collective-permute-start.39) | collective-permute-done | bytes 294944 | tf_op jit(solution)/shard_map/ppermute | solution.py:29
  220.5 7.5 %collective-permute-done.42 = bf16[2,112,768]{2,1,0:T(8,128)(2,1)S(1)} collective-permute-done((bf16[2,112,768]{2,1,0:T(8,128)(2,1)S(1)}, bf16[2,112,768]{2,1,0:T(8,128)(2,1)S(1)}, u32[]{:S(2)}, u32[]{:S(2)}) %collective-permute-start.42) | collective-permute-done | bytes 344096 | tf_op jit(solution)/shard_map/ppermute | solution.py:29
  233.2 11.5 %collective-permute-done.46 = bf16[1,192,384]{2,1,0:T(8,128)(2,1)S(1)} collective-permute-done((bf16[1,192,384]{2,1,0:T(8,128)(2,1)S(1)}, bf16[1,192,384]{2,1,0:T(8,128)(2,1)S(1)}, u32[]{:S(2)}, u32[]{:S(2)}) %collective-permute-start.46) | collective-permute-done | bytes 147488 | tf_op jit(solution)/shard_map/ppermute | solution.py:29
  249.2 13.4 %collective-permute-done.49 = bf16[1,192,384]{2,1,0:T(8,128)(2,1)S(1)} collective-permute-done((bf16[1,192,384]{2,1,0:T(8,128)(2,1)S(1)}, bf16[1,192,384]{2,1,0:T(8,128)(2,1)S(1)}, u32[]{:S(2)}, u32[]{:S(2)}) %collective-permute-start.49) | collective-permute-done | bytes 147488 | tf_op jit(solution)/shard_map/ppermute | solution.py:29
  271.0 5.6 %collective-permute-done.53 = bf16[2,192,384]{2,1,0:T(8,128)(2,1)S(1)} collective-permute-done((bf16[2,192,384]{2,1,0:T(8,128)(2,1)S(1)}, bf16[2,192,384]{2,1,0:T(8,128)(2,1)S(1)}, u32[]{:S(2)}, u32[]{:S(2)}) %collective-permute-start.53) | collective-permute-done | bytes 294944 | tf_op jit(solution)/shard_map/ppermute | solution.py:29
  281.5 9.2 %collective-permute-done.56 = bf16[4,192,384]{2,1,0:T(8,128)(2,1)S(1)} collective-permute-done((bf16[4,192,384]{2,1,0:T(8,128)(2,1)S(1)}, bf16[4,192,384]{2,1,0:T(8,128)(2,1)S(1)}, u32[]{:S(2)}, u32[]{:S(2)}) %collective-permute-start.56) | collective-permute-done | bytes 589856 | tf_op jit(solution)/shard_map/ppermute | solution.py:29
  300.8 5.4 %shard_map.288.refs_1_ = f32[768,3072]{1,0:T(8,128)} custom-call(s32[20]{0:T(128)} %concatenate.54.places, bf16[2,2,2,192,384]{4,3,2,1,0:T(8,128)(2,1)} %bitcast.95, bf16[2,2,2,192,384]{4,3,2,1,0:T(8,128)(2,1)} %bitcast.98), custom_call_target="tpu_custom_call" | custom-call | flops 1000 | bytes 1048576 | tf_op jit(solution)/shard_map/pallas_call | solution.py:525
  306.2 5.4 %shard_map.287.refs_1_ = f32[3072,768]{1,0:T(8,128)} custom-call(s32[20]{0:T(128)} %concatenate.54.places, bf16[8,96,768]{2,1,0:T(8,128)(2,1)} %pad_maximum_fusion.1.refs_0_, bf16[8,96,768]{2,1,0:T(8,128)(2,1)} %collective-permute-done.61.refs_1_), custom_call_target="tpu_custom_call" | custom-call | flops 1000 | bytes 1048576 | tf_op jit(solution)/shard_map/pallas_call | solution.py:525
  311.6 12.3 %collective-permute-done.58.refs_0_ = bf16[8,96,768]{2,1,0:T(8,128)(2,1)} collective-permute-done((bf16[8,96,768]{2,1,0:T(8,128)(2,1)}, bf16[8,96,768]{2,1,0:T(8,128)(2,1)}, u32[]{:S(2)}, u32[]{:S(2)}) %collective-permute-start.58) | collective-permute-done | bytes 1179680 | tf_op jit(solution)/shard_map/ppermute | solution.py:29
  328.6 3.2 shard_map.290.refs_1_
  331.8 7.8 %shard_map.291 = (f32[768,2304]{1,0:T(8,128)}, f32[768,768]{1,0:T(8,128)}, f32[2,16,768]{2,1,0:T(8,128)}) custom-call(s32[20]{0:T(128)} %concatenate.54.places, bf16[8,112,768]{2,1,0:T(8,128)(2,1)} %copy-done, bf16[8,112,768]{2,1,0:T(8,128)(2,1)} %collective-permute-done.66.refs_1_), custom_call_target="tpu_custom_call" | custom-call | flops 1000 | bytes 1048576 | tf_op jit(solution)/shard_map/pallas_call | solution.py:525
  341.7 10.9 %shard_map.292 = (f32[768,2304]{1,0:T(8,128)}, f32[768,768]{1,0:T(8,128)}, f32[2,16,768]{2,1,0:T(8,128)}) custom-call(s32[20]{0:T(128)} %concatenate.54.places, bf16[8,112,768]{2,1,0:T(8,128)(2,1)} %collective-permute-done.60.refs_0_, bf16[8,112,768]{2,1,0:T(8,128)(2,1)} %copy-done.8, ...), custom_call_target="tpu_custom_call", output_to_operand_aliasing={{0}: (3, {}), {1}: (4, {})} | custom-call | flops 1000 | bytes 1048576 | tf_op jit(solution)/shard_map/pallas_call | solution.py:525
  356.1 3.2 shard_map.294
  359.3 3.2 shard_map.293
  (317 shorter events, 129.8 us)
Async XLA Ops:
  107.8 33.7 %collective-permute-start.27 = (bf16[2,768,384]{2,1,0:T(8,128)(2,1)}, bf16[2,768,384]{2,1,0:T(8,128)(2,1)}, u32[]{:S(2)}, u32[]{:S(2)}) collective-permute-start(bf16[2,768,384]{2,1,0:T(8,128)(2,1)} %get-tuple-element.216), channel_id=1, source_target_pairs={{0,1},{1,0},{2,3},{3,2},{4,5},{5,4},{6,7},{7,6},{8,9},{9,8},{10,11... | collective-permute-start | bytes 3538952 | tf_op jit(solution)/shard_map/ppermute | solution.py:29
  113.0 28.5 %collective-permute-start.23 = (bf16[2,8,96,192]{3,2,1,0:T(8,128)(2,1)}, bf16[2,8,96,192]{3,2,1,0:T(8,128)(2,1)}, u32[]{:S(2)}, u32[]{:S(2)}) collective-permute-start(bf16[2,8,96,192]{3,2,1,0:T(8,128)(2,1)} %get-tuple-element.201), channel_id=1, source_target_pairs={{0,2},{1,3},{2,0},{3,1},{4,6},{5,7},{6,4},{7,5},{8,10},{9,11},{10,... | collective-permute-start | bytes 1769480 | tf_op jit(solution)/shard_map/ppermute | solution.py:29
  114.1 27.4 %collective-permute-start.21 = (bf16[384,768]{1,0:T(8,128)(2,1)}, bf16[384,768]{1,0:T(8,128)(2,1)}, u32[]{:S(2)}, u32[]{:S(2)}) collective-permute-start(bf16[384,768]{1,0:T(8,128)(2,1)} %get-tuple-element.199), channel_id=1, source_target_pairs={{0,4},{4,0},{8,12},{12,8},{16,20},{20,16},{24,28},{28,24},{1,5},{5... | collective-permute-start | bytes 1769480 | tf_op jit(solution)/shard_map/ppermute | solution.py:29
  115.7 25.9 %collective-permute-start.22 = (bf16[768,384]{1,0:T(8,128)(2,1)}, bf16[768,384]{1,0:T(8,128)(2,1)}, u32[]{:S(2)}, u32[]{:S(2)}) collective-permute-start(bf16[768,384]{1,0:T(8,128)(2,1)} %fusion.9), channel_id=1, source_target_pairs={{0,8},{4,12},{8,0},{12,4},{16,24},{20,28},{24,16},{28,20},{1,9},{5... | collective-permute-start | bytes 1769480 | tf_op jit(solution)/shard_map/ppermute | solution.py:29
  118.6 22.9 %collective-permute-start.26 = (bf16[2,2,192,256]{3,2,1,0:T(8,128)(2,1)S(1)}, bf16[2,2,192,256]{3,2,1,0:T(8,128)(2,1)S(1)}, u32[]{:S(2)}, u32[]{:S(2)}) collective-permute-start(bf16[2,2,192,256]{3,2,1,0:T(8,128)(2,1)S(1)} %copy-done.41), channel_id=1, source_target_pairs={{0,2},{1,3},{2,0},{3,1},{4,6},{5,7},{6,4},{7,5},{8,10},{9,11},{10,... | collective-permute-start | bytes 1179656 | tf_op jit(solution)/shard_map/ppermute | solution.py:29
  143.7 23.3 %collective-permute-start.33 = (bf16[2,256,768]{2,1,0:T(8,128)(2,1)}, bf16[2,256,768]{2,1,0:T(8,128)(2,1)}, u32[]{:S(2)}, u32[]{:S(2)}) collective-permute-start(bf16[2,256,768]{2,1,0:T(8,128)(2,1)} %get-tuple-element.240), channel_id=1, source_target_pairs={{0,1},{1,0},{2,3},{3,2},{4,5},{5,4},{6,7},{7,6},{8,9},{9,8},{10,11... | collective-permute-start | bytes 2359304 | tf_op jit(solution)/shard_map/ppermute | solution.py:29
  145.7 19.4 %collective-permute-start.34 = (bf16[8,96,192]{2,1,0:T(8,128)(2,1)}, bf16[8,96,192]{2,1,0:T(8,128)(2,1)S(1)}, u32[]{:S(2)}, u32[]{:S(2)}) collective-permute-start(bf16[8,96,192]{2,1,0:T(8,128)(2,1)} %fusion.12), channel_id=1, source_target_pairs={{0,1},{1,0},{2,3},{3,2},{4,5},{5,4},{6,7},{7,6},{8,9},{9,8},{10,11... | collective-permute-start | bytes 884744 | tf_op jit(solution)/shard_map/ppermute | solution.py:29
  146.1 24.5 %collective-permute-start.28 = (bf16[2,384,768]{2,1,0:T(8,128)(2,1)}, bf16[2,384,768]{2,1,0:T(8,128)(2,1)}, u32[]{:S(2)}, u32[]{:S(2)}) collective-permute-start(bf16[2,384,768]{2,1,0:T(8,128)(2,1)} %get-tuple-element.218), channel_id=1, source_target_pairs={{0,1},{1,0},{2,3},{3,2},{4,5},{5,4},{6,7},{7,6},{8,9},{9,8},{10,11... | collective-permute-start | bytes 3538952 | tf_op jit(solution)/shard_map/ppermute | solution.py:29
  149.2 19.3 %collective-permute-start.29 = (bf16[384,768]{1,0:T(8,128)(2,1)}, bf16[384,768]{1,0:T(8,128)(2,1)}, u32[]{:S(2)}, u32[]{:S(2)}) collective-permute-start(bf16[384,768]{1,0:T(8,128)(2,1)} %get-tuple-element.224), channel_id=1, source_target_pairs={{0,4},{4,0},{8,12},{12,8},{16,20},{20,16},{24,28},{28,24},{1,5},{5... | collective-permute-start | bytes 1769480 | tf_op jit(solution)/shard_map/ppermute | solution.py:29
  150.7 17.8 %collective-permute-start.30 = (bf16[768,384]{1,0:T(8,128)(2,1)}, bf16[768,384]{1,0:T(8,128)(2,1)}, u32[]{:S(2)}, u32[]{:S(2)}) collective-permute-start(bf16[768,384]{1,0:T(8,128)(2,1)} %fusion.11), channel_id=1, source_target_pairs={{0,8},{4,12},{8,0},{12,4},{16,24},{20,28},{24,16},{28,20},{1,9},{5... | collective-permute-start | bytes 1769480 | tf_op jit(solution)/shard_map/ppermute | solution.py:29
  168.5 20.2 %collective-permute-start.37 = (bf16[2,256,768]{2,1,0:T(8,128)(2,1)}, bf16[2,256,768]{2,1,0:T(8,128)(2,1)}, u32[]{:S(2)}, u32[]{:S(2)}) collective-permute-start(bf16[2,256,768]{2,1,0:T(8,128)(2,1)} %get-tuple-element.251), channel_id=1, source_target_pairs={{0,1},{1,0},{2,3},{3,2},{4,5},{5,4},{6,7},{7,6},{8,9},{9,8},{10,11... | collective-permute-start | bytes 2359304 | tf_op jit(solution)/shard_map/ppermute | solution.py:29
  173.1 17.6 %collective-permute-start.35 = (bf16[384,768]{1,0:T(8,128)(2,1)}, bf16[384,768]{1,0:T(8,128)(2,1)S(1)}, u32[]{:S(2)}, u32[]{:S(2)}) collective-permute-start(bf16[384,768]{1,0:T(8,128)(2,1)} %fusion.4), channel_id=1, source_target_pairs={{0,8},{4,12},{8,0},{12,4},{16,24},{20,28},{24,16},{28,20},{1,9},{5... | collective-permute-start | bytes 1769480 | tf_op jit(solution)/shard_map/ppermute | solution.py:29
  173.8 16.9 %collective-permute-start.36 = (bf16[768,384]{1,0:T(8,128)(2,1)}, bf16[768,384]{1,0:T(8,128)(2,1)S(1)}, u32[]{:S(2)}, u32[]{:S(2)}) collective-permute-start(bf16[768,384]{1,0:T(8,128)(2,1)} %fusion.3), channel_id=1, source_target_pairs={{0,4},{4,0},{8,12},{12,8},{16,20},{20,16},{24,28},{28,24},{1,5},{5... | collective-permute-start | bytes 1769480 | tf_op jit(solution)/shard_map/ppermute | solution.py:29
  197.1 20.1 %collective-permute-start.41 = (bf16[4,112,768]{2,1,0:T(8,128)(2,1)S(1)}, bf16[4,112,768]{2,1,0:T(8,128)(2,1)}, u32[]{:S(2)}, u32[]{:S(2)}) collective-permute-start(bf16[4,112,768]{2,1,0:T(8,128)(2,1)S(1)} %get-tuple-element.272), channel_id=1, source_target_pairs={{0,4},{4,0},{8,12},{12,8},{16,20},{20,16},{24,28},{28,24},{1,5},{5... | collective-permute-start | bytes 2064392 | tf_op jit(solution)/shard_map/ppermute | solution.py:29
  198.5 20.7 %collective-permute-start.43 = (bf16[2,256,768]{2,1,0:T(8,128)(2,1)}, bf16[2,256,768]{2,1,0:T(8,128)(2,1)}, u32[]{:S(2)}, u32[]{:S(2)}) collective-permute-start(bf16[2,256,768]{2,1,0:T(8,128)(2,1)} %get-tuple-element.274), channel_id=1, source_target_pairs={{0,1},{1,0},{2,3},{3,2},{4,5},{5,4},{6,7},{7,6},{8,9},{9,8},{10,11... | collective-permute-start | bytes 2359304 | tf_op jit(solution)/shard_map/ppermute | solution.py:29
  202.0 26.1 %collective-permute-start.44 = (bf16[256,768]{1,0:T(8,128)(2,1)}, bf16[256,768]{1,0:T(8,128)(2,1)S(1)}, u32[]{:S(2)}, u32[]{:S(2)}) collective-permute-start(bf16[256,768]{1,0:T(8,128)(2,1)} %get-tuple-element.276), channel_id=1, source_target_pairs={{0,2},{1,3},{2,0},{3,1},{4,6},{5,7},{6,4},{7,5},{8,10},{9,11},{10,... | collective-permute-start | bytes 1179656 | tf_op jit(solution)/shard_map/ppermute | solution.py:29
  232.3 35.3 %collective-permute-start.51 = (bf16[256,768]{1,0:T(8,128)(2,1)S(1)}, bf16[256,768]{1,0:T(8,128)(2,1)S(1)}, u32[]{:S(2)}, u32[]{:S(2)}) collective-permute-start(bf16[256,768]{1,0:T(8,128)(2,1)S(1)} %get-tuple-element.292), channel_id=1, source_target_pairs={{0,2},{1,3},{2,0},{3,1},{4,6},{5,7},{6,4},{7,5},{8,10},{9,11},{10,... | collective-permute-start | bytes 1179656 | tf_op jit(solution)/shard_map/ppermute | solution.py:29
  244.9 17.7 %collective-permute-start.49 = (bf16[1,192,384]{2,1,0:T(8,128)(2,1)S(1)}, bf16[1,192,384]{2,1,0:T(8,128)(2,1)S(1)}, u32[]{:S(2)}, u32[]{:S(2)}) collective-permute-start(bf16[1,192,384]{2,1,0:T(8,128)(2,1)S(1)} %add.247), channel_id=1, source_target_pairs={{0,16},{4,20},{8,24},{12,28},{16,0},{20,4},{24,8},{28,12},{1,17},{... | collective-permute-start | bytes 442376 | tf_op jit(solution)/shard_map/ppermute | solution.py:29
  245.0 20.7 %collective-permute-start.48 = (bf16[1,96,768]{2,1,0:T(8,128)(2,1)S(1)}, bf16[1,96,768]{2,1,0:T(8,128)(2,1)S(1)}, u32[]{:S(2)}, u32[]{:S(2)}) collective-permute-start(bf16[1,96,768]{2,1,0:T(8,128)(2,1)S(1)} %add.246), channel_id=1, source_target_pairs={{0,16},{4,20},{8,24},{12,28},{16,0},{20,4},{24,8},{28,12},{1,17},{... | collective-permute-start | bytes 442376 | tf_op jit(solution)/shard_map/ppermute | solution.py:29
  249.1 18.5 %collective-permute-start.50 = (bf16[1,112,768]{2,1,0:T(8,128)(2,1)S(1)}, bf16[1,112,768]{2,1,0:T(8,128)(2,1)S(1)}, u32[]{:S(2)}, u32[]{:S(2)}) collective-permute-start(bf16[1,112,768]{2,1,0:T(8,128)(2,1)S(1)} %add.248), channel_id=1, source_target_pairs={{0,16},{4,20},{8,24},{12,28},{16,0},{20,4},{24,8},{28,12},{1,17},{... | collective-permute-start | bytes 516104 | tf_op jit(solution)/shard_map/ppermute | solution.py:29
  294.2 30.6 %collective-permute-start.60 = (bf16[8,112,768]{2,1,0:T(8,128)(2,1)S(1)}, bf16[8,112,768]{2,1,0:T(8,128)(2,1)}, u32[]{:S(2)}, u32[]{:S(2)}) collective-permute-start(bf16[8,112,768]{2,1,0:T(8,128)(2,1)S(1)} %pad_maximum_fusion.refs_0_), channel_id=1, source_target_pairs={{0,2},{1,3},{2,0},{3,1},{4,6},{5,7},{6,4},{7,5},{8,10},{9,11},{10,... | collective-permute-start | bytes 4128776 | tf_op jit(solution)/shard_map/ppermute | solution.py:29
  295.7 28.2 %collective-permute-start.58 = (bf16[8,96,768]{2,1,0:T(8,128)(2,1)}, bf16[8,96,768]{2,1,0:T(8,128)(2,1)}, u32[]{:S(2)}, u32[]{:S(2)}) collective-permute-start(bf16[8,96,768]{2,1,0:T(8,128)(2,1)} %pad_maximum_fusion.1.refs_0_), channel_id=1, source_target_pairs={{0,4},{4,0},{8,12},{12,8},{16,20},{20,16},{24,28},{28,24},{1,5},{5... | collective-permute-start | bytes 3538952 | tf_op jit(solution)/shard_map/ppermute | solution.py:29
  297.1 27.7 %collective-permute-start.59 = (bf16[8,192,384]{2,1,0:T(8,128)(2,1)S(1)}, bf16[8,192,384]{2,1,0:T(8,128)(2,1)}, u32[]{:S(2)}, u32[]{:S(2)}) collective-permute-start(bf16[8,192,384]{2,1,0:T(8,128)(2,1)S(1)} %pad_maximum_fusion.2), channel_id=1, source_target_pairs={{0,8},{4,12},{8,0},{12,4},{16,24},{20,28},{24,16},{28,20},{1,9},{5... | collective-permute-start | bytes 3538952 | tf_op jit(solution)/shard_map/ppermute | solution.py:29
  300.7 31.1 %collective-permute-start.66 = (bf16[8,112,768]{2,1,0:T(8,128)(2,1)S(1)}, bf16[8,112,768]{2,1,0:T(8,128)(2,1)}, u32[]{:S(2)}, u32[]{:S(2)}) collective-permute-start(bf16[8,112,768]{2,1,0:T(8,128)(2,1)S(1)} %pad_maximum_fusion.refs_0_), channel_id=1, source_target_pairs={{0,1},{1,0},{2,3},{3,2},{4,5},{5,4},{6,7},{7,6},{8,9},{9,8},{10,11... | collective-permute-start | bytes 4128776 | tf_op jit(solution)/shard_map/ppermute | solution.py:29
  (99 other events, 772.9 us)

commit v5 on v4

--- a/solution.py
+++ b/solution.py
@@ -133,7 +133,7 @@
 ):
     first, last = index == 0, len(refs) > 14
     acc_in, acc_b = (None, None) if first else refs[:2]
-    (dx_keep, dx_send, grad_w, grad_b, g_tok, g_blk, d_qkv, tok, x_seq, acc, dx_s, sems) = refs[-12:]
+    (dx_keep, dx_send, grad_w, grad_w2, g_tok, g_blk, d_qkv, tok, x_seq, acc, dx_s, sems) = refs[-12:]
     bring_x = pltpu.make_async_copy(x_in, x_seq, sems.at[0])
     bring_x.start()
     if not first:
@@ -201,22 +201,24 @@
     if last:
         out_own, vectors = refs[2:4]
         inner = places[10]
-        turned = total.T
+        turned = total.T.astype(jnp.bfloat16)
         tile = out_own.shape[1]
         extra = grad_w.shape[1] - tile
-        grad_w[:, tile:, :] = jnp.zeros((8, extra, 4 * wide), jnp.bfloat16)
+        for half_w in (grad_w, grad_w2):
+            half_w[:, tile:, :] = jnp.zeros((8, extra, 2 * wide), jnp.bfloat16)
         for q in range(8):
-            grad_w[q ^ inner, :tile, : 3 * wide] = turned[q * tile : (q + 1) * tile].astype(
-                jnp.bfloat16
-            )
-        grad_w[:, :tile, 3 * wide :] = out_own[...]
+            rows = slice(q * tile, (q + 1) * tile)
+            grad_w[q ^ inner, :tile, :] = turned[rows, : 2 * wide]
+            grad_w2[q ^ inner, :tile, :wide] = turned[rows, 2 * wide :]
+        grad_w2[:, :tile, wide:] = out_own[...]
         row = lax.broadcasted_iota(jnp.int32, (extra, 1), 0)
         own_row = jnp.concatenate([sums[0:1, :], jnp.zeros((1, wide), jnp.float32)], axis=1)
-        grad_w[inner, tile:, :] = jnp.where(row == 10, own_row, vectors[...]).astype(jnp.bfloat16)
-        grad_b[...] = sums
+        tile_rows = jnp.where(row == 10, own_row, vectors[...]).astype(jnp.bfloat16)
+        grad_w[inner, tile:, :] = tile_rows[:, : 2 * wide]
+        grad_w2[inner, tile:, :] = tile_rows[:, 2 * wide :]
     else:
         grad_w[...] = total
-        grad_b[...] = sums
+        grad_w2[...] = sums
     for copy in sent:
         copy.wait()
 
@@ -272,12 +274,11 @@
     features = w_t.shape[1]
     block = 2 * quarter
     out = jax.ShapeDtypeStruct
-    grad = (
-        out((8, features // 8 + 16, 4 * wide), jnp.bfloat16)
-        if late
-        else out((3 * wide, features), jnp.float32)
-    )
-    outs = [out((2, quarter, features), jnp.bfloat16)] * 2 + [grad, out((8, 3 * wide), jnp.float32)]
+    if late:
+        grads = [out((8, features // 8 + 16, 2 * wide), jnp.bfloat16)] * 2
+    else:
+        grads = [out((3 * wide, features), jnp.float32), out((8, 3 * wide), jnp.float32)]
+    outs = [out((2, quarter, features), jnp.bfloat16)] * 2 + grads
     scratch = [
         pltpu.VMEM((4, wide, quarter), jnp.bfloat16),
         pltpu.VMEM((2, wide, block), jnp.bfloat16),
@@ -606,113 +607,139 @@
     )
 
 
-def place_rows(count, by_rows, places, *refs):
-    pieces, out = refs[:count], refs[-1]
-    tile = pieces[0].shape[-2]
-    for k, piece in enumerate(pieces):
+def place_tile(count, places, *refs):
+    out = refs[-1]
+    for k in range(count):
+
+        @pl.when(pl.program_id(0) >> 3 == k)
+        def copy():
+            out[...] = refs[k][0].astype(jnp.float32)
+
+
+def gather_down(places, pieces, x, begun, shape):
+    _, rows, cols = pieces[0].shape
+    count = len(pieces)
+
+    def source(k):
+        return pl.BlockSpec(
+            (1, rows, cols), lambda p, places: (jnp.clip(p - 8 * k, 0, 7), 0, 0)
+        )
+
+    def index(p, places):
+        core, l, y, h = p >> 3, (p >> 2) & 1, (p >> 1) & 1, p & 1
+        return (places[core * 4 + y * 2 + l] * 4 + ((h * 2 + x) ^ places[8]), 0)
+
+    return step_call(
+        functools.partial(place_tile, count),
+        places,
+        8 * count,
+        pieces + begun,
+        [source(k) for k in range(count)] + [pl.BlockSpec(memory_space=pl.ANY)] * len(begun),
+        jax.ShapeDtypeStruct(shape, jnp.float32),
+        pl.BlockSpec((rows, cols), index),
+        [],
+        1000,
+        {count + 1: 0} if begun else {},
+    )
+
+
+def place_rows(count, places, *refs):
+    out = refs[-1]
+    tile = refs[0].shape[1]
+    for k in range(count):
 
         @pl.when(pl.program_id(0) >> 1 == k)
         def copy():
             for q in range(4):
                 h, x = q >> 1, q & 1
-                block = piece[x * 2 + h] if by_rows else piece[x, 0, h]
-                out[pl.ds(pl.multiple_of((q ^ places[8]) * tile, tile), tile), :] = block.astype(
-                    jnp.float32
-                )
-
-
-def gather_hidden(places, pieces, core, bit, begun, shape, by_rows):
+                out[pl.ds(pl.multiple_of((q ^ places[8]) * tile, tile), tile), :] = refs[k][
+                    x * 2 + h
+                ].astype(jnp.float32)
+
+
+def gather_up(places, pieces, y, begun, shape):
     _, rows, cols = pieces[0].shape
-    if by_rows:
-        size = (4, rows, cols)
-    else:
-        pieces = [piece.reshape(2, 2, 2, rows, cols) for piece in pieces]
-        size = (2, 1, 2, rows, cols)
+    count = len(pieces)
 
     def source(k):
-        def index(p, places):
-            turn = jnp.clip(p - 2 * k, 0, 1)
-            return (turn, 0, 0) if by_rows else (0, turn, 0, 0, 0)
-
-        return pl.BlockSpec(size, index)
-
-    def index(p, places):
-        turn = p & 1
-        place = places[(core + (p >> 1)) * 4 + (bit * 2 + turn if by_rows else turn * 2 + bit)]
-        return (place, 0) if by_rows else (0, place)
-
-    begun = [] if begun is None else [begun]
-    count = len(pieces)
+        return pl.BlockSpec(
+            (4, rows, cols), lambda p, places: (jnp.clip(p - 2 * k, 0, 1), 0, 0)
+        )
+
     return step_call(
-        functools.partial(place_rows, count, by_rows),
+        functools.partial(place_rows, count),
         places,
         2 * count,
         pieces + begun,
         [source(k) for k in range(count)] + [pl.BlockSpec(memory_space=pl.ANY)] * len(begun),
         jax.ShapeDtypeStruct(shape, jnp.float32),
-        pl.BlockSpec((4 * rows, cols), index),
+        pl.BlockSpec(
+            (4 * rows, cols), lambda p, places: (0, places[(p >> 1) * 4 + y * 2 + (p & 1)])
+        ),
         [],
         1000,
         {count + 1: 0} if begun else {},
     )
 
 
-def place_heads(late, places, *refs):
-    pieces, (out, out_w, vectors) = refs[:2], refs[-3:]
+def place_heads(places, *refs):
+    pieces = refs[:-4]
+    out, out_w, vector_rows, head_rows = refs[-4:]
     mine, inner = places[9], places[10]
+    seq_parts = len(pieces)
     step = pl.program_id(0)
-    wide = out_w.shape[0]
+    wide = out_w.shape[0] // seq_parts
     rows, features = out.shape[0], out_w.shape[1]
-    seq_parts = features // wide
     f32 = jnp.float32
-    if late:
-        out[...] = refs[2][...]
-    for k, piece in enumerate(pieces):
-        r = k + 2 * late
-        block = piece[step ^ inner, :rows, : 3 * wide].astype(f32)
-        for j in range(seq_parts):
-
-            @pl.when((r ^ mine) == j)
-            def copy():
-                for section in range(3):
-                    start = section * features + j * wide
-                    out[:, start : start + wide] = block[:, section * wide : (section + 1) * wide]
-
-        @pl.when(step == k)
+    for m in range(seq_parts):
+
+        @pl.when(mine == m)
+        def copy():
+            blocks = [pieces[j ^ m][step ^ inner, :rows, : 3 * wide] for j in range(seq_parts)]
+            for section in range(3):
+                columns = slice(section * wide, (section + 1) * wide)
+                joined = jnp.concatenate([block[:, columns] for block in blocks], axis=1)
+                out[:, section * features : (section + 1) * features] = joined.astype(f32)
+
+        @pl.when((mine == m) & (step == 0))
+        def copy_vectors():
+            held = [pieces[j ^ m][inner, rows:, :].astype(f32) for j in range(seq_parts)]
+            total = held[0]
+            for other in held[1:]:
+                total = total + other
+            vector_rows[...] = total
+            for j in range(seq_parts):
+                head_rows[j : j + 1, :] = held[j][10:11, :]
+
+    for r, piece in enumerate(pieces):
+
+        @pl.when(step == r)
         def copy_out():
-            tile, width = wide // 2, features // 4
-            for q in range(8):
-                row, col = q // 4 * tile, q % 4 * width
-                out_w[row : row + tile, col : col + width] = piece[q ^ inner, :rows, 3 * wide :].astype(
-                    f32
+            for i in range(2):
+                joined = jnp.concatenate(
+                    [piece[(4 * i + q) ^ inner, :rows, 3 * wide :] for q in range(4)], axis=1
                 )
-            vectors[k] = piece[inner, rows:, :].astype(f32)
-
-
-def gather_heads(places, pieces, begun, shape):
+                first = pl.multiple_of((r ^ mine) * wide + i * rows, rows)
+                out_w[pl.ds(first, rows), :] = joined.astype(f32)
+
+
+def gather_heads(places, pieces, shape):
     out, f32 = jax.ShapeDtypeStruct, jnp.float32
     features = shape[0]
     rows = features // 8
-    wide = pieces[0].shape[2] // 4
-    late = begun is not None
-    extra = (2, pieces[0].shape[1] - rows, features)
-    main = pl.BlockSpec((rows, shape[1]), lambda p, places: (p, 0))
-
-    def own_rows(p, places):
-        return ((jnp.minimum(p, 1) + 2 * late) ^ places[9], 0)
-
+    square = (features, features)
+    extra = (pieces[0].shape[1] - rows, features)
     return step_call(
-        functools.partial(place_heads, int(late)),
+        place_heads,
         places,
         8,
-        pieces + (begun[:2] if late else []),
-        [whole_spec(p.shape) for p in pieces]
-        + ([main, pl.BlockSpec(memory_space=pl.ANY)] if late else []),
-        [out(shape, f32), out((features, features), f32), out(extra, f32)],
-        [main, pl.BlockSpec((wide, features), own_rows), whole_spec(extra)],
+        pieces,
+        [whole_spec(p.shape) for p in pieces],
+        [out(shape, f32), out(square, f32), out(extra, f32), out((8, features), f32)],
+        [pl.BlockSpec((rows, shape[1]), lambda p, places: (p, 0))]
+        + [whole_spec(square), whole_spec(extra), whole_spec((8, features))],
         [],
         1000,
-        {3: 0, 4: 1} if late else {},
     )
 
 
@@ -841,112 +868,134 @@
         far.append(sum_low(held[1], came[1]))
 
     sends = [
-        sum_low(keep_down[3], came_down1[1]),
-        sum_low(keep_up[3], came_up1[1]),
+        sum_low(keep_down[2:], came_down1),
+        sum_low(keep_up[1::2], jnp.stack([came_up0[1], came_up1[1]])),
         send_out,
     ]
     sends, first_came = lax.optimization_barrier((sends, first_came))
-    down_y1, up_l3, out_x = [exchange_bit(v, bit) for v, bit in zip(sends, "ylx")]
+    down_y, up_l, out_x = [exchange_bit(v, bit) for v, bit in zip(sends, "ylx")]
+    came_down0 = exchange_bit(send_down0, "c")
     total = attend(0, hand_on(d_contexts[0], d_contexts[1], first_came), ())
-    (down_y1, up_l3, out_x, total, parts[0], second_came, near_pair, came_up0, send_down0) = (
+    (down_y, up_l, out_x, total, parts[0], second_came, near_pair, came_down0) = (
         lax.optimization_barrier(
-            (down_y1, up_l3, out_x, total, parts[0], second_came, d_contexts[3:5])
-            + (came_up0, send_down0)
+            (down_y, up_l, out_x, total, parts[0], second_came, d_contexts[3:5], came_down0)
         )
     )
-    came_down0 = exchange_bit(send_down0, "c")
 
     sends = [
-        sum_low(keep_down[2], came_down1[0]),
-        sum_low(keep_up[1], came_up0[1]),
+        sum_low(keep_down[1], came_down0[1], down_y[1]),
+        sum_low(keep_up[2], came_up1[0], up_l[1]),
         sum_low(grad_out[1], out_x[1]),
     ]
     (sends, total) = lax.optimization_barrier((sends, total))
-    down_y0, up_l1, out_c = [exchange_bit(v, bit) for v, bit in zip(sends, "ylc")]
+    down_l, up_y, out_c = [exchange_bit(v, bit) for v, bit in zip(sends, "lyc")]
     cross(0)
     second_group = hand_on(*near_pair, second_came)
     for s in range(1, seq_count - 1):
         total = attend(s, second_group, total)
     out_own = sum_low(grad_out[0], out_x[0], out_c)
-    (down_y0, up_l1, total, parts[1:], near, far, out_own) = lax.optimization_barrier(
-        (down_y0, up_l1, total, parts[1:], near, far, out_own)
-    )
-
-    sends = [
-        sum_low(keep_down[1], came_down0[1], down_y1),
-        sum_low(keep_up[2], came_up1[0], up_l3),
-    ]
-    (sends, total) = lax.optimization_barrier((sends, total))
-    down_l, up_y = [exchange_bit(v, bit) for v, bit in zip(sends, "ly")]
+    (down_l, up_y, total, parts[1:], near, far, out_own) = lax.optimization_barrier(
+        (down_l, up_y, total, parts[1:], near, far, out_own)
+    )
+
+    down_own = sum_low(keep_down[0], came_down0[0], down_y[0], down_l)
+    down_own = down_own.reshape(2, 2, hidden // 32, features)
+    up_own = sum_low(keep_up[0], came_up0[0], up_l[0], up_y)
+    up_own = up_own.reshape(2, 2, features // 4, hidden // 8)
+    keeps, sends = [down_own[:, 0], up_own[0]], [down_own[:, 1], up_own[1]]
+    (keeps, sends, total) = lax.optimization_barrier((keeps, sends, total))
+    got = [exchange_bit(v, bit) for v, bit in zip(sends, "xh")]
     far_came = [exchange_bit(far[0], "x")]
     for s in range(1, seq_count - 1):
         cross(s)
-    total_w, _ = attend(seq_count - 1, second_group, total, (out_own, sums))
-
-    (down_l, up_y, far, far_came, total_w, parts[-1]) = lax.optimization_barrier(
-        (down_l, up_y, far, far_came, total_w, parts[-1])
-    )
-    down_own = sum_low(keep_down[0], came_down0[0], down_y0, down_l)
-    down_own = down_own.reshape(4, hidden // 32, features)
-    up_own = sum_low(keep_up[0], came_up0[0], up_l1, up_y)
-    up_own = up_own.reshape(2, 2, features // 4, hidden // 8)
-    keeps = [down_own[:2], up_own[:, 0], total_w[:4]]
-    sends = [down_own[2:], up_own[:, 1], total_w[4:]]
+    half_a, half_b = attend(seq_count - 1, second_group, total, (out_own, sums))
+
+    (keeps, got, far, far_came, half_a, half_b, parts[-1]) = lax.optimization_barrier(
+        (keeps, got, far, far_came, half_a, half_b, parts[-1])
+    )
+    down_own, up_own = [k + g for k, g in zip(keeps, got)]
+    half_b = half_b.reshape(2, 2, 2, *half_b.shape[1:])
+    keeps = [half_a[:4], half_b[:, 0], down_own[:1], up_own[:1]]
+    sends = [half_a[4:], half_b[:, 1], down_own[1:], up_own[1:]]
     (keeps, sends) = lax.optimization_barrier((keeps, sends))
-    got = [exchange_bit(v, bit) for v, bit in zip(sends, "hxy")]
+    got = [exchange_bit(v, bit) for v, bit in zip(sends, "ylhx")]
     far_came += [exchange_bit(v, "x") for v in far[1:]]
-    down_own, up_own, qkv_own = [k + g for k, g in zip(keeps, got)]
-    qkv_own = qkv_own[:2] + exchange_bit(qkv_own[2:], "l")
+    half_a, half_b, down, up = [k + g for k, g in zip(keeps, got)]
     far = []
     cross(seq_count - 1)
 
-    keeps = [down_own[:1], up_own[:1], qkv_own[:1]]
-    sends = [down_own[1:], up_own[1:], qkv_own[1:]]
-    (keeps, sends, far, far_came, near) = lax.optimization_barrier(
-        (keeps, sends, far, far_came, near)
-    )
-    got = [exchange_bit(v, bit) for v, bit in zip(sends, "xhh")]
+    keeps, sends = [half_a[:2], half_b[0]], [half_a[2:], half_b[1]]
+    down, up = add_extra(down), add_extra(up)
+    (keeps, sends, down, up, far, near) = lax.optimization_barrier(
+        (keeps, sends, down, up, far, near)
+    )
+    got = [exchange_bit(v, bit) for v, bit in zip(sends, "ly")]
+    came = exchange_bit(down, "h")
     far_came += [exchange_bit(v, "x") for v in far]
-    shards = [add_extra(k + g) for k, g in zip(keeps, got)]
-
+    down = jnp.concatenate([down, came])
+    both = jnp.concatenate([k + g for k, g in zip(keeps, got)], axis=2)
+
+    keep, send = both[:1], both[1:]
+    (keep, send, down, up) = lax.optimization_barrier((keep, send, down, up))
+    came, up_came = exchange_bit(send, "h"), exchange_bit(up, "h")
+    down = jnp.concatenate([down, exchange_bit(down, "y")])
+    up = jnp.concatenate([up, up_came])
+    both = add_extra(keep + came)
+
+    (both, down, up, far_came) = lax.optimization_barrier((both, down, up, far_came))
+    came = exchange_bit(both, "h")
+    down = jnp.concatenate([down, exchange_bit(down, "l")])
+    up = jnp.concatenate([up, exchange_bit(up, "x")])
+    both = jnp.concatenate([both, came])
     own_pos = mine * local_rows + jnp.arange(local_rows, dtype=jnp.int32)
     live = (own_pos[None, :] < lengths[:, None]).astype(f32)
     d_inputs = jnp.stack([n + f for n, f in zip(near, far_came)])
     grad_tokens = (d_inputs + d_first_in.reshape(seq_count, local_rows, features)) * live[:, :, None]
-    for bits in ("hhh", "xyl", "lxy"):
-        if bits == "xyl":
-            (shards, grad_tokens) = lax.optimization_barrier((shards, grad_tokens))
-        else:
-            shards = lax.optimization_barrier(shards)
-        shards = [
-            jnp.concatenate([shard, exchange_bit(shard, bit)]) for shard, bit in zip(shards, bits)
-        ]
-    shards = lax.optimization_barrier(shards)
-    last = [exchange_bit(shard, bit) for shard, bit in zip(shards, "ylx")]
-    near_c = [exchange_bit(shard, "c") for shard in shards]
-    shapes = ((hidden, features), (features, hidden))
-    early = [
-        gather_hidden(places, [shards[i], near_c[i]], 0, 0, None, shapes[i], i == 0) for i in (0, 1)
-    ]
-    qkv_part, out_part, first_vectors = gather_heads(
-        places, [shards[2], near_c[2]], None, (features, 3 * features)
-    )
-    (last, early) = lax.optimization_barrier((last, early))
-    far_c = [exchange_bit(shard, "c") for shard in last]
-    early = [gather_hidden(places, [last[i]], 0, 1, early[i], shapes[i], i == 0) for i in (0, 1)]
-    (far_c, early, qkv_part) = lax.optimization_barrier((far_c, early, qkv_part))
-    full_down, full_up = [
-        gather_hidden(places, [far_c[i]], 1, 1, early[i], shapes[i], i == 0) for i in (0, 1)
-    ]
-    full_qkv, full_out, last_vectors = gather_heads(
-        places, [last[2], far_c[2]], [qkv_part, out_part], (features, 3 * features)
-    )
-    held = jnp.concatenate([first_vectors, last_vectors])
-    rows = [lax.dynamic_index_in_dim(held, j ^ mine, keepdims=False) for j in range(seq_parts)]
-    vector_rows = rows[0]
-    for row in rows[1:]:
-        vector_rows = vector_rows + row
-    head_rows = jnp.stack([row[10] for row in rows])
+
+
+    (both, down, up, grad_tokens) = lax.optimization_barrier((both, down, up, grad_tokens))
+    down_first = exchange_bit(down[:4], "x")
+    came, up_came = exchange_bit(both, "y"), exchange_bit(up, "l")
+    both = jnp.concatenate([both, came])
+    up = jnp.concatenate([up, up_came])
+
+    (both, down, down_first, up) = lax.optimization_barrier((both, down, down_first, up))
+    came = exchange_bit(both, "l")
+    down_second = exchange_bit(down[4:], "x")
+    up_first = exchange_bit(up[:4], "y")
+    down_near = exchange_bit(down, "c")
+    down_last = jnp.concatenate([down_first, down_second])
+    both = jnp.stack([both.reshape(2, 2, *both.shape[1:]), came.reshape(2, 2, *came.shape[1:])], 1)
+    both = both.reshape(8, *both.shape[3:])
+
+    (both, down, down_near, down_last, up, up_first) = lax.optimization_barrier(
+        (both, down, down_near, down_last, up, up_first)
+    )
+    both_first = exchange_bit(both[:4], "x")
+    up_second = exchange_bit(up[4:], "y")
+    down_far = exchange_bit(down_last, "c")
+    up_near = exchange_bit(up, "c")
+    full_down = gather_down(places, [down, down_near], 0, [], (hidden, features))
+    up_last = jnp.concatenate([up_first, up_second])
+
+    (both, both_first, up, up_near, up_last, down_far, full_down) = lax.optimization_barrier(
+        (both, both_first, up, up_near, up_last, down_far, full_down)
+    )
+    both_second = exchange_bit(both[4:], "x")
+    up_far = exchange_bit(up_last, "c")
+    both_near = exchange_bit(both, "c")
+    full_down = gather_down(places, [down_last, down_far], 1, [full_down], (hidden, features))
+    full_up = gather_up(places, [up, up_near], 0, [], (features, hidden))
+    both_last = jnp.concatenate([both_first, both_second])
+
+    (both_last, both_near, up_far, full_down, full_up) = lax.optimization_barrier(
+        (both_last, both_near, up_far, full_down, full_up)
+    )
+    both_far = exchange_bit(both_last, "c")
+    full_up = gather_up(places, [up_last, up_far], 1, [full_up], (features, hidden))
+    full_qkv, full_out, vector_rows, head_rows = gather_heads(
+        places, [both, both_near, both_last, both_far], (features, 3 * features)
+    )
     (
         full_b_down,
         full_gain_two,

time: 369 us -> 360 us (0.976)
  waiting for transfers between devices: 108 us -> 96.2 us
  local copies, waits for them, and re-layouts: 18.7 us -> 26.2 us
  other arithmetic: 35.4 us -> 31.6 us
    ppermute x67 -> x70, waiting for transfers between devices: 108 us -> 96.2 us  [exchange(): lax.ppermute(array_in, axis, [(i, i ^ flip) for i in range(lax.axis_size(...]
    slice x7 -> x15, local copies, waits for them, and re-layouts: 0.96 us -> 4.96 us  [the longest x2 1.39 us: per_device(): came_up1[1]]
    convert_element_type x10 -> x9, other arithmetic: 20.8 us -> 17.6 us  [sum_low(): return total.astype(jnp.bfloat16)]
    ppermute x67 -> x70, starting transfers between devices: 51.3 us -> 53.3 us  [exchange(): lax.ppermute(array_in, axis, [(i, i ^ flip) for i in range(lax.axis_size(...]
    unnamed x117 -> x136, local copies, waits for them, and re-layouts: 7.57 us -> 9.34 us
    pallas_call x9 -> x6, Pallas kernels: 84.2 us -> 83.3 us  [step_call(): pl.pallas_call(body, out_shape=outs, grid_spec=pltpu.PrefetchScalarGridSp...]
  transfers between devices with their start and end apart: 67 -> 70, of which waited for: 23 -> 26; matrix products, arithmetic and copies ran while one was open for 9% -> 11% of each run, Pallas kernels for 24% -> 27%
where the time goes in v5:
time: 360 us; the launch traced here: 355 us
  Pallas kernels  146 us (41%)
  waiting for transfers between devices  96.2 us (27%)
  starting transfers between devices  53.3 us (15%)
  other arithmetic  31.6 us (9%)
  local copies, waits for them, and re-layouts  26.2 us (7%)
    ppermute x70, waiting for transfers between devices, exchange(): lax.ppermute(array_in, axis, [(i, i ^ flip) for i in range(lax.axis_size(...  96.2 us
    pallas_call x6, Pallas kernels, step_call(): pl.pallas_call(body, out_shape=outs, grid_spec=pltpu.PrefetchScalarGridSp...  83.3 us
    pallas_call x6, Pallas kernels, kernel_call(): pl.pallas_call(body, out_shape=outs, in_specs=[pl.BlockSpec(memory_space=...  63.2 us
    ppermute x70, starting transfers between devices, exchange(): lax.ppermute(array_in, axis, [(i, i ^ flip) for i in range(lax.axis_size(...  53.3 us
    convert_element_type x9, other arithmetic, sum_low(): return total.astype(jnp.bfloat16)  17.6 us
    unnamed x136, local copies, waits for them, and re-layouts  9.34 us
  transfers between devices with their start and end apart: 70, of which 26 were waited for; matrix products, arithmetic and copies ran while one was open for 11% of the time, Pallas kernels for 27%

profile of v5, /device:TPU:0, one launch (start us, length us, event | category | flops | bytes accessed | tf_op | source)
XLA Modules:
  0.0 355.5 jit_solution(6242560393016665725)
XLA Ops:
  17.6 8.4 %shard_map.280 = (bf16[192,256]{1,0:T(8,128)(2,1)}, bf16[192,256]{1,0:T(8,128)(2,1)}, bf16[192,256]{1,0:T(8,128)(2,1)}, bf16[192,256]{1,0:T(8,128)(2,1)}, bf16[1...) custom-call(s32[20]{0:T(128)} %concatenate.60.places, ...), custom_call_target="tpu_custom_call" | custom-call | flops 100000000 | bytes 1048576 | tf_op jit(solution)/shard_map/pallas_call | solution.py:230
  29.1 8.2 %shard_map.281 = (bf16[192,256]{1,0:T(8,128)(2,1)}, bf16[192,256]{1,0:T(8,128)(2,1)}, bf16[192,256]{1,0:T(8,128)(2,1)}, bf16[192,256]{1,0:T(8,128)(2,1)}, bf16[1...) custom-call(s32[20]{0:T(128)} %concatenate.60.places, ...), custom_call_target="tpu_custom_call" | custom-call | flops 100000000 | bytes 1048576 | tf_op jit(solution)/shard_map/pallas_call | solution.py:230
  41.8 8.2 %shard_map.282 = (bf16[192,256]{1,0:T(8,128)(2,1)}, bf16[192,256]{1,0:T(8,128)(2,1)}, bf16[192,256]{1,0:T(8,128)(2,1)}, bf16[192,256]{1,0:T(8,128)(2,1)}, bf16[1...) custom-call(s32[20]{0:T(128)} %concatenate.60.places, ...), custom_call_target="tpu_custom_call" | custom-call | flops 100000000 | bytes 1048576 | tf_op jit(solution)/shard_map/pallas_call | solution.py:230
  57.9 41.9 %shard_map.283 = (bf16[768,768]{1,0:T(8,128)(2,1)}, bf16[2,384,768]{2,1,0:T(8,128)(2,1)}, bf16[2,768,384]{2,1,0:T(8,128)(2,1)}, bf16[2,384,768]{2,1,0:T(8,128)(2...) custom-call(s32[20]{0:T(128)} %concatenate.60.places, ...), custom_call_target="tpu_custom_call" | custom-call | flops 24461180928 | bytes 1048576 | tf_op jit(solution)/shard_map/pallas_call | solution.py:526
  101.5 6.3 %collective-permute-done.19.g2 = bf16[2,1,192,256]{3,2,1,0:T(8,128)(2,1)S(1)} collective-permute-done((bf16[2,1,192,256]{3,2,1,0:T(8,128)(2,1)}, bf16[2,1,192,256]{3,2,1,0:T(8,128)(2,1)S(1)}, u32[]{:S(2)}, u32[]{:S(2)}) %collective-permute-start.19) | collective-permute-done | bytes 196640 | tf_op jit(solution)/shard_map/ppermute | solution.py:29
  108.4 3.1 add_convert_fusion.1
  122.2 12.5 %shard_map.284 = (bf16[2,256,768]{2,1,0:T(8,128)(2,1)}, bf16[2,256,768]{2,1,0:T(8,128)(2,1)}, f32[576,768]{1,0:T(8,128)}, f32[8,576]{1,0:T(8,128)}) custom-call(s32[20]{0:T(128)} %concatenate.60.places, bf16[1,192,256]{2,1,0:T(8,128)(2,1)} %get-tuple-element.218.g0, bf16[1,192,256]{2,1,0:T(8,128)(2,1)} %copy-done.39, bf16[2,1,192,256]{3,2,1,0:T(8,128)(2,1)} %copy-done.29, ...), custom_call_target="tpu_custom_call" | custom-call | flops 100000000 | bytes 1048576 | tf_op jit(solution)/shard_map/pallas_call | solution.py:230
  134.7 12.3 %collective-permute-done.27.g2 = bf16[2,2,192,256]{3,2,1,0:T(8,128)(2,1)S(1)} collective-permute-done((bf16[2,2,192,256]{3,2,1,0:T(8,128)(2,1)}, bf16[2,2,192,256]{3,2,1,0:T(8,128)(2,1)S(1)}, u32[]{:S(2)}, u32[]{:S(2)}) %collective-permute-start.27) | collective-permute-done | bytes 393248 | tf_op jit(solution)/shard_map/ppermute | solution.py:29
  156.7 12.8 %shard_map.285 = (bf16[2,256,768]{2,1,0:T(8,128)(2,1)}, bf16[2,256,768]{2,1,0:T(8,128)(2,1)}, f32[576,768]{1,0:T(8,128)}, f32[8,576]{1,0:T(8,128)}) custom-call(s32[20]{0:T(128)} %concatenate.60.places, bf16[2,192,256]{2,1,0:T(8,128)(2,1)} %get-tuple-element.242.g0, bf16[2,192,256]{2,1,0:T(8,128)(2,1)} %copy-done.25, bf16[2,2,192,256]{3,2,1,0:T(8,128)(2,1)} %copy-done.5, ...), custom_call_target="tpu_custom_call" | custom-call | flops 100000000 | bytes 1048576 | tf_op jit(solution)/shard_map/pallas_call | solution.py:230
  183.4 13.1 %shard_map.286 = (bf16[2,256,768]{2,1,0:T(8,128)(2,1)}, bf16[2,256,768]{2,1,0:T(8,128)(2,1)}, bf16[8,112,384]{2,1,0:T(8,128)(2,1)}, bf16[8,112,384]{2,1,0:T(8,128)(2,1)}) custom-call(s32[20]{0:T(128)} %concatenate.60.places, bf16[2,192,256]{2,1,0:T(8,128)(2,1)} %get-tuple-element.242.g0, bf16[2,192,256]{2,1,0:T(8,128)(2,1)} %copy-done.25, ...), custom_call_target="tpu_custom_call" | custom-call | flops 100000000 | bytes 1048576 | tf_op jit(solution)/shard_map/pallas_call | solution.py:230
  205.6 4.0 %collective-permute-done.42 = bf16[1,192,384]{2,1,0:T(8,128)(2,1)S(1)} collective-permute-done((bf16[1,192,384]{2,1,0:T(8,128)(2,1)S(1)}, bf16[1,192,384]{2,1,0:T(8,128)(2,1)S(1)}, u32[]{:S(2)}, u32[]{:S(2)}) %collective-permute-start.42) | collective-permute-done | bytes 147488 | tf_op jit(solution)/shard_map/ppermute | solution.py:29
  209.6 4.9 %collective-permute-done.41 = bf16[1,96,768]{2,1,0:T(8,128)(2,1)S(1)} collective-permute-done((bf16[1,96,768]{2,1,0:T(8,128)(2,1)S(1)}, bf16[1,96,768]{2,1,0:T(8,128)(2,1)S(1)}, u32[]{:S(2)}, u32[]{:S(2)}) %collective-permute-start.41) | collective-permute-done | bytes 147488 | tf_op jit(solution)/shard_map/ppermute | solution.py:29
  221.6 3.3 collective-permute-done.46
  230.7 7.0 %collective-permute-done.49 = bf16[1,192,384]{2,1,0:T(8,128)(2,1)S(1)} collective-permute-done((bf16[1,192,384]{2,1,0:T(8,128)(2,1)S(1)}, bf16[1,192,384]{2,1,0:T(8,128)(2,1)S(1)}, u32[]{:S(2)}, u32[]{:S(2)}) %collective-permute-start.49) | collective-permute-done | bytes 147488 | tf_op jit(solution)/shard_map/ppermute | solution.py:29
  237.8 3.2 collective-permute-done.47
  247.5 11.0 %collective-permute-done.52 = bf16[1,112,768]{2,1,0:T(8,128)(2,1)S(1)} collective-permute-done((bf16[1,112,768]{2,1,0:T(8,128)(2,1)S(1)}, bf16[1,112,768]{2,1,0:T(8,128)(2,1)S(1)}, u32[]{:S(2)}, u32[]{:S(2)}) %collective-permute-start.52) | collective-permute-done | bytes 172064 | tf_op jit(solution)/shard_map/ppermute | solution.py:29
  263.0 7.1 %collective-permute-done.55 = bf16[2,112,768]{2,1,0:T(8,128)(2,1)S(1)} collective-permute-done((bf16[2,112,768]{2,1,0:T(8,128)(2,1)S(1)}, bf16[2,112,768]{2,1,0:T(8,128)(2,1)S(1)}, u32[]{:S(2)}, u32[]{:S(2)}) %collective-permute-start.55) | collective-permute-done | bytes 344096 | tf_op jit(solution)/shard_map/ppermute | solution.py:29
  270.1 5.1 %collective-permute-done.57 = bf16[4,192,384]{2,1,0:T(8,128)(2,1)S(1)} collective-permute-done((bf16[4,192,384]{2,1,0:T(8,128)(2,1)S(1)}, bf16[4,192,384]{2,1,0:T(8,128)(2,1)S(1)}, u32[]{:S(2)}, u32[]{:S(2)}) %collective-permute-start.57) | collective-permute-done | bytes 589856 | tf_op jit(solution)/shard_map/ppermute | solution.py:29
  279.8 12.7 %collective-permute-done.60 = bf16[4,96,768]{2,1,0:T(8,128)(2,1)S(1)} collective-permute-done((bf16[4,96,768]{2,1,0:T(8,128)(2,1)S(1)}, bf16[4,96,768]{2,1,0:T(8,128)(2,1)S(1)}, u32[]{:S(2)}, u32[]{:S(2)}) %collective-permute-start.60) | collective-permute-done | bytes 589856 | tf_op jit(solution)/shard_map/ppermute | solution.py:29
  298.7 10.8 %shard_map.287.refs_2_ = f32[3072,768]{1,0:T(8,128)} custom-call(s32[20]{0:T(128)} %concatenate.60.places, bf16[8,96,768]{2,1,0:T(8,128)(2,1)} %copy-done.2, bf16[8,96,768]{2,1,0:T(8,128)(2,1)} %copy-done.15), custom_call_target="tpu_custom_call" | custom-call | flops 1000 | bytes 1048576 | tf_op jit(solution)/shard_map/pallas_call | solution.py:526
  316.8 5.4 %shard_map.289.refs_2_ = f32[768,3072]{1,0:T(8,128)} custom-call(s32[20]{0:T(128)} %concatenate.60.places, bf16[8,192,384]{2,1,0:T(8,128)(2,1)} %copy-done.1, bf16[8,192,384]{2,1,0:T(8,128)(2,1)} %collective-permute-done.63.refs_1_), custom_call_target="tpu_custom_call" | custom-call | flops 1000 | bytes 1048576 | tf_op jit(solution)/shard_map/pallas_call | solution.py:526
  322.2 10.8 %shard_map.288 = f32[3072,768]{1,0:T(8,128)} custom-call(s32[20]{0:T(128)} %concatenate.60.places, bf16[8,96,768]{2,1,0:T(8,128)(2,1)} %pad_maximum_fusion.4.refs_0_, bf16[8,96,768]{2,1,0:T(8,128)(2,1)} %collective-permute-done.65.refs_1_, f32[3072,768]{1,0:T(8,128)} %shard_map.287.refs_2_), custom_call_target="tpu_custom_call", output_to_operand_aliasing={{}: (3, {})} | custom-call | flops 1000 | bytes 1048576 | tf_op jit(solution)/shard_map/pallas_call | solution.py:526
  334.5 5.4 %shard_map.291 = f32[768,3072]{1,0:T(8,128)} custom-call(s32[20]{0:T(128)} %concatenate.60.places, bf16[8,192,384]{2,1,0:T(8,128)(2,1)} %copy-done.4, bf16[8,192,384]{2,1,0:T(8,128)(2,1)} %collective-permute-done.68.refs_1_, f32[768,3072]{1,0:T(8,128)} %shard_map.289.refs_2_), custom_call_target="tpu_custom_call", output_to_operand_aliasing={{}: (3, {})} | custom-call | flops 1000 | bytes 1048576 | tf_op jit(solution)/shard_map/pallas_call | solution.py:526
  341.0 9.1 %shard_map.290 = (f32[768,2304]{1,0:T(8,128)}, f32[768,768]{1,0:T(8,128)}, f32[16,768]{1,0:T(8,128)}, f32[8,768]{1,0:T(8,128)}) custom-call(s32[20]{0:T(128)} %concatenate.60.places, bf16[8,112,768]{2,1,0:T(8,128)(2,1)} %bitcast.90, bf16[8,112,768]{2,1,0:T(8,128)(2,1)} %collective-permute-done.67.refs_1_, bf16[8,112,768]{2,1,0:T(8,128)(2,1)} %copy-done.3, ...), custom_call_target="tpu_custom_call" | custom-call | flops 1000 | bytes 1048576 | tf_op jit(solution)/shard_map/pallas_call | solution.py:526
  (351 shorter events, 127.1 us)
Async XLA Ops:
  107.8 39.2 %collective-permute-start.28 = (bf16[2,384,768]{2,1,0:T(8,128)(2,1)}, bf16[2,384,768]{2,1,0:T(8,128)(2,1)}, u32[]{:S(2)}, u32[]{:S(2)}) collective-permute-start(bf16[2,384,768]{2,1,0:T(8,128)(2,1)} %get-tuple-element.232), channel_id=1, source_target_pairs={{0,1},{1,0},{2,3},{3,2},{4,5},{5,4},{6,7},{7,6},{8,9},{9,8},{10,11... | collective-permute-start | bytes 3538952 | tf_op jit(solution)/shard_map/ppermute | solution.py:29
  115.3 31.7 %collective-permute-start.22 = (bf16[2,384,768]{2,1,0:T(8,128)(2,1)}, bf16[2,384,768]{2,1,0:T(8,128)(2,1)}, u32[]{:S(2)}, u32[]{:S(2)}) collective-permute-start(bf16[2,384,768]{2,1,0:T(8,128)(2,1)} %add_convert_fusion.1), channel_id=1, source_target_pairs={{0,4},{4,0},{8,12},{12,8},{16,20},{20,16},{24,28},{28,24},{1,5},{5... | collective-permute-start | bytes 3538952 | tf_op jit(solution)/shard_map/ppermute | solution.py:29
  116.9 30.2 %collective-permute-start.23 = (bf16[2,768,384]{2,1,0:T(8,128)(2,1)}, bf16[2,768,384]{2,1,0:T(8,128)(2,1)}, u32[]{:S(2)}, u32[]{:S(2)}) collective-permute-start(bf16[2,768,384]{2,1,0:T(8,128)(2,1)} %add_convert_fusion), channel_id=1, source_target_pairs={{0,8},{4,12},{8,0},{12,4},{16,24},{20,28},{24,16},{28,20},{1,9},{5... | collective-permute-start | bytes 3538952 | tf_op jit(solution)/shard_map/ppermute | solution.py:29
  118.5 28.6 %collective-permute-start.24 = (bf16[2,8,96,192]{3,2,1,0:T(8,128)(2,1)}, bf16[2,8,96,192]{3,2,1,0:T(8,128)(2,1)S(1)}, u32[]{:S(2)}, u32[]{:S(2)}) collective-permute-start(bf16[2,8,96,192]{3,2,1,0:T(8,128)(2,1)} %get-tuple-element.217), channel_id=1, source_target_pairs={{0,2},{1,3},{2,0},{3,1},{4,6},{5,7},{6,4},{7,5},{8,10},{9,11},{10,... | collective-permute-start | bytes 1769480 | tf_op jit(solution)/shard_map/ppermute | solution.py:29
  121.1 26.0 %collective-permute-start.27 = (bf16[2,2,192,256]{3,2,1,0:T(8,128)(2,1)}, bf16[2,2,192,256]{3,2,1,0:T(8,128)(2,1)S(1)}, u32[]{:S(2)}, u32[]{:S(2)}) collective-permute-start(bf16[2,2,192,256]{3,2,1,0:T(8,128)(2,1)} %get-tuple-element.229), channel_id=1, source_target_pairs={{0,2},{1,3},{2,0},{3,1},{4,6},{5,7},{6,4},{7,5},{8,10},{9,11},{10,... | collective-permute-start | bytes 1179656 | tf_op jit(solution)/shard_map/ppermute | solution.py:29
  147.1 24.5 %collective-permute-start.33 = (bf16[2,256,768]{2,1,0:T(8,128)(2,1)}, bf16[2,256,768]{2,1,0:T(8,128)(2,1)}, u32[]{:S(2)}, u32[]{:S(2)}) collective-permute-start(bf16[2,256,768]{2,1,0:T(8,128)(2,1)} %get-tuple-element.256), channel_id=1, source_target_pairs={{0,1},{1,0},{2,3},{3,2},{4,5},{5,4},{6,7},{7,6},{8,9},{9,8},{10,11... | collective-permute-start | bytes 2359304 | tf_op jit(solution)/shard_map/ppermute | solution.py:29
  154.2 19.5 %collective-permute-start.29 = (bf16[384,768]{1,0:T(8,128)(2,1)}, bf16[384,768]{1,0:T(8,128)(2,1)}, u32[]{:S(2)}, u32[]{:S(2)}) collective-permute-start(bf16[384,768]{1,0:T(8,128)(2,1)} %fusion.4), channel_id=1, source_target_pairs={{0,8},{4,12},{8,0},{12,4},{16,24},{20,28},{24,16},{28,20},{1,9},{5... | collective-permute-start | bytes 1769480 | tf_op jit(solution)/shard_map/ppermute | solution.py:29
  155.5 18.2 %collective-permute-start.30 = (bf16[768,384]{1,0:T(8,128)(2,1)}, bf16[768,384]{1,0:T(8,128)(2,1)}, u32[]{:S(2)}, u32[]{:S(2)}) collective-permute-start(bf16[768,384]{1,0:T(8,128)(2,1)} %fusion.5), channel_id=1, source_target_pairs={{0,4},{4,0},{8,12},{12,8},{16,20},{20,16},{24,28},{28,24},{1,5},{5... | collective-permute-start | bytes 1769480 | tf_op jit(solution)/shard_map/ppermute | solution.py:29
  173.7 22.8 %collective-permute-start.37 = (bf16[2,256,768]{2,1,0:T(8,128)(2,1)}, bf16[2,256,768]{2,1,0:T(8,128)(2,1)}, u32[]{:S(2)}, u32[]{:S(2)}) collective-permute-start(bf16[2,256,768]{2,1,0:T(8,128)(2,1)} %get-tuple-element.268), channel_id=1, source_target_pairs={{0,1},{1,0},{2,3},{3,2},{4,5},{5,4},{6,7},{7,6},{8,9},{9,8},{10,11... | collective-permute-start | bytes 2359304 | tf_op jit(solution)/shard_map/ppermute | solution.py:29
  173.7 24.8 %collective-permute-start.38 = (bf16[256,768]{1,0:T(8,128)(2,1)}, bf16[256,768]{1,0:T(8,128)(2,1)S(1)}, u32[]{:S(2)}, u32[]{:S(2)}) collective-permute-start(bf16[256,768]{1,0:T(8,128)(2,1)} %get-tuple-element.266), channel_id=1, source_target_pairs={{0,2},{1,3},{2,0},{3,1},{4,6},{5,7},{6,4},{7,5},{8,10},{9,11},{10,... | collective-permute-start | bytes 1179656 | tf_op jit(solution)/shard_map/ppermute | solution.py:29
  179.9 18.7 %collective-permute-start.35 = (bf16[2,96,768]{2,1,0:T(8,128)(2,1)}, bf16[2,96,768]{2,1,0:T(8,128)(2,1)S(1)}, u32[]{:S(2)}, u32[]{:S(2)}) collective-permute-start(bf16[2,96,768]{2,1,0:T(8,128)(2,1)} %get-tuple-element.264), channel_id=1, source_target_pairs={{0,2},{1,3},{2,0},{3,1},{4,6},{5,7},{6,4},{7,5},{8,10},{9,11},{10,... | collective-permute-start | bytes 884744 | tf_op jit(solution)/shard_map/ppermute | solution.py:29
  180.8 17.8 %collective-permute-start.36 = (bf16[2,192,384]{2,1,0:T(8,128)(2,1)}, bf16[2,192,384]{2,1,0:T(8,128)(2,1)}, u32[]{:S(2)}, u32[]{:S(2)}) collective-permute-start(bf16[2,192,384]{2,1,0:T(8,128)(2,1)} %bitcast.25), channel_id=1, source_target_pairs={{0,16},{4,20},{8,24},{12,28},{16,0},{20,4},{24,8},{28,12},{1,17},{... | collective-permute-start | bytes 884744 | tf_op jit(solution)/shard_map/ppermute | solution.py:29
  219.5 21.5 %collective-permute-start.50 = (bf16[256,768]{1,0:T(8,128)(2,1)}, bf16[256,768]{1,0:T(8,128)(2,1)S(1)}, u32[]{:S(2)}, u32[]{:S(2)}) collective-permute-start(bf16[256,768]{1,0:T(8,128)(2,1)} %get-tuple-element.309), channel_id=1, source_target_pairs={{0,2},{1,3},{2,0},{3,1},{4,6},{5,7},{6,4},{7,5},{8,10},{9,11},{10,... | collective-permute-start | bytes 1179656 | tf_op jit(solution)/shard_map/ppermute | solution.py:29
  220.7 20.4 %collective-permute-start.51 = (bf16[256,768]{1,0:T(8,128)(2,1)}, bf16[256,768]{1,0:T(8,128)(2,1)S(1)}, u32[]{:S(2)}, u32[]{:S(2)}) collective-permute-start(bf16[256,768]{1,0:T(8,128)(2,1)} %get-tuple-element.310), channel_id=1, source_target_pairs={{0,2},{1,3},{2,0},{3,1},{4,6},{5,7},{6,4},{7,5},{8,10},{9,11},{10,... | collective-permute-start | bytes 1179656 | tf_op jit(solution)/shard_map/ppermute | solution.py:29
  241.1 17.5 %collective-permute-start.54 = (bf16[2,192,384]{2,1,0:T(8,128)(2,1)S(1)}, bf16[2,192,384]{2,1,0:T(8,128)(2,1)S(1)}, u32[]{:S(2)}, u32[]{:S(2)}) collective-permute-start(bf16[2,192,384]{2,1,0:T(8,128)(2,1)S(1)} %pad_maximum_fusion.11), channel_id=1, source_target_pairs={{0,2},{1,3},{2,0},{3,1},{4,6},{5,7},{6,4},{7,5},{8,10},{9,11},{10,... | collective-permute-start | bytes 884744 | tf_op jit(solution)/shard_map/ppermute | solution.py:29
  242.1 18.7 %collective-permute-start.53 = (bf16[4,96,768]{2,1,0:T(8,128)(2,1)S(1)}, bf16[4,96,768]{2,1,0:T(8,128)(2,1)S(1)}, u32[]{:S(2)}, u32[]{:S(2)}) collective-permute-start(bf16[4,96,768]{2,1,0:T(8,128)(2,1)S(1)} %pad_maximum_fusion.7), channel_id=1, source_target_pairs={{0,8},{4,12},{8,0},{12,4},{16,24},{20,28},{24,16},{28,20},{1,9},{5... | collective-permute-start | bytes 1769480 | tf_op jit(solution)/shard_map/ppermute | solution.py:29
  276.6 18.2 %collective-permute-start.59 = (bf16[8,96,768]{2,1,0:T(8,128)(2,1)S(1)}, bf16[8,96,768]{2,1,0:T(8,128)(2,1)S(1)}, u32[]{:S(2)}, u32[]{:S(2)}) collective-permute-start(bf16[8,96,768]{2,1,0:T(8,128)(2,1)S(1)} %pad_maximum_fusion.2.refs_0_), channel_id=1, source_target_pairs={{0,1},{1,0},{2,3},{3,2},{4,5},{5,4},{6,7},{7,6},{8,9},{9,8},{10,11... | collective-permute-start | bytes 3538952 | tf_op jit(solution)/shard_map/ppermute | solution.py:29
  277.1 17.6 %collective-permute-start.58 = (bf16[4,112,768]{2,1,0:T(8,128)(2,1)S(1)}, bf16[4,112,768]{2,1,0:T(8,128)(2,1)S(1)}, u32[]{:S(2)}, u32[]{:S(2)}) collective-permute-start(bf16[4,112,768]{2,1,0:T(8,128)(2,1)S(1)} %pad_maximum_fusion.6), channel_id=1, source_target_pairs={{0,8},{4,12},{8,0},{12,4},{16,24},{20,28},{24,16},{28,20},{1,9},{5... | collective-permute-start | bytes 2064392 | tf_op jit(solution)/shard_map/ppermute | solution.py:29
  294.9 20.0 %collective-permute-start.63 = (bf16[8,192,384]{2,1,0:T(8,128)(2,1)S(1)}, bf16[8,192,384]{2,1,0:T(8,128)(2,1)}, u32[]{:S(2)}, u32[]{:S(2)}) collective-permute-start(bf16[8,192,384]{2,1,0:T(8,128)(2,1)S(1)} %pad_maximum_fusion.3.refs_0_), channel_id=1, source_target_pairs={{0,1},{1,0},{2,3},{3,2},{4,5},{5,4},{6,7},{7,6},{8,9},{9,8},{10,11... | collective-permute-start | bytes 3538952 | tf_op jit(solution)/shard_map/ppermute | solution.py:29
  295.0 19.9 %collective-permute-start.65 = (bf16[8,96,768]{2,1,0:T(8,128)(2,1)}, bf16[8,96,768]{2,1,0:T(8,128)(2,1)}, u32[]{:S(2)}, u32[]{:S(2)}) collective-permute-start(bf16[8,96,768]{2,1,0:T(8,128)(2,1)} %pad_maximum_fusion.4.refs_0_), channel_id=1, source_target_pairs={{0,1},{1,0},{2,3},{3,2},{4,5},{5,4},{6,7},{7,6},{8,9},{9,8},{10,11... | collective-permute-start | bytes 3538952 | tf_op jit(solution)/shard_map/ppermute | solution.py:29
  297.4 17.5 %collective-permute-start.62 = (bf16[4,112,768]{2,1,0:T(8,128)(2,1)}, bf16[4,112,768]{2,1,0:T(8,128)(2,1)}, u32[]{:S(2)}, u32[]{:S(2)}) collective-permute-start(bf16[4,112,768]{2,1,0:T(8,128)(2,1)} %slice.270), channel_id=1, source_target_pairs={{0,2},{1,3},{2,0},{3,1},{4,6},{5,7},{6,4},{7,5},{8,10},{9,11},{10,... | collective-permute-start | bytes 2064392 | tf_op jit(solution)/shard_map/ppermute | solution.py:29
  314.9 19.6 %collective-permute-start.67 = (bf16[8,112,768]{2,1,0:T(8,128)(2,1)S(1)}, bf16[8,112,768]{2,1,0:T(8,128)(2,1)}, u32[]{:S(2)}, u32[]{:S(2)}) collective-permute-start(bf16[8,112,768]{2,1,0:T(8,128)(2,1)S(1)} %bitcast.88), channel_id=1, source_target_pairs={{0,1},{1,0},{2,3},{3,2},{4,5},{5,4},{6,7},{7,6},{8,9},{9,8},{10,11... | collective-permute-start | bytes 4128776 | tf_op jit(solution)/shard_map/ppermute | solution.py:29
  314.9 19.6 %collective-permute-start.68 = (bf16[8,192,384]{2,1,0:T(8,128)(2,1)S(1)}, bf16[8,192,384]{2,1,0:T(8,128)(2,1)}, u32[]{:S(2)}, u32[]{:S(2)}) collective-permute-start(bf16[8,192,384]{2,1,0:T(8,128)(2,1)S(1)} %pad_maximum_fusion.5.refs_0_), channel_id=1, source_target_pairs={{0,1},{1,0},{2,3},{3,2},{4,5},{5,4},{6,7},{7,6},{8,9},{9,8},{10,11... | collective-permute-start | bytes 3538952 | tf_op jit(solution)/shard_map/ppermute | solution.py:29
  315.4 17.6 %collective-permute-start.66 = (bf16[4,112,768]{2,1,0:T(8,128)(2,1)S(1)}, bf16[4,112,768]{2,1,0:T(8,128)(2,1)}, u32[]{:S(2)}, u32[]{:S(2)}) collective-permute-start(bf16[4,112,768]{2,1,0:T(8,128)(2,1)S(1)} %slice.272), channel_id=1, source_target_pairs={{0,2},{1,3},{2,0},{3,1},{4,6},{5,7},{6,4},{7,5},{8,10},{9,11},{10,... | collective-permute-start | bytes 2064392 | tf_op jit(solution)/shard_map/ppermute | solution.py:29
  (113 other events, 840.4 us)

commit v6 on v5

--- a/solution.py
+++ b/solution.py
@@ -607,45 +607,9 @@
     )
 
 
-def place_tile(count, places, *refs):
-    out = refs[-1]
-    for k in range(count):
-
-        @pl.when(pl.program_id(0) >> 3 == k)
-        def copy():
-            out[...] = refs[k][0].astype(jnp.float32)
-
-
-def gather_down(places, pieces, x, begun, shape):
-    _, rows, cols = pieces[0].shape
-    count = len(pieces)
-
-    def source(k):
-        return pl.BlockSpec(
-            (1, rows, cols), lambda p, places: (jnp.clip(p - 8 * k, 0, 7), 0, 0)
-        )
-
-    def index(p, places):
-        core, l, y, h = p >> 3, (p >> 2) & 1, (p >> 1) & 1, p & 1
-        return (places[core * 4 + y * 2 + l] * 4 + ((h * 2 + x) ^ places[8]), 0)
-
-    return step_call(
-        functools.partial(place_tile, count),
-        places,
-        8 * count,
-        pieces + begun,
-        [source(k) for k in range(count)] + [pl.BlockSpec(memory_space=pl.ANY)] * len(begun),
-        jax.ShapeDtypeStruct(shape, jnp.float32),
-        pl.BlockSpec((rows, cols), index),
-        [],
-        1000,
-        {count + 1: 0} if begun else {},
-    )
-
-
 def place_rows(count, places, *refs):
     out = refs[-1]
-    tile = refs[0].shape[1]
+    tile = refs[0].shape[-2]
     for k in range(count):
 
         @pl.when(pl.program_id(0) >> 1 == k)
@@ -653,29 +617,32 @@
             for q in range(4):
                 h, x = q >> 1, q & 1
                 out[pl.ds(pl.multiple_of((q ^ places[8]) * tile, tile), tile), :] = refs[k][
-                    x * 2 + h
+                    x, 0, h
                 ].astype(jnp.float32)
 
 
-def gather_up(places, pieces, y, begun, shape):
+def gather_hidden(places, pieces, core, late, begun, shape, by_rows):
     _, rows, cols = pieces[0].shape
     count = len(pieces)
 
     def source(k):
         return pl.BlockSpec(
-            (4, rows, cols), lambda p, places: (jnp.clip(p - 2 * k, 0, 1), 0, 0)
+            (2, 1, 2, rows, cols), lambda p, places: (0, jnp.clip(p - 2 * k, 0, 1), 0, 0, 0)
         )
+
+    def index(p, places):
+        turn = p & 1
+        outer = (core + (p >> 1)) * 4 + (late * 2 + turn if by_rows else turn * 2 + late)
+        return (places[outer], 0) if by_rows else (0, places[outer])
 
     return step_call(
         functools.partial(place_rows, count),
         places,
         2 * count,
-        pieces + begun,
+        [piece.reshape(2, 2, 2, rows, cols) for piece in pieces] + begun,
         [source(k) for k in range(count)] + [pl.BlockSpec(memory_space=pl.ANY)] * len(begun),
         jax.ShapeDtypeStruct(shape, jnp.float32),
-        pl.BlockSpec(
-            (4 * rows, cols), lambda p, places: (0, places[(p >> 1) * 4 + y * 2 + (p & 1)])
-        ),
+        pl.BlockSpec((4 * rows, cols), index),
         [],
         1000,
         {count + 1: 0} if begun else {},
@@ -870,83 +837,74 @@
     sends = [
         sum_low(keep_down[2:], came_down1),
         sum_low(keep_up[1::2], jnp.stack([came_up0[1], came_up1[1]])),
-        send_out,
     ]
     sends, first_came = lax.optimization_barrier((sends, first_came))
-    down_y, up_l, out_x = [exchange_bit(v, bit) for v, bit in zip(sends, "ylx")]
+    down_y, up_l = [exchange_bit(v, bit) for v, bit in zip(sends, "yl")]
     came_down0 = exchange_bit(send_down0, "c")
     total = attend(0, hand_on(d_contexts[0], d_contexts[1], first_came), ())
-    (down_y, up_l, out_x, total, parts[0], second_came, near_pair, came_down0) = (
-        lax.optimization_barrier(
-            (down_y, up_l, out_x, total, parts[0], second_came, d_contexts[3:5], came_down0)
-        )
+    (total, parts[0], second_came, near_pair, came_down0, send_out) = lax.optimization_barrier(
+        (total, parts[0], second_came, d_contexts[3:5], came_down0, send_out)
+    )
+
+    out_x = exchange_bit(send_out, "x")
+    second_group = hand_on(*near_pair, second_came)
+    cross(0)
+    for s in range(1, seq_count - 1):
+        total = attend(s, second_group, total)
+    (down_y, up_l, out_x, total, parts[1:], near, far) = lax.optimization_barrier(
+        (down_y, up_l, out_x, total, parts[1:], near, far)
     )
 
     sends = [
         sum_low(keep_down[1], came_down0[1], down_y[1]),
         sum_low(keep_up[2], came_up1[0], up_l[1]),
-        sum_low(grad_out[1], out_x[1]),
     ]
-    (sends, total) = lax.optimization_barrier((sends, total))
-    down_l, up_y, out_c = [exchange_bit(v, bit) for v, bit in zip(sends, "lyc")]
-    cross(0)
-    second_group = hand_on(*near_pair, second_came)
+    out_c = exchange_bit(sum_low(grad_out[1], out_x[1]), "c")
+    out_own = sum_low(grad_out[0], out_x[0], out_c)
+    (sends, total, out_own, far) = lax.optimization_barrier((sends, total, out_own, far))
+    down_l, up_y = [exchange_bit(v, bit) for v, bit in zip(sends, "ly")]
+    far_came = [exchange_bit(far[0], "x")]
     for s in range(1, seq_count - 1):
-        total = attend(s, second_group, total)
-    out_own = sum_low(grad_out[0], out_x[0], out_c)
-    (down_l, up_y, total, parts[1:], near, far, out_own) = lax.optimization_barrier(
-        (down_l, up_y, total, parts[1:], near, far, out_own)
-    )
-
+        cross(s)
+    half_a, half_b = attend(seq_count - 1, second_group, total, (out_own, sums))
+
+    (down_l, up_y, far, far_came, half_a, half_b, parts[-1]) = lax.optimization_barrier(
+        (down_l, up_y, far, far_came, half_a, half_b, parts[-1])
+    )
     down_own = sum_low(keep_down[0], came_down0[0], down_y[0], down_l)
     down_own = down_own.reshape(2, 2, hidden // 32, features)
     up_own = sum_low(keep_up[0], came_up0[0], up_l[0], up_y)
     up_own = up_own.reshape(2, 2, features // 4, hidden // 8)
-    keeps, sends = [down_own[:, 0], up_own[0]], [down_own[:, 1], up_own[1]]
-    (keeps, sends, total) = lax.optimization_barrier((keeps, sends, total))
-    got = [exchange_bit(v, bit) for v, bit in zip(sends, "xh")]
-    far_came = [exchange_bit(far[0], "x")]
-    for s in range(1, seq_count - 1):
-        cross(s)
-    half_a, half_b = attend(seq_count - 1, second_group, total, (out_own, sums))
-
-    (keeps, got, far, far_came, half_a, half_b, parts[-1]) = lax.optimization_barrier(
-        (keeps, got, far, far_came, half_a, half_b, parts[-1])
-    )
-    down_own, up_own = [k + g for k, g in zip(keeps, got)]
     half_b = half_b.reshape(2, 2, 2, *half_b.shape[1:])
-    keeps = [half_a[:4], half_b[:, 0], down_own[:1], up_own[:1]]
-    sends = [half_a[4:], half_b[:, 1], down_own[1:], up_own[1:]]
+    keeps = [half_a[:4], half_b[:, 0], down_own[:, 0], up_own[0]]
+    sends = [half_a[4:], half_b[:, 1], down_own[:, 1], up_own[1]]
     (keeps, sends) = lax.optimization_barrier((keeps, sends))
-    got = [exchange_bit(v, bit) for v, bit in zip(sends, "ylhx")]
+    got = [exchange_bit(v, bit) for v, bit in zip(sends, "ylxh")]
     far_came += [exchange_bit(v, "x") for v in far[1:]]
     half_a, half_b, down, up = [k + g for k, g in zip(keeps, got)]
     far = []
     cross(seq_count - 1)
 
-    keeps, sends = [half_a[:2], half_b[0]], [half_a[2:], half_b[1]]
+    keeps = [half_a[:2], half_b[0], down[:1], up[:1]]
+    sends = [half_a[2:], half_b[1], down[1:], up[1:]]
+    (keeps, sends, far, near) = lax.optimization_barrier((keeps, sends, far, near))
+    got = [exchange_bit(v, bit) for v, bit in zip(sends, "lyhx")]
+    far_came += [exchange_bit(v, "x") for v in far]
+    half_a, half_b, down, up = [k + g for k, g in zip(keeps, got)]
     down, up = add_extra(down), add_extra(up)
-    (keeps, sends, down, up, far, near) = lax.optimization_barrier(
-        (keeps, sends, down, up, far, near)
-    )
-    got = [exchange_bit(v, bit) for v, bit in zip(sends, "ly")]
-    came = exchange_bit(down, "h")
-    far_came += [exchange_bit(v, "x") for v in far]
-    down = jnp.concatenate([down, came])
-    both = jnp.concatenate([k + g for k, g in zip(keeps, got)], axis=2)
+    both = jnp.concatenate([half_a, half_b], axis=2)
 
     keep, send = both[:1], both[1:]
     (keep, send, down, up) = lax.optimization_barrier((keep, send, down, up))
-    came, up_came = exchange_bit(send, "h"), exchange_bit(up, "h")
-    down = jnp.concatenate([down, exchange_bit(down, "y")])
+    came, down_came = exchange_bit(send, "h"), exchange_bit(down, "h")
+    both = add_extra(keep + came)
+    down = jnp.concatenate([down, down_came])
+
+    (both, down, up, far_came) = lax.optimization_barrier((both, down, up, far_came))
+    came, up_came = exchange_bit(both, "h"), exchange_bit(up, "h")
+    down = jnp.concatenate([down, exchange_bit(down, "l")])
+    both = jnp.concatenate([both, came])
     up = jnp.concatenate([up, up_came])
-    both = add_extra(keep + came)
-
-    (both, down, up, far_came) = lax.optimization_barrier((both, down, up, far_came))
-    came = exchange_bit(both, "h")
-    down = jnp.concatenate([down, exchange_bit(down, "l")])
-    up = jnp.concatenate([up, exchange_bit(up, "x")])
-    both = jnp.concatenate([both, came])
     own_pos = mine * local_rows + jnp.arange(local_rows, dtype=jnp.int32)
     live = (own_pos[None, :] < lengths[:, None]).astype(f32)
     d_inputs = jnp.stack([n + f for n, f in zip(near, far_came)])
@@ -954,48 +912,59 @@
 
 
     (both, down, up, grad_tokens) = lax.optimization_barrier((both, down, up, grad_tokens))
-    down_first = exchange_bit(down[:4], "x")
-    came, up_came = exchange_bit(both, "y"), exchange_bit(up, "l")
+    came = exchange_bit(both, "y")
+    down = jnp.concatenate([down, exchange_bit(down, "x")])
+    up = jnp.concatenate([up, exchange_bit(up, "y")])
     both = jnp.concatenate([both, came])
-    up = jnp.concatenate([up, up_came])
-
-    (both, down, down_first, up) = lax.optimization_barrier((both, down, down_first, up))
+
+    (both, down, up) = lax.optimization_barrier((both, down, up))
     came = exchange_bit(both, "l")
-    down_second = exchange_bit(down[4:], "x")
-    up_first = exchange_bit(up[:4], "y")
+    down_first = exchange_bit(down[:4], "y")
+    up_came = exchange_bit(up, "x")
     down_near = exchange_bit(down, "c")
-    down_last = jnp.concatenate([down_first, down_second])
     both = jnp.stack([both.reshape(2, 2, *both.shape[1:]), came.reshape(2, 2, *came.shape[1:])], 1)
     both = both.reshape(8, *both.shape[3:])
-
-    (both, down, down_near, down_last, up, up_first) = lax.optimization_barrier(
-        (both, down, down_near, down_last, up, up_first)
+    up = jnp.concatenate([up, up_came])
+
+    (both, down, down_near, down_first, up) = lax.optimization_barrier(
+        (both, down, down_near, down_first, up)
     )
     both_first = exchange_bit(both[:4], "x")
-    up_second = exchange_bit(up[4:], "y")
+    down_second = exchange_bit(down[4:], "y")
+    up_first = exchange_bit(up[:4], "l")
+    up_near = exchange_bit(up, "c")
+    full_down = gather_hidden(places, [down, down_near], 0, 0, [], (hidden, features), True)
+    down_last = jnp.concatenate([down_first, down_second])
+
+    (both, both_first, up, up_near, up_first, down_last, full_down) = lax.optimization_barrier(
+        (both, both_first, up, up_near, up_first, down_last, full_down)
+    )
+    both_second = exchange_bit(both[4:6], "x")
+    up_second = exchange_bit(up[4:6], "l")
     down_far = exchange_bit(down_last, "c")
-    up_near = exchange_bit(up, "c")
-    full_down = gather_down(places, [down, down_near], 0, [], (hidden, features))
-    up_last = jnp.concatenate([up_first, up_second])
-
-    (both, both_first, up, up_near, up_last, down_far, full_down) = lax.optimization_barrier(
-        (both, both_first, up, up_near, up_last, down_far, full_down)
-    )
-    both_second = exchange_bit(both[4:], "x")
-    up_far = exchange_bit(up_last, "c")
+    full_up = gather_hidden(places, [up, up_near], 0, 0, [], (features, hidden), False)
+
+    (both, both_second, up, up_second, down_far, full_up) = lax.optimization_barrier(
+        (both, both_second, up, up_second, down_far, full_up)
+    )
+    both_third = exchange_bit(both[6:], "x")
+    up_third = exchange_bit(up[6:], "l")
     both_near = exchange_bit(both, "c")
-    full_down = gather_down(places, [down_last, down_far], 1, [full_down], (hidden, features))
-    full_up = gather_up(places, [up, up_near], 0, [], (features, hidden))
-    both_last = jnp.concatenate([both_first, both_second])
-
-    (both_last, both_near, up_far, full_down, full_up) = lax.optimization_barrier(
-        (both_last, both_near, up_far, full_down, full_up)
-    )
-    both_far = exchange_bit(both_last, "c")
-    full_up = gather_up(places, [up_last, up_far], 1, [full_up], (features, hidden))
+    full_down = gather_hidden(
+        places, [down_last, down_far], 0, 1, [full_down], (hidden, features), True
+    )
+    (both_third, both_near, up_third, full_down) = lax.optimization_barrier(
+        (both_third, both_near, up_third, full_down)
+    )
+    both_last = jnp.concatenate([both_first, both_second, both_third])
+    up_last = jnp.concatenate([up_first, up_second, up_third])
+    both_far, up_far = exchange_bit(both_last, "c"), exchange_bit(up_last, "c")
+    full_up = gather_hidden(places, [up_last], 0, 1, [full_up], (features, hidden), False)
+    (both_far, full_up) = lax.optimization_barrier((both_far, full_up))
     full_qkv, full_out, vector_rows, head_rows = gather_heads(
         places, [both, both_near, both_last, both_far], (features, 3 * features)
     )
+    full_up = gather_hidden(places, [up_far], 1, 1, [full_up], (features, hidden), False)
     (
         full_b_down,
         full_gain_two,

time: 360 us -> 365 us (1.014)
  local copies, waits for them, and re-layouts: 26.2 us -> 41 us
  Pallas kernels: 146 us -> 137 us
  waiting for transfers between devices: 96.2 us -> 99.9 us
    pallas_call x6 -> x7, Pallas kernels: 83.3 us -> 73.5 us  [step_call(): pl.pallas_call(body, out_shape=outs, grid_spec=pltpu.PrefetchScalarGridSp...]
    unnamed x136 -> x144, local copies, waits for them, and re-layouts: 9.34 us -> 16.4 us
    slice x10 -> x12, local copies, waits for them, and re-layouts: 1.83 us -> 8.21 us  [the longest x3 2.08 us: per_device(): sends = [half_a[2:], half_b[1], down[1:], up[1:]]]
    ppermute x70 -> x72, waiting for transfers between devices: 96.2 us -> 99.9 us  [exchange(): lax.ppermute(array_in, axis, [(i, i ^ flip) for i in range(lax.axis_size(...]
    ppermute x70 -> x72, starting transfers between devices: 53.3 us -> 52.6 us  [exchange(): lax.ppermute(array_in, axis, [(i, i ^ flip) for i in range(lax.axis_size(...]
  transfers between devices with their start and end apart: 70 -> 72, of which waited for: 26 -> 28; matrix products, arithmetic and copies ran while one was open for 11% -> 13% of each run, Pallas kernels for 27% -> 25%
where the time goes in v6:
time: 365 us; the launch traced here: 360 us
  Pallas kernels  137 us (38%)
  waiting for transfers between devices  99.9 us (27%)
  starting transfers between devices  52.6 us (14%)
  local copies, waits for them, and re-layouts  41 us (11%)
  other arithmetic  28 us (8%)
    ppermute x72, waiting for transfers between devices, exchange(): lax.ppermute(array_in, axis, [(i, i ^ flip) for i in range(lax.axis_size(...  99.9 us
    pallas_call x7, Pallas kernels, step_call(): pl.pallas_call(body, out_shape=outs, grid_spec=pltpu.PrefetchScalarGridSp...  73.5 us
    pallas_call x6, Pallas kernels, kernel_call(): pl.pallas_call(body, out_shape=outs, in_specs=[pl.BlockSpec(memory_space=...  63 us
    ppermute x72, starting transfers between devices, exchange(): lax.ppermute(array_in, axis, [(i, i ^ flip) for i in range(lax.axis_size(...  52.6 us
    unnamed x144, local copies, waits for them, and re-layouts  16.4 us
    convert_element_type x9, other arithmetic, sum_low(): return total.astype(jnp.bfloat16)  15.9 us
  transfers between devices with their start and end apart: 72, of which 28 were waited for; matrix products, arithmetic and copies ran while one was open for 13% of the time, Pallas kernels for 25%

profile of v6, /device:TPU:0, one launch (start us, length us, event | category | flops | bytes accessed | tf_op | source)
XLA Modules:
  0.0 360.0 jit_solution(15646573340470809451)
XLA Ops:
  2.0 3.0 collective-permute-start
  17.6 8.3 %shard_map.280 = (bf16[192,256]{1,0:T(8,128)(2,1)}, bf16[192,256]{1,0:T(8,128)(2,1)}, bf16[192,256]{1,0:T(8,128)(2,1)}, bf16[192,256]{1,0:T(8,128)(2,1)}, bf16[1...) custom-call(s32[20]{0:T(128)} %concatenate.60.places, ...), custom_call_target="tpu_custom_call" | custom-call | flops 100000000 | bytes 1048576 | tf_op jit(solution)/shard_map/pallas_call | solution.py:230
  29.1 8.2 %shard_map.281 = (bf16[192,256]{1,0:T(8,128)(2,1)}, bf16[192,256]{1,0:T(8,128)(2,1)}, bf16[192,256]{1,0:T(8,128)(2,1)}, bf16[192,256]{1,0:T(8,128)(2,1)}, bf16[1...) custom-call(s32[20]{0:T(128)} %concatenate.60.places, ...), custom_call_target="tpu_custom_call" | custom-call | flops 100000000 | bytes 1048576 | tf_op jit(solution)/shard_map/pallas_call | solution.py:230
  41.7 8.2 %shard_map.282 = (bf16[192,256]{1,0:T(8,128)(2,1)}, bf16[192,256]{1,0:T(8,128)(2,1)}, bf16[192,256]{1,0:T(8,128)(2,1)}, bf16[192,256]{1,0:T(8,128)(2,1)}, bf16[1...) custom-call(s32[20]{0:T(128)} %concatenate.60.places, ...), custom_call_target="tpu_custom_call" | custom-call | flops 100000000 | bytes 1048576 | tf_op jit(solution)/shard_map/pallas_call | solution.py:230
  57.9 41.8 %shard_map.283 = (bf16[768,768]{1,0:T(8,128)(2,1)}, bf16[2,384,768]{2,1,0:T(8,128)(2,1)}, bf16[2,768,384]{2,1,0:T(8,128)(2,1)}, bf16[2,384,768]{2,1,0:T(8,128)(2...) custom-call(s32[20]{0:T(128)} %concatenate.60.places, ...), custom_call_target="tpu_custom_call" | custom-call | flops 24461180928 | bytes 1048576 | tf_op jit(solution)/shard_map/pallas_call | solution.py:526
  101.5 6.3 %collective-permute-done.20.g2 = bf16[2,1,192,256]{3,2,1,0:T(8,128)(2,1)S(1)} collective-permute-done((bf16[2,1,192,256]{3,2,1,0:T(8,128)(2,1)}, bf16[2,1,192,256]{3,2,1,0:T(8,128)(2,1)S(1)}, u32[]{:S(2)}, u32[]{:S(2)}) %collective-permute-start.20) | collective-permute-done | bytes 196640 | tf_op jit(solution)/shard_map/ppermute | solution.py:29
  120.4 12.4 %shard_map.284 = (bf16[2,256,768]{2,1,0:T(8,128)(2,1)}, bf16[2,256,768]{2,1,0:T(8,128)(2,1)}, f32[576,768]{1,0:T(8,128)}, f32[8,576]{1,0:T(8,128)}) custom-call(s32[20]{0:T(128)} %concatenate.60.places, bf16[1,192,256]{2,1,0:T(8,128)(2,1)} %get-tuple-element.202.g0, bf16[1,192,256]{2,1,0:T(8,128)(2,1)} %copy-done.42, bf16[2,1,192,256]{3,2,1,0:T(8,128)(2,1)} %copy-done.29, ...), custom_call_target="tpu_custom_call" | custom-call | flops 100000000 | bytes 1048576 | tf_op jit(solution)/shard_map/pallas_call | solution.py:230
  137.6 12.7 %shard_map.285 = (bf16[2,256,768]{2,1,0:T(8,128)(2,1)}, bf16[2,256,768]{2,1,0:T(8,128)(2,1)}, f32[576,768]{1,0:T(8,128)}, f32[8,576]{1,0:T(8,128)}) custom-call(s32[20]{0:T(128)} %concatenate.60.places, bf16[2,192,256]{2,1,0:T(8,128)(2,1)} %get-tuple-element.231.g0, bf16[2,192,256]{2,1,0:T(8,128)(2,1)} %copy-done.25, bf16[2,2,192,256]{3,2,1,0:T(8,128)(2,1)} %copy-done.6, ...), custom_call_target="tpu_custom_call" | custom-call | flops 100000000 | bytes 1048576 | tf_op jit(solution)/shard_map/pallas_call | solution.py:230
  164.0 13.1 %shard_map.286 = (bf16[2,256,768]{2,1,0:T(8,128)(2,1)}, bf16[2,256,768]{2,1,0:T(8,128)(2,1)}, bf16[8,112,384]{2,1,0:T(8,128)(2,1)}, bf16[8,112,384]{2,1,0:T(8,128)(2,1)}) custom-call(s32[20]{0:T(128)} %concatenate.60.places, bf16[2,192,256]{2,1,0:T(8,128)(2,1)} %get-tuple-element.231.g0, bf16[2,192,256]{2,1,0:T(8,128)(2,1)} %copy-done.25, ...), custom_call_target="tpu_custom_call" | custom-call | flops 100000000 | bytes 1048576 | tf_op jit(solution)/shard_map/pallas_call | solution.py:230
  191.3 8.9 %collective-permute-done.40 = bf16[2,192,384]{2,1,0:T(8,128)(2,1)S(1)} collective-permute-done((bf16[2,192,384]{2,1,0:T(8,128)(2,1)S(1)}, bf16[2,192,384]{2,1,0:T(8,128)(2,1)S(1)}, u32[]{:S(2)}, u32[]{:S(2)}) %collective-permute-start.40) | collective-permute-done | bytes 294944 | tf_op jit(solution)/shard_map/ppermute | solution.py:29
  223.4 9.9 %collective-permute-done.47 = bf16[1,96,768]{2,1,0:T(8,128)(2,1)S(1)} collective-permute-done((bf16[1,96,768]{2,1,0:T(8,128)(2,1)S(1)}, bf16[1,96,768]{2,1,0:T(8,128)(2,1)S(1)}, u32[]{:S(2)}, u32[]{:S(2)}) %collective-permute-start.47) | collective-permute-done | bytes 147488 | tf_op jit(solution)/shard_map/ppermute | solution.py:29
  244.3 7.0 %collective-permute-done.50 = bf16[1,112,768]{2,1,0:T(8,128)(2,1)S(1)} collective-permute-done((bf16[1,112,768]{2,1,0:T(8,128)(2,1)S(1)}, bf16[1,112,768]{2,1,0:T(8,128)(2,1)S(1)}, u32[]{:S(2)}, u32[]{:S(2)}) %collective-permute-start.50) | collective-permute-done | bytes 172064 | tf_op jit(solution)/shard_map/ppermute | solution.py:29
  253.6 7.9 %collective-permute-done.55 = bf16[2,192,384]{2,1,0:T(8,128)(2,1)S(1)} collective-permute-done((bf16[2,192,384]{2,1,0:T(8,128)(2,1)S(1)}, bf16[2,192,384]{2,1,0:T(8,128)(2,1)S(1)}, u32[]{:S(2)}, u32[]{:S(2)}) %collective-permute-start.55) | collective-permute-done | bytes 294944 | tf_op jit(solution)/shard_map/ppermute | solution.py:29
  261.5 6.1 %collective-permute-done.53 = bf16[2,112,768]{2,1,0:T(8,128)(2,1)S(1)} collective-permute-done((bf16[2,112,768]{2,1,0:T(8,128)(2,1)S(1)}, bf16[2,112,768]{2,1,0:T(8,128)(2,1)S(1)}, u32[]{:S(2)}, u32[]{:S(2)}) %collective-permute-start.53) | collective-permute-done | bytes 344096 | tf_op jit(solution)/shard_map/ppermute | solution.py:29
  270.1 13.6 %collective-permute-done.59 = bf16[4,192,384]{2,1,0:T(8,128)(2,1)S(1)} collective-permute-done((bf16[4,192,384]{2,1,0:T(8,128)(2,1)S(1)}, bf16[4,192,384]{2,1,0:T(8,128)(2,1)S(1)}, u32[]{:S(2)}, u32[]{:S(2)}) %collective-permute-start.59) | collective-permute-done | bytes 589856 | tf_op jit(solution)/shard_map/ppermute | solution.py:29
  283.8 3.3 collective-permute-done.56
  291.3 5.4 %shard_map.287.refs_2_ = f32[3072,768]{1,0:T(8,128)} custom-call(s32[20]{0:T(128)} %concatenate.60.places, bf16[2,2,2,96,768]{4,3,2,1,0:T(8,128)(2,1)} %bitcast.101, bf16[2,2,2,96,768]{4,3,2,1,0:T(8,128)(2,1)} %bitcast.107), custom_call_target="tpu_custom_call" | custom-call | flops 1000 | bytes 1048576 | tf_op jit(solution)/shard_map/pallas_call | solution.py:526
  296.7 7.7 %collective-permute-done.63 = bf16[4,96,768]{2,1,0:T(8,128)(2,1)} collective-permute-done((bf16[4,96,768]{2,1,0:T(8,128)(2,1)}, bf16[4,96,768]{2,1,0:T(8,128)(2,1)}, u32[]{:S(2)}, u32[]{:S(2)}) %collective-permute-start.63) | collective-permute-done | bytes 589856 | tf_op jit(solution)/shard_map/ppermute | solution.py:29
  309.8 5.4 %shard_map.288.refs_1_ = f32[768,3072]{1,0:T(8,128)} custom-call(s32[20]{0:T(128)} %concatenate.60.places, bf16[2,2,2,192,384]{4,3,2,1,0:T(8,128)(2,1)} %bitcast.100, bf16[2,2,2,192,384]{4,3,2,1,0:T(8,128)(2,1)} %bitcast.47.refs_1_), custom_call_target="tpu_custom_call" | custom-call | flops 1000 | bytes 1048576 | tf_op jit(solution)/shard_map/pallas_call | solution.py:526
  315.2 3.6 %collective-permute-done.65 = bf16[2,192,384]{2,1,0:T(8,128)(2,1)S(1)} collective-permute-done((bf16[2,192,384]{2,1,0:T(8,128)(2,1)}, bf16[2,192,384]{2,1,0:T(8,128)(2,1)S(1)}, u32[]{:S(2)}, u32[]{:S(2)}) %collective-permute-start.65) | collective-permute-done | bytes 294944 | tf_op jit(solution)/shard_map/ppermute | solution.py:29
  325.0 5.4 %shard_map.289 = f32[3072,768]{1,0:T(8,128)} custom-call(s32[20]{0:T(128)} %concatenate.60.places, bf16[2,2,2,96,768]{4,3,2,1,0:T(8,128)(2,1)} %bitcast.102, bf16[2,2,2,96,768]{4,3,2,1,0:T(8,128)(2,1)} %bitcast.49.refs_1_, f32[3072,768]{1,0:T(8,128)} %shard_map.287.refs_2_), custom_call_target="tpu_custom_call", output_to_operand_aliasing={{}: (3, {})} | custom-call | flops 1000 | bytes 1048576 | tf_op jit(solution)/shard_map/pallas_call | solution.py:526
  338.0 3.2 shard_map.290.refs_1_
  342.4 9.1 %shard_map.291 = (f32[768,2304]{1,0:T(8,128)}, f32[768,768]{1,0:T(8,128)}, f32[16,768]{1,0:T(8,128)}, f32[8,768]{1,0:T(8,128)}) custom-call(s32[20]{0:T(128)} %concatenate.60.places, bf16[8,112,768]{2,1,0:T(8,128)(2,1)} %bitcast.99, bf16[8,112,768]{2,1,0:T(8,128)(2,1)} %copy-done.14, bf16[8,112,768]{2,1,0:T(8,128)(2,1)} %copy-done.4, ...), custom_call_target="tpu_custom_call" | custom-call | flops 1000 | bytes 1048576 | tf_op jit(solution)/shard_map/pallas_call | solution.py:526
  356.5 3.2 shard_map.292
  (366 shorter events, 144.1 us)
Async XLA Ops:
  107.8 25.1 %collective-permute-start.25 = (bf16[2,384,768]{2,1,0:T(8,128)(2,1)}, bf16[2,384,768]{2,1,0:T(8,128)(2,1)}, u32[]{:S(2)}, u32[]{:S(2)}) collective-permute-start(bf16[2,384,768]{2,1,0:T(8,128)(2,1)} %get-tuple-element.225), channel_id=1, source_target_pairs={{0,1},{1,0},{2,3},{3,2},{4,5},{5,4},{6,7},{7,6},{8,9},{9,8},{10,11... | collective-permute-start | bytes 3538952 | tf_op jit(solution)/shard_map/ppermute | solution.py:29
  108.3 24.5 %collective-permute-start.24 = (bf16[2,2,192,256]{3,2,1,0:T(8,128)(2,1)}, bf16[2,2,192,256]{3,2,1,0:T(8,128)(2,1)S(1)}, u32[]{:S(2)}, u32[]{:S(2)}) collective-permute-start(bf16[2,2,192,256]{3,2,1,0:T(8,128)(2,1)} %get-tuple-element.222), channel_id=1, source_target_pairs={{0,2},{1,3},{2,0},{3,1},{4,6},{5,7},{6,4},{7,5},{8,10},{9,11},{10,... | collective-permute-start | bytes 1179656 | tf_op jit(solution)/shard_map/ppermute | solution.py:29
  115.3 38.2 %collective-permute-start.26 = (bf16[2,384,768]{2,1,0:T(8,128)(2,1)S(1)}, bf16[2,384,768]{2,1,0:T(8,128)(2,1)S(1)}, u32[]{:S(2)}, u32[]{:S(2)}) collective-permute-start(bf16[2,384,768]{2,1,0:T(8,128)(2,1)S(1)} %add_convert_fusion.1), channel_id=1, source_target_pairs={{0,4},{4,0},{8,12},{12,8},{16,20},{20,16},{24,28},{28,24},{1,5},{5... | collective-permute-start | bytes 3538952 | tf_op jit(solution)/shard_map/ppermute | solution.py:29
  116.8 36.6 %collective-permute-start.27 = (bf16[2,768,384]{2,1,0:T(8,128)(2,1)}, bf16[2,768,384]{2,1,0:T(8,128)(2,1)}, u32[]{:S(2)}, u32[]{:S(2)}) collective-permute-start(bf16[2,768,384]{2,1,0:T(8,128)(2,1)} %add_convert_fusion), channel_id=1, source_target_pairs={{0,8},{4,12},{8,0},{12,4},{16,24},{20,28},{24,16},{28,20},{1,9},{5... | collective-permute-start | bytes 3538952 | tf_op jit(solution)/shard_map/ppermute | solution.py:29
  132.9 17.5 %collective-permute-start.31 = (bf16[2,256,768]{2,1,0:T(8,128)(2,1)}, bf16[2,256,768]{2,1,0:T(8,128)(2,1)}, u32[]{:S(2)}, u32[]{:S(2)}) collective-permute-start(bf16[2,256,768]{2,1,0:T(8,128)(2,1)} %get-tuple-element.245), channel_id=1, source_target_pairs={{0,1},{1,0},{2,3},{3,2},{4,5},{5,4},{6,7},{7,6},{8,9},{9,8},{10,11... | collective-permute-start | bytes 2359304 | tf_op jit(solution)/shard_map/ppermute | solution.py:29
  133.5 19.9 %collective-permute-start.28 = (bf16[2,8,96,192]{3,2,1,0:T(8,128)(2,1)}, bf16[2,8,96,192]{3,2,1,0:T(8,128)(2,1)}, u32[]{:S(2)}, u32[]{:S(2)}) collective-permute-start(bf16[2,8,96,192]{3,2,1,0:T(8,128)(2,1)} %get-tuple-element.230), channel_id=1, source_target_pairs={{0,2},{1,3},{2,0},{3,1},{4,6},{5,7},{6,4},{7,5},{8,10},{9,11},{10,... | collective-permute-start | bytes 1769480 | tf_op jit(solution)/shard_map/ppermute | solution.py:29
  155.0 22.1 %collective-permute-start.35 = (bf16[2,256,768]{2,1,0:T(8,128)(2,1)}, bf16[2,256,768]{2,1,0:T(8,128)(2,1)S(1)}, u32[]{:S(2)}, u32[]{:S(2)}) collective-permute-start(bf16[2,256,768]{2,1,0:T(8,128)(2,1)} %get-tuple-element.257), channel_id=1, source_target_pairs={{0,1},{1,0},{2,3},{3,2},{4,5},{5,4},{6,7},{7,6},{8,9},{9,8},{10,11... | collective-permute-start | bytes 2359304 | tf_op jit(solution)/shard_map/ppermute | solution.py:29
  161.9 16.2 %collective-permute-start.33 = (bf16[384,768]{1,0:T(8,128)(2,1)}, bf16[384,768]{1,0:T(8,128)(2,1)}, u32[]{:S(2)}, u32[]{:S(2)}) collective-permute-start(bf16[384,768]{1,0:T(8,128)(2,1)} %fusion.4), channel_id=1, source_target_pairs={{0,8},{4,12},{8,0},{12,4},{16,24},{20,28},{24,16},{28,20},{1,9},{5... | collective-permute-start | bytes 1769480 | tf_op jit(solution)/shard_map/ppermute | solution.py:29
  162.3 15.7 %collective-permute-start.34 = (bf16[768,384]{1,0:T(8,128)(2,1)}, bf16[768,384]{1,0:T(8,128)(2,1)}, u32[]{:S(2)}, u32[]{:S(2)}) collective-permute-start(bf16[768,384]{1,0:T(8,128)(2,1)} %fusion.5), channel_id=1, source_target_pairs={{0,4},{4,0},{8,12},{12,8},{16,20},{20,16},{24,28},{28,24},{1,5},{5... | collective-permute-start | bytes 1769480 | tf_op jit(solution)/shard_map/ppermute | solution.py:29
  184.6 15.6 %collective-permute-start.40 = (bf16[2,192,384]{2,1,0:T(8,128)(2,1)S(1)}, bf16[2,192,384]{2,1,0:T(8,128)(2,1)S(1)}, u32[]{:S(2)}, u32[]{:S(2)}) collective-permute-start(bf16[2,192,384]{2,1,0:T(8,128)(2,1)S(1)} %bitcast.112), channel_id=1, source_target_pairs={{0,16},{4,20},{8,24},{12,28},{16,0},{20,4},{24,8},{28,12},{1,17},{... | collective-permute-start | bytes 884744 | tf_op jit(solution)/shard_map/ppermute | solution.py:29
  188.2 17.3 %collective-permute-start.41 = (bf16[2,256,768]{2,1,0:T(8,128)(2,1)S(1)}, bf16[2,256,768]{2,1,0:T(8,128)(2,1)S(1)}, u32[]{:S(2)}, u32[]{:S(2)}) collective-permute-start(bf16[2,256,768]{2,1,0:T(8,128)(2,1)S(1)} %copy-done.53), channel_id=1, source_target_pairs={{0,1},{1,0},{2,3},{3,2},{4,5},{5,4},{6,7},{7,6},{8,9},{9,8},{10,11... | collective-permute-start | bytes 2359304 | tf_op jit(solution)/shard_map/ppermute | solution.py:29
  188.2 15.7 %collective-permute-start.38 = (bf16[2,2,112,384]{3,2,1,0:T(8,128)(2,1)S(1)}, bf16[2,2,112,384]{3,2,1,0:T(8,128)(2,1)S(1)}, u32[]{:S(2)}, u32[]{:S(2)}) collective-permute-start(bf16[2,2,112,384]{3,2,1,0:T(8,128)(2,1)S(1)} %get-tuple-element.277), channel_id=1, source_target_pairs={{0,8},{4,12},{8,0},{12,4},{16,24},{20,28},{24,16},{28,20},{1,9},{5... | collective-permute-start | bytes 1032200 | tf_op jit(solution)/shard_map/ppermute | solution.py:29
  212.0 24.2 %collective-permute-start.48 = (bf16[256,768]{1,0:T(8,128)(2,1)}, bf16[256,768]{1,0:T(8,128)(2,1)S(1)}, u32[]{:S(2)}, u32[]{:S(2)}) collective-permute-start(bf16[256,768]{1,0:T(8,128)(2,1)} %get-tuple-element.298), channel_id=1, source_target_pairs={{0,2},{1,3},{2,0},{3,1},{4,6},{5,7},{6,4},{7,5},{8,10},{9,11},{10,... | collective-permute-start | bytes 1179656 | tf_op jit(solution)/shard_map/ppermute | solution.py:29
  213.5 22.7 %collective-permute-start.49 = (bf16[256,768]{1,0:T(8,128)(2,1)}, bf16[256,768]{1,0:T(8,128)(2,1)S(1)}, u32[]{:S(2)}, u32[]{:S(2)}) collective-permute-start(bf16[256,768]{1,0:T(8,128)(2,1)} %get-tuple-element.299), channel_id=1, source_target_pairs={{0,2},{1,3},{2,0},{3,1},{4,6},{5,7},{6,4},{7,5},{8,10},{9,11},{10,... | collective-permute-start | bytes 1179656 | tf_op jit(solution)/shard_map/ppermute | solution.py:29
  251.4 16.3 %collective-permute-start.54 = (bf16[4,96,768]{2,1,0:T(8,128)(2,1)S(1)}, bf16[4,96,768]{2,1,0:T(8,128)(2,1)S(1)}, u32[]{:S(2)}, u32[]{:S(2)}) collective-permute-start(bf16[4,96,768]{2,1,0:T(8,128)(2,1)S(1)} %pad_maximum_fusion.5), channel_id=1, source_target_pairs={{0,2},{1,3},{2,0},{3,1},{4,6},{5,7},{6,4},{7,5},{8,10},{9,11},{10,... | collective-permute-start | bytes 1769480 | tf_op jit(solution)/shard_map/ppermute | solution.py:29
  251.6 16.1 %collective-permute-start.53 = (bf16[2,112,768]{2,1,0:T(8,128)(2,1)S(1)}, bf16[2,112,768]{2,1,0:T(8,128)(2,1)S(1)}, u32[]{:S(2)}, u32[]{:S(2)}) collective-permute-start(bf16[2,112,768]{2,1,0:T(8,128)(2,1)S(1)} %pad_maximum_fusion.7), channel_id=1, source_target_pairs={{0,4},{4,0},{8,12},{12,8},{16,20},{20,16},{24,28},{28,24},{1,5},{5... | collective-permute-start | bytes 1032200 | tf_op jit(solution)/shard_map/ppermute | solution.py:29
  267.9 19.5 %collective-permute-start.57 = (bf16[8,96,768]{2,1,0:T(8,128)(2,1)S(1)}, bf16[8,96,768]{2,1,0:T(8,128)(2,1)S(1)}, u32[]{:S(2)}, u32[]{:S(2)}) collective-permute-start(bf16[8,96,768]{2,1,0:T(8,128)(2,1)S(1)} %pad_maximum_fusion.1), channel_id=1, source_target_pairs={{0,1},{1,0},{2,3},{3,2},{4,5},{5,4},{6,7},{7,6},{8,9},{9,8},{10,11... | collective-permute-start | bytes 3538952 | tf_op jit(solution)/shard_map/ppermute | solution.py:29
  267.9 15.7 %collective-permute-start.59 = (bf16[4,192,384]{2,1,0:T(8,128)(2,1)S(1)}, bf16[4,192,384]{2,1,0:T(8,128)(2,1)S(1)}, u32[]{:S(2)}, u32[]{:S(2)}) collective-permute-start(bf16[4,192,384]{2,1,0:T(8,128)(2,1)S(1)} %pad_maximum_fusion.6), channel_id=1, source_target_pairs={{0,2},{1,3},{2,0},{3,1},{4,6},{5,7},{6,4},{7,5},{8,10},{9,11},{10,... | collective-permute-start | bytes 1769480 | tf_op jit(solution)/shard_map/ppermute | solution.py:29
  269.7 17.5 %collective-permute-start.56 = (bf16[4,112,768]{2,1,0:T(8,128)(2,1)S(1)}, bf16[4,112,768]{2,1,0:T(8,128)(2,1)S(1)}, u32[]{:S(2)}, u32[]{:S(2)}) collective-permute-start(bf16[4,112,768]{2,1,0:T(8,128)(2,1)S(1)} %pad_maximum_fusion.4), channel_id=1, source_target_pairs={{0,8},{4,12},{8,0},{12,4},{16,24},{20,28},{24,16},{28,20},{1,9},{5... | collective-permute-start | bytes 2064392 | tf_op jit(solution)/shard_map/ppermute | solution.py:29
  269.7 17.6 %collective-permute-start.58 = (bf16[4,96,768]{2,1,0:T(8,128)(2,1)S(1)}, bf16[4,96,768]{2,1,0:T(8,128)(2,1)S(1)}, u32[]{:S(2)}, u32[]{:S(2)}) collective-permute-start(bf16[4,96,768]{2,1,0:T(8,128)(2,1)S(1)} %slice.273), channel_id=1, source_target_pairs={{0,4},{4,0},{8,12},{12,8},{16,20},{20,16},{24,28},{28,24},{1,5},{5... | collective-permute-start | bytes 1769480 | tf_op jit(solution)/shard_map/ppermute | solution.py:29
  287.4 20.1 %collective-permute-start.61 = (bf16[8,192,384]{2,1,0:T(8,128)(2,1)S(1)}, bf16[8,192,384]{2,1,0:T(8,128)(2,1)}, u32[]{:S(2)}, u32[]{:S(2)}) collective-permute-start(bf16[8,192,384]{2,1,0:T(8,128)(2,1)S(1)} %pad_maximum_fusion.2), channel_id=1, source_target_pairs={{0,1},{1,0},{2,3},{3,2},{4,5},{5,4},{6,7},{7,6},{8,9},{9,8},{10,11... | collective-permute-start | bytes 3538952 | tf_op jit(solution)/shard_map/ppermute | solution.py:29
  288.5 15.9 %collective-permute-start.63 = (bf16[4,96,768]{2,1,0:T(8,128)(2,1)}, bf16[4,96,768]{2,1,0:T(8,128)(2,1)}, u32[]{:S(2)}, u32[]{:S(2)}) collective-permute-start(bf16[4,96,768]{2,1,0:T(8,128)(2,1)} %slice.276), channel_id=1, source_target_pairs={{0,4},{4,0},{8,12},{12,8},{16,20},{20,16},{24,28},{28,24},{1,5},{5... | collective-permute-start | bytes 1769480 | tf_op jit(solution)/shard_map/ppermute | solution.py:29
  289.7 17.7 %collective-permute-start.60 = (bf16[4,112,768]{2,1,0:T(8,128)(2,1)}, bf16[4,112,768]{2,1,0:T(8,128)(2,1)}, u32[]{:S(2)}, u32[]{:S(2)}) collective-permute-start(bf16[4,112,768]{2,1,0:T(8,128)(2,1)} %slice.274), channel_id=1, source_target_pairs={{0,2},{1,3},{2,0},{3,1},{4,6},{5,7},{6,4},{7,5},{8,10},{9,11},{10,... | collective-permute-start | bytes 2064392 | tf_op jit(solution)/shard_map/ppermute | solution.py:29
  337.0 19.5 %collective-permute-start.71 = (bf16[8,192,384]{2,1,0:T(8,128)(2,1)S(1)}, bf16[8,192,384]{2,1,0:T(8,128)(2,1)}, u32[]{:S(2)}, u32[]{:S(2)}) collective-permute-start(bf16[8,192,384]{2,1,0:T(8,128)(2,1)S(1)} %constant_dynamic-update-slice_fusion.3), channel_id=1, source_target_pairs={{0,1},{1,0},{2,3},{3,2},{4,5},{5,4},{6,7},{7,6},{8,9},{9,8},{10,11... | collective-permute-start | bytes 3538952 | tf_op jit(solution)/shard_map/ppermute | solution.py:29
  (117 other events, 869.5 us)

commit v7 on v5

--- a/solution.py
+++ b/solution.py
@@ -607,140 +607,158 @@
     )
 
 
-def place_tile(count, places, *refs):
-    out = refs[-1]
-    for k in range(count):
-
-        @pl.when(pl.program_id(0) >> 3 == k)
-        def copy():
-            out[...] = refs[k][0].astype(jnp.float32)
-
-
-def gather_down(places, pieces, x, begun, shape):
+def place_tiles(count, split, x, places, *refs):
+    sources, out = refs[:count], refs[-4]
+    held, main, sems = refs[-3:]
+    inner = places[8]
+    _, rows, cols = sources[0].shape
+    bring = [
+        pltpu.make_async_copy(source, held.at[k], sems.at[k]) for k, source in enumerate(sources)
+    ]
+    for copy in bring:
+        copy.start()
+    sent = []
+    for k, copy in enumerate(bring):
+        copy.wait()
+        for n in range(2 if split else 8):
+            slot = sems.at[count + len(sent)]
+            if split:
+                block = places[k * 4 + x * 2 + n]
+                for q in range(4):
+                    first = pl.multiple_of((q ^ inner) * rows, rows)
+                    main[2 * k + n, pl.ds(first, rows), :] = held[
+                        k, n * 4 + (q & 1) * 2 + (q >> 1)
+                    ].astype(jnp.float32)
+                target = out.at[:, pl.ds(pl.multiple_of(block * cols, cols), cols)]
+                sent.append(pltpu.make_async_copy(main.at[2 * k + n], target, slot))
+            else:
+                l, y, h = n >> 2, (n >> 1) & 1, n & 1
+                block = places[k * 4 + y * 2 + l] * 4 + ((h * 2 + x) ^ inner)
+                main[8 * k + n] = held[k, n].astype(jnp.float32)
+                target = out.at[pl.ds(pl.multiple_of(block * rows, rows), rows)]
+                sent.append(pltpu.make_async_copy(main.at[8 * k + n], target, slot))
+            sent[-1].start()
+    for copy in sent:
+        copy.wait()
+
+
+def gather_tiles(places, pieces, late, begun, shape, split):
     _, rows, cols = pieces[0].shape
     count = len(pieces)
-
-    def source(k):
-        return pl.BlockSpec(
-            (1, rows, cols), lambda p, places: (jnp.clip(p - 8 * k, 0, 7), 0, 0)
+    away = pl.BlockSpec(memory_space=pl.ANY)
+    main = (2 * count, 4 * rows, cols) if split else (8 * count, rows, cols)
+    return pl.pallas_call(
+        functools.partial(place_tiles, count, split, late),
+        out_shape=jax.ShapeDtypeStruct(shape, jnp.float32),
+        in_specs=[pl.BlockSpec(memory_space=pltpu.SMEM)] + [away] * (count + len(begun)),
+        out_specs=away,
+        scratch_shapes=[
+            pltpu.VMEM((count, 8, rows, cols), jnp.bfloat16),
+            pltpu.VMEM(main, jnp.float32),
+            pltpu.SemaphoreType.DMA((count + main[0],)),
+        ],
+        input_output_aliases={count + 1: 0} if begun else {},
+        compiler_params=pltpu.CompilerParams(vmem_limit_bytes=VMEM_LIMIT),
+    )(places, *pieces, *begun)
+
+
+def place_heads(seq_parts, places, *refs):
+    sources, refs = refs[: 2 * seq_parts], refs[2 * seq_parts :]
+    out, out_w, vector_rows, head_rows = refs[:4]
+    pieces = refs[4 : seq_parts + 4]
+    main, side, sems = refs[seq_parts + 4 :]
+    mine, inner = places[9], places[10]
+    blocks, rows, _ = main.shape
+    features = side.shape[2]
+    wide = features // seq_parts
+    f32 = jnp.float32
+    half = blocks // 2
+    bring = [
+        pltpu.make_async_copy(
+            source, pieces[i >> 1].at[pl.ds((i & 1) * half, half)], sems.at[2 * blocks + i]
         )
-
-    def index(p, places):
-        core, l, y, h = p >> 3, (p >> 2) & 1, (p >> 1) & 1, p & 1
-        return (places[core * 4 + y * 2 + l] * 4 + ((h * 2 + x) ^ places[8]), 0)
-
-    return step_call(
-        functools.partial(place_tile, count),
-        places,
-        8 * count,
-        pieces + begun,
-        [source(k) for k in range(count)] + [pl.BlockSpec(memory_space=pl.ANY)] * len(begun),
-        jax.ShapeDtypeStruct(shape, jnp.float32),
-        pl.BlockSpec((rows, cols), index),
-        [],
-        1000,
-        {count + 1: 0} if begun else {},
-    )
-
-
-def place_rows(count, places, *refs):
-    out = refs[-1]
-    tile = refs[0].shape[1]
-    for k in range(count):
-
-        @pl.when(pl.program_id(0) >> 1 == k)
-        def copy():
-            for q in range(4):
-                h, x = q >> 1, q & 1
-                out[pl.ds(pl.multiple_of((q ^ places[8]) * tile, tile), tile), :] = refs[k][
-                    x * 2 + h
-                ].astype(jnp.float32)
-
-
-def gather_up(places, pieces, y, begun, shape):
-    _, rows, cols = pieces[0].shape
-    count = len(pieces)
-
-    def source(k):
-        return pl.BlockSpec(
-            (4, rows, cols), lambda p, places: (jnp.clip(p - 2 * k, 0, 1), 0, 0)
-        )
-
-    return step_call(
-        functools.partial(place_rows, count),
-        places,
-        2 * count,
-        pieces + begun,
-        [source(k) for k in range(count)] + [pl.BlockSpec(memory_space=pl.ANY)] * len(begun),
-        jax.ShapeDtypeStruct(shape, jnp.float32),
-        pl.BlockSpec(
-            (4 * rows, cols), lambda p, places: (0, places[(p >> 1) * 4 + y * 2 + (p & 1)])
-        ),
-        [],
-        1000,
-        {count + 1: 0} if begun else {},
-    )
-
-
-def place_heads(places, *refs):
-    pieces = refs[:-4]
-    out, out_w, vector_rows, head_rows = refs[-4:]
-    mine, inner = places[9], places[10]
-    seq_parts = len(pieces)
-    step = pl.program_id(0)
-    wide = out_w.shape[0] // seq_parts
-    rows, features = out.shape[0], out_w.shape[1]
-    f32 = jnp.float32
+        for i, source in enumerate(sources)
+    ]
+    for copy in bring:
+        copy.start()
+    for copy in bring:
+        copy.wait()
+
+    def leave(p, source, target, slot):
+        first = pl.multiple_of(p * rows, rows)
+        return pltpu.make_async_copy(source.at[p], target.at[pl.ds(first, rows)], sems.at[slot + p])
+
+    def one_block(p, carry):
+        for m in range(seq_parts):
+
+            @pl.when(mine == m)
+            def copy():
+                parts = [pieces[j ^ m][p ^ inner, :rows, : 3 * wide] for j in range(seq_parts)]
+                for section in range(3):
+                    columns = slice(section * wide, (section + 1) * wide)
+                    joined = jnp.concatenate([part[:, columns] for part in parts], axis=1)
+                    main[p, :, section * features : (section + 1) * features] = joined.astype(f32)
+
+        leave(p, main, out, 0).start()
+        for r, piece in enumerate(pieces):
+
+            @pl.when(((r ^ mine) == p >> 1))
+            def copy_side():
+                first = (p & 1) * 4
+                joined = jnp.concatenate(
+                    [piece[(first + q) ^ inner, :rows, 3 * wide :] for q in range(4)], axis=1
+                )
+                side[p] = joined.astype(f32)
+
+        leave(p, side, out_w, blocks).start()
+        return carry
+
+    lax.fori_loop(0, blocks, one_block, 0)
     for m in range(seq_parts):
 
         @pl.when(mine == m)
-        def copy():
-            blocks = [pieces[j ^ m][step ^ inner, :rows, : 3 * wide] for j in range(seq_parts)]
-            for section in range(3):
-                columns = slice(section * wide, (section + 1) * wide)
-                joined = jnp.concatenate([block[:, columns] for block in blocks], axis=1)
-                out[:, section * features : (section + 1) * features] = joined.astype(f32)
-
-        @pl.when((mine == m) & (step == 0))
         def copy_vectors():
             held = [pieces[j ^ m][inner, rows:, :].astype(f32) for j in range(seq_parts)]
             total = held[0]
             for other in held[1:]:
                 total = total + other
             vector_rows[...] = total
+            head_rows[...] = jnp.zeros_like(head_rows)
             for j in range(seq_parts):
                 head_rows[j : j + 1, :] = held[j][10:11, :]
 
-    for r, piece in enumerate(pieces):
-
-        @pl.when(step == r)
-        def copy_out():
-            for i in range(2):
-                joined = jnp.concatenate(
-                    [piece[(4 * i + q) ^ inner, :rows, 3 * wide :] for q in range(4)], axis=1
-                )
-                first = pl.multiple_of((r ^ mine) * wide + i * rows, rows)
-                out_w[pl.ds(first, rows), :] = joined.astype(f32)
-
-
-def gather_heads(places, pieces, shape):
+    for p in range(blocks):
+        leave(p, main, out, 0).wait()
+        leave(p, side, out_w, blocks).wait()
+
+
+def gather_heads(places, halves, shape):
     out, f32 = jax.ShapeDtypeStruct, jnp.float32
     features = shape[0]
     rows = features // 8
-    square = (features, features)
-    extra = (pieces[0].shape[1] - rows, features)
-    return step_call(
-        place_heads,
-        places,
-        8,
-        pieces,
-        [whole_spec(p.shape) for p in pieces],
-        [out(shape, f32), out(square, f32), out(extra, f32), out((8, features), f32)],
-        [pl.BlockSpec((rows, shape[1]), lambda p, places: (p, 0))]
-        + [whole_spec(square), whole_spec(extra), whole_spec((8, features))],
-        [],
-        1000,
-    )
+    extra = (halves[0].shape[1] - rows, features)
+    count = len(halves) // 2
+    piece = (8, *halves[0].shape[1:])
+    away = pl.BlockSpec(memory_space=pl.ANY)
+    here = pl.BlockSpec(memory_space=pltpu.VMEM)
+    return pl.pallas_call(
+        functools.partial(place_heads, count),
+        out_shape=[
+            out(shape, f32),
+            out((features, features), f32),
+            out(extra, f32),
+            out((8, features), f32),
+        ],
+        in_specs=[pl.BlockSpec(memory_space=pltpu.SMEM)] + [away] * len(halves),
+        out_specs=[away, away, here, here],
+        scratch_shapes=[pltpu.VMEM(piece, halves[0].dtype)] * count
+        + [
+            pltpu.VMEM((8, rows, shape[1]), f32),
+            pltpu.VMEM((8, rows, features), f32),
+            pltpu.SemaphoreType.DMA((16 + len(halves),)),
+        ],
+        compiler_params=pltpu.CompilerParams(vmem_limit_bytes=VMEM_LIMIT),
+    )(places, *halves)
 
 
 def per_device(
@@ -902,9 +920,9 @@
     down_own = down_own.reshape(2, 2, hidden // 32, features)
     up_own = sum_low(keep_up[0], came_up0[0], up_l[0], up_y)
     up_own = up_own.reshape(2, 2, features // 4, hidden // 8)
-    keeps, sends = [down_own[:, 0], up_own[0]], [down_own[:, 1], up_own[1]]
+    keeps, sends = [down_own[:, 0], up_own[:, 0]], [down_own[:, 1], up_own[:, 1]]
     (keeps, sends, total) = lax.optimization_barrier((keeps, sends, total))
-    got = [exchange_bit(v, bit) for v, bit in zip(sends, "xh")]
+    got = [exchange_bit(v, "x") for v in sends]
     far_came = [exchange_bit(far[0], "x")]
     for s in range(1, seq_count - 1):
         cross(s)
@@ -913,40 +931,34 @@
     (keeps, got, far, far_came, half_a, half_b, parts[-1]) = lax.optimization_barrier(
         (keeps, got, far, far_came, half_a, half_b, parts[-1])
     )
-    down_own, up_own = [k + g for k, g in zip(keeps, got)]
+    down, up = [k + g for k, g in zip(keeps, got)]
     half_b = half_b.reshape(2, 2, 2, *half_b.shape[1:])
-    keeps = [half_a[:4], half_b[:, 0], down_own[:1], up_own[:1]]
-    sends = [half_a[4:], half_b[:, 1], down_own[1:], up_own[1:]]
-    (keeps, sends) = lax.optimization_barrier((keeps, sends))
-    got = [exchange_bit(v, bit) for v, bit in zip(sends, "ylhx")]
+    keeps = [half_a[:4], half_b[:, 0], down]
+    sends = [half_a[4:], half_b[:, 1], down]
+    (keeps, sends, up) = lax.optimization_barrier((keeps, sends, up))
+    got = [exchange_bit(v, bit) for v, bit in zip(sends, "ylh")]
     far_came += [exchange_bit(v, "x") for v in far[1:]]
-    half_a, half_b, down, up = [k + g for k, g in zip(keeps, got)]
+    half_a, half_b, down = [k + g for k, g in zip(keeps, (*got[:2], got[2][::-1]))]
     far = []
     cross(seq_count - 1)
 
-    keeps, sends = [half_a[:2], half_b[0]], [half_a[2:], half_b[1]]
-    down, up = add_extra(down), add_extra(up)
-    (keeps, sends, down, up, far, near) = lax.optimization_barrier(
-        (keeps, sends, down, up, far, near)
-    )
-    got = [exchange_bit(v, bit) for v, bit in zip(sends, "ly")]
-    came = exchange_bit(down, "h")
+    keeps = [half_a[:2], half_b[0], up]
+    sends = [half_a[2:], half_b[1], up]
+    down = add_extra(down)
+    (keeps, sends, down, far, near) = lax.optimization_barrier((keeps, sends, down, far, near))
+    got = [exchange_bit(v, bit) for v, bit in zip(sends, "lyh")]
+    down_came = exchange_bit(down, "y")
     far_came += [exchange_bit(v, "x") for v in far]
-    down = jnp.concatenate([down, came])
-    both = jnp.concatenate([k + g for k, g in zip(keeps, got)], axis=2)
-
-    keep, send = both[:1], both[1:]
-    (keep, send, down, up) = lax.optimization_barrier((keep, send, down, up))
-    came, up_came = exchange_bit(send, "h"), exchange_bit(up, "h")
-    down = jnp.concatenate([down, exchange_bit(down, "y")])
+    half_a, half_b, up = [k + g for k, g in zip(keeps, (*got[:2], got[2][::-1]))]
+    up = add_extra(up)
+    both = jnp.concatenate([half_a, half_b], axis=2)
+    down = jnp.concatenate([down, down_came])
+
+    (both, down, up, far_came) = lax.optimization_barrier((both, down, up, far_came))
+    came, up_came = exchange_bit(both, "h"), exchange_bit(up, "x")
+    down = jnp.concatenate([down, exchange_bit(down, "l")])
+    both = add_extra(both + came[::-1])
     up = jnp.concatenate([up, up_came])
-    both = add_extra(keep + came)
-
-    (both, down, up, far_came) = lax.optimization_barrier((both, down, up, far_came))
-    came = exchange_bit(both, "h")
-    down = jnp.concatenate([down, exchange_bit(down, "l")])
-    up = jnp.concatenate([up, exchange_bit(up, "x")])
-    both = jnp.concatenate([both, came])
     own_pos = mine * local_rows + jnp.arange(local_rows, dtype=jnp.int32)
     live = (own_pos[None, :] < lengths[:, None]).astype(f32)
     d_inputs = jnp.stack([n + f for n, f in zip(near, far_came)])
@@ -975,7 +987,7 @@
     up_second = exchange_bit(up[4:], "y")
     down_far = exchange_bit(down_last, "c")
     up_near = exchange_bit(up, "c")
-    full_down = gather_down(places, [down, down_near], 0, [], (hidden, features))
+    full_down = gather_tiles(places, [down, down_near], 0, [], (hidden, features), False)
     up_last = jnp.concatenate([up_first, up_second])
 
     (both, both_first, up, up_near, up_last, down_far, full_down) = lax.optimization_barrier(
@@ -984,17 +996,21 @@
     both_second = exchange_bit(both[4:], "x")
     up_far = exchange_bit(up_last, "c")
     both_near = exchange_bit(both, "c")
-    full_down = gather_down(places, [down_last, down_far], 1, [full_down], (hidden, features))
-    full_up = gather_up(places, [up, up_near], 0, [], (features, hidden))
-    both_last = jnp.concatenate([both_first, both_second])
-
-    (both_last, both_near, up_far, full_down, full_up) = lax.optimization_barrier(
-        (both_last, both_near, up_far, full_down, full_up)
-    )
-    both_far = exchange_bit(both_last, "c")
-    full_up = gather_up(places, [up_last, up_far], 1, [full_up], (features, hidden))
+    full_down = gather_tiles(
+        places, [down_last, down_far], 1, [full_down], (hidden, features), False
+    )
+    full_up = gather_tiles(places, [up, up_near], 0, [], (features, hidden), True)
+    full_up = gather_tiles(places, [up_last, up_far], 1, [full_up], (features, hidden), True)
+
+    (both_second, both_near, full_down, full_up) = lax.optimization_barrier(
+        (both_second, both_near, full_down, full_up)
+    )
+    first_far, second_far = exchange_bit(both_first, "c"), exchange_bit(both_second, "c")
     full_qkv, full_out, vector_rows, head_rows = gather_heads(
-        places, [both, both_near, both_last, both_far], (features, 3 * features)
+        places,
+        [both[:4], both[4:], both_near[:4], both_near[4:]]
+        + [both_first, both_second, first_far, second_far],
+        (features, 3 * features),
     )
     (
         full_b_down,

time: 360 us -> 358 us (level)
  waiting for transfers between devices: 96.2 us -> 117 us
  Pallas kernels: 146 us -> 130 us
  starting transfers between devices: 53.3 us -> 46.7 us
    pallas_call x6 -> x1, Pallas kernels: 83.3 us -> 41.8 us  [step_call(): pl.pallas_call(body, out_shape=outs, grid_spec=pltpu.PrefetchScalarGridSp...]
    pallas_call x0 -> x5, Pallas kernels: none -> 24.8 us  [the longest x4 17 us: gather_tiles(): pl.pallas_call(functools.partial(place_tiles, count, split, late), out_sh...]
    ppermute x70 -> x68, waiting for transfers between devices: 96.2 us -> 117 us  [exchange(): lax.ppermute(array_in, axis, [(i, i ^ flip) for i in range(lax.axis_size(...]
    ppermute x70 -> x68, starting transfers between devices: 53.3 us -> 46.7 us  [exchange(): lax.ppermute(array_in, axis, [(i, i ^ flip) for i in range(lax.axis_size(...]
  transfers between devices with their start and end apart: 70 -> 68, of which waited for: 26 -> 32; matrix products, arithmetic and copies ran while one was open for 11% -> 11% of each run, Pallas kernels for 27% -> 23%
where the time goes in v7:
time: 358 us; the launch traced here: 353 us
  Pallas kernels  130 us (36%)
  waiting for transfers between devices  117 us (33%)
  starting transfers between devices  46.7 us (13%)
  other arithmetic  30.3 us (8%)
  local copies, waits for them, and re-layouts  27.5 us (8%)
    ppermute x68, waiting for transfers between devices, exchange(): lax.ppermute(array_in, axis, [(i, i ^ flip) for i in range(lax.axis_size(...  117 us
    pallas_call x6, Pallas kernels, kernel_call(): pl.pallas_call(body, out_shape=outs, in_specs=[pl.BlockSpec(memory_space=...  63.1 us
    ppermute x68, starting transfers between devices, exchange(): lax.ppermute(array_in, axis, [(i, i ^ flip) for i in range(lax.axis_size(...  46.7 us
    pallas_call x1, Pallas kernels, step_call(): pl.pallas_call(body, out_shape=outs, grid_spec=pltpu.PrefetchScalarGridSp...  41.8 us
    convert_element_type x9, other arithmetic, sum_low(): return total.astype(jnp.bfloat16)  17.1 us
    pallas_call x4, Pallas kernels, gather_tiles(): pl.pallas_call(functools.partial(place_tiles, count, split, late), out_sh...  17 us
    pallas_call x1, Pallas kernels, gather_heads(): pl.pallas_call(functools.partial(place_heads, count), out_shape=[out(shap...  7.8 us
    unnamed x136, local copies, waits for them, and re-layouts  7.26 us
  transfers between devices with their start and end apart: 68, of which 32 were waited for; matrix products, arithmetic and copies ran while one was open for 11% of the time, Pallas kernels for 23%

profile of v7, /device:TPU:0, one launch (start us, length us, event | category | flops | bytes accessed | tf_op | source)
XLA Modules:
  0.0 353.3 jit_solution(4666148697132879269)
XLA Ops:
  17.6 8.4 %shard_map.280 = (bf16[192,256]{1,0:T(8,128)(2,1)}, bf16[192,256]{1,0:T(8,128)(2,1)}, bf16[192,256]{1,0:T(8,128)(2,1)}, bf16[192,256]{1,0:T(8,128)(2,1)}, bf16[1...) custom-call(s32[20]{0:T(128)} %concatenate.48.places, ...), custom_call_target="tpu_custom_call" | custom-call | flops 100000000 | bytes 1048576 | tf_op jit(solution)/shard_map/pallas_call | solution.py:230
  29.1 8.2 %shard_map.281 = (bf16[192,256]{1,0:T(8,128)(2,1)}, bf16[192,256]{1,0:T(8,128)(2,1)}, bf16[192,256]{1,0:T(8,128)(2,1)}, bf16[192,256]{1,0:T(8,128)(2,1)}, bf16[1...) custom-call(s32[20]{0:T(128)} %concatenate.48.places, ...), custom_call_target="tpu_custom_call" | custom-call | flops 100000000 | bytes 1048576 | tf_op jit(solution)/shard_map/pallas_call | solution.py:230
  41.8 8.2 %shard_map.282 = (bf16[192,256]{1,0:T(8,128)(2,1)}, bf16[192,256]{1,0:T(8,128)(2,1)}, bf16[192,256]{1,0:T(8,128)(2,1)}, bf16[192,256]{1,0:T(8,128)(2,1)}, bf16[1...) custom-call(s32[20]{0:T(128)} %concatenate.48.places, ...), custom_call_target="tpu_custom_call" | custom-call | flops 100000000 | bytes 1048576 | tf_op jit(solution)/shard_map/pallas_call | solution.py:230
  59.9 41.8 %shard_map.283 = (bf16[768,768]{1,0:T(8,128)(2,1)}, bf16[2,384,768]{2,1,0:T(8,128)(2,1)}, bf16[2,768,384]{2,1,0:T(8,128)(2,1)}, bf16[2,384,768]{2,1,0:T(8,128)(2...) custom-call(s32[20]{0:T(128)} %concatenate.48.places, ...), custom_call_target="tpu_custom_call" | custom-call | flops 24461180928 | bytes 1048576 | tf_op jit(solution)/shard_map/pallas_call | solution.py:526
  103.0 6.5 %collective-permute-done.19.g2 = bf16[2,1,192,256]{3,2,1,0:T(8,128)(2,1)S(1)} collective-permute-done((bf16[2,1,192,256]{3,2,1,0:T(8,128)(2,1)}, bf16[2,1,192,256]{3,2,1,0:T(8,128)(2,1)S(1)}, u32[]{:S(2)}, u32[]{:S(2)}) %collective-permute-start.19) | collective-permute-done | bytes 196640 | tf_op jit(solution)/shard_map/ppermute | solution.py:29
  123.5 12.4 %shard_map.284 = (bf16[2,256,768]{2,1,0:T(8,128)(2,1)}, bf16[2,256,768]{2,1,0:T(8,128)(2,1)}, f32[576,768]{1,0:T(8,128)}, f32[8,576]{1,0:T(8,128)}) custom-call(s32[20]{0:T(128)} %concatenate.48.places, bf16[1,192,256]{2,1,0:T(8,128)(2,1)} %get-tuple-element.213.g0, bf16[1,192,256]{2,1,0:T(8,128)(2,1)} %copy-done.39, bf16[2,1,192,256]{3,2,1,0:T(8,128)(2,1)} %copy-done.28, ...), custom_call_target="tpu_custom_call" | custom-call | flops 100000000 | bytes 1048576 | tf_op jit(solution)/shard_map/pallas_call | solution.py:230
  135.9 12.8 %collective-permute-done.27.g2 = bf16[2,2,192,256]{3,2,1,0:T(8,128)(2,1)S(1)} collective-permute-done((bf16[2,2,192,256]{3,2,1,0:T(8,128)(2,1)}, bf16[2,2,192,256]{3,2,1,0:T(8,128)(2,1)S(1)}, u32[]{:S(2)}, u32[]{:S(2)}) %collective-permute-start.27) | collective-permute-done | bytes 393248 | tf_op jit(solution)/shard_map/ppermute | solution.py:29
  157.1 12.8 %shard_map.285 = (bf16[2,256,768]{2,1,0:T(8,128)(2,1)}, bf16[2,256,768]{2,1,0:T(8,128)(2,1)}, f32[576,768]{1,0:T(8,128)}, f32[8,576]{1,0:T(8,128)}) custom-call(s32[20]{0:T(128)} %concatenate.48.places, bf16[2,192,256]{2,1,0:T(8,128)(2,1)} %get-tuple-element.237.g0, bf16[2,192,256]{2,1,0:T(8,128)(2,1)} %copy-done.22, bf16[2,2,192,256]{3,2,1,0:T(8,128)(2,1)} %copy-done.4, ...), custom_call_target="tpu_custom_call" | custom-call | flops 100000000 | bytes 1048576 | tf_op jit(solution)/shard_map/pallas_call | solution.py:230
  182.0 13.1 %shard_map.286 = (bf16[2,256,768]{2,1,0:T(8,128)(2,1)}, bf16[2,256,768]{2,1,0:T(8,128)(2,1)}, bf16[8,112,384]{2,1,0:T(8,128)(2,1)}, bf16[8,112,384]{2,1,0:T(8,128)(2,1)}) custom-call(s32[20]{0:T(128)} %concatenate.48.places, bf16[2,192,256]{2,1,0:T(8,128)(2,1)} %get-tuple-element.237.g0, bf16[2,192,256]{2,1,0:T(8,128)(2,1)} %copy-done.22, ...), custom_call_target="tpu_custom_call" | custom-call | flops 100000000 | bytes 1048576 | tf_op jit(solution)/shard_map/pallas_call | solution.py:230
  196.5 4.1 %collective-permute-done.36 = bf16[2,192,384]{2,1,0:T(8,128)(2,1)} collective-permute-done((bf16[2,192,384]{2,1,0:T(8,128)(2,1)}, bf16[2,192,384]{2,1,0:T(8,128)(2,1)}, u32[]{:S(2)}, u32[]{:S(2)}) %collective-permute-start.36) | collective-permute-done | bytes 294944 | tf_op jit(solution)/shard_map/ppermute | solution.py:29
  209.4 10.7 %collective-permute-done.41 = bf16[2,96,768]{2,1,0:T(8,128)(2,1)S(1)} collective-permute-done((bf16[2,96,768]{2,1,0:T(8,128)(2,1)S(1)}, bf16[2,96,768]{2,1,0:T(8,128)(2,1)S(1)}, u32[]{:S(2)}, u32[]{:S(2)}) %collective-permute-start.41) | collective-permute-done | bytes 294944 | tf_op jit(solution)/shard_map/ppermute | solution.py:29
  234.4 5.3 %collective-permute-done.46 = bf16[2,192,384]{2,1,0:T(8,128)(2,1)S(1)} collective-permute-done((bf16[2,192,384]{2,1,0:T(8,128)(2,1)S(1)}, bf16[2,192,384]{2,1,0:T(8,128)(2,1)S(1)}, u32[]{:S(2)}, u32[]{:S(2)}) %collective-permute-start.46) | collective-permute-done | bytes 294944 | tf_op jit(solution)/shard_map/ppermute | solution.py:29
  239.8 5.7 %collective-permute-done.48 = bf16[256,768]{1,0:T(8,128)(2,1)S(1)} collective-permute-done((bf16[256,768]{1,0:T(8,128)(2,1)S(1)}, bf16[256,768]{1,0:T(8,128)(2,1)S(1)}, u32[]{:S(2)}, u32[]{:S(2)}) %collective-permute-start.48) | collective-permute-done | bytes 393248 | tf_op jit(solution)/shard_map/ppermute | solution.py:29
  253.9 7.3 %collective-permute-done.49 = bf16[2,112,768]{2,1,0:T(8,128)(2,1)S(1)} collective-permute-done((bf16[2,112,768]{2,1,0:T(8,128)(2,1)S(1)}, bf16[2,112,768]{2,1,0:T(8,128)(2,1)S(1)}, u32[]{:S(2)}, u32[]{:S(2)}) %collective-permute-start.49) | collective-permute-done | bytes 344096 | tf_op jit(solution)/shard_map/ppermute | solution.py:29
  261.4 4.9 %collective-permute-done.50 = bf16[4,96,768]{2,1,0:T(8,128)(2,1)S(1)} collective-permute-done((bf16[4,96,768]{2,1,0:T(8,128)(2,1)S(1)}, bf16[4,96,768]{2,1,0:T(8,128)(2,1)S(1)}, u32[]{:S(2)}, u32[]{:S(2)}) %collective-permute-start.50) | collective-permute-done | bytes 589856 | tf_op jit(solution)/shard_map/ppermute | solution.py:29
  268.9 4.9 %collective-permute-done.52 = bf16[2,112,768]{2,1,0:T(8,128)(2,1)S(1)} collective-permute-done((bf16[2,112,768]{2,1,0:T(8,128)(2,1)S(1)}, bf16[2,112,768]{2,1,0:T(8,128)(2,1)S(1)}, u32[]{:S(2)}, u32[]{:S(2)}) %collective-permute-start.52) | collective-permute-done | bytes 344096 | tf_op jit(solution)/shard_map/ppermute | solution.py:29
  273.9 4.3 %collective-permute-done.54 = bf16[4,192,384]{2,1,0:T(8,128)(2,1)S(1)} collective-permute-done((bf16[4,192,384]{2,1,0:T(8,128)(2,1)S(1)}, bf16[4,192,384]{2,1,0:T(8,128)(2,1)S(1)}, u32[]{:S(2)}, u32[]{:S(2)}) %collective-permute-start.54) | collective-permute-done | bytes 589856 | tf_op jit(solution)/shard_map/ppermute | solution.py:29
  282.1 13.3 %collective-permute-done.57 = bf16[4,96,768]{2,1,0:T(8,128)(2,1)S(1)} collective-permute-done((bf16[4,96,768]{2,1,0:T(8,128)(2,1)S(1)}, bf16[4,96,768]{2,1,0:T(8,128)(2,1)S(1)}, u32[]{:S(2)}, u32[]{:S(2)}) %collective-permute-start.57) | collective-permute-done | bytes 589856 | tf_op jit(solution)/shard_map/ppermute | solution.py:29
  301.8 4.3 %shard_map.287.refs_2_ = f32[3072,768]{1,0:T(8,128)} custom-call(s32[20]{0:T(128)} %concatenate.48.places, bf16[8,96,768]{2,1,0:T(8,128)(2,1)} %copy-done.1, bf16[8,96,768]{2,1,0:T(8,128)(2,1)} %copy-done.12), custom_call_target="tpu_custom_call" | custom-call | tf_op jit(solution)/shard_map/pallas_call | solution.py:650
  306.1 8.0 %collective-permute-done.61 = bf16[4,192,384]{2,1,0:T(8,128)(2,1)} collective-permute-done((bf16[4,192,384]{2,1,0:T(8,128)(2,1)S(1)}, bf16[4,192,384]{2,1,0:T(8,128)(2,1)}, u32[]{:S(2)}, u32[]{:S(2)}) %collective-permute-start.61) | collective-permute-done | bytes 589856 | tf_op jit(solution)/shard_map/ppermute | solution.py:29
  320.7 4.3 %shard_map.288 = f32[3072,768]{1,0:T(8,128)} custom-call(s32[20]{0:T(128)} %concatenate.48.places, bf16[8,96,768]{2,1,0:T(8,128)(2,1)} %pad_maximum_fusion.3.refs_0_, bf16[8,96,768]{2,1,0:T(8,128)(2,1)} %collective-permute-done.62.refs_1_, f32[3072,768]{1,0:T(8,128)} %shard_map.287.refs_2_), custom_call_target="tpu_custom_call", output_to_operand_aliasing={{}: (3, {})} | custom-call | tf_op jit(solution)/shard_map/pallas_call | solution.py:650
  325.0 4.2 %shard_map.289.refs_2_ = f32[768,3072]{1,0:T(8,128)} custom-call(s32[20]{0:T(128)} %concatenate.48.places, bf16[8,192,384]{2,1,0:T(8,128)(2,1)} %copy-done, bf16[8,192,384]{2,1,0:T(8,128)(2,1)} %collective-permute-done.60.refs_1_), custom_call_target="tpu_custom_call" | custom-call | tf_op jit(solution)/shard_map/pallas_call | solution.py:650
  329.3 4.2 %shard_map.290 = f32[768,3072]{1,0:T(8,128)} custom-call(s32[20]{0:T(128)} %concatenate.48.places, bf16[8,192,384]{2,1,0:T(8,128)(2,1)} %copy-done.2, bf16[8,192,384]{2,1,0:T(8,128)(2,1)} %collective-permute-done.65.refs_1_, f32[768,3072]{1,0:T(8,128)} %shard_map.289.refs_2_), custom_call_target="tpu_custom_call", output_to_operand_aliasing={{}: (3, {})} | custom-call | tf_op jit(solution)/shard_map/pallas_call | solution.py:650
  340.1 7.8 %shard_map.291 = (f32[768,2304]{1,0:T(8,128)}, f32[768,768]{1,0:T(8,128)}, f32[16,768]{1,0:T(8,128)}, f32[8,768]{1,0:T(8,128)}) custom-call(s32[20]{0:T(128)} %concatenate.48.places, bf16[4,112,768]{2,1,0:T(8,128)(2,1)} %get-tuple-element.359.refs_0_, bf16[4,112,768]{2,1,0:T(8,128)(2,1)} %copy-done.3, bf16[4,112,768]{2,1,0:T(8,128)(2,1)} %get-tuple-element.357.refs_2_, ...), custom_call_target="tpu_custom_call" | custom-call | tf_op jit(solution)/shard_map/pallas_call | solution.py:744
  (342 shorter events, 134.1 us)
Async XLA Ops:
  109.4 39.2 %collective-permute-start.28 = (bf16[2,384,768]{2,1,0:T(8,128)(2,1)}, bf16[2,384,768]{2,1,0:T(8,128)(2,1)}, u32[]{:S(2)}, u32[]{:S(2)}) collective-permute-start(bf16[2,384,768]{2,1,0:T(8,128)(2,1)} %get-tuple-element.227), channel_id=1, source_target_pairs={{0,1},{1,0},{2,3},{3,2},{4,5},{5,4},{6,7},{7,6},{8,9},{9,8},{10,11... | collective-permute-start | bytes 3538952 | tf_op jit(solution)/shard_map/ppermute | solution.py:29
  116.9 31.7 %collective-permute-start.22 = (bf16[2,384,768]{2,1,0:T(8,128)(2,1)}, bf16[2,384,768]{2,1,0:T(8,128)(2,1)}, u32[]{:S(2)}, u32[]{:S(2)}) collective-permute-start(bf16[2,384,768]{2,1,0:T(8,128)(2,1)} %add_convert_fusion.1), channel_id=1, source_target_pairs={{0,4},{4,0},{8,12},{12,8},{16,20},{20,16},{24,28},{28,24},{1,5},{5... | collective-permute-start | bytes 3538952 | tf_op jit(solution)/shard_map/ppermute | solution.py:29
  118.5 30.2 %collective-permute-start.23 = (bf16[2,768,384]{2,1,0:T(8,128)(2,1)}, bf16[2,768,384]{2,1,0:T(8,128)(2,1)S(1)}, u32[]{:S(2)}, u32[]{:S(2)}) collective-permute-start(bf16[2,768,384]{2,1,0:T(8,128)(2,1)} %add_convert_fusion), channel_id=1, source_target_pairs={{0,8},{4,12},{8,0},{12,4},{16,24},{20,28},{24,16},{28,20},{1,9},{5... | collective-permute-start | bytes 3538952 | tf_op jit(solution)/shard_map/ppermute | solution.py:29
  120.0 28.6 %collective-permute-start.24 = (bf16[2,8,96,192]{3,2,1,0:T(8,128)(2,1)}, bf16[2,8,96,192]{3,2,1,0:T(8,128)(2,1)}, u32[]{:S(2)}, u32[]{:S(2)}) collective-permute-start(bf16[2,8,96,192]{3,2,1,0:T(8,128)(2,1)} %get-tuple-element.212), channel_id=1, source_target_pairs={{0,2},{1,3},{2,0},{3,1},{4,6},{5,7},{6,4},{7,5},{8,10},{9,11},{10,... | collective-permute-start | bytes 1769480 | tf_op jit(solution)/shard_map/ppermute | solution.py:29
  122.7 26.0 %collective-permute-start.27 = (bf16[2,2,192,256]{3,2,1,0:T(8,128)(2,1)}, bf16[2,2,192,256]{3,2,1,0:T(8,128)(2,1)S(1)}, u32[]{:S(2)}, u32[]{:S(2)}) collective-permute-start(bf16[2,2,192,256]{3,2,1,0:T(8,128)(2,1)} %get-tuple-element.224), channel_id=1, source_target_pairs={{0,2},{1,3},{2,0},{3,1},{4,6},{5,7},{6,4},{7,5},{8,10},{9,11},{10,... | collective-permute-start | bytes 1179656 | tf_op jit(solution)/shard_map/ppermute | solution.py:29
  148.7 23.3 %collective-permute-start.33 = (bf16[2,256,768]{2,1,0:T(8,128)(2,1)}, bf16[2,256,768]{2,1,0:T(8,128)(2,1)}, u32[]{:S(2)}, u32[]{:S(2)}) collective-permute-start(bf16[2,256,768]{2,1,0:T(8,128)(2,1)} %get-tuple-element.251), channel_id=1, source_target_pairs={{0,1},{1,0},{2,3},{3,2},{4,5},{5,4},{6,7},{7,6},{8,9},{9,8},{10,11... | collective-permute-start | bytes 2359304 | tf_op jit(solution)/shard_map/ppermute | solution.py:29
  154.8 19.3 %collective-permute-start.29 = (bf16[384,768]{1,0:T(8,128)(2,1)}, bf16[384,768]{1,0:T(8,128)(2,1)}, u32[]{:S(2)}, u32[]{:S(2)}) collective-permute-start(bf16[384,768]{1,0:T(8,128)(2,1)} %fusion.4), channel_id=1, source_target_pairs={{0,8},{4,12},{8,0},{12,4},{16,24},{20,28},{24,16},{28,20},{1,9},{5... | collective-permute-start | bytes 1769480 | tf_op jit(solution)/shard_map/ppermute | solution.py:29
  155.6 18.5 %collective-permute-start.30 = (bf16[768,384]{1,0:T(8,128)(2,1)}, bf16[768,384]{1,0:T(8,128)(2,1)}, u32[]{:S(2)}, u32[]{:S(2)}) collective-permute-start(bf16[768,384]{1,0:T(8,128)(2,1)} %fusion.5), channel_id=1, source_target_pairs={{0,4},{4,0},{8,12},{12,8},{16,20},{20,16},{24,28},{28,24},{1,5},{5... | collective-permute-start | bytes 1769480 | tf_op jit(solution)/shard_map/ppermute | solution.py:29
  176.1 19.1 %collective-permute-start.37 = (bf16[2,256,768]{2,1,0:T(8,128)(2,1)}, bf16[2,256,768]{2,1,0:T(8,128)(2,1)}, u32[]{:S(2)}, u32[]{:S(2)}) collective-permute-start(bf16[2,256,768]{2,1,0:T(8,128)(2,1)} %get-tuple-element.263), channel_id=1, source_target_pairs={{0,1},{1,0},{2,3},{3,2},{4,5},{5,4},{6,7},{7,6},{8,9},{9,8},{10,11... | collective-permute-start | bytes 2359304 | tf_op jit(solution)/shard_map/ppermute | solution.py:29
  176.4 24.3 %collective-permute-start.38 = (bf16[256,768]{1,0:T(8,128)(2,1)}, bf16[256,768]{1,0:T(8,128)(2,1)}, u32[]{:S(2)}, u32[]{:S(2)}) collective-permute-start(bf16[256,768]{1,0:T(8,128)(2,1)} %get-tuple-element.261), channel_id=1, source_target_pairs={{0,2},{1,3},{2,0},{3,1},{4,6},{5,7},{6,4},{7,5},{8,10},{9,11},{10,... | collective-permute-start | bytes 1179656 | tf_op jit(solution)/shard_map/ppermute | solution.py:29
  180.0 16.6 %collective-permute-start.35 = (bf16[2,96,768]{2,1,0:T(8,128)(2,1)}, bf16[2,96,768]{2,1,0:T(8,128)(2,1)S(1)}, u32[]{:S(2)}, u32[]{:S(2)}) collective-permute-start(bf16[2,96,768]{2,1,0:T(8,128)(2,1)} %get-tuple-element.259), channel_id=1, source_target_pairs={{0,2},{1,3},{2,0},{3,1},{4,6},{5,7},{6,4},{7,5},{8,10},{9,11},{10,... | collective-permute-start | bytes 884744 | tf_op jit(solution)/shard_map/ppermute | solution.py:29
  181.3 19.3 %collective-permute-start.36 = (bf16[2,192,384]{2,1,0:T(8,128)(2,1)}, bf16[2,192,384]{2,1,0:T(8,128)(2,1)}, u32[]{:S(2)}, u32[]{:S(2)}) collective-permute-start(bf16[2,192,384]{2,1,0:T(8,128)(2,1)} %get-tuple-element.260), channel_id=1, source_target_pairs={{0,2},{1,3},{2,0},{3,1},{4,6},{5,7},{6,4},{7,5},{8,10},{9,11},{10,... | collective-permute-start | bytes 884744 | tf_op jit(solution)/shard_map/ppermute | solution.py:29
  245.4 15.8 %collective-permute-start.49 = (bf16[2,112,768]{2,1,0:T(8,128)(2,1)S(1)}, bf16[2,112,768]{2,1,0:T(8,128)(2,1)S(1)}, u32[]{:S(2)}, u32[]{:S(2)}) collective-permute-start(bf16[2,112,768]{2,1,0:T(8,128)(2,1)S(1)} %pad_maximum_fusion.8), channel_id=1, source_target_pairs={{0,16},{4,20},{8,24},{12,28},{16,0},{20,4},{24,8},{28,12},{1,17},{... | collective-permute-start | bytes 1032200 | tf_op jit(solution)/shard_map/ppermute | solution.py:29
  245.7 20.6 %collective-permute-start.50 = (bf16[4,96,768]{2,1,0:T(8,128)(2,1)S(1)}, bf16[4,96,768]{2,1,0:T(8,128)(2,1)S(1)}, u32[]{:S(2)}, u32[]{:S(2)}) collective-permute-start(bf16[4,96,768]{2,1,0:T(8,128)(2,1)S(1)} %pad_maximum_fusion.6), channel_id=1, source_target_pairs={{0,8},{4,12},{8,0},{12,4},{16,24},{20,28},{24,16},{28,20},{1,9},{5... | collective-permute-start | bytes 1769480 | tf_op jit(solution)/shard_map/ppermute | solution.py:29
  279.5 18.4 %collective-permute-start.56 = (bf16[8,96,768]{2,1,0:T(8,128)(2,1)S(1)}, bf16[8,96,768]{2,1,0:T(8,128)(2,1)S(1)}, u32[]{:S(2)}, u32[]{:S(2)}) collective-permute-start(bf16[8,96,768]{2,1,0:T(8,128)(2,1)S(1)} %pad_maximum_fusion.1.refs_0_), channel_id=1, source_target_pairs={{0,1},{1,0},{2,3},{3,2},{4,5},{5,4},{6,7},{7,6},{8,9},{9,8},{10,11... | collective-permute-start | bytes 3538952 | tf_op jit(solution)/shard_map/ppermute | solution.py:29
  279.6 15.8 %collective-permute-start.57 = (bf16[4,96,768]{2,1,0:T(8,128)(2,1)S(1)}, bf16[4,96,768]{2,1,0:T(8,128)(2,1)S(1)}, u32[]{:S(2)}, u32[]{:S(2)}) collective-permute-start(bf16[4,96,768]{2,1,0:T(8,128)(2,1)S(1)} %slice.252), channel_id=1, source_target_pairs={{0,2},{1,3},{2,0},{3,1},{4,6},{5,7},{6,4},{7,5},{8,10},{9,11},{10,... | collective-permute-start | bytes 1769480 | tf_op jit(solution)/shard_map/ppermute | solution.py:29
  280.2 17.6 %collective-permute-start.55 = (bf16[4,112,768]{2,1,0:T(8,128)(2,1)S(1)}, bf16[4,112,768]{2,1,0:T(8,128)(2,1)S(1)}, u32[]{:S(2)}, u32[]{:S(2)}) collective-permute-start(bf16[4,112,768]{2,1,0:T(8,128)(2,1)S(1)} %pad_maximum_fusion.5), channel_id=1, source_target_pairs={{0,8},{4,12},{8,0},{12,4},{16,24},{20,28},{24,16},{28,20},{1,9},{5... | collective-permute-start | bytes 2064392 | tf_op jit(solution)/shard_map/ppermute | solution.py:29
  281.7 16.2 %collective-permute-start.58 = (bf16[4,192,384]{2,1,0:T(8,128)(2,1)S(1)}, bf16[4,192,384]{2,1,0:T(8,128)(2,1)S(1)}, u32[]{:S(2)}, u32[]{:S(2)}) collective-permute-start(bf16[4,192,384]{2,1,0:T(8,128)(2,1)S(1)} %slice.253), channel_id=1, source_target_pairs={{0,4},{4,0},{8,12},{12,8},{16,20},{20,16},{24,28},{28,24},{1,5},{5... | collective-permute-start | bytes 1769480 | tf_op jit(solution)/shard_map/ppermute | solution.py:29
  297.9 19.8 %collective-permute-start.60 = (bf16[8,192,384]{2,1,0:T(8,128)(2,1)S(1)}, bf16[8,192,384]{2,1,0:T(8,128)(2,1)}, u32[]{:S(2)}, u32[]{:S(2)}) collective-permute-start(bf16[8,192,384]{2,1,0:T(8,128)(2,1)S(1)} %pad_maximum_fusion.2.refs_0_), channel_id=1, source_target_pairs={{0,1},{1,0},{2,3},{3,2},{4,5},{5,4},{6,7},{7,6},{8,9},{9,8},{10,11... | collective-permute-start | bytes 3538952 | tf_op jit(solution)/shard_map/ppermute | solution.py:29
  298.0 19.8 %collective-permute-start.62 = (bf16[8,96,768]{2,1,0:T(8,128)(2,1)}, bf16[8,96,768]{2,1,0:T(8,128)(2,1)}, u32[]{:S(2)}, u32[]{:S(2)}) collective-permute-start(bf16[8,96,768]{2,1,0:T(8,128)(2,1)} %pad_maximum_fusion.3.refs_0_), channel_id=1, source_target_pairs={{0,1},{1,0},{2,3},{3,2},{4,5},{5,4},{6,7},{7,6},{8,9},{9,8},{10,11... | collective-permute-start | bytes 3538952 | tf_op jit(solution)/shard_map/ppermute | solution.py:29
  300.3 17.5 %collective-permute-start.59 = (bf16[4,112,768]{2,1,0:T(8,128)(2,1)}, bf16[4,112,768]{2,1,0:T(8,128)(2,1)}, u32[]{:S(2)}, u32[]{:S(2)}) collective-permute-start(bf16[4,112,768]{2,1,0:T(8,128)(2,1)} %slice.254), channel_id=1, source_target_pairs={{0,2},{1,3},{2,0},{3,1},{4,6},{5,7},{6,4},{7,5},{8,10},{9,11},{10,... | collective-permute-start | bytes 2064392 | tf_op jit(solution)/shard_map/ppermute | solution.py:29
  317.8 19.0 %collective-permute-start.64 = (bf16[8,112,768]{2,1,0:T(8,128)(2,1)S(1)}, bf16[8,112,768]{2,1,0:T(8,128)(2,1)}, u32[]{:S(2)}, u32[]{:S(2)}) collective-permute-start(bf16[8,112,768]{2,1,0:T(8,128)(2,1)S(1)} %bitcast.95), channel_id=1, source_target_pairs={{0,1},{1,0},{2,3},{3,2},{4,5},{5,4},{6,7},{7,6},{8,9},{9,8},{10,11... | collective-permute-start | bytes 4128776 | tf_op jit(solution)/shard_map/ppermute | solution.py:29
  319.3 17.5 %collective-permute-start.63 = (bf16[4,112,768]{2,1,0:T(8,128)(2,1)S(1)}, bf16[4,112,768]{2,1,0:T(8,128)(2,1)}, u32[]{:S(2)}, u32[]{:S(2)}) collective-permute-start(bf16[4,112,768]{2,1,0:T(8,128)(2,1)S(1)} %get-tuple-element.358.refs_1_), channel_id=1, source_target_pairs={{0,2},{1,3},{2,0},{3,1},{4,6},{5,7},{6,4},{7,5},{8,10},{9,11},{10,... | collective-permute-start | bytes 2064392 | tf_op jit(solution)/shard_map/ppermute | solution.py:29
  320.7 18.5 %collective-permute-start.66 = (bf16[4,112,768]{2,1,0:T(8,128)(2,1)}, bf16[4,112,768]{2,1,0:T(8,128)(2,1)}, u32[]{:S(2)}, u32[]{:S(2)}) collective-permute-start(bf16[4,112,768]{2,1,0:T(8,128)(2,1)} %collective-permute-done.59.refs_4_), channel_id=1, source_target_pairs={{0,1},{1,0},{2,3},{3,2},{4,5},{5,4},{6,7},{7,6},{8,9},{9,8},{10,11... | collective-permute-start | bytes 2064392 | tf_op jit(solution)/shard_map/ppermute | solution.py:29
  (111 other events, 800.7 us)

commit v8 on v7

--- a/solution.py
+++ b/solution.py
@@ -607,8 +607,8 @@
     )
 
 
-def place_tiles(count, split, x, places, *refs):
-    sources, out = refs[:count], refs[-4]
+def place_tiles(by_rows, late, places, *refs):
+    sources, out = refs[:2], refs[-4]
     held, main, sems = refs[-3:]
     inner = places[8]
     _, rows, cols = sources[0].shape
@@ -620,50 +620,45 @@
     sent = []
     for k, copy in enumerate(bring):
         copy.wait()
-        for n in range(2 if split else 8):
-            slot = sems.at[count + len(sent)]
-            if split:
-                block = places[k * 4 + x * 2 + n]
-                for q in range(4):
-                    first = pl.multiple_of((q ^ inner) * rows, rows)
-                    main[2 * k + n, pl.ds(first, rows), :] = held[
-                        k, n * 4 + (q & 1) * 2 + (q >> 1)
-                    ].astype(jnp.float32)
+        for l in range(2):
+            block = places[k * 4 + late * 2 + l]
+            place = 2 * k + l
+            for q in range(4):
+                first = pl.multiple_of((q ^ inner) * rows, rows)
+                main[place, pl.ds(first, rows), :] = held[k, l * 4 + (q & 1) * 2 + (q >> 1)].astype(
+                    jnp.float32
+                )
+            if by_rows:
+                target = out.at[pl.ds(pl.multiple_of(block * 4 * rows, 4 * rows), 4 * rows)]
+            else:
                 target = out.at[:, pl.ds(pl.multiple_of(block * cols, cols), cols)]
-                sent.append(pltpu.make_async_copy(main.at[2 * k + n], target, slot))
-            else:
-                l, y, h = n >> 2, (n >> 1) & 1, n & 1
-                block = places[k * 4 + y * 2 + l] * 4 + ((h * 2 + x) ^ inner)
-                main[8 * k + n] = held[k, n].astype(jnp.float32)
-                target = out.at[pl.ds(pl.multiple_of(block * rows, rows), rows)]
-                sent.append(pltpu.make_async_copy(main.at[8 * k + n], target, slot))
+            sent.append(pltpu.make_async_copy(main.at[place], target, sems.at[2 + place]))
             sent[-1].start()
     for copy in sent:
         copy.wait()
 
 
-def gather_tiles(places, pieces, late, begun, shape, split):
+def gather_tiles(places, pieces, late, begun, shape, by_rows):
     _, rows, cols = pieces[0].shape
-    count = len(pieces)
     away = pl.BlockSpec(memory_space=pl.ANY)
-    main = (2 * count, 4 * rows, cols) if split else (8 * count, rows, cols)
     return pl.pallas_call(
-        functools.partial(place_tiles, count, split, late),
+        functools.partial(place_tiles, by_rows, late),
         out_shape=jax.ShapeDtypeStruct(shape, jnp.float32),
-        in_specs=[pl.BlockSpec(memory_space=pltpu.SMEM)] + [away] * (count + len(begun)),
+        in_specs=[pl.BlockSpec(memory_space=pltpu.SMEM)] + [away] * (2 + len(begun)),
         out_specs=away,
         scratch_shapes=[
-            pltpu.VMEM((count, 8, rows, cols), jnp.bfloat16),
-            pltpu.VMEM(main, jnp.float32),
-            pltpu.SemaphoreType.DMA((count + main[0],)),
+            pltpu.VMEM((2, 8, rows, cols), jnp.bfloat16),
+            pltpu.VMEM((4, 4 * rows, cols), jnp.float32),
+            pltpu.SemaphoreType.DMA((6,)),
         ],
-        input_output_aliases={count + 1: 0} if begun else {},
+        input_output_aliases={3: 0} if begun else {},
         compiler_params=pltpu.CompilerParams(vmem_limit_bytes=VMEM_LIMIT),
     )(places, *pieces, *begun)
 
 
-def place_heads(seq_parts, places, *refs):
-    sources, refs = refs[: 2 * seq_parts], refs[2 * seq_parts :]
+def place_heads(parts, places, *refs):
+    seq_parts = parts[-1][0] + 1
+    sources, refs = refs[: len(parts)], refs[len(parts) :]
     out, out_w, vector_rows, head_rows = refs[:4]
     pieces = refs[4 : seq_parts + 4]
     main, side, sems = refs[seq_parts + 4 :]
@@ -672,12 +667,11 @@
     features = side.shape[2]
     wide = features // seq_parts
     f32 = jnp.float32
-    half = blocks // 2
     bring = [
         pltpu.make_async_copy(
-            source, pieces[i >> 1].at[pl.ds((i & 1) * half, half)], sems.at[2 * blocks + i]
+            source, pieces[r].at[pl.ds(first, source.shape[0])], sems.at[2 * blocks + i]
         )
-        for i, source in enumerate(sources)
+        for i, (source, (r, first)) in enumerate(zip(sources, parts))
     ]
     for copy in bring:
         copy.start()
@@ -693,10 +687,10 @@
 
             @pl.when(mine == m)
             def copy():
-                parts = [pieces[j ^ m][p ^ inner, :rows, : 3 * wide] for j in range(seq_parts)]
+                near = [pieces[j ^ m][p ^ inner, :rows, : 3 * wide] for j in range(seq_parts)]
                 for section in range(3):
                     columns = slice(section * wide, (section + 1) * wide)
-                    joined = jnp.concatenate([part[:, columns] for part in parts], axis=1)
+                    joined = jnp.concatenate([part[:, columns] for part in near], axis=1)
                     main[p, :, section * features : (section + 1) * features] = joined.astype(f32)
 
         leave(p, main, out, 0).start()
@@ -732,33 +726,33 @@
         leave(p, side, out_w, blocks).wait()
 
 
-def gather_heads(places, halves, shape):
+def gather_heads(places, sources, parts, shape):
     out, f32 = jax.ShapeDtypeStruct, jnp.float32
     features = shape[0]
     rows = features // 8
-    extra = (halves[0].shape[1] - rows, features)
-    count = len(halves) // 2
-    piece = (8, *halves[0].shape[1:])
+    extra = (sources[0].shape[1] - rows, features)
+    count = parts[-1][0] + 1
+    piece = (8, *sources[0].shape[1:])
     away = pl.BlockSpec(memory_space=pl.ANY)
     here = pl.BlockSpec(memory_space=pltpu.VMEM)
     return pl.pallas_call(
-        functools.partial(place_heads, count),
+        functools.partial(place_heads, parts),
         out_shape=[
             out(shape, f32),
             out((features, features), f32),
             out(extra, f32),
             out((8, features), f32),
         ],
-        in_specs=[pl.BlockSpec(memory_space=pltpu.SMEM)] + [away] * len(halves),
+        in_specs=[pl.BlockSpec(memory_space=pltpu.SMEM)] + [away] * len(sources),
         out_specs=[away, away, here, here],
-        scratch_shapes=[pltpu.VMEM(piece, halves[0].dtype)] * count
+        scratch_shapes=[pltpu.VMEM(piece, sources[0].dtype)] * count
         + [
             pltpu.VMEM((8, rows, shape[1]), f32),
             pltpu.VMEM((8, rows, features), f32),
-            pltpu.SemaphoreType.DMA((16 + len(halves),)),
+            pltpu.SemaphoreType.DMA((16 + len(sources),)),
         ],
         compiler_params=pltpu.CompilerParams(vmem_limit_bytes=VMEM_LIMIT),
-    )(places, *halves)
+    )(places, *sources)
 
 
 def per_device(
@@ -888,77 +882,75 @@
     sends = [
         sum_low(keep_down[2:], came_down1),
         sum_low(keep_up[1::2], jnp.stack([came_up0[1], came_up1[1]])),
-        send_out,
     ]
     sends, first_came = lax.optimization_barrier((sends, first_came))
-    down_y, up_l, out_x = [exchange_bit(v, bit) for v, bit in zip(sends, "ylx")]
+    down_y, up_l = [exchange_bit(v, bit) for v, bit in zip(sends, "yl")]
     came_down0 = exchange_bit(send_down0, "c")
     total = attend(0, hand_on(d_contexts[0], d_contexts[1], first_came), ())
-    (down_y, up_l, out_x, total, parts[0], second_came, near_pair, came_down0) = (
-        lax.optimization_barrier(
-            (down_y, up_l, out_x, total, parts[0], second_came, d_contexts[3:5], came_down0)
-        )
+    (total, parts[0], second_came, near_pair, came_down0, send_out) = lax.optimization_barrier(
+        (total, parts[0], second_came, d_contexts[3:5], came_down0, send_out)
+    )
+
+    out_x = exchange_bit(send_out, "x")
+    second_group = hand_on(*near_pair, second_came)
+    cross(0)
+    for s in range(1, seq_count - 1):
+        total = attend(s, second_group, total)
+    (down_y, up_l, out_x, total, parts[1:], near, far) = lax.optimization_barrier(
+        (down_y, up_l, out_x, total, parts[1:], near, far)
     )
 
     sends = [
         sum_low(keep_down[1], came_down0[1], down_y[1]),
         sum_low(keep_up[2], came_up1[0], up_l[1]),
-        sum_low(grad_out[1], out_x[1]),
     ]
-    (sends, total) = lax.optimization_barrier((sends, total))
-    down_l, up_y, out_c = [exchange_bit(v, bit) for v, bit in zip(sends, "lyc")]
-    cross(0)
-    second_group = hand_on(*near_pair, second_came)
+    out_c = exchange_bit(sum_low(grad_out[1], out_x[1]), "c")
+    out_own = sum_low(grad_out[0], out_x[0], out_c)
+    (sends, total, out_own, far) = lax.optimization_barrier((sends, total, out_own, far))
+    down_l, up_y = [exchange_bit(v, bit) for v, bit in zip(sends, "ly")]
+    far_came = [exchange_bit(far[0], "x")]
     for s in range(1, seq_count - 1):
-        total = attend(s, second_group, total)
-    out_own = sum_low(grad_out[0], out_x[0], out_c)
-    (down_l, up_y, total, parts[1:], near, far, out_own) = lax.optimization_barrier(
-        (down_l, up_y, total, parts[1:], near, far, out_own)
-    )
-
+        cross(s)
+    half_a, half_b = attend(seq_count - 1, second_group, total, (out_own, sums))
+
+    (down_l, up_y, far, far_came, half_a, half_b, parts[-1]) = lax.optimization_barrier(
+        (down_l, up_y, far, far_came, half_a, half_b, parts[-1])
+    )
     down_own = sum_low(keep_down[0], came_down0[0], down_y[0], down_l)
     down_own = down_own.reshape(2, 2, hidden // 32, features)
     up_own = sum_low(keep_up[0], came_up0[0], up_l[0], up_y)
     up_own = up_own.reshape(2, 2, features // 4, hidden // 8)
-    keeps, sends = [down_own[:, 0], up_own[:, 0]], [down_own[:, 1], up_own[:, 1]]
-    (keeps, sends, total) = lax.optimization_barrier((keeps, sends, total))
-    got = [exchange_bit(v, "x") for v in sends]
-    far_came = [exchange_bit(far[0], "x")]
-    for s in range(1, seq_count - 1):
-        cross(s)
-    half_a, half_b = attend(seq_count - 1, second_group, total, (out_own, sums))
-
-    (keeps, got, far, far_came, half_a, half_b, parts[-1]) = lax.optimization_barrier(
-        (keeps, got, far, far_came, half_a, half_b, parts[-1])
-    )
-    down, up = [k + g for k, g in zip(keeps, got)]
     half_b = half_b.reshape(2, 2, 2, *half_b.shape[1:])
-    keeps = [half_a[:4], half_b[:, 0], down]
-    sends = [half_a[4:], half_b[:, 1], down]
-    (keeps, sends, up) = lax.optimization_barrier((keeps, sends, up))
-    got = [exchange_bit(v, bit) for v, bit in zip(sends, "ylh")]
-    far_came += [exchange_bit(v, "x") for v in far[1:]]
-    half_a, half_b, down = [k + g for k, g in zip(keeps, (*got[:2], got[2][::-1]))]
+    keeps = [half_a[:4], half_b[:, 0], down_own[:, 0], up_own[:, 0]]
+    sends = [half_a[4:], half_b[:, 1], down_own[:, 1], up_own[:, 1]]
+    (keeps, sends) = lax.optimization_barrier((keeps, sends))
+    got = [exchange_bit(v, bit) for v, bit in zip(sends, "ylxx")]
+    half_a, half_b, down, up = [k + g for k, g in zip(keeps, got)]
+    near_far = far[1:]
     far = []
     cross(seq_count - 1)
 
-    keeps = [half_a[:2], half_b[0], up]
-    sends = [half_a[2:], half_b[1], up]
-    down = add_extra(down)
-    (keeps, sends, down, far, near) = lax.optimization_barrier((keeps, sends, down, far, near))
-    got = [exchange_bit(v, bit) for v, bit in zip(sends, "lyh")]
-    down_came = exchange_bit(down, "y")
+    keeps, sends = [half_a[:2], half_b[0]], [half_a[2:], half_b[1]]
+    (keeps, sends, down, up, far, near_far, near) = lax.optimization_barrier(
+        (keeps, sends, down, up, far, near_far, near)
+    )
+    got = [exchange_bit(v, bit) for v, bit in zip(sends, "ly")]
+    down_came = exchange_bit(down, "h")
+    far_came += [exchange_bit(v, "x") for v in near_far]
+    both = jnp.concatenate([k + g for k, g in zip(keeps, got)], axis=2)
+    down = add_extra(down + down_came[::-1])
+
+    (both, down, up, far, far_came) = lax.optimization_barrier((both, down, up, far, far_came))
     far_came += [exchange_bit(v, "x") for v in far]
-    half_a, half_b, up = [k + g for k, g in zip(keeps, (*got[:2], got[2][::-1]))]
-    up = add_extra(up)
-    both = jnp.concatenate([half_a, half_b], axis=2)
-    down = jnp.concatenate([down, down_came])
+    came = exchange_bit(both, "h")
+    down = jnp.concatenate([down, exchange_bit(down, "x")])
+    both = add_extra(both + came[::-1])
 
     (both, down, up, far_came) = lax.optimization_barrier((both, down, up, far_came))
-    came, up_came = exchange_bit(both, "h"), exchange_bit(up, "x")
+    came, up_came = exchange_bit(both, "y"), exchange_bit(up, "h")
     down = jnp.concatenate([down, exchange_bit(down, "l")])
-    both = add_extra(both + came[::-1])
-    up = jnp.concatenate([up, up_came])
+    both = jnp.concatenate([both, came])
+    up = add_extra(up + up_came[::-1])
     own_pos = mine * local_rows + jnp.arange(local_rows, dtype=jnp.int32)
     live = (own_pos[None, :] < lengths[:, None]).astype(f32)
     d_inputs = jnp.stack([n + f for n, f in zip(near, far_came)])
@@ -966,52 +958,56 @@
 
 
     (both, down, up, grad_tokens) = lax.optimization_barrier((both, down, up, grad_tokens))
-    down_first = exchange_bit(down[:4], "x")
-    came, up_came = exchange_bit(both, "y"), exchange_bit(up, "l")
-    both = jnp.concatenate([both, came])
-    up = jnp.concatenate([up, up_came])
-
-    (both, down, down_first, up) = lax.optimization_barrier((both, down, down_first, up))
     came = exchange_bit(both, "l")
-    down_second = exchange_bit(down[4:], "x")
-    up_first = exchange_bit(up[:4], "y")
+    down_first = exchange_bit(down[:4], "y")
+    up_came = exchange_bit(up, "x")
     down_near = exchange_bit(down, "c")
-    down_last = jnp.concatenate([down_first, down_second])
     both = jnp.stack([both.reshape(2, 2, *both.shape[1:]), came.reshape(2, 2, *came.shape[1:])], 1)
     both = both.reshape(8, *both.shape[3:])
-
-    (both, down, down_near, down_last, up, up_first) = lax.optimization_barrier(
-        (both, down, down_near, down_last, up, up_first)
+    up = jnp.concatenate([up, up_came])
+
+    (both, down, down_near, down_first, up) = lax.optimization_barrier(
+        (both, down, down_near, down_first, up)
     )
     both_first = exchange_bit(both[:4], "x")
-    up_second = exchange_bit(up[4:], "y")
+    down_second = exchange_bit(down[4:], "y")
+    up_came = exchange_bit(up, "l")
+    full_down = gather_tiles(places, [down, down_near], 0, [], (hidden, features), True)
+    down_last = jnp.concatenate([down_first, down_second])
+    up = jnp.concatenate([up, up_came])
+
+    (both, both_first, up, down_last, full_down) = lax.optimization_barrier(
+        (both, both_first, up, down_last, full_down)
+    )
+    both_second = exchange_bit(both[4:], "x")
+    up_first = exchange_bit(up[:4], "y")
     down_far = exchange_bit(down_last, "c")
-    up_near = exchange_bit(up, "c")
-    full_down = gather_tiles(places, [down, down_near], 0, [], (hidden, features), False)
-    up_last = jnp.concatenate([up_first, up_second])
-
-    (both, both_first, up, up_near, up_last, down_far, full_down) = lax.optimization_barrier(
-        (both, both_first, up, up_near, up_last, down_far, full_down)
-    )
-    both_second = exchange_bit(both[4:], "x")
-    up_far = exchange_bit(up_last, "c")
-    both_near = exchange_bit(both, "c")
-    full_down = gather_tiles(
-        places, [down_last, down_far], 1, [full_down], (hidden, features), False
-    )
-    full_up = gather_tiles(places, [up, up_near], 0, [], (features, hidden), True)
-    full_up = gather_tiles(places, [up_last, up_far], 1, [full_up], (features, hidden), True)
-
-    (both_second, both_near, full_down, full_up) = lax.optimization_barrier(
-        (both_second, both_near, full_down, full_up)
-    )
+    both_near, up_near = exchange_bit(both, "c"), exchange_bit(up, "c")
+    full_down = gather_tiles(places, [down_last, down_far], 1, [full_down], (hidden, features), True)
+    full_up = gather_tiles(places, [up, up_near], 0, [], (features, hidden), False)
+
+    (both_second, both_near, up, up_first, full_down, full_up) = lax.optimization_barrier(
+        (both_second, both_near, up, up_first, full_down, full_up)
+    )
+    up_second = exchange_bit(up[4:6], "y")
     first_far, second_far = exchange_bit(both_first, "c"), exchange_bit(both_second, "c")
+
+    (up, up_second, first_far, second_far) = lax.optimization_barrier(
+        (up, up_second, first_far, second_far)
+    )
+    up_third = exchange_bit(up[6:], "y")
     full_qkv, full_out, vector_rows, head_rows = gather_heads(
         places,
-        [both[:4], both[4:], both_near[:4], both_near[4:]]
-        + [both_first, both_second, first_far, second_far],
+        [both, both_near, both_first, both_second, first_far, second_far],
+        ((0, 0), (1, 0), (2, 0), (2, 4), (3, 0), (3, 4)),
         (features, 3 * features),
     )
+    (up_third, full_qkv, vector_rows, head_rows) = lax.optimization_barrier(
+        (up_third, full_qkv, vector_rows, head_rows)
+    )
+    up_last = jnp.concatenate([up_first, up_second, up_third])
+    up_far = exchange_bit(up_last, "c")
+    full_up = gather_tiles(places, [up_last, up_far], 1, [full_up], (features, hidden), False)
     (
         full_b_down,
         full_gain_two,

time: 358 us -> 356 us (level)
    unnamed x136 -> x148, local copies, waits for them, and re-layouts: 7.26 us -> 12.2 us
    ppermute x68 -> x69, starting transfers between devices: 46.7 us -> 46 us  [exchange(): lax.ppermute(array_in, axis, [(i, i ^ flip) for i in range(lax.axis_size(...]
    ppermute x68 -> x69, waiting for transfers between devices: 117 us -> 117 us  [exchange(): lax.ppermute(array_in, axis, [(i, i ^ flip) for i in range(lax.axis_size(...]
  transfers between devices with their start and end apart: 68 -> 69, of which waited for: 32 -> 29; matrix products, arithmetic and copies ran while one was open for 11% -> 11% of each run, Pallas kernels for 23% -> 24%
where the time goes in v8:
time: 356 us; the launch traced here: 352 us
  Pallas kernels  130 us (37%)
  waiting for transfers between devices  117 us (33%)
  starting transfers between devices  46 us (13%)
  other arithmetic  30.7 us (9%)
  local copies, waits for them, and re-layouts  26.8 us (8%)
    ppermute x69, waiting for transfers between devices, exchange(): lax.ppermute(array_in, axis, [(i, i ^ flip) for i in range(lax.axis_size(...  117 us
    pallas_call x6, Pallas kernels, kernel_call(): pl.pallas_call(body, out_shape=outs, in_specs=[pl.BlockSpec(memory_space=...  63.1 us
    ppermute x69, starting transfers between devices, exchange(): lax.ppermute(array_in, axis, [(i, i ^ flip) for i in range(lax.axis_size(...  46 us
    pallas_call x1, Pallas kernels, step_call(): pl.pallas_call(body, out_shape=outs, grid_spec=pltpu.PrefetchScalarGridSp...  41.8 us
    pallas_call x4, Pallas kernels, gather_tiles(): pl.pallas_call(functools.partial(place_tiles, by_rows, late), out_shape=j...  17.1 us
    convert_element_type x9, other arithmetic, sum_low(): return total.astype(jnp.bfloat16)  16 us
    unnamed x148, local copies, waits for them, and re-layouts  12.2 us
    pallas_call x1, Pallas kernels, gather_heads(): pl.pallas_call(functools.partial(place_heads, parts), out_shape=[out(shap...  7.78 us
  transfers between devices with their start and end apart: 69, of which 29 were waited for; matrix products, arithmetic and copies ran while one was open for 11% of the time, Pallas kernels for 24%

profile of v8, /device:TPU:0, one launch (start us, length us, event | category | flops | bytes accessed | tf_op | source)
XLA Modules:
  0.0 351.9 jit_solution(9765696061459956260)
XLA Ops:
  18.3 8.4 %shard_map.280 = (bf16[192,256]{1,0:T(8,128)(2,1)}, bf16[192,256]{1,0:T(8,128)(2,1)}, bf16[192,256]{1,0:T(8,128)(2,1)}, bf16[192,256]{1,0:T(8,128)(2,1)}, bf16[1...) custom-call(s32[20]{0:T(128)} %concatenate.48.places, ...), custom_call_target="tpu_custom_call" | custom-call | flops 100000000 | bytes 1048576 | tf_op jit(solution)/shard_map/pallas_call | solution.py:230
  29.8 8.2 %shard_map.281 = (bf16[192,256]{1,0:T(8,128)(2,1)}, bf16[192,256]{1,0:T(8,128)(2,1)}, bf16[192,256]{1,0:T(8,128)(2,1)}, bf16[192,256]{1,0:T(8,128)(2,1)}, bf16[1...) custom-call(s32[20]{0:T(128)} %concatenate.48.places, ...), custom_call_target="tpu_custom_call" | custom-call | flops 100000000 | bytes 1048576 | tf_op jit(solution)/shard_map/pallas_call | solution.py:230
  42.5 8.2 %shard_map.282 = (bf16[192,256]{1,0:T(8,128)(2,1)}, bf16[192,256]{1,0:T(8,128)(2,1)}, bf16[192,256]{1,0:T(8,128)(2,1)}, bf16[192,256]{1,0:T(8,128)(2,1)}, bf16[1...) custom-call(s32[20]{0:T(128)} %concatenate.48.places, ...), custom_call_target="tpu_custom_call" | custom-call | flops 100000000 | bytes 1048576 | tf_op jit(solution)/shard_map/pallas_call | solution.py:230
  60.7 41.8 %shard_map.283 = (bf16[768,768]{1,0:T(8,128)(2,1)}, bf16[2,384,768]{2,1,0:T(8,128)(2,1)}, bf16[2,768,384]{2,1,0:T(8,128)(2,1)}, bf16[2,384,768]{2,1,0:T(8,128)(2...) custom-call(s32[20]{0:T(128)} %concatenate.48.places, ...), custom_call_target="tpu_custom_call" | custom-call | flops 24461180928 | bytes 1048576 | tf_op jit(solution)/shard_map/pallas_call | solution.py:526
  103.6 6.5 %collective-permute-done.20.g2 = bf16[2,1,192,256]{3,2,1,0:T(8,128)(2,1)S(1)} collective-permute-done((bf16[2,1,192,256]{3,2,1,0:T(8,128)(2,1)}, bf16[2,1,192,256]{3,2,1,0:T(8,128)(2,1)S(1)}, u32[]{:S(2)}, u32[]{:S(2)}) %collective-permute-start.20) | collective-permute-done | bytes 196640 | tf_op jit(solution)/shard_map/ppermute | solution.py:29
  122.9 12.4 %shard_map.284 = (bf16[2,256,768]{2,1,0:T(8,128)(2,1)}, bf16[2,256,768]{2,1,0:T(8,128)(2,1)}, f32[576,768]{1,0:T(8,128)}, f32[8,576]{1,0:T(8,128)}) custom-call(s32[20]{0:T(128)} %concatenate.48.places, bf16[1,192,256]{2,1,0:T(8,128)(2,1)} %get-tuple-element.200.g0, bf16[1,192,256]{2,1,0:T(8,128)(2,1)} %copy-done.44, bf16[2,1,192,256]{3,2,1,0:T(8,128)(2,1)} %copy-done.31, ...), custom_call_target="tpu_custom_call" | custom-call | flops 100000000 | bytes 1048576 | tf_op jit(solution)/shard_map/pallas_call | solution.py:230
  140.0 12.7 %shard_map.285 = (bf16[2,256,768]{2,1,0:T(8,128)(2,1)}, bf16[2,256,768]{2,1,0:T(8,128)(2,1)}, f32[576,768]{1,0:T(8,128)}, f32[8,576]{1,0:T(8,128)}) custom-call(s32[20]{0:T(128)} %concatenate.48.places, bf16[2,192,256]{2,1,0:T(8,128)(2,1)} %get-tuple-element.229.g0, bf16[2,192,256]{2,1,0:T(8,128)(2,1)} %copy-done.25, bf16[2,2,192,256]{3,2,1,0:T(8,128)(2,1)} %copy-done.6, ...), custom_call_target="tpu_custom_call" | custom-call | flops 100000000 | bytes 1048576 | tf_op jit(solution)/shard_map/pallas_call | solution.py:230
  165.9 13.1 %shard_map.286 = (bf16[2,256,768]{2,1,0:T(8,128)(2,1)}, bf16[2,256,768]{2,1,0:T(8,128)(2,1)}, bf16[8,112,384]{2,1,0:T(8,128)(2,1)}, bf16[8,112,384]{2,1,0:T(8,128)(2,1)}) custom-call(s32[20]{0:T(128)} %concatenate.48.places, bf16[2,192,256]{2,1,0:T(8,128)(2,1)} %get-tuple-element.229.g0, bf16[2,192,256]{2,1,0:T(8,128)(2,1)} %copy-done.25, ...), custom_call_target="tpu_custom_call" | custom-call | flops 100000000 | bytes 1048576 | tf_op jit(solution)/shard_map/pallas_call | solution.py:230
  191.6 7.8 %collective-permute-done.39 = bf16[2,96,768]{2,1,0:T(8,128)(2,1)S(1)} collective-permute-done((bf16[2,96,768]{2,1,0:T(8,128)(2,1)S(1)}, bf16[2,96,768]{2,1,0:T(8,128)(2,1)S(1)}, u32[]{:S(2)}, u32[]{:S(2)}) %collective-permute-start.39) | collective-permute-done | bytes 294944 | tf_op jit(solution)/shard_map/ppermute | solution.py:29
  199.4 5.9 %collective-permute-done.40 = bf16[2,192,384]{2,1,0:T(8,128)(2,1)S(1)} collective-permute-done((bf16[2,192,384]{2,1,0:T(8,128)(2,1)S(1)}, bf16[2,192,384]{2,1,0:T(8,128)(2,1)S(1)}, u32[]{:S(2)}, u32[]{:S(2)}) %collective-permute-start.40) | collective-permute-done | bytes 294944 | tf_op jit(solution)/shard_map/ppermute | solution.py:29
  212.6 7.6 %collective-permute-done.42 = bf16[2,112,384]{2,1,0:T(8,128)(2,1)} collective-permute-done((bf16[2,112,384]{2,1,0:T(8,128)(2,1)}, bf16[2,112,384]{2,1,0:T(8,128)(2,1)}, u32[]{:S(2)}, u32[]{:S(2)}) %collective-permute-start.42) | collective-permute-done | bytes 172064 | tf_op jit(solution)/shard_map/ppermute | solution.py:29
  226.7 7.7 %collective-permute-done.47 = bf16[2,96,768]{2,1,0:T(8,128)(2,1)S(1)} collective-permute-done((bf16[2,96,768]{2,1,0:T(8,128)(2,1)S(1)}, bf16[2,96,768]{2,1,0:T(8,128)(2,1)S(1)}, u32[]{:S(2)}, u32[]{:S(2)}) %collective-permute-start.47) | collective-permute-done | bytes 294944 | tf_op jit(solution)/shard_map/ppermute | solution.py:29
  234.5 9.0 %collective-permute-done.46 = bf16[2,112,768]{2,1,0:T(8,128)(2,1)S(1)} collective-permute-done((bf16[2,112,768]{2,1,0:T(8,128)(2,1)S(1)}, bf16[2,112,768]{2,1,0:T(8,128)(2,1)S(1)}, u32[]{:S(2)}, u32[]{:S(2)}) %collective-permute-start.46) | collective-permute-done | bytes 344096 | tf_op jit(solution)/shard_map/ppermute | solution.py:29
  250.0 9.0 %collective-permute-done.51 = bf16[2,192,384]{2,1,0:T(8,128)(2,1)S(1)} collective-permute-done((bf16[2,192,384]{2,1,0:T(8,128)(2,1)S(1)}, bf16[2,192,384]{2,1,0:T(8,128)(2,1)S(1)}, u32[]{:S(2)}, u32[]{:S(2)}) %collective-permute-start.51) | collective-permute-done | bytes 294944 | tf_op jit(solution)/shard_map/ppermute | solution.py:29
  259.2 6.6 %collective-permute-done.50 = bf16[4,96,768]{2,1,0:T(8,128)(2,1)S(1)} collective-permute-done((bf16[4,96,768]{2,1,0:T(8,128)(2,1)S(1)}, bf16[4,96,768]{2,1,0:T(8,128)(2,1)S(1)}, u32[]{:S(2)}, u32[]{:S(2)}) %collective-permute-start.50) | collective-permute-done | bytes 589856 | tf_op jit(solution)/shard_map/ppermute | solution.py:29
  268.1 8.5 %collective-permute-done.55 = bf16[2,192,384]{2,1,0:T(8,128)(2,1)S(1)} collective-permute-done((bf16[2,192,384]{2,1,0:T(8,128)(2,1)S(1)}, bf16[2,192,384]{2,1,0:T(8,128)(2,1)S(1)}, u32[]{:S(2)}, u32[]{:S(2)}) %collective-permute-start.55) | collective-permute-done | bytes 294944 | tf_op jit(solution)/shard_map/ppermute | solution.py:29
  276.7 7.1 %collective-permute-done.52 = bf16[4,112,768]{2,1,0:T(8,128)(2,1)S(1)} collective-permute-done((bf16[4,112,768]{2,1,0:T(8,128)(2,1)S(1)}, bf16[4,112,768]{2,1,0:T(8,128)(2,1)S(1)}, u32[]{:S(2)}, u32[]{:S(2)}) %collective-permute-start.52) | collective-permute-done | bytes 688160 | tf_op jit(solution)/shard_map/ppermute | solution.py:29
  287.3 4.2 %shard_map.287.refs_2_ = f32[3072,768]{1,0:T(8,128)} custom-call(s32[20]{0:T(128)} %concatenate.48.places, bf16[8,96,768]{2,1,0:T(8,128)(2,1)} %copy-done.1, bf16[8,96,768]{2,1,0:T(8,128)(2,1)} %copy-done.14), custom_call_target="tpu_custom_call" | custom-call | tf_op jit(solution)/shard_map/pallas_call | solution.py:644
  291.6 7.5 %collective-permute-done.57 = bf16[4,192,384]{2,1,0:T(8,128)(2,1)} collective-permute-done((bf16[4,192,384]{2,1,0:T(8,128)(2,1)S(1)}, bf16[4,192,384]{2,1,0:T(8,128)(2,1)}, u32[]{:S(2)}, u32[]{:S(2)}) %collective-permute-start.57) | collective-permute-done | bytes 589856 | tf_op jit(solution)/shard_map/ppermute | solution.py:29
  311.2 4.2 %shard_map.289.refs_2_ = f32[768,3072]{1,0:T(8,128)} custom-call(s32[20]{0:T(128)} %concatenate.48.places, bf16[8,192,384]{2,1,0:T(8,128)(2,1)} %copy-done.2, bf16[8,192,384]{2,1,0:T(8,128)(2,1)} %copy-done.16), custom_call_target="tpu_custom_call" | custom-call | tf_op jit(solution)/shard_map/pallas_call | solution.py:644
  315.5 4.4 %shard_map.288 = f32[3072,768]{1,0:T(8,128)} custom-call(s32[20]{0:T(128)} %concatenate.48.places, bf16[8,96,768]{2,1,0:T(8,128)(2,1)} %copy-done.4, bf16[8,96,768]{2,1,0:T(8,128)(2,1)} %collective-permute-done.62.refs_1_, f32[3072,768]{1,0:T(8,128)} %shard_map.287.refs_2_), custom_call_target="tpu_custom_call", output_to_operand_aliasing={{}: (3, {})} | custom-call | tf_op jit(solution)/shard_map/pallas_call | solution.py:644
  324.3 8.6 %collective-permute-done.64 = bf16[2,192,384]{2,1,0:T(8,128)(2,1)S(1)} collective-permute-done((bf16[2,192,384]{2,1,0:T(8,128)(2,1)S(1)}, bf16[2,192,384]{2,1,0:T(8,128)(2,1)S(1)}, u32[]{:S(2)}, u32[]{:S(2)}) %collective-permute-start.64) | collective-permute-done | bytes 294944 | tf_op jit(solution)/shard_map/ppermute | solution.py:29
  334.9 7.8 %shard_map.290 = (f32[768,2304]{1,0:T(8,128)}, f32[768,768]{1,0:T(8,128)}, f32[16,768]{1,0:T(8,128)}, f32[8,768]{1,0:T(8,128)}) custom-call(s32[20]{0:T(128)} %concatenate.48.places, bf16[8,112,768]{2,1,0:T(8,128)(2,1)} %bitcast.97, bf16[8,112,768]{2,1,0:T(8,128)(2,1)} %collective-permute-done.60.refs_1_, ...), custom_call_target="tpu_custom_call" | custom-call | tf_op jit(solution)/shard_map/pallas_call | solution.py:738
  347.4 4.2 %shard_map.291 = f32[768,3072]{1,0:T(8,128)} custom-call(s32[20]{0:T(128)} %concatenate.48.places, bf16[8,192,384]{2,1,0:T(8,128)(2,1)} %copy-done.5, bf16[8,192,384]{2,1,0:T(8,128)(2,1)} %copy-done.15, f32[768,3072]{1,0:T(8,128)} %shard_map.289.refs_2_), custom_call_target="tpu_custom_call", output_to_operand_aliasing={{}: (3, {})} | custom-call | tf_op jit(solution)/shard_map/pallas_call | solution.py:644
  (356 shorter events, 128.5 us)
Async XLA Ops:
  110.2 25.1 %collective-permute-start.25 = (bf16[2,384,768]{2,1,0:T(8,128)(2,1)}, bf16[2,384,768]{2,1,0:T(8,128)(2,1)}, u32[]{:S(2)}, u32[]{:S(2)}) collective-permute-start(bf16[2,384,768]{2,1,0:T(8,128)(2,1)} %get-tuple-element.223), channel_id=1, source_target_pairs={{0,1},{1,0},{2,3},{3,2},{4,5},{5,4},{6,7},{7,6},{8,9},{9,8},{10,11... | collective-permute-start | bytes 3538952 | tf_op jit(solution)/shard_map/ppermute | solution.py:29
  110.7 24.6 %collective-permute-start.24 = (bf16[2,2,192,256]{3,2,1,0:T(8,128)(2,1)}, bf16[2,2,192,256]{3,2,1,0:T(8,128)(2,1)S(1)}, u32[]{:S(2)}, u32[]{:S(2)}) collective-permute-start(bf16[2,2,192,256]{3,2,1,0:T(8,128)(2,1)} %get-tuple-element.220), channel_id=1, source_target_pairs={{0,2},{1,3},{2,0},{3,1},{4,6},{5,7},{6,4},{7,5},{8,10},{9,11},{10,... | collective-permute-start | bytes 1179656 | tf_op jit(solution)/shard_map/ppermute | solution.py:29
  117.7 38.2 %collective-permute-start.26 = (bf16[2,384,768]{2,1,0:T(8,128)(2,1)S(1)}, bf16[2,384,768]{2,1,0:T(8,128)(2,1)}, u32[]{:S(2)}, u32[]{:S(2)}) collective-permute-start(bf16[2,384,768]{2,1,0:T(8,128)(2,1)S(1)} %add_convert_fusion.1), channel_id=1, source_target_pairs={{0,4},{4,0},{8,12},{12,8},{16,20},{20,16},{24,28},{28,24},{1,5},{5... | collective-permute-start | bytes 3538952 | tf_op jit(solution)/shard_map/ppermute | solution.py:29
  119.2 36.6 %collective-permute-start.27 = (bf16[2,768,384]{2,1,0:T(8,128)(2,1)}, bf16[2,768,384]{2,1,0:T(8,128)(2,1)S(1)}, u32[]{:S(2)}, u32[]{:S(2)}) collective-permute-start(bf16[2,768,384]{2,1,0:T(8,128)(2,1)} %add_convert_fusion), channel_id=1, source_target_pairs={{0,8},{4,12},{8,0},{12,4},{16,24},{20,28},{24,16},{28,20},{1,9},{5... | collective-permute-start | bytes 3538952 | tf_op jit(solution)/shard_map/ppermute | solution.py:29
  135.3 17.5 %collective-permute-start.31 = (bf16[2,256,768]{2,1,0:T(8,128)(2,1)}, bf16[2,256,768]{2,1,0:T(8,128)(2,1)}, u32[]{:S(2)}, u32[]{:S(2)}) collective-permute-start(bf16[2,256,768]{2,1,0:T(8,128)(2,1)} %get-tuple-element.243), channel_id=1, source_target_pairs={{0,1},{1,0},{2,3},{3,2},{4,5},{5,4},{6,7},{7,6},{8,9},{9,8},{10,11... | collective-permute-start | bytes 2359304 | tf_op jit(solution)/shard_map/ppermute | solution.py:29
  136.0 19.9 %collective-permute-start.28 = (bf16[2,8,96,192]{3,2,1,0:T(8,128)(2,1)}, bf16[2,8,96,192]{3,2,1,0:T(8,128)(2,1)}, u32[]{:S(2)}, u32[]{:S(2)}) collective-permute-start(bf16[2,8,96,192]{3,2,1,0:T(8,128)(2,1)} %get-tuple-element.228), channel_id=1, source_target_pairs={{0,2},{1,3},{2,0},{3,1},{4,6},{5,7},{6,4},{7,5},{8,10},{9,11},{10,... | collective-permute-start | bytes 1769480 | tf_op jit(solution)/shard_map/ppermute | solution.py:29
  157.4 21.7 %collective-permute-start.35 = (bf16[2,256,768]{2,1,0:T(8,128)(2,1)}, bf16[2,256,768]{2,1,0:T(8,128)(2,1)S(1)}, u32[]{:S(2)}, u32[]{:S(2)}) collective-permute-start(bf16[2,256,768]{2,1,0:T(8,128)(2,1)} %get-tuple-element.255), channel_id=1, source_target_pairs={{0,1},{1,0},{2,3},{3,2},{4,5},{5,4},{6,7},{7,6},{8,9},{9,8},{10,11... | collective-permute-start | bytes 2359304 | tf_op jit(solution)/shard_map/ppermute | solution.py:29
  164.3 15.6 %collective-permute-start.33 = (bf16[384,768]{1,0:T(8,128)(2,1)}, bf16[384,768]{1,0:T(8,128)(2,1)}, u32[]{:S(2)}, u32[]{:S(2)}) collective-permute-start(bf16[384,768]{1,0:T(8,128)(2,1)} %fusion.4), channel_id=1, source_target_pairs={{0,8},{4,12},{8,0},{12,4},{16,24},{20,28},{24,16},{28,20},{1,9},{5... | collective-permute-start | bytes 1769480 | tf_op jit(solution)/shard_map/ppermute | solution.py:29
  186.5 18.9 %collective-permute-start.37 = (bf16[4,112,384]{2,1,0:T(8,128)(2,1)S(1)}, bf16[4,112,384]{2,1,0:T(8,128)(2,1)S(1)}, u32[]{:S(2)}, u32[]{:S(2)}) collective-permute-start(bf16[4,112,384]{2,1,0:T(8,128)(2,1)S(1)} %get-tuple-element.273), channel_id=1, source_target_pairs={{0,4},{4,0},{8,12},{12,8},{16,20},{20,16},{24,28},{28,24},{1,5},{5... | collective-permute-start | bytes 1032200 | tf_op jit(solution)/shard_map/ppermute | solution.py:29
  188.0 17.5 %collective-permute-start.38 = (bf16[2,2,112,384]{3,2,1,0:T(8,128)(2,1)S(1)}, bf16[2,2,112,384]{3,2,1,0:T(8,128)(2,1)S(1)}, u32[]{:S(2)}, u32[]{:S(2)}) collective-permute-start(bf16[2,2,112,384]{3,2,1,0:T(8,128)(2,1)S(1)} %get-tuple-element.275), channel_id=1, source_target_pairs={{0,8},{4,12},{8,0},{12,4},{16,24},{20,28},{24,16},{28,20},{1,9},{5... | collective-permute-start | bytes 1032200 | tf_op jit(solution)/shard_map/ppermute | solution.py:29
  189.5 16.8 %collective-permute-start.41 = (bf16[2,256,768]{2,1,0:T(8,128)(2,1)S(1)}, bf16[2,256,768]{2,1,0:T(8,128)(2,1)S(1)}, u32[]{:S(2)}, u32[]{:S(2)}) collective-permute-start(bf16[2,256,768]{2,1,0:T(8,128)(2,1)S(1)} %copy-done.56), channel_id=1, source_target_pairs={{0,1},{1,0},{2,3},{3,2},{4,5},{5,4},{6,7},{7,6},{8,9},{9,8},{10,11... | collective-permute-start | bytes 2359304 | tf_op jit(solution)/shard_map/ppermute | solution.py:29
  207.6 15.9 %collective-permute-start.44 = (bf16[2,96,768]{2,1,0:T(8,128)(2,1)S(1)}, bf16[2,96,768]{2,1,0:T(8,128)(2,1)}, u32[]{:S(2)}, u32[]{:S(2)}) collective-permute-start(bf16[2,96,768]{2,1,0:T(8,128)(2,1)S(1)} %add.206), channel_id=1, source_target_pairs={{0,16},{4,20},{8,24},{12,28},{16,0},{20,4},{24,8},{28,12},{1,17},{... | collective-permute-start | bytes 884744 | tf_op jit(solution)/shard_map/ppermute | solution.py:29
  226.1 17.5 %collective-permute-start.46 = (bf16[2,112,768]{2,1,0:T(8,128)(2,1)S(1)}, bf16[2,112,768]{2,1,0:T(8,128)(2,1)S(1)}, u32[]{:S(2)}, u32[]{:S(2)}) collective-permute-start(bf16[2,112,768]{2,1,0:T(8,128)(2,1)S(1)} %pad_maximum_fusion.7), channel_id=1, source_target_pairs={{0,16},{4,20},{8,24},{12,28},{16,0},{20,4},{24,8},{28,12},{1,17},{... | collective-permute-start | bytes 1032200 | tf_op jit(solution)/shard_map/ppermute | solution.py:29
  226.1 17.5 %collective-permute-start.48 = (bf16[256,768]{1,0:T(8,128)(2,1)S(1)}, bf16[256,768]{1,0:T(8,128)(2,1)S(1)}, u32[]{:S(2)}, u32[]{:S(2)}) collective-permute-start(bf16[256,768]{1,0:T(8,128)(2,1)S(1)} %copy-done.36), channel_id=1, source_target_pairs={{0,2},{1,3},{2,0},{3,1},{4,6},{5,7},{6,4},{7,5},{8,10},{9,11},{10,... | collective-permute-start | bytes 1179656 | tf_op jit(solution)/shard_map/ppermute | solution.py:29
  243.7 15.4 %collective-permute-start.49 = (bf16[2,112,768]{2,1,0:T(8,128)(2,1)S(1)}, bf16[2,112,768]{2,1,0:T(8,128)(2,1)S(1)}, u32[]{:S(2)}, u32[]{:S(2)}) collective-permute-start(bf16[2,112,768]{2,1,0:T(8,128)(2,1)S(1)} %reverse_add_fusion), channel_id=1, source_target_pairs={{0,4},{4,0},{8,12},{12,8},{16,20},{20,16},{24,28},{28,24},{1,5},{5... | collective-permute-start | bytes 1032200 | tf_op jit(solution)/shard_map/ppermute | solution.py:29
  244.3 21.5 %collective-permute-start.50 = (bf16[4,96,768]{2,1,0:T(8,128)(2,1)S(1)}, bf16[4,96,768]{2,1,0:T(8,128)(2,1)S(1)}, u32[]{:S(2)}, u32[]{:S(2)}) collective-permute-start(bf16[4,96,768]{2,1,0:T(8,128)(2,1)S(1)} %pad_maximum_fusion.5), channel_id=1, source_target_pairs={{0,8},{4,12},{8,0},{12,4},{16,24},{20,28},{24,16},{28,20},{1,9},{5... | collective-permute-start | bytes 1769480 | tf_op jit(solution)/shard_map/ppermute | solution.py:29
  265.8 18.1 %collective-permute-start.53 = (bf16[8,96,768]{2,1,0:T(8,128)(2,1)S(1)}, bf16[8,96,768]{2,1,0:T(8,128)(2,1)S(1)}, u32[]{:S(2)}, u32[]{:S(2)}) collective-permute-start(bf16[8,96,768]{2,1,0:T(8,128)(2,1)S(1)} %pad_maximum_fusion.1.refs_0_), channel_id=1, source_target_pairs={{0,1},{1,0},{2,3},{3,2},{4,5},{5,4},{6,7},{7,6},{8,9},{9,8},{10,11... | collective-permute-start | bytes 3538952 | tf_op jit(solution)/shard_map/ppermute | solution.py:29
  265.9 17.9 %collective-permute-start.52 = (bf16[4,112,768]{2,1,0:T(8,128)(2,1)S(1)}, bf16[4,112,768]{2,1,0:T(8,128)(2,1)S(1)}, u32[]{:S(2)}, u32[]{:S(2)}) collective-permute-start(bf16[4,112,768]{2,1,0:T(8,128)(2,1)S(1)} %pad_maximum_fusion.4), channel_id=1, source_target_pairs={{0,8},{4,12},{8,0},{12,4},{16,24},{20,28},{24,16},{28,20},{1,9},{5... | collective-permute-start | bytes 2064392 | tf_op jit(solution)/shard_map/ppermute | solution.py:29
  266.1 17.9 %collective-permute-start.54 = (bf16[4,96,768]{2,1,0:T(8,128)(2,1)S(1)}, bf16[4,96,768]{2,1,0:T(8,128)(2,1)S(1)}, u32[]{:S(2)}, u32[]{:S(2)}) collective-permute-start(bf16[4,96,768]{2,1,0:T(8,128)(2,1)S(1)} %slice.244), channel_id=1, source_target_pairs={{0,4},{4,0},{8,12},{12,8},{16,20},{20,16},{24,28},{28,24},{1,5},{5... | collective-permute-start | bytes 1769480 | tf_op jit(solution)/shard_map/ppermute | solution.py:29
  284.3 15.9 %collective-permute-start.58 = (bf16[4,96,768]{2,1,0:T(8,128)(2,1)S(1)}, bf16[4,96,768]{2,1,0:T(8,128)(2,1)}, u32[]{:S(2)}, u32[]{:S(2)}) collective-permute-start(bf16[4,96,768]{2,1,0:T(8,128)(2,1)S(1)} %slice.246), channel_id=1, source_target_pairs={{0,4},{4,0},{8,12},{12,8},{16,20},{20,16},{24,28},{28,24},{1,5},{5... | collective-permute-start | bytes 1769480 | tf_op jit(solution)/shard_map/ppermute | solution.py:29
  286.8 16.9 %collective-permute-start.56 = (bf16[4,112,768]{2,1,0:T(8,128)(2,1)}, bf16[4,112,768]{2,1,0:T(8,128)(2,1)}, u32[]{:S(2)}, u32[]{:S(2)}) collective-permute-start(bf16[4,112,768]{2,1,0:T(8,128)(2,1)} %slice.245), channel_id=1, source_target_pairs={{0,2},{1,3},{2,0},{3,1},{4,6},{5,7},{6,4},{7,5},{8,10},{9,11},{10,... | collective-permute-start | bytes 2064392 | tf_op jit(solution)/shard_map/ppermute | solution.py:29
  303.7 19.6 %collective-permute-start.60 = (bf16[8,112,768]{2,1,0:T(8,128)(2,1)S(1)}, bf16[8,112,768]{2,1,0:T(8,128)(2,1)}, u32[]{:S(2)}, u32[]{:S(2)}) collective-permute-start(bf16[8,112,768]{2,1,0:T(8,128)(2,1)S(1)} %bitcast.95), channel_id=1, source_target_pairs={{0,1},{1,0},{2,3},{3,2},{4,5},{5,4},{6,7},{7,6},{8,9},{9,8},{10,11... | collective-permute-start | bytes 4128776 | tf_op jit(solution)/shard_map/ppermute | solution.py:29
  305.1 18.2 %collective-permute-start.59 = (bf16[4,112,768]{2,1,0:T(8,128)(2,1)}, bf16[4,112,768]{2,1,0:T(8,128)(2,1)}, u32[]{:S(2)}, u32[]{:S(2)}) collective-permute-start(bf16[4,112,768]{2,1,0:T(8,128)(2,1)} %slice.247), channel_id=1, source_target_pairs={{0,2},{1,3},{2,0},{3,1},{4,6},{5,7},{6,4},{7,5},{8,10},{9,11},{10,... | collective-permute-start | bytes 2064392 | tf_op jit(solution)/shard_map/ppermute | solution.py:29
  306.6 15.8 %collective-permute-start.61 = (bf16[4,192,384]{2,1,0:T(8,128)(2,1)}, bf16[4,192,384]{2,1,0:T(8,128)(2,1)}, u32[]{:S(2)}, u32[]{:S(2)}) collective-permute-start(bf16[4,192,384]{2,1,0:T(8,128)(2,1)} %slice.248), channel_id=1, source_target_pairs={{0,4},{4,0},{8,12},{12,8},{16,20},{20,16},{24,28},{28,24},{1,5},{5... | collective-permute-start | bytes 1769480 | tf_op jit(solution)/shard_map/ppermute | solution.py:29
  (117 other events, 865.0 us)

commit v9 on v8

--- a/solution.py
+++ b/solution.py
@@ -608,7 +608,7 @@
 
 
 def place_tiles(by_rows, late, places, *refs):
-    sources, out = refs[:2], refs[-4]
+    sources, out = refs[:4], refs[-4]
     held, main, sems = refs[-3:]
     inner = places[8]
     _, rows, cols = sources[0].shape
@@ -617,43 +617,44 @@
     ]
     for copy in bring:
         copy.start()
+    for copy in bring:
+        copy.wait()
     sent = []
-    for k, copy in enumerate(bring):
-        copy.wait()
+    for k in range(2):
         for l in range(2):
             block = places[k * 4 + late * 2 + l]
             place = 2 * k + l
             for q in range(4):
+                h, x = q >> 1, q & 1
+                half, n = (x, l * 2 + h) if by_rows else (l, x * 2 + h)
                 first = pl.multiple_of((q ^ inner) * rows, rows)
-                main[place, pl.ds(first, rows), :] = held[k, l * 4 + (q & 1) * 2 + (q >> 1)].astype(
-                    jnp.float32
-                )
+                main[place, pl.ds(first, rows), :] = held[2 * k + half, n].astype(jnp.float32)
             if by_rows:
                 target = out.at[pl.ds(pl.multiple_of(block * 4 * rows, 4 * rows), 4 * rows)]
             else:
                 target = out.at[:, pl.ds(pl.multiple_of(block * cols, cols), cols)]
-            sent.append(pltpu.make_async_copy(main.at[place], target, sems.at[2 + place]))
+            sent.append(pltpu.make_async_copy(main.at[place], target, sems.at[4 + place]))
             sent[-1].start()
     for copy in sent:
         copy.wait()
 
 
-def gather_tiles(places, pieces, late, begun, shape, by_rows):
-    _, rows, cols = pieces[0].shape
+def gather_tiles(places, halves, late, begun, shape, by_rows):
+    _, rows, cols = halves[0].shape
     away = pl.BlockSpec(memory_space=pl.ANY)
     return pl.pallas_call(
         functools.partial(place_tiles, by_rows, late),
         out_shape=jax.ShapeDtypeStruct(shape, jnp.float32),
-        in_specs=[pl.BlockSpec(memory_space=pltpu.SMEM)] + [away] * (2 + len(begun)),
+        in_specs=[pl.BlockSpec(memory_space=pltpu.SMEM)] + [away] * (4 + len(begun)),
         out_specs=away,
         scratch_shapes=[
-            pltpu.VMEM((2, 8, rows, cols), jnp.bfloat16),
+            pltpu.VMEM((4, 4, rows, cols), jnp.bfloat16),
             pltpu.VMEM((4, 4 * rows, cols), jnp.float32),
-            pltpu.SemaphoreType.DMA((6,)),
+            pltpu.SemaphoreType.DMA((8,)),
         ],
-        input_output_aliases={3: 0} if begun else {},
+        input_output_aliases={5: 0} if begun else {},
         compiler_params=pltpu.CompilerParams(vmem_limit_bytes=VMEM_LIMIT),
-    )(places, *pieces, *begun)
+    )(places, *halves, *begun)
 
 
 def place_heads(parts, places, *refs):
@@ -923,7 +924,6 @@
     half_b = half_b.reshape(2, 2, 2, *half_b.shape[1:])
     keeps = [half_a[:4], half_b[:, 0], down_own[:, 0], up_own[:, 0]]
     sends = [half_a[4:], half_b[:, 1], down_own[:, 1], up_own[:, 1]]
-    (keeps, sends) = lax.optimization_barrier((keeps, sends))
     got = [exchange_bit(v, bit) for v, bit in zip(sends, "ylxx")]
     half_a, half_b, down, up = [k + g for k, g in zip(keeps, got)]
     near_far = far[1:]
@@ -943,12 +943,12 @@
     (both, down, up, far, far_came) = lax.optimization_barrier((both, down, up, far, far_came))
     far_came += [exchange_bit(v, "x") for v in far]
     came = exchange_bit(both, "h")
-    down = jnp.concatenate([down, exchange_bit(down, "x")])
+    down = jnp.concatenate([down, exchange_bit(down, "l")])
     both = add_extra(both + came[::-1])
 
     (both, down, up, far_came) = lax.optimization_barrier((both, down, up, far_came))
     came, up_came = exchange_bit(both, "y"), exchange_bit(up, "h")
-    down = jnp.concatenate([down, exchange_bit(down, "l")])
+    down_hi = exchange_bit(down, "x")
     both = jnp.concatenate([both, came])
     up = add_extra(up + up_came[::-1])
     own_pos = mine * local_rows + jnp.arange(local_rows, dtype=jnp.int32)
@@ -957,57 +957,66 @@
     grad_tokens = (d_inputs + d_first_in.reshape(seq_count, local_rows, features)) * live[:, :, None]
 
 
-    (both, down, up, grad_tokens) = lax.optimization_barrier((both, down, up, grad_tokens))
+    (both, down, down_hi, up, grad_tokens) = lax.optimization_barrier(
+        (both, down, down_hi, up, grad_tokens)
+    )
     came = exchange_bit(both, "l")
-    down_first = exchange_bit(down[:4], "y")
+    down_far = [exchange_bit(down, "y")]
     up_came = exchange_bit(up, "x")
-    down_near = exchange_bit(down, "c")
-    both = jnp.stack([both.reshape(2, 2, *both.shape[1:]), came.reshape(2, 2, *came.shape[1:])], 1)
-    both = both.reshape(8, *both.shape[3:])
+    down_own = [down, down_hi]
+    down_near = [exchange_bit(half, "c") for half in down_own]
+    both = [jnp.concatenate([v[:2] for v in (both, came)]), jnp.concatenate([v[2:] for v in (both, came)])]
     up = jnp.concatenate([up, up_came])
 
-    (both, down, down_near, down_first, up) = lax.optimization_barrier(
-        (both, down, down_near, down_first, up)
-    )
-    both_first = exchange_bit(both[:4], "x")
-    down_second = exchange_bit(down[4:], "y")
-    up_came = exchange_bit(up, "l")
-    full_down = gather_tiles(places, [down, down_near], 0, [], (hidden, features), True)
-    down_last = jnp.concatenate([down_first, down_second])
-    up = jnp.concatenate([up, up_came])
-
-    (both, both_first, up, down_last, full_down) = lax.optimization_barrier(
-        (both, both_first, up, down_last, full_down)
-    )
-    both_second = exchange_bit(both[4:], "x")
-    up_first = exchange_bit(up[:4], "y")
-    down_far = exchange_bit(down_last, "c")
-    both_near, up_near = exchange_bit(both, "c"), exchange_bit(up, "c")
-    full_down = gather_tiles(places, [down_last, down_far], 1, [full_down], (hidden, features), True)
-    full_up = gather_tiles(places, [up, up_near], 0, [], (features, hidden), False)
-
-    (both_second, both_near, up, up_first, full_down, full_up) = lax.optimization_barrier(
-        (both_second, both_near, up, up_first, full_down, full_up)
-    )
-    up_second = exchange_bit(up[4:6], "y")
-    first_far, second_far = exchange_bit(both_first, "c"), exchange_bit(both_second, "c")
-
-    (up, up_second, first_far, second_far) = lax.optimization_barrier(
-        (up, up_second, first_far, second_far)
-    )
-    up_third = exchange_bit(up[6:], "y")
+    (both, down_own, down_near, down_far, up) = lax.optimization_barrier(
+        (both, down_own, down_near, down_far, up)
+    )
+    across = [exchange_bit(both[0], "x")]
+    down_far.append(exchange_bit(down_own[1], "y"))
+    up_hi = exchange_bit(up, "l")
+    across_down = [exchange_bit(down_far[0], "c")]
+    both_near = [exchange_bit(both[0], "c")]
+    full_down = gather_tiles(places, down_own + down_near, 0, [], (hidden, features), True)
+
+    (both, across, up, up_hi, down_far, across_down, both_near, full_down) = (
+        lax.optimization_barrier(
+            (both, across, up, up_hi, down_far, across_down, both_near, full_down)
+        )
+    )
+    across.append(exchange_bit(both[1], "x"))
+    up_far = [exchange_bit(up, "y")]
+    across_down.append(exchange_bit(down_far[1], "c"))
+    up_own = [up, up_hi]
+    up_near = [exchange_bit(half, "c") for half in up_own]
+    full_down = gather_tiles(
+        places, down_far + across_down, 1, [full_down], (hidden, features), True
+    )
+    full_up = gather_tiles(places, up_own + up_near, 0, [], (features, hidden), False)
+
+    (both, across, up_hi, up_far, full_down, full_up) = lax.optimization_barrier(
+        (both, across, up_hi, up_far, full_down, full_up)
+    )
+    up_second = [exchange_bit(up_hi[:2], "y")]
+    both_near.append(exchange_bit(both[1], "c"))
+    both_far = [exchange_bit(half, "c") for half in across]
+
+    (up_hi, up_second, both_near, both_far) = lax.optimization_barrier(
+        (up_hi, up_second, both_near, both_far)
+    )
+    up_second.append(exchange_bit(up_hi[2:], "y"))
+    across_up = [exchange_bit(up_far[0], "c")]
     full_qkv, full_out, vector_rows, head_rows = gather_heads(
         places,
-        [both, both_near, both_first, both_second, first_far, second_far],
-        ((0, 0), (1, 0), (2, 0), (2, 4), (3, 0), (3, 4)),
+        both + both_near + across + both_far,
+        tuple((r, first) for r in range(4) for first in (0, 4)),
         (features, 3 * features),
     )
-    (up_third, full_qkv, vector_rows, head_rows) = lax.optimization_barrier(
-        (up_third, full_qkv, vector_rows, head_rows)
-    )
-    up_last = jnp.concatenate([up_first, up_second, up_third])
-    up_far = exchange_bit(up_last, "c")
-    full_up = gather_tiles(places, [up_last, up_far], 1, [full_up], (features, hidden), False)
+    (up_second, across_up, full_qkv, vector_rows, head_rows) = lax.optimization_barrier(
+        (up_second, across_up, full_qkv, vector_rows, head_rows)
+    )
+    up_far.append(jnp.concatenate(up_second))
+    across_up.append(exchange_bit(up_far[1], "c"))
+    full_up = gather_tiles(places, up_far + across_up, 1, [full_up], (features, hidden), False)
     (
         full_b_down,
         full_gain_two,

time: 356 us -> 340 us (0.955)
  waiting for transfers between devices: 117 us -> 95.7 us
  starting transfers between devices: 46 us -> 56.7 us
  local copies, waits for them, and re-layouts: 26.8 us -> 22.5 us
    ppermute x69 -> x74, waiting for transfers between devices: 117 us -> 95.7 us  [exchange(): lax.ppermute(array_in, axis, [(i, i ^ flip) for i in range(lax.axis_size(...]
    ppermute x69 -> x74, starting transfers between devices: 46 us -> 56.7 us  [exchange(): lax.ppermute(array_in, axis, [(i, i ^ flip) for i in range(lax.axis_size(...]
    unnamed x148 -> x161, local copies, waits for them, and re-layouts: 12.2 us -> 10 us
  transfers between devices with their start and end apart: 69 -> 74, of which waited for: 29 -> 30; matrix products, arithmetic and copies ran while one was open for 11% -> 10% of each run, Pallas kernels for 24% -> 25%
where the time goes in v9:
time: 340 us; the launch traced here: 336 us
  Pallas kernels  131 us (39%)
  waiting for transfers between devices  95.7 us (28%)
  starting transfers between devices  56.7 us (17%)
  other arithmetic  27.7 us (8%)
  local copies, waits for them, and re-layouts  22.5 us (7%)
    ppermute x74, waiting for transfers between devices, exchange(): lax.ppermute(array_in, axis, [(i, i ^ flip) for i in range(lax.axis_size(...  95.7 us
    pallas_call x6, Pallas kernels, kernel_call(): pl.pallas_call(body, out_shape=outs, in_specs=[pl.BlockSpec(memory_space=...  63.1 us
    ppermute x74, starting transfers between devices, exchange(): lax.ppermute(array_in, axis, [(i, i ^ flip) for i in range(lax.axis_size(...  56.7 us
    pallas_call x1, Pallas kernels, step_call(): pl.pallas_call(body, out_shape=outs, grid_spec=pltpu.PrefetchScalarGridSp...  41.8 us
    pallas_call x4, Pallas kernels, gather_tiles(): pl.pallas_call(functools.partial(place_tiles, by_rows, late), out_shape=j...  18.5 us
    convert_element_type x9, other arithmetic, sum_low(): return total.astype(jnp.bfloat16)  16.1 us
    unnamed x161, local copies, waits for them, and re-layouts  10 us
    pallas_call x1, Pallas kernels, gather_heads(): pl.pallas_call(functools.partial(place_heads, parts), out_shape=[out(shap...  7.8 us
  transfers between devices with their start and end apart: 74, of which 30 were waited for; matrix products, arithmetic and copies ran while one was open for 10% of the time, Pallas kernels for 25%

profile of v9, /device:TPU:0, one launch (start us, length us, event | category | flops | bytes accessed | tf_op | source)
XLA Modules:
  0.0 335.7 jit_solution(15697259592953023349)
XLA Ops:
  18.3 8.4 %shard_map.280 = (bf16[192,256]{1,0:T(8,128)(2,1)}, bf16[192,256]{1,0:T(8,128)(2,1)}, bf16[192,256]{1,0:T(8,128)(2,1)}, bf16[192,256]{1,0:T(8,128)(2,1)}, bf16[1...) custom-call(s32[20]{0:T(128)} %concatenate.45.places, ...), custom_call_target="tpu_custom_call" | custom-call | flops 100000000 | bytes 1048576 | tf_op jit(solution)/shard_map/pallas_call | solution.py:230
  29.8 8.2 %shard_map.281 = (bf16[192,256]{1,0:T(8,128)(2,1)}, bf16[192,256]{1,0:T(8,128)(2,1)}, bf16[192,256]{1,0:T(8,128)(2,1)}, bf16[192,256]{1,0:T(8,128)(2,1)}, bf16[1...) custom-call(s32[20]{0:T(128)} %concatenate.45.places, ...), custom_call_target="tpu_custom_call" | custom-call | flops 100000000 | bytes 1048576 | tf_op jit(solution)/shard_map/pallas_call | solution.py:230
  42.5 8.2 %shard_map.282 = (bf16[192,256]{1,0:T(8,128)(2,1)}, bf16[192,256]{1,0:T(8,128)(2,1)}, bf16[192,256]{1,0:T(8,128)(2,1)}, bf16[192,256]{1,0:T(8,128)(2,1)}, bf16[1...) custom-call(s32[20]{0:T(128)} %concatenate.45.places, ...), custom_call_target="tpu_custom_call" | custom-call | flops 100000000 | bytes 1048576 | tf_op jit(solution)/shard_map/pallas_call | solution.py:230
  60.6 41.8 %shard_map.283 = (bf16[768,768]{1,0:T(8,128)(2,1)}, bf16[2,384,768]{2,1,0:T(8,128)(2,1)}, bf16[2,768,384]{2,1,0:T(8,128)(2,1)}, bf16[2,384,768]{2,1,0:T(8,128)(2...) custom-call(s32[20]{0:T(128)} %concatenate.45.places, ...), custom_call_target="tpu_custom_call" | custom-call | flops 24461180928 | bytes 1048576 | tf_op jit(solution)/shard_map/pallas_call | solution.py:526
  103.5 6.6 %collective-permute-done.20.g2 = bf16[2,1,192,256]{3,2,1,0:T(8,128)(2,1)S(1)} collective-permute-done((bf16[2,1,192,256]{3,2,1,0:T(8,128)(2,1)}, bf16[2,1,192,256]{3,2,1,0:T(8,128)(2,1)S(1)}, u32[]{:S(2)}, u32[]{:S(2)}) %collective-permute-start.20) | collective-permute-done | bytes 196640 | tf_op jit(solution)/shard_map/ppermute | solution.py:29
  122.8 12.4 %shard_map.284 = (bf16[2,256,768]{2,1,0:T(8,128)(2,1)}, bf16[2,256,768]{2,1,0:T(8,128)(2,1)}, f32[576,768]{1,0:T(8,128)}, f32[8,576]{1,0:T(8,128)}) custom-call(s32[20]{0:T(128)} %concatenate.45.places, bf16[1,192,256]{2,1,0:T(8,128)(2,1)} %get-tuple-element.207.g0, bf16[1,192,256]{2,1,0:T(8,128)(2,1)} %copy-done.51, bf16[2,1,192,256]{3,2,1,0:T(8,128)(2,1)} %copy-done.36, ...), custom_call_target="tpu_custom_call" | custom-call | flops 100000000 | bytes 1048576 | tf_op jit(solution)/shard_map/pallas_call | solution.py:230
  140.0 12.7 %shard_map.285 = (bf16[2,256,768]{2,1,0:T(8,128)(2,1)}, bf16[2,256,768]{2,1,0:T(8,128)(2,1)}, f32[576,768]{1,0:T(8,128)}, f32[8,576]{1,0:T(8,128)}) custom-call(s32[20]{0:T(128)} %concatenate.45.places, bf16[2,192,256]{2,1,0:T(8,128)(2,1)} %get-tuple-element.236.g0, bf16[2,192,256]{2,1,0:T(8,128)(2,1)} %copy-done.23, bf16[2,2,192,256]{3,2,1,0:T(8,128)(2,1)} %copy-done.2, ...), custom_call_target="tpu_custom_call" | custom-call | flops 100000000 | bytes 1048576 | tf_op jit(solution)/shard_map/pallas_call | solution.py:230
  165.8 13.1 %shard_map.286 = (bf16[2,256,768]{2,1,0:T(8,128)(2,1)}, bf16[2,256,768]{2,1,0:T(8,128)(2,1)}, bf16[8,112,384]{2,1,0:T(8,128)(2,1)}, bf16[8,112,384]{2,1,0:T(8,128)(2,1)}) custom-call(s32[20]{0:T(128)} %concatenate.45.places, bf16[2,192,256]{2,1,0:T(8,128)(2,1)} %get-tuple-element.236.g0, bf16[2,192,256]{2,1,0:T(8,128)(2,1)} %copy-done.23, ...), custom_call_target="tpu_custom_call" | custom-call | flops 100000000 | bytes 1048576 | tf_op jit(solution)/shard_map/pallas_call | solution.py:230
  189.4 4.7 %collective-permute-done.40 = bf16[2,192,384]{2,1,0:T(8,128)(2,1)S(1)} collective-permute-done((bf16[2,192,384]{2,1,0:T(8,128)(2,1)S(1)}, bf16[2,192,384]{2,1,0:T(8,128)(2,1)S(1)}, u32[]{:S(2)}, u32[]{:S(2)}) %collective-permute-start.40) | collective-permute-done | bytes 294944 | tf_op jit(solution)/shard_map/ppermute | solution.py:29
  194.1 4.4 %collective-permute-done.39 = bf16[2,96,768]{2,1,0:T(8,128)(2,1)S(1)} collective-permute-done((bf16[2,96,768]{2,1,0:T(8,128)(2,1)S(1)}, bf16[2,96,768]{2,1,0:T(8,128)(2,1)S(1)}, u32[]{:S(2)}, u32[]{:S(2)}) %collective-permute-start.39) | collective-permute-done | bytes 294944 | tf_op jit(solution)/shard_map/ppermute | solution.py:29
  208.2 4.0 %collective-permute-done.42 = bf16[2,112,384]{2,1,0:T(8,128)(2,1)} collective-permute-done((bf16[2,112,384]{2,1,0:T(8,128)(2,1)}, bf16[2,112,384]{2,1,0:T(8,128)(2,1)}, u32[]{:S(2)}, u32[]{:S(2)}) %collective-permute-start.42) | collective-permute-done | bytes 172064 | tf_op jit(solution)/shard_map/ppermute | solution.py:29
  222.3 8.3 %collective-permute-done.47 = bf16[2,96,768]{2,1,0:T(8,128)(2,1)S(1)} collective-permute-done((bf16[2,96,768]{2,1,0:T(8,128)(2,1)S(1)}, bf16[2,96,768]{2,1,0:T(8,128)(2,1)S(1)}, u32[]{:S(2)}, u32[]{:S(2)}) %collective-permute-start.47) | collective-permute-done | bytes 294944 | tf_op jit(solution)/shard_map/ppermute | solution.py:29
  230.7 5.5 %collective-permute-done.46 = bf16[2,112,768]{2,1,0:T(8,128)(2,1)S(1)} collective-permute-done((bf16[2,112,768]{2,1,0:T(8,128)(2,1)S(1)}, bf16[2,112,768]{2,1,0:T(8,128)(2,1)S(1)}, u32[]{:S(2)}, u32[]{:S(2)}) %collective-permute-start.46) | collective-permute-done | bytes 344096 | tf_op jit(solution)/shard_map/ppermute | solution.py:29
  242.9 8.5 %collective-permute-done.51 = bf16[2,192,384]{2,1,0:T(8,128)(2,1)S(1)} collective-permute-done((bf16[2,192,384]{2,1,0:T(8,128)(2,1)S(1)}, bf16[2,192,384]{2,1,0:T(8,128)(2,1)S(1)}, u32[]{:S(2)}, u32[]{:S(2)}) %collective-permute-start.51) | collective-permute-done | bytes 294944 | tf_op jit(solution)/shard_map/ppermute | solution.py:29
  257.3 4.2 %collective-permute-done.56 = bf16[2,192,384]{2,1,0:T(8,128)(2,1)S(1)} collective-permute-done((bf16[2,192,384]{2,1,0:T(8,128)(2,1)S(1)}, bf16[2,192,384]{2,1,0:T(8,128)(2,1)S(1)}, u32[]{:S(2)}, u32[]{:S(2)}) %collective-permute-start.56) | collective-permute-done | bytes 294944 | tf_op jit(solution)/shard_map/ppermute | solution.py:29
  261.6 7.4 %collective-permute-done.52 = bf16[4,112,768]{2,1,0:T(8,128)(2,1)S(1)} collective-permute-done((bf16[4,112,768]{2,1,0:T(8,128)(2,1)S(1)}, bf16[4,112,768]{2,1,0:T(8,128)(2,1)S(1)}, u32[]{:S(2)}, u32[]{:S(2)}) %collective-permute-start.52) | collective-permute-done | bytes 688160 | tf_op jit(solution)/shard_map/ppermute | solution.py:29
  273.6 4.6 %shard_map.287.refs_4_ = f32[3072,768]{1,0:T(8,128)} custom-call(s32[20]{0:T(128)} %concatenate.45.places, bf16[4,96,768]{2,1,0:T(8,128)(2,1)} %copy-done.3, bf16[4,96,768]{2,1,0:T(8,128)(2,1)} %collective-permute-done.50.refs_1_, bf16[4,96,768]{2,1,0:T(8,128)(2,1)} %copy-done.32, bf16[4,96,768]{2,1,0:T(8,128)(2,1)} %copy-done.33), custom_call_target="tpu_custom_call" | custom-call | tf_op jit(solution)/shard_map/pallas_call | solution.py:645
  278.2 8.0 %collective-permute-done.58.refs_1_ = bf16[4,192,384]{2,1,0:T(8,128)(2,1)S(1)} collective-permute-done((bf16[4,192,384]{2,1,0:T(8,128)(2,1)S(1)}, bf16[4,192,384]{2,1,0:T(8,128)(2,1)S(1)}, u32[]{:S(2)}, u32[]{:S(2)}) %collective-permute-start.58) | collective-permute-done | bytes 589856 | tf_op jit(solution)/shard_map/ppermute | solution.py:29
  293.0 4.6 %shard_map.289.refs_4_ = f32[768,3072]{1,0:T(8,128)} custom-call(s32[20]{0:T(128)} %concatenate.45.places, bf16[4,192,384]{2,1,0:T(8,128)(2,1)} %copy-done.6, bf16[4,192,384]{2,1,0:T(8,128)(2,1)} %copy-done.4, bf16[4,192,384]{2,1,0:T(8,128)(2,1)} %collective-permute-done.65.refs_2_, bf16[4,192,384]{2,1,0:T(8,128)(2,1)} %copy-done.35), custom_call_target="tpu_custom_call" | custom-call | tf_op jit(solution)/shard_map/pallas_call | solution.py:645
  297.6 4.7 %shard_map.288 = f32[3072,768]{1,0:T(8,128)} custom-call(s32[20]{0:T(128)} %concatenate.45.places, bf16[4,96,768]{2,1,0:T(8,128)(2,1)} %collective-permute-done.55.refs_0_, bf16[4,96,768]{2,1,0:T(8,128)(2,1)} %collective-permute-done.59.refs_1_, bf16[4,96,768]{2,1,0:T(8,128)(2,1)} %collective-permute-done.60.refs_2_, ...), custom_call_target="tpu_custom_call", output_to_operand_aliasing={{}: (5, {})} | custom-call | tf_op jit(solution)/shard_map/pallas_call | solution.py:645
  302.3 3.4 %collective-permute-done.63.refs_0_ = bf16[4,192,384]{2,1,0:T(8,128)(2,1)} collective-permute-done((bf16[4,192,384]{2,1,0:T(8,128)(2,1)S(1)}, bf16[4,192,384]{2,1,0:T(8,128)(2,1)}, u32[]{:S(2)}, u32[]{:S(2)}) %collective-permute-start.63) | collective-permute-done | bytes 589856 | tf_op jit(solution)/shard_map/ppermute | solution.py:29
  307.8 8.2 %collective-permute-done.67 = bf16[2,192,384]{2,1,0:T(8,128)(2,1)S(1)} collective-permute-done((bf16[2,192,384]{2,1,0:T(8,128)(2,1)S(1)}, bf16[2,192,384]{2,1,0:T(8,128)(2,1)S(1)}, u32[]{:S(2)}, u32[]{:S(2)}) %collective-permute-start.67) | collective-permute-done | bytes 294944 | tf_op jit(solution)/shard_map/ppermute | solution.py:29
  318.6 7.8 %shard_map.290 = (f32[768,2304]{1,0:T(8,128)}, f32[768,768]{1,0:T(8,128)}, f32[16,768]{1,0:T(8,128)}, f32[8,768]{1,0:T(8,128)}) custom-call(s32[20]{0:T(128)} %concatenate.45.places, bf16[4,112,768]{2,1,0:T(8,128)(2,1)} %copy-done.1, bf16[4,112,768]{2,1,0:T(8,128)(2,1)} %copy-done, bf16[4,112,768]{2,1,0:T(8,128)(2,1)} %copy-done.26, ...), custom_call_target="tpu_custom_call" | custom-call | tf_op jit(solution)/shard_map/pallas_call | solution.py:739
  330.9 4.6 %shard_map.291 = f32[768,3072]{1,0:T(8,128)} custom-call(s32[20]{0:T(128)} %concatenate.45.places, bf16[4,192,384]{2,1,0:T(8,128)(2,1)} %collective-permute-done.63.refs_0_, bf16[4,192,384]{2,1,0:T(8,128)(2,1)} %copy-done.14, bf16[4,192,384]{2,1,0:T(8,128)(2,1)} %copy-done.31, bf16[4,192,384]{2,1,0:T(8,128)(2,1)} %copy-done.34, ...), custom_call_target="tpu_custom_call", output_to_operand_aliasing={{}: (5, {})} | custom-call | tf_op jit(solution)/shard_map/pallas_call | solution.py:645
  (374 shorter events, 129.4 us)
Async XLA Ops:
  2.0 14.8 %collective-permute-start.1 = (bf16[256,768]{1,0:T(8,128)(2,1)S(1)}, bf16[256,768]{1,0:T(8,128)(2,1)S(1)}, u32[]{:S(2)}, u32[]{:S(2)}) collective-permute-start(bf16[256,768]{1,0:T(8,128)(2,1)S(1)} %get-tuple-element.372.x0), channel_id=1, source_target_pairs={{0,1},{1,0},{2,3},{3,2},{4,5},{5,4},{6,7},{7,6},{8,9},{9,8},{10,11... | collective-permute-start | bytes 1179656 | tf_op jit(solution)/shard_map/ppermute | solution.py:29
  110.1 25.1 %collective-permute-start.25 = (bf16[2,384,768]{2,1,0:T(8,128)(2,1)}, bf16[2,384,768]{2,1,0:T(8,128)(2,1)}, u32[]{:S(2)}, u32[]{:S(2)}) collective-permute-start(bf16[2,384,768]{2,1,0:T(8,128)(2,1)} %get-tuple-element.230), channel_id=1, source_target_pairs={{0,1},{1,0},{2,3},{3,2},{4,5},{5,4},{6,7},{7,6},{8,9},{9,8},{10,11... | collective-permute-start | bytes 3538952 | tf_op jit(solution)/shard_map/ppermute | solution.py:29
  110.6 24.6 %collective-permute-start.24 = (bf16[2,2,192,256]{3,2,1,0:T(8,128)(2,1)}, bf16[2,2,192,256]{3,2,1,0:T(8,128)(2,1)S(1)}, u32[]{:S(2)}, u32[]{:S(2)}) collective-permute-start(bf16[2,2,192,256]{3,2,1,0:T(8,128)(2,1)} %get-tuple-element.227), channel_id=1, source_target_pairs={{0,2},{1,3},{2,0},{3,1},{4,6},{5,7},{6,4},{7,5},{8,10},{9,11},{10,... | collective-permute-start | bytes 1179656 | tf_op jit(solution)/shard_map/ppermute | solution.py:29
  117.7 38.2 %collective-permute-start.26 = (bf16[2,384,768]{2,1,0:T(8,128)(2,1)S(1)}, bf16[2,384,768]{2,1,0:T(8,128)(2,1)}, u32[]{:S(2)}, u32[]{:S(2)}) collective-permute-start(bf16[2,384,768]{2,1,0:T(8,128)(2,1)S(1)} %add_convert_fusion.1), channel_id=1, source_target_pairs={{0,4},{4,0},{8,12},{12,8},{16,20},{20,16},{24,28},{28,24},{1,5},{5... | collective-permute-start | bytes 3538952 | tf_op jit(solution)/shard_map/ppermute | solution.py:29
  119.2 36.6 %collective-permute-start.27 = (bf16[2,768,384]{2,1,0:T(8,128)(2,1)}, bf16[2,768,384]{2,1,0:T(8,128)(2,1)S(1)}, u32[]{:S(2)}, u32[]{:S(2)}) collective-permute-start(bf16[2,768,384]{2,1,0:T(8,128)(2,1)} %add_convert_fusion), channel_id=1, source_target_pairs={{0,8},{4,12},{8,0},{12,4},{16,24},{20,28},{24,16},{28,20},{1,9},{5... | collective-permute-start | bytes 3538952 | tf_op jit(solution)/shard_map/ppermute | solution.py:29
  135.3 17.5 %collective-permute-start.31 = (bf16[2,256,768]{2,1,0:T(8,128)(2,1)}, bf16[2,256,768]{2,1,0:T(8,128)(2,1)}, u32[]{:S(2)}, u32[]{:S(2)}) collective-permute-start(bf16[2,256,768]{2,1,0:T(8,128)(2,1)} %get-tuple-element.250), channel_id=1, source_target_pairs={{0,1},{1,0},{2,3},{3,2},{4,5},{5,4},{6,7},{7,6},{8,9},{9,8},{10,11... | collective-permute-start | bytes 2359304 | tf_op jit(solution)/shard_map/ppermute | solution.py:29
  135.9 19.9 %collective-permute-start.28 = (bf16[2,8,96,192]{3,2,1,0:T(8,128)(2,1)}, bf16[2,8,96,192]{3,2,1,0:T(8,128)(2,1)}, u32[]{:S(2)}, u32[]{:S(2)}) collective-permute-start(bf16[2,8,96,192]{3,2,1,0:T(8,128)(2,1)} %get-tuple-element.235), channel_id=1, source_target_pairs={{0,2},{1,3},{2,0},{3,1},{4,6},{5,7},{6,4},{7,5},{8,10},{9,11},{10,... | collective-permute-start | bytes 1769480 | tf_op jit(solution)/shard_map/ppermute | solution.py:29
  157.3 21.6 %collective-permute-start.35 = (bf16[2,256,768]{2,1,0:T(8,128)(2,1)}, bf16[2,256,768]{2,1,0:T(8,128)(2,1)S(1)}, u32[]{:S(2)}, u32[]{:S(2)}) collective-permute-start(bf16[2,256,768]{2,1,0:T(8,128)(2,1)} %get-tuple-element.262), channel_id=1, source_target_pairs={{0,1},{1,0},{2,3},{3,2},{4,5},{5,4},{6,7},{7,6},{8,9},{9,8},{10,11... | collective-permute-start | bytes 2359304 | tf_op jit(solution)/shard_map/ppermute | solution.py:29
  164.3 15.6 %collective-permute-start.33 = (bf16[384,768]{1,0:T(8,128)(2,1)}, bf16[384,768]{1,0:T(8,128)(2,1)}, u32[]{:S(2)}, u32[]{:S(2)}) collective-permute-start(bf16[384,768]{1,0:T(8,128)(2,1)} %fusion.4), channel_id=1, source_target_pairs={{0,8},{4,12},{8,0},{12,4},{16,24},{20,28},{24,16},{28,20},{1,9},{5... | collective-permute-start | bytes 1769480 | tf_op jit(solution)/shard_map/ppermute | solution.py:29
  164.8 15.3 %collective-permute-start.34 = (bf16[768,384]{1,0:T(8,128)(2,1)}, bf16[768,384]{1,0:T(8,128)(2,1)}, u32[]{:S(2)}, u32[]{:S(2)}) collective-permute-start(bf16[768,384]{1,0:T(8,128)(2,1)} %fusion.5), channel_id=1, source_target_pairs={{0,4},{4,0},{8,12},{12,8},{16,20},{20,16},{24,28},{28,24},{1,5},{5... | collective-permute-start | bytes 1769480 | tf_op jit(solution)/shard_map/ppermute | solution.py:29
  165.2 14.6 %collective-permute-start.36 = (bf16[256,768]{1,0:T(8,128)(2,1)S(1)}, bf16[256,768]{1,0:T(8,128)(2,1)S(1)}, u32[]{:S(2)}, u32[]{:S(2)}) collective-permute-start(bf16[256,768]{1,0:T(8,128)(2,1)S(1)} %get-tuple-element.260), channel_id=1, source_target_pairs={{0,2},{1,3},{2,0},{3,1},{4,6},{5,7},{6,4},{7,5},{8,10},{9,11},{10,... | collective-permute-start | bytes 1179656 | tf_op jit(solution)/shard_map/ppermute | solution.py:29
  201.0 14.5 %collective-permute-start.44 = (bf16[2,96,768]{2,1,0:T(8,128)(2,1)S(1)}, bf16[2,96,768]{2,1,0:T(8,128)(2,1)}, u32[]{:S(2)}, u32[]{:S(2)}) collective-permute-start(bf16[2,96,768]{2,1,0:T(8,128)(2,1)S(1)} %fusion.12), channel_id=1, source_target_pairs={{0,16},{4,20},{8,24},{12,28},{16,0},{20,4},{24,8},{28,12},{1,17},{... | collective-permute-start | bytes 884744 | tf_op jit(solution)/shard_map/ppermute | solution.py:29
  217.8 18.3 %collective-permute-start.46 = (bf16[2,112,768]{2,1,0:T(8,128)(2,1)S(1)}, bf16[2,112,768]{2,1,0:T(8,128)(2,1)S(1)}, u32[]{:S(2)}, u32[]{:S(2)}) collective-permute-start(bf16[2,112,768]{2,1,0:T(8,128)(2,1)S(1)} %pad_maximum_fusion.5), channel_id=1, source_target_pairs={{0,16},{4,20},{8,24},{12,28},{16,0},{20,4},{24,8},{28,12},{1,17},{... | collective-permute-start | bytes 1032200 | tf_op jit(solution)/shard_map/ppermute | solution.py:29
  220.8 15.5 %collective-permute-start.48 = (bf16[256,768]{1,0:T(8,128)(2,1)S(1)}, bf16[256,768]{1,0:T(8,128)(2,1)S(1)}, u32[]{:S(2)}, u32[]{:S(2)}) collective-permute-start(bf16[256,768]{1,0:T(8,128)(2,1)S(1)} %copy-done.41), channel_id=1, source_target_pairs={{0,2},{1,3},{2,0},{3,1},{4,6},{5,7},{6,4},{7,5},{8,10},{9,11},{10,... | collective-permute-start | bytes 1179656 | tf_op jit(solution)/shard_map/ppermute | solution.py:29
  236.3 15.2 %collective-permute-start.51 = (bf16[2,192,384]{2,1,0:T(8,128)(2,1)S(1)}, bf16[2,192,384]{2,1,0:T(8,128)(2,1)S(1)}, u32[]{:S(2)}, u32[]{:S(2)}) collective-permute-start(bf16[2,192,384]{2,1,0:T(8,128)(2,1)S(1)} %fusion.11), channel_id=1, source_target_pairs={{0,16},{4,20},{8,24},{12,28},{16,0},{20,4},{24,8},{28,12},{1,17},{... | collective-permute-start | bytes 884744 | tf_op jit(solution)/shard_map/ppermute | solution.py:29
  236.3 15.2 %collective-permute-start.49 = (bf16[2,112,768]{2,1,0:T(8,128)(2,1)S(1)}, bf16[2,112,768]{2,1,0:T(8,128)(2,1)S(1)}, u32[]{:S(2)}, u32[]{:S(2)}) collective-permute-start(bf16[2,112,768]{2,1,0:T(8,128)(2,1)S(1)} %reverse_add_fusion), channel_id=1, source_target_pairs={{0,4},{4,0},{8,12},{12,8},{16,20},{20,16},{24,28},{28,24},{1,5},{5... | collective-permute-start | bytes 1032200 | tf_op jit(solution)/shard_map/ppermute | solution.py:29
  252.1 16.9 %collective-permute-start.52 = (bf16[4,112,768]{2,1,0:T(8,128)(2,1)S(1)}, bf16[4,112,768]{2,1,0:T(8,128)(2,1)S(1)}, u32[]{:S(2)}, u32[]{:S(2)}) collective-permute-start(bf16[4,112,768]{2,1,0:T(8,128)(2,1)S(1)} %pad_maximum_fusion), channel_id=1, source_target_pairs={{0,8},{4,12},{8,0},{12,4},{16,24},{20,28},{24,16},{28,20},{1,9},{5... | collective-permute-start | bytes 2064392 | tf_op jit(solution)/shard_map/ppermute | solution.py:29
  269.3 19.4 %collective-permute-start.61 = (bf16[4,112,768]{2,1,0:T(8,128)(2,1)S(1)}, bf16[4,112,768]{2,1,0:T(8,128)(2,1)S(1)}, u32[]{:S(2)}, u32[]{:S(2)}) collective-permute-start(bf16[4,112,768]{2,1,0:T(8,128)(2,1)S(1)} %pad_maximum_fusion.1.refs_0_), channel_id=1, source_target_pairs={{0,1},{1,0},{2,3},{3,2},{4,5},{5,4},{6,7},{7,6},{8,9},{9,8},{10,11... | collective-permute-start | bytes 2064392 | tf_op jit(solution)/shard_map/ppermute | solution.py:29
  270.4 18.3 %collective-permute-start.57 = (bf16[4,112,768]{2,1,0:T(8,128)(2,1)S(1)}, bf16[4,112,768]{2,1,0:T(8,128)(2,1)S(1)}, u32[]{:S(2)}, u32[]{:S(2)}) collective-permute-start(bf16[4,112,768]{2,1,0:T(8,128)(2,1)S(1)} %pad_maximum_fusion.1.refs_0_), channel_id=1, source_target_pairs={{0,2},{1,3},{2,0},{3,1},{4,6},{5,7},{6,4},{7,5},{8,10},{9,11},{10,... | collective-permute-start | bytes 2064392 | tf_op jit(solution)/shard_map/ppermute | solution.py:29
  271.8 14.4 %collective-permute-start.58 = (bf16[4,192,384]{2,1,0:T(8,128)(2,1)S(1)}, bf16[4,192,384]{2,1,0:T(8,128)(2,1)S(1)}, u32[]{:S(2)}, u32[]{:S(2)}) collective-permute-start(bf16[4,192,384]{2,1,0:T(8,128)(2,1)S(1)} %pad_maximum_fusion.4.refs_0_), channel_id=1, source_target_pairs={{0,8},{4,12},{8,0},{12,4},{16,24},{20,28},{24,16},{28,20},{1,9},{5... | collective-permute-start | bytes 1769480 | tf_op jit(solution)/shard_map/ppermute | solution.py:29
  272.6 16.1 %collective-permute-start.59 = (bf16[4,96,768]{2,1,0:T(8,128)(2,1)}, bf16[4,96,768]{2,1,0:T(8,128)(2,1)}, u32[]{:S(2)}, u32[]{:S(2)}) collective-permute-start(bf16[4,96,768]{2,1,0:T(8,128)(2,1)} %collective-permute-done.50.refs_1_), channel_id=1, source_target_pairs={{0,4},{4,0},{8,12},{12,8},{16,20},{20,16},{24,28},{28,24},{1,5},{5... | collective-permute-start | bytes 1769480 | tf_op jit(solution)/shard_map/ppermute | solution.py:29
  288.7 17.2 %collective-permute-start.62 = (bf16[4,112,768]{2,1,0:T(8,128)(2,1)S(1)}, bf16[4,112,768]{2,1,0:T(8,128)(2,1)}, u32[]{:S(2)}, u32[]{:S(2)}) collective-permute-start(bf16[4,112,768]{2,1,0:T(8,128)(2,1)S(1)} %pad_maximum_fusion.2.refs_1_), channel_id=1, source_target_pairs={{0,2},{1,3},{2,0},{3,1},{4,6},{5,7},{6,4},{7,5},{8,10},{9,11},{10,... | collective-permute-start | bytes 2064392 | tf_op jit(solution)/shard_map/ppermute | solution.py:29
  289.9 15.8 %collective-permute-start.63 = (bf16[4,192,384]{2,1,0:T(8,128)(2,1)S(1)}, bf16[4,192,384]{2,1,0:T(8,128)(2,1)}, u32[]{:S(2)}, u32[]{:S(2)}) collective-permute-start(bf16[4,192,384]{2,1,0:T(8,128)(2,1)S(1)} %pad_maximum_fusion.4.refs_0_), channel_id=1, source_target_pairs={{0,4},{4,0},{8,12},{12,8},{16,20},{20,16},{24,28},{28,24},{1,5},{5... | collective-permute-start | bytes 1769480 | tf_op jit(solution)/shard_map/ppermute | solution.py:29
  307.6 18.8 %collective-permute-start.72 = (bf16[4,192,384]{2,1,0:T(8,128)(2,1)}, bf16[4,192,384]{2,1,0:T(8,128)(2,1)S(1)}, u32[]{:S(2)}, u32[]{:S(2)}) collective-permute-start(bf16[4,192,384]{2,1,0:T(8,128)(2,1)} %collective-permute-done.63.refs_0_), channel_id=1, source_target_pairs={{0,1},{1,0},{2,3},{3,2},{4,5},{5,4},{6,7},{7,6},{8,9},{9,8},{10,11... | collective-permute-start | bytes 1769480 | tf_op jit(solution)/shard_map/ppermute | solution.py:29
  (129 other events, 983.0 us)

commit v10 on v9

--- a/solution.py
+++ b/solution.py
@@ -199,7 +199,12 @@
         bring_acc.wait()
         total, sums = total + acc[...], sums + acc_b[...]
     if last:
-        out_own, vectors = refs[2:4]
+        grad_out, out_x, out_c, vectors = refs[2:6]
+        out_own = (
+            grad_out[0].astype(jnp.float32)
+            + out_x[0].astype(jnp.float32)
+            + out_c[...].astype(jnp.float32)
+        ).astype(jnp.bfloat16)
         inner = places[10]
         turned = total.T.astype(jnp.bfloat16)
         tile = out_own.shape[1]
@@ -210,7 +215,7 @@
             rows = slice(q * tile, (q + 1) * tile)
             grad_w[q ^ inner, :tile, :] = turned[rows, : 2 * wide]
             grad_w2[q ^ inner, :tile, :wide] = turned[rows, 2 * wide :]
-        grad_w2[:, :tile, wide:] = out_own[...]
+        grad_w2[:, :tile, wide:] = out_own
         row = lax.broadcasted_iota(jnp.int32, (extra, 1), 0)
         own_row = jnp.concatenate([sums[0:1, :], jnp.zeros((1, wide), jnp.float32)], axis=1)
         tile_rows = jnp.where(row == 10, own_row, vectors[...]).astype(jnp.bfloat16)
@@ -906,13 +911,14 @@
         sum_low(keep_up[2], came_up1[0], up_l[1]),
     ]
     out_c = exchange_bit(sum_low(grad_out[1], out_x[1]), "c")
-    out_own = sum_low(grad_out[0], out_x[0], out_c)
-    (sends, total, out_own, far) = lax.optimization_barrier((sends, total, out_own, far))
+    (sends, total, out_c, far) = lax.optimization_barrier((sends, total, out_c, far))
     down_l, up_y = [exchange_bit(v, bit) for v, bit in zip(sends, "ly")]
     far_came = [exchange_bit(far[0], "x")]
     for s in range(1, seq_count - 1):
         cross(s)
-    half_a, half_b = attend(seq_count - 1, second_group, total, (out_own, sums))
+    half_a, half_b = attend(
+        seq_count - 1, second_group, total, (grad_out, out_x, out_c, sums)
+    )
 
     (down_l, up_y, far, far_came, half_a, half_b, parts[-1]) = lax.optimization_barrier(
         (down_l, up_y, far, far_came, half_a, half_b, parts[-1])
@@ -996,14 +1002,14 @@
     (both, across, up_hi, up_far, full_down, full_up) = lax.optimization_barrier(
         (both, across, up_hi, up_far, full_down, full_up)
     )
-    up_second = [exchange_bit(up_hi[:2], "y")]
+    up_second = [exchange_bit(up_hi[:1], "y")]
     both_near.append(exchange_bit(both[1], "c"))
     both_far = [exchange_bit(half, "c") for half in across]
 
     (up_hi, up_second, both_near, both_far) = lax.optimization_barrier(
         (up_hi, up_second, both_near, both_far)
     )
-    up_second.append(exchange_bit(up_hi[2:], "y"))
+    up_second.append(exchange_bit(up_hi[1:], "y"))
     across_up = [exchange_bit(up_far[0], "c")]
     full_qkv, full_out, vector_rows, head_rows = gather_heads(
         places,

time: 340 us -> 335 us (0.985)
    convert_element_type x9 -> x8, other arithmetic: 16.1 us -> 14 us  [sum_low(): return total.astype(jnp.bfloat16)]
    unnamed x161 -> x155, local copies, waits for them, and re-layouts: 10 us -> 8.29 us
  transfers between devices with their start and end apart: 74 -> 74, of which waited for: 30 -> 30; matrix products, arithmetic and copies ran while one was open for 10% -> 9% of each run, Pallas kernels for 25% -> 26%
where the time goes in v10:
time: 335 us; the launch traced here: 331 us
  Pallas kernels  131 us (39%)
  waiting for transfers between devices  94.6 us (28%)
  starting transfers between devices  56.6 us (17%)
  other arithmetic  25.6 us (8%)
  local copies, waits for them, and re-layouts  20.8 us (6%)
    ppermute x74, waiting for transfers between devices, exchange(): lax.ppermute(array_in, axis, [(i, i ^ flip) for i in range(lax.axis_size(...  94.6 us
    pallas_call x6, Pallas kernels, kernel_call(): pl.pallas_call(body, out_shape=outs, in_specs=[pl.BlockSpec(memory_space=...  63.4 us
    ppermute x74, starting transfers between devices, exchange(): lax.ppermute(array_in, axis, [(i, i ^ flip) for i in range(lax.axis_size(...  56.6 us
    pallas_call x1, Pallas kernels, step_call(): pl.pallas_call(body, out_shape=outs, grid_spec=pltpu.PrefetchScalarGridSp...  41.8 us
    pallas_call x4, Pallas kernels, gather_tiles(): pl.pallas_call(functools.partial(place_tiles, by_rows, late), out_shape=j...  18.5 us
    convert_element_type x8, other arithmetic, sum_low(): return total.astype(jnp.bfloat16)  14 us
    unnamed x155, local copies, waits for them, and re-layouts  8.29 us
    pallas_call x1, Pallas kernels, gather_heads(): pl.pallas_call(functools.partial(place_heads, parts), out_shape=[out(shap...  7.79 us
  transfers between devices with their start and end apart: 74, of which 30 were waited for; matrix products, arithmetic and copies ran while one was open for 9% of the time, Pallas kernels for 26%

profile of v10, /device:TPU:0, one launch (start us, length us, event | category | flops | bytes accessed | tf_op | source)
XLA Modules:
  0.0 331.1 jit_solution(17939513731189070914)
XLA Ops:
  18.3 8.3 %shard_map.280 = (bf16[192,256]{1,0:T(8,128)(2,1)}, bf16[192,256]{1,0:T(8,128)(2,1)}, bf16[192,256]{1,0:T(8,128)(2,1)}, bf16[192,256]{1,0:T(8,128)(2,1)}, bf16[1...) custom-call(s32[20]{0:T(128)} %concatenate.45.places, ...), custom_call_target="tpu_custom_call" | custom-call | flops 100000000 | bytes 1048576 | tf_op jit(solution)/shard_map/pallas_call | solution.py:235
  29.8 8.2 %shard_map.281 = (bf16[192,256]{1,0:T(8,128)(2,1)}, bf16[192,256]{1,0:T(8,128)(2,1)}, bf16[192,256]{1,0:T(8,128)(2,1)}, bf16[192,256]{1,0:T(8,128)(2,1)}, bf16[1...) custom-call(s32[20]{0:T(128)} %concatenate.45.places, ...), custom_call_target="tpu_custom_call" | custom-call | flops 100000000 | bytes 1048576 | tf_op jit(solution)/shard_map/pallas_call | solution.py:235
  42.5 8.2 %shard_map.282 = (bf16[192,256]{1,0:T(8,128)(2,1)}, bf16[192,256]{1,0:T(8,128)(2,1)}, bf16[192,256]{1,0:T(8,128)(2,1)}, bf16[192,256]{1,0:T(8,128)(2,1)}, bf16[1...) custom-call(s32[20]{0:T(128)} %concatenate.45.places, ...), custom_call_target="tpu_custom_call" | custom-call | flops 100000000 | bytes 1048576 | tf_op jit(solution)/shard_map/pallas_call | solution.py:235
  60.6 41.8 %shard_map.283 = (bf16[768,768]{1,0:T(8,128)(2,1)}, bf16[2,384,768]{2,1,0:T(8,128)(2,1)}, bf16[2,768,384]{2,1,0:T(8,128)(2,1)}, bf16[2,384,768]{2,1,0:T(8,128)(2...) custom-call(s32[20]{0:T(128)} %concatenate.45.places, ...), custom_call_target="tpu_custom_call" | custom-call | flops 24461180928 | bytes 1048576 | tf_op jit(solution)/shard_map/pallas_call | solution.py:531
  103.5 6.6 %collective-permute-done.20.g2 = bf16[2,1,192,256]{3,2,1,0:T(8,128)(2,1)S(1)} collective-permute-done((bf16[2,1,192,256]{3,2,1,0:T(8,128)(2,1)}, bf16[2,1,192,256]{3,2,1,0:T(8,128)(2,1)S(1)}, u32[]{:S(2)}, u32[]{:S(2)}) %collective-permute-start.20) | collective-permute-done | bytes 196640 | tf_op jit(solution)/shard_map/ppermute | solution.py:29
  122.8 12.4 %shard_map.284 = (bf16[2,256,768]{2,1,0:T(8,128)(2,1)}, bf16[2,256,768]{2,1,0:T(8,128)(2,1)}, f32[576,768]{1,0:T(8,128)}, f32[8,576]{1,0:T(8,128)}) custom-call(s32[20]{0:T(128)} %concatenate.45.places, bf16[1,192,256]{2,1,0:T(8,128)(2,1)} %get-tuple-element.207.g0, bf16[1,192,256]{2,1,0:T(8,128)(2,1)} %copy-done.48, bf16[2,1,192,256]{3,2,1,0:T(8,128)(2,1)} %copy-done.34, ...), custom_call_target="tpu_custom_call" | custom-call | flops 100000000 | bytes 1048576 | tf_op jit(solution)/shard_map/pallas_call | solution.py:235
  140.0 12.7 %shard_map.285 = (bf16[2,256,768]{2,1,0:T(8,128)(2,1)}, bf16[2,256,768]{2,1,0:T(8,128)(2,1)}, f32[576,768]{1,0:T(8,128)}, f32[8,576]{1,0:T(8,128)}) custom-call(s32[20]{0:T(128)} %concatenate.45.places, bf16[2,192,256]{2,1,0:T(8,128)(2,1)} %get-tuple-element.236.g0, bf16[2,192,256]{2,1,0:T(8,128)(2,1)} %copy-done.22, bf16[2,2,192,256]{3,2,1,0:T(8,128)(2,1)} %copy-done.2, ...), custom_call_target="tpu_custom_call" | custom-call | flops 100000000 | bytes 1048576 | tf_op jit(solution)/shard_map/pallas_call | solution.py:235
  162.6 13.6 %shard_map.286 = (bf16[2,256,768]{2,1,0:T(8,128)(2,1)}, bf16[2,256,768]{2,1,0:T(8,128)(2,1)}, bf16[8,112,384]{2,1,0:T(8,128)(2,1)}, bf16[8,112,384]{2,1,0:T(8,128)(2,1)}) custom-call(s32[20]{0:T(128)} %concatenate.45.places, bf16[2,192,256]{2,1,0:T(8,128)(2,1)} %get-tuple-element.236.g0, bf16[2,192,256]{2,1,0:T(8,128)(2,1)} %copy-done.22, ...), custom_call_target="tpu_custom_call" | custom-call | flops 100000000 | bytes 1048576 | tf_op jit(solution)/shard_map/pallas_call | solution.py:235
  186.5 4.6 %collective-permute-done.40 = bf16[2,192,384]{2,1,0:T(8,128)(2,1)S(1)} collective-permute-done((bf16[2,192,384]{2,1,0:T(8,128)(2,1)S(1)}, bf16[2,192,384]{2,1,0:T(8,128)(2,1)S(1)}, u32[]{:S(2)}, u32[]{:S(2)}) %collective-permute-start.40) | collective-permute-done | bytes 294944 | tf_op jit(solution)/shard_map/ppermute | solution.py:29
  191.1 4.6 %collective-permute-done.39 = bf16[2,96,768]{2,1,0:T(8,128)(2,1)S(1)} collective-permute-done((bf16[2,96,768]{2,1,0:T(8,128)(2,1)S(1)}, bf16[2,96,768]{2,1,0:T(8,128)(2,1)S(1)}, u32[]{:S(2)}, u32[]{:S(2)}) %collective-permute-start.39) | collective-permute-done | bytes 294944 | tf_op jit(solution)/shard_map/ppermute | solution.py:29
  205.3 4.2 %collective-permute-done.42 = bf16[2,112,384]{2,1,0:T(8,128)(2,1)} collective-permute-done((bf16[2,112,384]{2,1,0:T(8,128)(2,1)}, bf16[2,112,384]{2,1,0:T(8,128)(2,1)}, u32[]{:S(2)}, u32[]{:S(2)}) %collective-permute-start.42) | collective-permute-done | bytes 172064 | tf_op jit(solution)/shard_map/ppermute | solution.py:29
  219.4 8.8 %collective-permute-done.47 = bf16[2,96,768]{2,1,0:T(8,128)(2,1)S(1)} collective-permute-done((bf16[2,96,768]{2,1,0:T(8,128)(2,1)S(1)}, bf16[2,96,768]{2,1,0:T(8,128)(2,1)S(1)}, u32[]{:S(2)}, u32[]{:S(2)}) %collective-permute-start.47) | collective-permute-done | bytes 294944 | tf_op jit(solution)/shard_map/ppermute | solution.py:29
  228.2 5.0 %collective-permute-done.46 = bf16[2,112,768]{2,1,0:T(8,128)(2,1)S(1)} collective-permute-done((bf16[2,112,768]{2,1,0:T(8,128)(2,1)S(1)}, bf16[2,112,768]{2,1,0:T(8,128)(2,1)S(1)}, u32[]{:S(2)}, u32[]{:S(2)}) %collective-permute-start.46) | collective-permute-done | bytes 344096 | tf_op jit(solution)/shard_map/ppermute | solution.py:29
  240.1 8.4 %collective-permute-done.51 = bf16[2,192,384]{2,1,0:T(8,128)(2,1)S(1)} collective-permute-done((bf16[2,192,384]{2,1,0:T(8,128)(2,1)S(1)}, bf16[2,192,384]{2,1,0:T(8,128)(2,1)S(1)}, u32[]{:S(2)}, u32[]{:S(2)}) %collective-permute-start.51) | collective-permute-done | bytes 294944 | tf_op jit(solution)/shard_map/ppermute | solution.py:29
  254.4 4.2 %collective-permute-done.56 = bf16[2,192,384]{2,1,0:T(8,128)(2,1)S(1)} collective-permute-done((bf16[2,192,384]{2,1,0:T(8,128)(2,1)S(1)}, bf16[2,192,384]{2,1,0:T(8,128)(2,1)S(1)}, u32[]{:S(2)}, u32[]{:S(2)}) %collective-permute-start.56) | collective-permute-done | bytes 294944 | tf_op jit(solution)/shard_map/ppermute | solution.py:29
  258.7 7.3 %collective-permute-done.52 = bf16[4,112,768]{2,1,0:T(8,128)(2,1)S(1)} collective-permute-done((bf16[4,112,768]{2,1,0:T(8,128)(2,1)S(1)}, bf16[4,112,768]{2,1,0:T(8,128)(2,1)S(1)}, u32[]{:S(2)}, u32[]{:S(2)}) %collective-permute-start.52) | collective-permute-done | bytes 688160 | tf_op jit(solution)/shard_map/ppermute | solution.py:29
  270.8 4.6 %shard_map.287.refs_4_ = f32[3072,768]{1,0:T(8,128)} custom-call(s32[20]{0:T(128)} %concatenate.45.places, bf16[4,96,768]{2,1,0:T(8,128)(2,1)} %copy-done.3, bf16[4,96,768]{2,1,0:T(8,128)(2,1)} %collective-permute-done.50.refs_1_, bf16[4,96,768]{2,1,0:T(8,128)(2,1)} %copy-done.30, bf16[4,96,768]{2,1,0:T(8,128)(2,1)} %copy-done.31), custom_call_target="tpu_custom_call" | custom-call | tf_op jit(solution)/shard_map/pallas_call | solution.py:650
  275.4 8.0 %collective-permute-done.58.refs_1_ = bf16[4,192,384]{2,1,0:T(8,128)(2,1)S(1)} collective-permute-done((bf16[4,192,384]{2,1,0:T(8,128)(2,1)S(1)}, bf16[4,192,384]{2,1,0:T(8,128)(2,1)S(1)}, u32[]{:S(2)}, u32[]{:S(2)}) %collective-permute-start.58) | collective-permute-done | bytes 589856 | tf_op jit(solution)/shard_map/ppermute | solution.py:29
  290.1 4.6 %shard_map.289.refs_4_ = f32[768,3072]{1,0:T(8,128)} custom-call(s32[20]{0:T(128)} %concatenate.45.places, bf16[4,192,384]{2,1,0:T(8,128)(2,1)} %copy-done.6, bf16[4,192,384]{2,1,0:T(8,128)(2,1)} %copy-done.4, bf16[4,192,384]{2,1,0:T(8,128)(2,1)} %collective-permute-done.65.refs_2_, bf16[4,192,384]{2,1,0:T(8,128)(2,1)} %copy-done.33), custom_call_target="tpu_custom_call" | custom-call | tf_op jit(solution)/shard_map/pallas_call | solution.py:650
  294.7 4.7 %shard_map.288 = f32[3072,768]{1,0:T(8,128)} custom-call(s32[20]{0:T(128)} %concatenate.45.places, bf16[4,96,768]{2,1,0:T(8,128)(2,1)} %collective-permute-done.55.refs_0_, bf16[4,96,768]{2,1,0:T(8,128)(2,1)} %collective-permute-done.59.refs_1_, bf16[4,96,768]{2,1,0:T(8,128)(2,1)} %collective-permute-done.60.refs_2_, ...), custom_call_target="tpu_custom_call", output_to_operand_aliasing={{}: (5, {})} | custom-call | tf_op jit(solution)/shard_map/pallas_call | solution.py:650
  299.5 3.4 %collective-permute-done.63.refs_0_ = bf16[4,192,384]{2,1,0:T(8,128)(2,1)} collective-permute-done((bf16[4,192,384]{2,1,0:T(8,128)(2,1)S(1)}, bf16[4,192,384]{2,1,0:T(8,128)(2,1)}, u32[]{:S(2)}, u32[]{:S(2)}) %collective-permute-start.63) | collective-permute-done | bytes 589856 | tf_op jit(solution)/shard_map/ppermute | solution.py:29
  304.9 5.0 %collective-permute-done.67 = bf16[1,192,384]{2,1,0:T(8,128)(2,1)S(1)} collective-permute-done((bf16[1,192,384]{2,1,0:T(8,128)(2,1)S(1)}, bf16[1,192,384]{2,1,0:T(8,128)(2,1)S(1)}, u32[]{:S(2)}, u32[]{:S(2)}) %collective-permute-start.67) | collective-permute-done | bytes 147488 | tf_op jit(solution)/shard_map/ppermute | solution.py:29
  311.1 7.8 %shard_map.290 = (f32[768,2304]{1,0:T(8,128)}, f32[768,768]{1,0:T(8,128)}, f32[16,768]{1,0:T(8,128)}, f32[8,768]{1,0:T(8,128)}) custom-call(s32[20]{0:T(128)} %concatenate.45.places, bf16[4,112,768]{2,1,0:T(8,128)(2,1)} %copy-done.1, bf16[4,112,768]{2,1,0:T(8,128)(2,1)} %copy-done, bf16[4,112,768]{2,1,0:T(8,128)(2,1)} %copy-done.25, ...), custom_call_target="tpu_custom_call" | custom-call | tf_op jit(solution)/shard_map/pallas_call | solution.py:744
  326.3 4.6 %shard_map.291 = f32[768,3072]{1,0:T(8,128)} custom-call(s32[20]{0:T(128)} %concatenate.45.places, bf16[4,192,384]{2,1,0:T(8,128)(2,1)} %collective-permute-done.63.refs_0_, bf16[4,192,384]{2,1,0:T(8,128)(2,1)} %copy-done.18, bf16[4,192,384]{2,1,0:T(8,128)(2,1)} %copy-done.29, bf16[4,192,384]{2,1,0:T(8,128)(2,1)} %copy-done.32, ...), custom_call_target="tpu_custom_call", output_to_operand_aliasing={{}: (5, {})} | custom-call | tf_op jit(solution)/shard_map/pallas_call | solution.py:650
  (367 shorter events, 127.6 us)
Async XLA Ops:
  2.0 14.8 %collective-permute-start.1 = (bf16[256,768]{1,0:T(8,128)(2,1)S(1)}, bf16[256,768]{1,0:T(8,128)(2,1)S(1)}, u32[]{:S(2)}, u32[]{:S(2)}) collective-permute-start(bf16[256,768]{1,0:T(8,128)(2,1)S(1)} %get-tuple-element.372.x0), channel_id=1, source_target_pairs={{0,1},{1,0},{2,3},{3,2},{4,5},{5,4},{6,7},{7,6},{8,9},{9,8},{10,11... | collective-permute-start | bytes 1179656 | tf_op jit(solution)/shard_map/ppermute | solution.py:29
  110.1 25.1 %collective-permute-start.25 = (bf16[2,384,768]{2,1,0:T(8,128)(2,1)}, bf16[2,384,768]{2,1,0:T(8,128)(2,1)}, u32[]{:S(2)}, u32[]{:S(2)}) collective-permute-start(bf16[2,384,768]{2,1,0:T(8,128)(2,1)} %get-tuple-element.230), channel_id=1, source_target_pairs={{0,1},{1,0},{2,3},{3,2},{4,5},{5,4},{6,7},{7,6},{8,9},{9,8},{10,11... | collective-permute-start | bytes 3538952 | tf_op jit(solution)/shard_map/ppermute | solution.py:29
  110.6 24.5 %collective-permute-start.24 = (bf16[2,2,192,256]{3,2,1,0:T(8,128)(2,1)}, bf16[2,2,192,256]{3,2,1,0:T(8,128)(2,1)S(1)}, u32[]{:S(2)}, u32[]{:S(2)}) collective-permute-start(bf16[2,2,192,256]{3,2,1,0:T(8,128)(2,1)} %get-tuple-element.227), channel_id=1, source_target_pairs={{0,2},{1,3},{2,0},{3,1},{4,6},{5,7},{6,4},{7,5},{8,10},{9,11},{10,... | collective-permute-start | bytes 1179656 | tf_op jit(solution)/shard_map/ppermute | solution.py:29
  117.6 38.1 %collective-permute-start.26 = (bf16[2,384,768]{2,1,0:T(8,128)(2,1)S(1)}, bf16[2,384,768]{2,1,0:T(8,128)(2,1)}, u32[]{:S(2)}, u32[]{:S(2)}) collective-permute-start(bf16[2,384,768]{2,1,0:T(8,128)(2,1)S(1)} %add_convert_fusion.1), channel_id=1, source_target_pairs={{0,4},{4,0},{8,12},{12,8},{16,20},{20,16},{24,28},{28,24},{1,5},{5... | collective-permute-start | bytes 3538952 | tf_op jit(solution)/shard_map/ppermute | solution.py:29
  119.2 36.5 %collective-permute-start.27 = (bf16[2,768,384]{2,1,0:T(8,128)(2,1)}, bf16[2,768,384]{2,1,0:T(8,128)(2,1)}, u32[]{:S(2)}, u32[]{:S(2)}) collective-permute-start(bf16[2,768,384]{2,1,0:T(8,128)(2,1)} %add_convert_fusion), channel_id=1, source_target_pairs={{0,8},{4,12},{8,0},{12,4},{16,24},{20,28},{24,16},{28,20},{1,9},{5... | collective-permute-start | bytes 3538952 | tf_op jit(solution)/shard_map/ppermute | solution.py:29
  135.2 17.5 %collective-permute-start.31 = (bf16[2,256,768]{2,1,0:T(8,128)(2,1)}, bf16[2,256,768]{2,1,0:T(8,128)(2,1)}, u32[]{:S(2)}, u32[]{:S(2)}) collective-permute-start(bf16[2,256,768]{2,1,0:T(8,128)(2,1)} %get-tuple-element.250), channel_id=1, source_target_pairs={{0,1},{1,0},{2,3},{3,2},{4,5},{5,4},{6,7},{7,6},{8,9},{9,8},{10,11... | collective-permute-start | bytes 2359304 | tf_op jit(solution)/shard_map/ppermute | solution.py:29
  135.9 19.8 %collective-permute-start.28 = (bf16[2,8,96,192]{3,2,1,0:T(8,128)(2,1)}, bf16[2,8,96,192]{3,2,1,0:T(8,128)(2,1)S(1)}, u32[]{:S(2)}, u32[]{:S(2)}) collective-permute-start(bf16[2,8,96,192]{3,2,1,0:T(8,128)(2,1)} %get-tuple-element.235), channel_id=1, source_target_pairs={{0,2},{1,3},{2,0},{3,1},{4,6},{5,7},{6,4},{7,5},{8,10},{9,11},{10,... | collective-permute-start | bytes 1769480 | tf_op jit(solution)/shard_map/ppermute | solution.py:29
  155.9 20.3 %collective-permute-start.35 = (bf16[2,256,768]{2,1,0:T(8,128)(2,1)}, bf16[2,256,768]{2,1,0:T(8,128)(2,1)S(1)}, u32[]{:S(2)}, u32[]{:S(2)}) collective-permute-start(bf16[2,256,768]{2,1,0:T(8,128)(2,1)} %get-tuple-element.262), channel_id=1, source_target_pairs={{0,1},{1,0},{2,3},{3,2},{4,5},{5,4},{6,7},{7,6},{8,9},{9,8},{10,11... | collective-permute-start | bytes 2359304 | tf_op jit(solution)/shard_map/ppermute | solution.py:29
  161.2 16.0 %collective-permute-start.33 = (bf16[384,768]{1,0:T(8,128)(2,1)}, bf16[384,768]{1,0:T(8,128)(2,1)}, u32[]{:S(2)}, u32[]{:S(2)}) collective-permute-start(bf16[384,768]{1,0:T(8,128)(2,1)} %fusion.3), channel_id=1, source_target_pairs={{0,8},{4,12},{8,0},{12,4},{16,24},{20,28},{24,16},{28,20},{1,9},{5... | collective-permute-start | bytes 1769480 | tf_op jit(solution)/shard_map/ppermute | solution.py:29
  161.6 15.5 %collective-permute-start.34 = (bf16[768,384]{1,0:T(8,128)(2,1)}, bf16[768,384]{1,0:T(8,128)(2,1)}, u32[]{:S(2)}, u32[]{:S(2)}) collective-permute-start(bf16[768,384]{1,0:T(8,128)(2,1)} %fusion.4), channel_id=1, source_target_pairs={{0,4},{4,0},{8,12},{12,8},{16,20},{20,16},{24,28},{28,24},{1,5},{5... | collective-permute-start | bytes 1769480 | tf_op jit(solution)/shard_map/ppermute | solution.py:29
  162.1 15.0 %collective-permute-start.36 = (bf16[256,768]{1,0:T(8,128)(2,1)}, bf16[256,768]{1,0:T(8,128)(2,1)S(1)}, u32[]{:S(2)}, u32[]{:S(2)}) collective-permute-start(bf16[256,768]{1,0:T(8,128)(2,1)} %get-tuple-element.260), channel_id=1, source_target_pairs={{0,2},{1,3},{2,0},{3,1},{4,6},{5,7},{6,4},{7,5},{8,10},{9,11},{10,... | collective-permute-start | bytes 1179656 | tf_op jit(solution)/shard_map/ppermute | solution.py:29
  198.2 14.7 %collective-permute-start.44 = (bf16[2,96,768]{2,1,0:T(8,128)(2,1)S(1)}, bf16[2,96,768]{2,1,0:T(8,128)(2,1)}, u32[]{:S(2)}, u32[]{:S(2)}) collective-permute-start(bf16[2,96,768]{2,1,0:T(8,128)(2,1)S(1)} %fusion.11), channel_id=1, source_target_pairs={{0,16},{4,20},{8,24},{12,28},{16,0},{20,4},{24,8},{28,12},{1,17},{... | collective-permute-start | bytes 884744 | tf_op jit(solution)/shard_map/ppermute | solution.py:29
  215.1 18.2 %collective-permute-start.46 = (bf16[2,112,768]{2,1,0:T(8,128)(2,1)S(1)}, bf16[2,112,768]{2,1,0:T(8,128)(2,1)S(1)}, u32[]{:S(2)}, u32[]{:S(2)}) collective-permute-start(bf16[2,112,768]{2,1,0:T(8,128)(2,1)S(1)} %pad_maximum_fusion.5), channel_id=1, source_target_pairs={{0,16},{4,20},{8,24},{12,28},{16,0},{20,4},{24,8},{28,12},{1,17},{... | collective-permute-start | bytes 1032200 | tf_op jit(solution)/shard_map/ppermute | solution.py:29
  217.9 15.4 %collective-permute-start.48 = (bf16[256,768]{1,0:T(8,128)(2,1)S(1)}, bf16[256,768]{1,0:T(8,128)(2,1)S(1)}, u32[]{:S(2)}, u32[]{:S(2)}) collective-permute-start(bf16[256,768]{1,0:T(8,128)(2,1)S(1)} %copy-done.40), channel_id=1, source_target_pairs={{0,2},{1,3},{2,0},{3,1},{4,6},{5,7},{6,4},{7,5},{8,10},{9,11},{10,... | collective-permute-start | bytes 1179656 | tf_op jit(solution)/shard_map/ppermute | solution.py:29
  233.3 15.1 %collective-permute-start.51 = (bf16[2,192,384]{2,1,0:T(8,128)(2,1)S(1)}, bf16[2,192,384]{2,1,0:T(8,128)(2,1)S(1)}, u32[]{:S(2)}, u32[]{:S(2)}) collective-permute-start(bf16[2,192,384]{2,1,0:T(8,128)(2,1)S(1)} %fusion.10), channel_id=1, source_target_pairs={{0,16},{4,20},{8,24},{12,28},{16,0},{20,4},{24,8},{28,12},{1,17},{... | collective-permute-start | bytes 884744 | tf_op jit(solution)/shard_map/ppermute | solution.py:29
  233.4 15.1 %collective-permute-start.49 = (bf16[2,112,768]{2,1,0:T(8,128)(2,1)S(1)}, bf16[2,112,768]{2,1,0:T(8,128)(2,1)S(1)}, u32[]{:S(2)}, u32[]{:S(2)}) collective-permute-start(bf16[2,112,768]{2,1,0:T(8,128)(2,1)S(1)} %reverse_add_fusion), channel_id=1, source_target_pairs={{0,4},{4,0},{8,12},{12,8},{16,20},{20,16},{24,28},{28,24},{1,5},{5... | collective-permute-start | bytes 1032200 | tf_op jit(solution)/shard_map/ppermute | solution.py:29
  235.0 14.2 %collective-permute-start.50 = (bf16[4,96,768]{2,1,0:T(8,128)(2,1)S(1)}, bf16[4,96,768]{2,1,0:T(8,128)(2,1)}, u32[]{:S(2)}, u32[]{:S(2)}) collective-permute-start(bf16[4,96,768]{2,1,0:T(8,128)(2,1)S(1)} %pad_maximum_fusion.3.refs_0_), channel_id=1, source_target_pairs={{0,2},{1,3},{2,0},{3,1},{4,6},{5,7},{6,4},{7,5},{8,10},{9,11},{10,... | collective-permute-start | bytes 1769480 | tf_op jit(solution)/shard_map/ppermute | solution.py:29
  249.2 16.8 %collective-permute-start.52 = (bf16[4,112,768]{2,1,0:T(8,128)(2,1)S(1)}, bf16[4,112,768]{2,1,0:T(8,128)(2,1)S(1)}, u32[]{:S(2)}, u32[]{:S(2)}) collective-permute-start(bf16[4,112,768]{2,1,0:T(8,128)(2,1)S(1)} %pad_maximum_fusion), channel_id=1, source_target_pairs={{0,8},{4,12},{8,0},{12,4},{16,24},{20,28},{24,16},{28,20},{1,9},{5... | collective-permute-start | bytes 2064392 | tf_op jit(solution)/shard_map/ppermute | solution.py:29
  266.3 19.6 %collective-permute-start.61 = (bf16[4,112,768]{2,1,0:T(8,128)(2,1)S(1)}, bf16[4,112,768]{2,1,0:T(8,128)(2,1)S(1)}, u32[]{:S(2)}, u32[]{:S(2)}) collective-permute-start(bf16[4,112,768]{2,1,0:T(8,128)(2,1)S(1)} %pad_maximum_fusion.1.refs_0_), channel_id=1, source_target_pairs={{0,1},{1,0},{2,3},{3,2},{4,5},{5,4},{6,7},{7,6},{8,9},{9,8},{10,11... | collective-permute-start | bytes 2064392 | tf_op jit(solution)/shard_map/ppermute | solution.py:29
  267.4 18.4 %collective-permute-start.57 = (bf16[4,112,768]{2,1,0:T(8,128)(2,1)S(1)}, bf16[4,112,768]{2,1,0:T(8,128)(2,1)S(1)}, u32[]{:S(2)}, u32[]{:S(2)}) collective-permute-start(bf16[4,112,768]{2,1,0:T(8,128)(2,1)S(1)} %pad_maximum_fusion.1.refs_0_), channel_id=1, source_target_pairs={{0,2},{1,3},{2,0},{3,1},{4,6},{5,7},{6,4},{7,5},{8,10},{9,11},{10,... | collective-permute-start | bytes 2064392 | tf_op jit(solution)/shard_map/ppermute | solution.py:29
  269.0 14.4 %collective-permute-start.58 = (bf16[4,192,384]{2,1,0:T(8,128)(2,1)S(1)}, bf16[4,192,384]{2,1,0:T(8,128)(2,1)S(1)}, u32[]{:S(2)}, u32[]{:S(2)}) collective-permute-start(bf16[4,192,384]{2,1,0:T(8,128)(2,1)S(1)} %pad_maximum_fusion.4.refs_0_), channel_id=1, source_target_pairs={{0,8},{4,12},{8,0},{12,4},{16,24},{20,28},{24,16},{28,20},{1,9},{5... | collective-permute-start | bytes 1769480 | tf_op jit(solution)/shard_map/ppermute | solution.py:29
  269.8 16.1 %collective-permute-start.59 = (bf16[4,96,768]{2,1,0:T(8,128)(2,1)}, bf16[4,96,768]{2,1,0:T(8,128)(2,1)}, u32[]{:S(2)}, u32[]{:S(2)}) collective-permute-start(bf16[4,96,768]{2,1,0:T(8,128)(2,1)} %collective-permute-done.50.refs_1_), channel_id=1, source_target_pairs={{0,4},{4,0},{8,12},{12,8},{16,20},{20,16},{24,28},{28,24},{1,5},{5... | collective-permute-start | bytes 1769480 | tf_op jit(solution)/shard_map/ppermute | solution.py:29
  285.9 17.2 %collective-permute-start.62 = (bf16[4,112,768]{2,1,0:T(8,128)(2,1)S(1)}, bf16[4,112,768]{2,1,0:T(8,128)(2,1)}, u32[]{:S(2)}, u32[]{:S(2)}) collective-permute-start(bf16[4,112,768]{2,1,0:T(8,128)(2,1)S(1)} %pad_maximum_fusion.2.refs_1_), channel_id=1, source_target_pairs={{0,2},{1,3},{2,0},{3,1},{4,6},{5,7},{6,4},{7,5},{8,10},{9,11},{10,... | collective-permute-start | bytes 2064392 | tf_op jit(solution)/shard_map/ppermute | solution.py:29
  287.0 15.8 %collective-permute-start.63 = (bf16[4,192,384]{2,1,0:T(8,128)(2,1)S(1)}, bf16[4,192,384]{2,1,0:T(8,128)(2,1)}, u32[]{:S(2)}, u32[]{:S(2)}) collective-permute-start(bf16[4,192,384]{2,1,0:T(8,128)(2,1)S(1)} %pad_maximum_fusion.4.refs_0_), channel_id=1, source_target_pairs={{0,4},{4,0},{8,12},{12,8},{16,20},{20,16},{24,28},{28,24},{1,5},{5... | collective-permute-start | bytes 1769480 | tf_op jit(solution)/shard_map/ppermute | solution.py:29
  (126 other events, 964.6 us)

commit v11 on v10

--- a/solution.py
+++ b/solution.py
@@ -612,8 +612,9 @@
     )
 
 
-def place_tiles(by_rows, late, places, *refs):
-    sources, out = refs[:4], refs[-4]
+def place_tiles(by_rows, late, some, places, *refs):
+    count = 2 * (2 if by_rows else len(some))
+    sources, out = refs[:count], refs[-4]
     held, main, sems = refs[-3:]
     inner = places[8]
     _, rows, cols = sources[0].shape
@@ -626,38 +627,39 @@
         copy.wait()
     sent = []
     for k in range(2):
-        for l in range(2):
+        for i, l in enumerate(some):
             block = places[k * 4 + late * 2 + l]
-            place = 2 * k + l
+            place = len(some) * k + i
             for q in range(4):
                 h, x = q >> 1, q & 1
-                half, n = (x, l * 2 + h) if by_rows else (l, x * 2 + h)
+                half, n = (2 * k + x, l * 2 + h) if by_rows else (place, x * 2 + h)
                 first = pl.multiple_of((q ^ inner) * rows, rows)
-                main[place, pl.ds(first, rows), :] = held[2 * k + half, n].astype(jnp.float32)
+                main[place, pl.ds(first, rows), :] = held[half, n].astype(jnp.float32)
             if by_rows:
                 target = out.at[pl.ds(pl.multiple_of(block * 4 * rows, 4 * rows), 4 * rows)]
             else:
                 target = out.at[:, pl.ds(pl.multiple_of(block * cols, cols), cols)]
-            sent.append(pltpu.make_async_copy(main.at[place], target, sems.at[4 + place]))
+            sent.append(pltpu.make_async_copy(main.at[place], target, sems.at[count + place]))
             sent[-1].start()
     for copy in sent:
         copy.wait()
 
 
-def gather_tiles(places, halves, late, begun, shape, by_rows):
+def gather_tiles(places, halves, late, begun, shape, by_rows, some=(0, 1)):
     _, rows, cols = halves[0].shape
+    count = len(halves)
     away = pl.BlockSpec(memory_space=pl.ANY)
     return pl.pallas_call(
-        functools.partial(place_tiles, by_rows, late),
+        functools.partial(place_tiles, by_rows, late, some),
         out_shape=jax.ShapeDtypeStruct(shape, jnp.float32),
-        in_specs=[pl.BlockSpec(memory_space=pltpu.SMEM)] + [away] * (4 + len(begun)),
+        in_specs=[pl.BlockSpec(memory_space=pltpu.SMEM)] + [away] * (count + len(begun)),
         out_specs=away,
         scratch_shapes=[
-            pltpu.VMEM((4, 4, rows, cols), jnp.bfloat16),
-            pltpu.VMEM((4, 4 * rows, cols), jnp.float32),
-            pltpu.SemaphoreType.DMA((8,)),
+            pltpu.VMEM((count, 4, rows, cols), jnp.bfloat16),
+            pltpu.VMEM((2 * len(some), 4 * rows, cols), jnp.float32),
+            pltpu.SemaphoreType.DMA((count + 2 * len(some),)),
         ],
-        input_output_aliases={5: 0} if begun else {},
+        input_output_aliases={count + 1: 0} if begun else {},
         compiler_params=pltpu.CompilerParams(vmem_limit_bytes=VMEM_LIMIT),
     )(places, *halves, *begun)
 
@@ -1006,8 +1008,8 @@
     both_near.append(exchange_bit(both[1], "c"))
     both_far = [exchange_bit(half, "c") for half in across]
 
-    (up_hi, up_second, both_near, both_far) = lax.optimization_barrier(
-        (up_hi, up_second, both_near, both_far)
+    (up_hi, up_second, up_far, both_near, both_far) = lax.optimization_barrier(
+        (up_hi, up_second, up_far, both_near, both_far)
     )
     up_second.append(exchange_bit(up_hi[1:], "y"))
     across_up = [exchange_bit(up_far[0], "c")]
@@ -1017,12 +1019,22 @@
         tuple((r, first) for r in range(4) for first in (0, 4)),
         (features, 3 * features),
     )
-    (up_second, across_up, full_qkv, vector_rows, head_rows) = lax.optimization_barrier(
-        (up_second, across_up, full_qkv, vector_rows, head_rows)
-    )
-    up_far.append(jnp.concatenate(up_second))
-    across_up.append(exchange_bit(up_far[1], "c"))
-    full_up = gather_tiles(places, up_far + across_up, 1, [full_up], (features, hidden), False)
+    full_up = gather_tiles(
+        places, up_far + across_up, 1, [full_up], (features, hidden), False, (0,)
+    )
+    (up_second, full_up, full_qkv, vector_rows, head_rows) = lax.optimization_barrier(
+        (up_second, full_up, full_qkv, vector_rows, head_rows)
+    )
+    up_last = jnp.concatenate(up_second)
+    full_up = gather_tiles(
+        places,
+        [up_last, exchange_bit(up_last, "c")],
+        1,
+        [full_up],
+        (features, hidden),
+        False,
+        (1,),
+    )
     (
         full_b_down,
         full_gain_two,

time: 335 us -> 335 us (level)
    pallas_call x4 -> x5, Pallas kernels: 18.5 us -> 20.7 us  [gather_tiles(): pl.pallas_call(functools.partial(place_tiles, by_rows, late, some), out_s...]
  transfers between devices with their start and end apart: 74 -> 74, of which waited for: 30 -> 29; matrix products, arithmetic and copies ran while one was open for 9% -> 9% of each run, Pallas kernels for 26% -> 27%
where the time goes in v11:
time: 335 us; the launch traced here: 331 us
  Pallas kernels  134 us (40%)
  waiting for transfers between devices  91.9 us (27%)
  starting transfers between devices  56.7 us (17%)
  other arithmetic  25.6 us (8%)
  local copies, waits for them, and re-layouts  21.6 us (6%)
    ppermute x74, waiting for transfers between devices, exchange(): lax.ppermute(array_in, axis, [(i, i ^ flip) for i in range(lax.axis_size(...  91.9 us
    pallas_call x6, Pallas kernels, kernel_call(): pl.pallas_call(body, out_shape=outs, in_specs=[pl.BlockSpec(memory_space=...  63.4 us
    ppermute x74, starting transfers between devices, exchange(): lax.ppermute(array_in, axis, [(i, i ^ flip) for i in range(lax.axis_size(...  56.7 us
    pallas_call x1, Pallas kernels, step_call(): pl.pallas_call(body, out_shape=outs, grid_spec=pltpu.PrefetchScalarGridSp...  41.8 us
    pallas_call x5, Pallas kernels, gather_tiles(): pl.pallas_call(functools.partial(place_tiles, by_rows, late, some), out_s...  20.7 us
    convert_element_type x8, other arithmetic, sum_low(): return total.astype(jnp.bfloat16)  14 us
    unnamed x155, local copies, waits for them, and re-layouts  9.11 us
    pallas_call x1, Pallas kernels, gather_heads(): pl.pallas_call(functools.partial(place_heads, parts), out_shape=[out(shap...  7.79 us
  transfers between devices with their start and end apart: 74, of which 29 were waited for; matrix products, arithmetic and copies ran while one was open for 9% of the time, Pallas kernels for 27%

profile of v11, /device:TPU:0, one launch (start us, length us, event | category | flops | bytes accessed | tf_op | source)
XLA Modules:
  0.0 331.5 jit_solution(152720063001364462)
XLA Ops:
  18.3 8.3 %shard_map.280 = (bf16[192,256]{1,0:T(8,128)(2,1)}, bf16[192,256]{1,0:T(8,128)(2,1)}, bf16[192,256]{1,0:T(8,128)(2,1)}, bf16[192,256]{1,0:T(8,128)(2,1)}, bf16[1...) custom-call(s32[20]{0:T(128)} %concatenate.45.places, ...), custom_call_target="tpu_custom_call" | custom-call | flops 100000000 | bytes 1048576 | tf_op jit(solution)/shard_map/pallas_call | solution.py:235
  29.8 8.2 %shard_map.281 = (bf16[192,256]{1,0:T(8,128)(2,1)}, bf16[192,256]{1,0:T(8,128)(2,1)}, bf16[192,256]{1,0:T(8,128)(2,1)}, bf16[192,256]{1,0:T(8,128)(2,1)}, bf16[1...) custom-call(s32[20]{0:T(128)} %concatenate.45.places, ...), custom_call_target="tpu_custom_call" | custom-call | flops 100000000 | bytes 1048576 | tf_op jit(solution)/shard_map/pallas_call | solution.py:235
  42.5 8.2 %shard_map.282 = (bf16[192,256]{1,0:T(8,128)(2,1)}, bf16[192,256]{1,0:T(8,128)(2,1)}, bf16[192,256]{1,0:T(8,128)(2,1)}, bf16[192,256]{1,0:T(8,128)(2,1)}, bf16[1...) custom-call(s32[20]{0:T(128)} %concatenate.45.places, ...), custom_call_target="tpu_custom_call" | custom-call | flops 100000000 | bytes 1048576 | tf_op jit(solution)/shard_map/pallas_call | solution.py:235
  60.6 41.8 %shard_map.283 = (bf16[768,768]{1,0:T(8,128)(2,1)}, bf16[2,384,768]{2,1,0:T(8,128)(2,1)}, bf16[2,768,384]{2,1,0:T(8,128)(2,1)}, bf16[2,384,768]{2,1,0:T(8,128)(2...) custom-call(s32[20]{0:T(128)} %concatenate.45.places, ...), custom_call_target="tpu_custom_call" | custom-call | flops 24461180928 | bytes 1048576 | tf_op jit(solution)/shard_map/pallas_call | solution.py:531
  103.5 6.6 %collective-permute-done.20.g2 = bf16[2,1,192,256]{3,2,1,0:T(8,128)(2,1)S(1)} collective-permute-done((bf16[2,1,192,256]{3,2,1,0:T(8,128)(2,1)}, bf16[2,1,192,256]{3,2,1,0:T(8,128)(2,1)S(1)}, u32[]{:S(2)}, u32[]{:S(2)}) %collective-permute-start.20) | collective-permute-done | bytes 196640 | tf_op jit(solution)/shard_map/ppermute | solution.py:29
  122.8 12.4 %shard_map.284 = (bf16[2,256,768]{2,1,0:T(8,128)(2,1)}, bf16[2,256,768]{2,1,0:T(8,128)(2,1)}, f32[576,768]{1,0:T(8,128)}, f32[8,576]{1,0:T(8,128)}) custom-call(s32[20]{0:T(128)} %concatenate.45.places, bf16[1,192,256]{2,1,0:T(8,128)(2,1)} %get-tuple-element.208.g0, bf16[1,192,256]{2,1,0:T(8,128)(2,1)} %copy-done.48, bf16[2,1,192,256]{3,2,1,0:T(8,128)(2,1)} %copy-done.34, ...), custom_call_target="tpu_custom_call" | custom-call | flops 100000000 | bytes 1048576 | tf_op jit(solution)/shard_map/pallas_call | solution.py:235
  140.0 12.7 %shard_map.285 = (bf16[2,256,768]{2,1,0:T(8,128)(2,1)}, bf16[2,256,768]{2,1,0:T(8,128)(2,1)}, f32[576,768]{1,0:T(8,128)}, f32[8,576]{1,0:T(8,128)}) custom-call(s32[20]{0:T(128)} %concatenate.45.places, bf16[2,192,256]{2,1,0:T(8,128)(2,1)} %get-tuple-element.237.g0, bf16[2,192,256]{2,1,0:T(8,128)(2,1)} %copy-done.22, bf16[2,2,192,256]{3,2,1,0:T(8,128)(2,1)} %copy-done.2, ...), custom_call_target="tpu_custom_call" | custom-call | flops 100000000 | bytes 1048576 | tf_op jit(solution)/shard_map/pallas_call | solution.py:235
  162.6 13.6 %shard_map.286 = (bf16[2,256,768]{2,1,0:T(8,128)(2,1)}, bf16[2,256,768]{2,1,0:T(8,128)(2,1)}, bf16[8,112,384]{2,1,0:T(8,128)(2,1)}, bf16[8,112,384]{2,1,0:T(8,128)(2,1)}) custom-call(s32[20]{0:T(128)} %concatenate.45.places, bf16[2,192,256]{2,1,0:T(8,128)(2,1)} %get-tuple-element.237.g0, bf16[2,192,256]{2,1,0:T(8,128)(2,1)} %copy-done.22, ...), custom_call_target="tpu_custom_call" | custom-call | flops 100000000 | bytes 1048576 | tf_op jit(solution)/shard_map/pallas_call | solution.py:235
  186.5 4.6 %collective-permute-done.40 = bf16[2,192,384]{2,1,0:T(8,128)(2,1)S(1)} collective-permute-done((bf16[2,192,384]{2,1,0:T(8,128)(2,1)S(1)}, bf16[2,192,384]{2,1,0:T(8,128)(2,1)S(1)}, u32[]{:S(2)}, u32[]{:S(2)}) %collective-permute-start.40) | collective-permute-done | bytes 294944 | tf_op jit(solution)/shard_map/ppermute | solution.py:29
  191.1 4.6 %collective-permute-done.39 = bf16[2,96,768]{2,1,0:T(8,128)(2,1)S(1)} collective-permute-done((bf16[2,96,768]{2,1,0:T(8,128)(2,1)S(1)}, bf16[2,96,768]{2,1,0:T(8,128)(2,1)S(1)}, u32[]{:S(2)}, u32[]{:S(2)}) %collective-permute-start.39) | collective-permute-done | bytes 294944 | tf_op jit(solution)/shard_map/ppermute | solution.py:29
  205.3 4.2 %collective-permute-done.42 = bf16[2,112,384]{2,1,0:T(8,128)(2,1)} collective-permute-done((bf16[2,112,384]{2,1,0:T(8,128)(2,1)}, bf16[2,112,384]{2,1,0:T(8,128)(2,1)}, u32[]{:S(2)}, u32[]{:S(2)}) %collective-permute-start.42) | collective-permute-done | bytes 172064 | tf_op jit(solution)/shard_map/ppermute | solution.py:29
  219.4 8.8 %collective-permute-done.47 = bf16[2,96,768]{2,1,0:T(8,128)(2,1)S(1)} collective-permute-done((bf16[2,96,768]{2,1,0:T(8,128)(2,1)S(1)}, bf16[2,96,768]{2,1,0:T(8,128)(2,1)S(1)}, u32[]{:S(2)}, u32[]{:S(2)}) %collective-permute-start.47) | collective-permute-done | bytes 294944 | tf_op jit(solution)/shard_map/ppermute | solution.py:29
  228.2 5.0 %collective-permute-done.46 = bf16[2,112,768]{2,1,0:T(8,128)(2,1)S(1)} collective-permute-done((bf16[2,112,768]{2,1,0:T(8,128)(2,1)S(1)}, bf16[2,112,768]{2,1,0:T(8,128)(2,1)S(1)}, u32[]{:S(2)}, u32[]{:S(2)}) %collective-permute-start.46) | collective-permute-done | bytes 344096 | tf_op jit(solution)/shard_map/ppermute | solution.py:29
  240.1 8.4 %collective-permute-done.51 = bf16[2,192,384]{2,1,0:T(8,128)(2,1)S(1)} collective-permute-done((bf16[2,192,384]{2,1,0:T(8,128)(2,1)S(1)}, bf16[2,192,384]{2,1,0:T(8,128)(2,1)S(1)}, u32[]{:S(2)}, u32[]{:S(2)}) %collective-permute-start.51) | collective-permute-done | bytes 294944 | tf_op jit(solution)/shard_map/ppermute | solution.py:29
  254.4 4.2 %collective-permute-done.56 = bf16[2,192,384]{2,1,0:T(8,128)(2,1)S(1)} collective-permute-done((bf16[2,192,384]{2,1,0:T(8,128)(2,1)S(1)}, bf16[2,192,384]{2,1,0:T(8,128)(2,1)S(1)}, u32[]{:S(2)}, u32[]{:S(2)}) %collective-permute-start.56) | collective-permute-done | bytes 294944 | tf_op jit(solution)/shard_map/ppermute | solution.py:29
  258.7 7.3 %collective-permute-done.52 = bf16[4,112,768]{2,1,0:T(8,128)(2,1)S(1)} collective-permute-done((bf16[4,112,768]{2,1,0:T(8,128)(2,1)S(1)}, bf16[4,112,768]{2,1,0:T(8,128)(2,1)S(1)}, u32[]{:S(2)}, u32[]{:S(2)}) %collective-permute-start.52) | collective-permute-done | bytes 688160 | tf_op jit(solution)/shard_map/ppermute | solution.py:29
  270.8 4.6 %shard_map.287.refs_4_ = f32[3072,768]{1,0:T(8,128)} custom-call(s32[20]{0:T(128)} %concatenate.45.places, bf16[4,96,768]{2,1,0:T(8,128)(2,1)} %copy-done.3, bf16[4,96,768]{2,1,0:T(8,128)(2,1)} %collective-permute-done.50.refs_1_, bf16[4,96,768]{2,1,0:T(8,128)(2,1)} %copy-done.29, bf16[4,96,768]{2,1,0:T(8,128)(2,1)} %copy-done.30), custom_call_target="tpu_custom_call" | custom-call | tf_op jit(solution)/shard_map/pallas_call | solution.py:652
  275.4 8.0 %collective-permute-done.58.refs_1_ = bf16[4,192,384]{2,1,0:T(8,128)(2,1)S(1)} collective-permute-done((bf16[4,192,384]{2,1,0:T(8,128)(2,1)S(1)}, bf16[4,192,384]{2,1,0:T(8,128)(2,1)S(1)}, u32[]{:S(2)}, u32[]{:S(2)}) %collective-permute-start.58) | collective-permute-done | bytes 589856 | tf_op jit(solution)/shard_map/ppermute | solution.py:29
  290.1 4.6 %shard_map.289.refs_2_ = f32[768,3072]{1,0:T(8,128)} custom-call(s32[20]{0:T(128)} %concatenate.45.places, bf16[4,192,384]{2,1,0:T(8,128)(2,1)} %copy-done.6, bf16[4,192,384]{2,1,0:T(8,128)(2,1)} %copy-done.4, bf16[4,192,384]{2,1,0:T(8,128)(2,1)} %collective-permute-done.65.refs_2_, bf16[4,192,384]{2,1,0:T(8,128)(2,1)} %copy-done.33), custom_call_target="tpu_custom_call" | custom-call | tf_op jit(solution)/shard_map/pallas_call | solution.py:652
  294.7 4.7 %shard_map.288 = f32[3072,768]{1,0:T(8,128)} custom-call(s32[20]{0:T(128)} %concatenate.45.places, bf16[4,96,768]{2,1,0:T(8,128)(2,1)} %collective-permute-done.55.refs_0_, bf16[4,96,768]{2,1,0:T(8,128)(2,1)} %collective-permute-done.59.refs_1_, bf16[4,96,768]{2,1,0:T(8,128)(2,1)} %collective-permute-done.60.refs_2_, ...), custom_call_target="tpu_custom_call", output_to_operand_aliasing={{}: (5, {})} | custom-call | tf_op jit(solution)/shard_map/pallas_call | solution.py:652
  304.8 5.2 %collective-permute-done.67 = bf16[1,192,384]{2,1,0:T(8,128)(2,1)S(1)} collective-permute-done((bf16[1,192,384]{2,1,0:T(8,128)(2,1)S(1)}, bf16[1,192,384]{2,1,0:T(8,128)(2,1)S(1)}, u32[]{:S(2)}, u32[]{:S(2)}) %collective-permute-start.67) | collective-permute-done | bytes 147488 | tf_op jit(solution)/shard_map/ppermute | solution.py:29
  311.2 7.8 %shard_map.291 = (f32[768,2304]{1,0:T(8,128)}, f32[768,768]{1,0:T(8,128)}, f32[16,768]{1,0:T(8,128)}, f32[8,768]{1,0:T(8,128)}) custom-call(s32[20]{0:T(128)} %concatenate.45.places, bf16[4,112,768]{2,1,0:T(8,128)(2,1)} %copy-done.1, bf16[4,112,768]{2,1,0:T(8,128)(2,1)} %copy-done, bf16[4,112,768]{2,1,0:T(8,128)(2,1)} %copy-done.25, ...), custom_call_target="tpu_custom_call" | custom-call | tf_op jit(solution)/shard_map/pallas_call | solution.py:746
  319.9 3.4 %shard_map.290.refs_2_ = f32[768,3072]{1,0:T(8,128)} custom-call(s32[20]{0:T(128)} %concatenate.45.places, bf16[4,192,384]{2,1,0:T(8,128)(2,1)} %collective-permute-done.63.refs_0_, bf16[4,192,384]{2,1,0:T(8,128)(2,1)} %copy-done.32, f32[768,3072]{1,0:T(8,128)} %shard_map.289.refs_2_), custom_call_target="tpu_custom_call", output_to_operand_aliasing={{}: (3, {})} | custom-call | tf_op jit(solution)/shard_map/pallas_call | solution.py:652
  327.8 3.4 %shard_map.292 = f32[768,3072]{1,0:T(8,128)} custom-call(s32[20]{0:T(128)} %concatenate.45.places, bf16[4,192,384]{2,1,0:T(8,128)(2,1)} %copy-done.18, bf16[4,192,384]{2,1,0:T(8,128)(2,1)} %copy-done.31, f32[768,3072]{1,0:T(8,128)} %shard_map.290.refs_2_), custom_call_target="tpu_custom_call", output_to_operand_aliasing={{}: (3, {})} | custom-call | tf_op jit(solution)/shard_map/pallas_call | solution.py:652
  (368 shorter events, 128.9 us)
Async XLA Ops:
  2.0 14.8 %collective-permute-start.1 = (bf16[256,768]{1,0:T(8,128)(2,1)S(1)}, bf16[256,768]{1,0:T(8,128)(2,1)S(1)}, u32[]{:S(2)}, u32[]{:S(2)}) collective-permute-start(bf16[256,768]{1,0:T(8,128)(2,1)S(1)} %get-tuple-element.374.x0), channel_id=1, source_target_pairs={{0,1},{1,0},{2,3},{3,2},{4,5},{5,4},{6,7},{7,6},{8,9},{9,8},{10,11... | collective-permute-start | bytes 1179656 | tf_op jit(solution)/shard_map/ppermute | solution.py:29
  110.1 25.1 %collective-permute-start.25 = (bf16[2,384,768]{2,1,0:T(8,128)(2,1)}, bf16[2,384,768]{2,1,0:T(8,128)(2,1)}, u32[]{:S(2)}, u32[]{:S(2)}) collective-permute-start(bf16[2,384,768]{2,1,0:T(8,128)(2,1)} %get-tuple-element.231), channel_id=1, source_target_pairs={{0,1},{1,0},{2,3},{3,2},{4,5},{5,4},{6,7},{7,6},{8,9},{9,8},{10,11... | collective-permute-start | bytes 3538952 | tf_op jit(solution)/shard_map/ppermute | solution.py:29
  110.6 24.5 %collective-permute-start.24 = (bf16[2,2,192,256]{3,2,1,0:T(8,128)(2,1)}, bf16[2,2,192,256]{3,2,1,0:T(8,128)(2,1)S(1)}, u32[]{:S(2)}, u32[]{:S(2)}) collective-permute-start(bf16[2,2,192,256]{3,2,1,0:T(8,128)(2,1)} %get-tuple-element.228), channel_id=1, source_target_pairs={{0,2},{1,3},{2,0},{3,1},{4,6},{5,7},{6,4},{7,5},{8,10},{9,11},{10,... | collective-permute-start | bytes 1179656 | tf_op jit(solution)/shard_map/ppermute | solution.py:29
  117.6 38.1 %collective-permute-start.26 = (bf16[2,384,768]{2,1,0:T(8,128)(2,1)S(1)}, bf16[2,384,768]{2,1,0:T(8,128)(2,1)}, u32[]{:S(2)}, u32[]{:S(2)}) collective-permute-start(bf16[2,384,768]{2,1,0:T(8,128)(2,1)S(1)} %add_convert_fusion.1), channel_id=1, source_target_pairs={{0,4},{4,0},{8,12},{12,8},{16,20},{20,16},{24,28},{28,24},{1,5},{5... | collective-permute-start | bytes 3538952 | tf_op jit(solution)/shard_map/ppermute | solution.py:29
  119.2 36.5 %collective-permute-start.27 = (bf16[2,768,384]{2,1,0:T(8,128)(2,1)}, bf16[2,768,384]{2,1,0:T(8,128)(2,1)}, u32[]{:S(2)}, u32[]{:S(2)}) collective-permute-start(bf16[2,768,384]{2,1,0:T(8,128)(2,1)} %add_convert_fusion), channel_id=1, source_target_pairs={{0,8},{4,12},{8,0},{12,4},{16,24},{20,28},{24,16},{28,20},{1,9},{5... | collective-permute-start | bytes 3538952 | tf_op jit(solution)/shard_map/ppermute | solution.py:29
  135.2 17.5 %collective-permute-start.31 = (bf16[2,256,768]{2,1,0:T(8,128)(2,1)}, bf16[2,256,768]{2,1,0:T(8,128)(2,1)}, u32[]{:S(2)}, u32[]{:S(2)}) collective-permute-start(bf16[2,256,768]{2,1,0:T(8,128)(2,1)} %get-tuple-element.251), channel_id=1, source_target_pairs={{0,1},{1,0},{2,3},{3,2},{4,5},{5,4},{6,7},{7,6},{8,9},{9,8},{10,11... | collective-permute-start | bytes 2359304 | tf_op jit(solution)/shard_map/ppermute | solution.py:29
  135.9 19.8 %collective-permute-start.28 = (bf16[2,8,96,192]{3,2,1,0:T(8,128)(2,1)}, bf16[2,8,96,192]{3,2,1,0:T(8,128)(2,1)S(1)}, u32[]{:S(2)}, u32[]{:S(2)}) collective-permute-start(bf16[2,8,96,192]{3,2,1,0:T(8,128)(2,1)} %get-tuple-element.236), channel_id=1, source_target_pairs={{0,2},{1,3},{2,0},{3,1},{4,6},{5,7},{6,4},{7,5},{8,10},{9,11},{10,... | collective-permute-start | bytes 1769480 | tf_op jit(solution)/shard_map/ppermute | solution.py:29
  155.9 20.3 %collective-permute-start.35 = (bf16[2,256,768]{2,1,0:T(8,128)(2,1)}, bf16[2,256,768]{2,1,0:T(8,128)(2,1)S(1)}, u32[]{:S(2)}, u32[]{:S(2)}) collective-permute-start(bf16[2,256,768]{2,1,0:T(8,128)(2,1)} %get-tuple-element.263), channel_id=1, source_target_pairs={{0,1},{1,0},{2,3},{3,2},{4,5},{5,4},{6,7},{7,6},{8,9},{9,8},{10,11... | collective-permute-start | bytes 2359304 | tf_op jit(solution)/shard_map/ppermute | solution.py:29
  161.2 16.0 %collective-permute-start.33 = (bf16[384,768]{1,0:T(8,128)(2,1)}, bf16[384,768]{1,0:T(8,128)(2,1)}, u32[]{:S(2)}, u32[]{:S(2)}) collective-permute-start(bf16[384,768]{1,0:T(8,128)(2,1)} %fusion.3), channel_id=1, source_target_pairs={{0,8},{4,12},{8,0},{12,4},{16,24},{20,28},{24,16},{28,20},{1,9},{5... | collective-permute-start | bytes 1769480 | tf_op jit(solution)/shard_map/ppermute | solution.py:29
  161.6 15.5 %collective-permute-start.34 = (bf16[768,384]{1,0:T(8,128)(2,1)}, bf16[768,384]{1,0:T(8,128)(2,1)}, u32[]{:S(2)}, u32[]{:S(2)}) collective-permute-start(bf16[768,384]{1,0:T(8,128)(2,1)} %fusion.4), channel_id=1, source_target_pairs={{0,4},{4,0},{8,12},{12,8},{16,20},{20,16},{24,28},{28,24},{1,5},{5... | collective-permute-start | bytes 1769480 | tf_op jit(solution)/shard_map/ppermute | solution.py:29
  162.1 15.0 %collective-permute-start.36 = (bf16[256,768]{1,0:T(8,128)(2,1)}, bf16[256,768]{1,0:T(8,128)(2,1)S(1)}, u32[]{:S(2)}, u32[]{:S(2)}) collective-permute-start(bf16[256,768]{1,0:T(8,128)(2,1)} %get-tuple-element.261), channel_id=1, source_target_pairs={{0,2},{1,3},{2,0},{3,1},{4,6},{5,7},{6,4},{7,5},{8,10},{9,11},{10,... | collective-permute-start | bytes 1179656 | tf_op jit(solution)/shard_map/ppermute | solution.py:29
  198.2 14.7 %collective-permute-start.44 = (bf16[2,96,768]{2,1,0:T(8,128)(2,1)S(1)}, bf16[2,96,768]{2,1,0:T(8,128)(2,1)}, u32[]{:S(2)}, u32[]{:S(2)}) collective-permute-start(bf16[2,96,768]{2,1,0:T(8,128)(2,1)S(1)} %fusion.11), channel_id=1, source_target_pairs={{0,16},{4,20},{8,24},{12,28},{16,0},{20,4},{24,8},{28,12},{1,17},{... | collective-permute-start | bytes 884744 | tf_op jit(solution)/shard_map/ppermute | solution.py:29
  215.1 18.2 %collective-permute-start.46 = (bf16[2,112,768]{2,1,0:T(8,128)(2,1)S(1)}, bf16[2,112,768]{2,1,0:T(8,128)(2,1)S(1)}, u32[]{:S(2)}, u32[]{:S(2)}) collective-permute-start(bf16[2,112,768]{2,1,0:T(8,128)(2,1)S(1)} %pad_maximum_fusion.5), channel_id=1, source_target_pairs={{0,16},{4,20},{8,24},{12,28},{16,0},{20,4},{24,8},{28,12},{1,17},{... | collective-permute-start | bytes 1032200 | tf_op jit(solution)/shard_map/ppermute | solution.py:29
  217.9 15.4 %collective-permute-start.48 = (bf16[256,768]{1,0:T(8,128)(2,1)S(1)}, bf16[256,768]{1,0:T(8,128)(2,1)S(1)}, u32[]{:S(2)}, u32[]{:S(2)}) collective-permute-start(bf16[256,768]{1,0:T(8,128)(2,1)S(1)} %copy-done.40), channel_id=1, source_target_pairs={{0,2},{1,3},{2,0},{3,1},{4,6},{5,7},{6,4},{7,5},{8,10},{9,11},{10,... | collective-permute-start | bytes 1179656 | tf_op jit(solution)/shard_map/ppermute | solution.py:29
  233.3 15.1 %collective-permute-start.51 = (bf16[2,192,384]{2,1,0:T(8,128)(2,1)S(1)}, bf16[2,192,384]{2,1,0:T(8,128)(2,1)S(1)}, u32[]{:S(2)}, u32[]{:S(2)}) collective-permute-start(bf16[2,192,384]{2,1,0:T(8,128)(2,1)S(1)} %fusion.10), channel_id=1, source_target_pairs={{0,16},{4,20},{8,24},{12,28},{16,0},{20,4},{24,8},{28,12},{1,17},{... | collective-permute-start | bytes 884744 | tf_op jit(solution)/shard_map/ppermute | solution.py:29
  233.4 15.1 %collective-permute-start.49 = (bf16[2,112,768]{2,1,0:T(8,128)(2,1)S(1)}, bf16[2,112,768]{2,1,0:T(8,128)(2,1)S(1)}, u32[]{:S(2)}, u32[]{:S(2)}) collective-permute-start(bf16[2,112,768]{2,1,0:T(8,128)(2,1)S(1)} %reverse_add_fusion), channel_id=1, source_target_pairs={{0,4},{4,0},{8,12},{12,8},{16,20},{20,16},{24,28},{28,24},{1,5},{5... | collective-permute-start | bytes 1032200 | tf_op jit(solution)/shard_map/ppermute | solution.py:29
  235.0 14.2 %collective-permute-start.50 = (bf16[4,96,768]{2,1,0:T(8,128)(2,1)S(1)}, bf16[4,96,768]{2,1,0:T(8,128)(2,1)}, u32[]{:S(2)}, u32[]{:S(2)}) collective-permute-start(bf16[4,96,768]{2,1,0:T(8,128)(2,1)S(1)} %pad_maximum_fusion.3.refs_0_), channel_id=1, source_target_pairs={{0,2},{1,3},{2,0},{3,1},{4,6},{5,7},{6,4},{7,5},{8,10},{9,11},{10,... | collective-permute-start | bytes 1769480 | tf_op jit(solution)/shard_map/ppermute | solution.py:29
  249.2 16.8 %collective-permute-start.52 = (bf16[4,112,768]{2,1,0:T(8,128)(2,1)S(1)}, bf16[4,112,768]{2,1,0:T(8,128)(2,1)S(1)}, u32[]{:S(2)}, u32[]{:S(2)}) collective-permute-start(bf16[4,112,768]{2,1,0:T(8,128)(2,1)S(1)} %pad_maximum_fusion), channel_id=1, source_target_pairs={{0,8},{4,12},{8,0},{12,4},{16,24},{20,28},{24,16},{28,20},{1,9},{5... | collective-permute-start | bytes 2064392 | tf_op jit(solution)/shard_map/ppermute | solution.py:29
  266.3 19.6 %collective-permute-start.61 = (bf16[4,112,768]{2,1,0:T(8,128)(2,1)S(1)}, bf16[4,112,768]{2,1,0:T(8,128)(2,1)S(1)}, u32[]{:S(2)}, u32[]{:S(2)}) collective-permute-start(bf16[4,112,768]{2,1,0:T(8,128)(2,1)S(1)} %pad_maximum_fusion.1.refs_0_), channel_id=1, source_target_pairs={{0,1},{1,0},{2,3},{3,2},{4,5},{5,4},{6,7},{7,6},{8,9},{9,8},{10,11... | collective-permute-start | bytes 2064392 | tf_op jit(solution)/shard_map/ppermute | solution.py:29
  267.4 18.4 %collective-permute-start.57 = (bf16[4,112,768]{2,1,0:T(8,128)(2,1)S(1)}, bf16[4,112,768]{2,1,0:T(8,128)(2,1)S(1)}, u32[]{:S(2)}, u32[]{:S(2)}) collective-permute-start(bf16[4,112,768]{2,1,0:T(8,128)(2,1)S(1)} %pad_maximum_fusion.1.refs_0_), channel_id=1, source_target_pairs={{0,2},{1,3},{2,0},{3,1},{4,6},{5,7},{6,4},{7,5},{8,10},{9,11},{10,... | collective-permute-start | bytes 2064392 | tf_op jit(solution)/shard_map/ppermute | solution.py:29
  269.0 14.4 %collective-permute-start.58 = (bf16[4,192,384]{2,1,0:T(8,128)(2,1)S(1)}, bf16[4,192,384]{2,1,0:T(8,128)(2,1)S(1)}, u32[]{:S(2)}, u32[]{:S(2)}) collective-permute-start(bf16[4,192,384]{2,1,0:T(8,128)(2,1)S(1)} %pad_maximum_fusion.4.refs_0_), channel_id=1, source_target_pairs={{0,8},{4,12},{8,0},{12,4},{16,24},{20,28},{24,16},{28,20},{1,9},{5... | collective-permute-start | bytes 1769480 | tf_op jit(solution)/shard_map/ppermute | solution.py:29
  269.8 16.1 %collective-permute-start.59 = (bf16[4,96,768]{2,1,0:T(8,128)(2,1)}, bf16[4,96,768]{2,1,0:T(8,128)(2,1)}, u32[]{:S(2)}, u32[]{:S(2)}) collective-permute-start(bf16[4,96,768]{2,1,0:T(8,128)(2,1)} %collective-permute-done.50.refs_1_), channel_id=1, source_target_pairs={{0,4},{4,0},{8,12},{12,8},{16,20},{20,16},{24,28},{28,24},{1,5},{5... | collective-permute-start | bytes 1769480 | tf_op jit(solution)/shard_map/ppermute | solution.py:29
  285.9 17.2 %collective-permute-start.62 = (bf16[4,112,768]{2,1,0:T(8,128)(2,1)S(1)}, bf16[4,112,768]{2,1,0:T(8,128)(2,1)}, u32[]{:S(2)}, u32[]{:S(2)}) collective-permute-start(bf16[4,112,768]{2,1,0:T(8,128)(2,1)S(1)} %pad_maximum_fusion.2.refs_1_), channel_id=1, source_target_pairs={{0,2},{1,3},{2,0},{3,1},{4,6},{5,7},{6,4},{7,5},{8,10},{9,11},{10,... | collective-permute-start | bytes 2064392 | tf_op jit(solution)/shard_map/ppermute | solution.py:29
  287.0 15.8 %collective-permute-start.63 = (bf16[4,192,384]{2,1,0:T(8,128)(2,1)S(1)}, bf16[4,192,384]{2,1,0:T(8,128)(2,1)}, u32[]{:S(2)}, u32[]{:S(2)}) collective-permute-start(bf16[4,192,384]{2,1,0:T(8,128)(2,1)S(1)} %pad_maximum_fusion.4.refs_0_), channel_id=1, source_target_pairs={{0,4},{4,0},{8,12},{12,8},{16,20},{20,16},{24,28},{28,24},{1,5},{5... | collective-permute-start | bytes 1769480 | tf_op jit(solution)/shard_map/ppermute | solution.py:29
  (126 other events, 952.7 us)

commit v12 on v11

--- a/solution.py
+++ b/solution.py
@@ -939,8 +939,8 @@
     cross(seq_count - 1)
 
     keeps, sends = [half_a[:2], half_b[0]], [half_a[2:], half_b[1]]
-    (keeps, sends, down, up, far, near_far, near) = lax.optimization_barrier(
-        (keeps, sends, down, up, far, near_far, near)
+    (keeps, sends, up, far, near_far, near) = lax.optimization_barrier(
+        (keeps, sends, up, far, near_far, near)
     )
     got = [exchange_bit(v, bit) for v, bit in zip(sends, "ly")]
     down_came = exchange_bit(down, "h")

time: 335 us -> 328 us (0.979)
  waiting for transfers between devices: 91.9 us -> 86.5 us
    ppermute x74, waiting for transfers between devices: 91.9 us -> 86.5 us  [exchange(): lax.ppermute(array_in, axis, [(i, i ^ flip) for i in range(lax.axis_size(...]
  transfers between devices with their start and end apart: 74 -> 74, of which waited for: 29 -> 30; matrix products, arithmetic and copies ran while one was open for 9% -> 10% of each run, Pallas kernels for 27% -> 27%
where the time goes in v12:
time: 328 us; the launch traced here: 324 us
  Pallas kernels  134 us (41%)
  waiting for transfers between devices  86.5 us (26%)
  starting transfers between devices  55.6 us (17%)
  other arithmetic  23.8 us (7%)
  local copies, waits for them, and re-layouts  22.4 us (7%)
    ppermute x74, waiting for transfers between devices, exchange(): lax.ppermute(array_in, axis, [(i, i ^ flip) for i in range(lax.axis_size(...  86.5 us
    pallas_call x6, Pallas kernels, kernel_call(): pl.pallas_call(body, out_shape=outs, in_specs=[pl.BlockSpec(memory_space=...  63.4 us
    ppermute x74, starting transfers between devices, exchange(): lax.ppermute(array_in, axis, [(i, i ^ flip) for i in range(lax.axis_size(...  55.6 us
    pallas_call x1, Pallas kernels, step_call(): pl.pallas_call(body, out_shape=outs, grid_spec=pltpu.PrefetchScalarGridSp...  41.8 us
    pallas_call x5, Pallas kernels, gather_tiles(): pl.pallas_call(functools.partial(place_tiles, by_rows, late, some), out_s...  20.7 us
    convert_element_type x8, other arithmetic, sum_low(): return total.astype(jnp.bfloat16)  14 us
    unnamed x155, local copies, waits for them, and re-layouts  9.85 us
    pallas_call x1, Pallas kernels, gather_heads(): pl.pallas_call(functools.partial(place_heads, parts), out_shape=[out(shap...  7.79 us
  transfers between devices with their start and end apart: 74, of which 30 were waited for; matrix products, arithmetic and copies ran while one was open for 10% of the time, Pallas kernels for 27%

profile of v12, /device:TPU:0, one launch (start us, length us, event | category | flops | bytes accessed | tf_op | source)
XLA Modules:
  0.0 324.0 jit_solution(13724165415345157170)
XLA Ops:
  18.3 8.3 %shard_map.280 = (bf16[192,256]{1,0:T(8,128)(2,1)}, bf16[192,256]{1,0:T(8,128)(2,1)}, bf16[192,256]{1,0:T(8,128)(2,1)}, bf16[192,256]{1,0:T(8,128)(2,1)}, bf16[1...) custom-call(s32[20]{0:T(128)} %concatenate.45.places, ...), custom_call_target="tpu_custom_call" | custom-call | flops 100000000 | bytes 1048576 | tf_op jit(solution)/shard_map/pallas_call | solution.py:235
  29.8 8.2 %shard_map.281 = (bf16[192,256]{1,0:T(8,128)(2,1)}, bf16[192,256]{1,0:T(8,128)(2,1)}, bf16[192,256]{1,0:T(8,128)(2,1)}, bf16[192,256]{1,0:T(8,128)(2,1)}, bf16[1...) custom-call(s32[20]{0:T(128)} %concatenate.45.places, ...), custom_call_target="tpu_custom_call" | custom-call | flops 100000000 | bytes 1048576 | tf_op jit(solution)/shard_map/pallas_call | solution.py:235
  42.5 8.2 %shard_map.282 = (bf16[192,256]{1,0:T(8,128)(2,1)}, bf16[192,256]{1,0:T(8,128)(2,1)}, bf16[192,256]{1,0:T(8,128)(2,1)}, bf16[192,256]{1,0:T(8,128)(2,1)}, bf16[1...) custom-call(s32[20]{0:T(128)} %concatenate.45.places, ...), custom_call_target="tpu_custom_call" | custom-call | flops 100000000 | bytes 1048576 | tf_op jit(solution)/shard_map/pallas_call | solution.py:235
  60.6 41.8 %shard_map.283 = (bf16[768,768]{1,0:T(8,128)(2,1)}, bf16[2,384,768]{2,1,0:T(8,128)(2,1)}, bf16[2,768,384]{2,1,0:T(8,128)(2,1)}, bf16[2,384,768]{2,1,0:T(8,128)(2...) custom-call(s32[20]{0:T(128)} %concatenate.45.places, ...), custom_call_target="tpu_custom_call" | custom-call | flops 24461180928 | bytes 1048576 | tf_op jit(solution)/shard_map/pallas_call | solution.py:531
  103.5 6.6 %collective-permute-done.20.g2 = bf16[2,1,192,256]{3,2,1,0:T(8,128)(2,1)S(1)} collective-permute-done((bf16[2,1,192,256]{3,2,1,0:T(8,128)(2,1)}, bf16[2,1,192,256]{3,2,1,0:T(8,128)(2,1)S(1)}, u32[]{:S(2)}, u32[]{:S(2)}) %collective-permute-start.20) | collective-permute-done | bytes 196640 | tf_op jit(solution)/shard_map/ppermute | solution.py:29
  122.8 12.4 %shard_map.284 = (bf16[2,256,768]{2,1,0:T(8,128)(2,1)}, bf16[2,256,768]{2,1,0:T(8,128)(2,1)}, f32[576,768]{1,0:T(8,128)}, f32[8,576]{1,0:T(8,128)}) custom-call(s32[20]{0:T(128)} %concatenate.45.places, bf16[1,192,256]{2,1,0:T(8,128)(2,1)} %get-tuple-element.207.g0, bf16[1,192,256]{2,1,0:T(8,128)(2,1)} %copy-done.48, bf16[2,1,192,256]{3,2,1,0:T(8,128)(2,1)} %copy-done.34, ...), custom_call_target="tpu_custom_call" | custom-call | flops 100000000 | bytes 1048576 | tf_op jit(solution)/shard_map/pallas_call | solution.py:235
  140.0 12.7 %shard_map.285 = (bf16[2,256,768]{2,1,0:T(8,128)(2,1)}, bf16[2,256,768]{2,1,0:T(8,128)(2,1)}, f32[576,768]{1,0:T(8,128)}, f32[8,576]{1,0:T(8,128)}) custom-call(s32[20]{0:T(128)} %concatenate.45.places, bf16[2,192,256]{2,1,0:T(8,128)(2,1)} %get-tuple-element.236.g0, bf16[2,192,256]{2,1,0:T(8,128)(2,1)} %copy-done.22, bf16[2,2,192,256]{3,2,1,0:T(8,128)(2,1)} %copy-done.2, ...), custom_call_target="tpu_custom_call" | custom-call | flops 100000000 | bytes 1048576 | tf_op jit(solution)/shard_map/pallas_call | solution.py:235
  162.6 13.6 %shard_map.286 = (bf16[2,256,768]{2,1,0:T(8,128)(2,1)}, bf16[2,256,768]{2,1,0:T(8,128)(2,1)}, bf16[8,112,384]{2,1,0:T(8,128)(2,1)}, bf16[8,112,384]{2,1,0:T(8,128)(2,1)}) custom-call(s32[20]{0:T(128)} %concatenate.45.places, bf16[2,192,256]{2,1,0:T(8,128)(2,1)} %get-tuple-element.236.g0, bf16[2,192,256]{2,1,0:T(8,128)(2,1)} %copy-done.22, ...), custom_call_target="tpu_custom_call" | custom-call | flops 100000000 | bytes 1048576 | tf_op jit(solution)/shard_map/pallas_call | solution.py:235
  194.7 4.3 %collective-permute-done.38 = bf16[2,2,112,384]{3,2,1,0:T(8,128)(2,1)S(1)} collective-permute-done((bf16[2,2,112,384]{3,2,1,0:T(8,128)(2,1)S(1)}, bf16[2,2,112,384]{3,2,1,0:T(8,128)(2,1)S(1)}, u32[]{:S(2)}, u32[]{:S(2)}) %collective-permute-start.38) | collective-permute-done | bytes 344096 | tf_op jit(solution)/shard_map/ppermute | solution.py:29
  208.9 4.1 %collective-permute-start.46 = (bf16[2,112,768]{2,1,0:T(8,128)(2,1)S(1)}, bf16[2,112,768]{2,1,0:T(8,128)(2,1)S(1)}, u32[]{:S(2)}, u32[]{:S(2)}) collective-permute-start(bf16[2,112,768]{2,1,0:T(8,128)(2,1)S(1)} %pad_maximum_fusion.5), channel_id=1, source_target_pairs={{0,16},{4,20},{8,24},{12,28},{16,0},{20,4},{24,8},{28,12},{1,17},{... | collective-permute-start | bytes 1032200 | tf_op jit(solution)/shard_map/ppermute | solution.py:29
  213.1 6.0 %collective-permute-done.47 = bf16[2,96,768]{2,1,0:T(8,128)(2,1)S(1)} collective-permute-done((bf16[2,96,768]{2,1,0:T(8,128)(2,1)S(1)}, bf16[2,96,768]{2,1,0:T(8,128)(2,1)S(1)}, u32[]{:S(2)}, u32[]{:S(2)}) %collective-permute-start.47) | collective-permute-done | bytes 294944 | tf_op jit(solution)/shard_map/ppermute | solution.py:29
  219.2 5.5 %collective-permute-done.46 = bf16[2,112,768]{2,1,0:T(8,128)(2,1)S(1)} collective-permute-done((bf16[2,112,768]{2,1,0:T(8,128)(2,1)S(1)}, bf16[2,112,768]{2,1,0:T(8,128)(2,1)S(1)}, u32[]{:S(2)}, u32[]{:S(2)}) %collective-permute-start.46) | collective-permute-done | bytes 344096 | tf_op jit(solution)/shard_map/ppermute | solution.py:29
  231.9 5.2 %collective-permute-done.51 = bf16[2,192,384]{2,1,0:T(8,128)(2,1)S(1)} collective-permute-done((bf16[2,192,384]{2,1,0:T(8,128)(2,1)S(1)}, bf16[2,192,384]{2,1,0:T(8,128)(2,1)S(1)}, u32[]{:S(2)}, u32[]{:S(2)}) %collective-permute-start.51) | collective-permute-done | bytes 294944 | tf_op jit(solution)/shard_map/ppermute | solution.py:29
  237.5 8.4 %collective-permute-start.52 = (bf16[4,112,768]{2,1,0:T(8,128)(2,1)S(1)}, bf16[4,112,768]{2,1,0:T(8,128)(2,1)S(1)}, u32[]{:S(2)}, u32[]{:S(2)}) collective-permute-start(bf16[4,112,768]{2,1,0:T(8,128)(2,1)S(1)} %pad_maximum_fusion), channel_id=1, source_target_pairs={{0,8},{4,12},{8,0},{12,4},{16,24},{20,28},{24,16},{28,20},{1,9},{5... | collective-permute-start | bytes 2064392 | tf_op jit(solution)/shard_map/ppermute | solution.py:29
  247.4 5.2 %collective-permute-done.56 = bf16[2,192,384]{2,1,0:T(8,128)(2,1)S(1)} collective-permute-done((bf16[2,192,384]{2,1,0:T(8,128)(2,1)S(1)}, bf16[2,192,384]{2,1,0:T(8,128)(2,1)S(1)}, u32[]{:S(2)}, u32[]{:S(2)}) %collective-permute-start.56) | collective-permute-done | bytes 294944 | tf_op jit(solution)/shard_map/ppermute | solution.py:29
  252.7 5.4 %collective-permute-done.52 = bf16[4,112,768]{2,1,0:T(8,128)(2,1)S(1)} collective-permute-done((bf16[4,112,768]{2,1,0:T(8,128)(2,1)S(1)}, bf16[4,112,768]{2,1,0:T(8,128)(2,1)S(1)}, u32[]{:S(2)}, u32[]{:S(2)}) %collective-permute-start.52) | collective-permute-done | bytes 688160 | tf_op jit(solution)/shard_map/ppermute | solution.py:29
  262.4 4.6 %shard_map.287.refs_4_ = f32[3072,768]{1,0:T(8,128)} custom-call(s32[20]{0:T(128)} %concatenate.45.places, bf16[4,96,768]{2,1,0:T(8,128)(2,1)} %copy-done.3, bf16[4,96,768]{2,1,0:T(8,128)(2,1)} %collective-permute-done.50.refs_1_, bf16[4,96,768]{2,1,0:T(8,128)(2,1)} %copy-done.29, bf16[4,96,768]{2,1,0:T(8,128)(2,1)} %copy-done.30), custom_call_target="tpu_custom_call" | custom-call | tf_op jit(solution)/shard_map/pallas_call | solution.py:652
  267.0 7.8 %collective-permute-done.58.refs_1_ = bf16[4,192,384]{2,1,0:T(8,128)(2,1)S(1)} collective-permute-done((bf16[4,192,384]{2,1,0:T(8,128)(2,1)S(1)}, bf16[4,192,384]{2,1,0:T(8,128)(2,1)S(1)}, u32[]{:S(2)}, u32[]{:S(2)}) %collective-permute-start.58) | collective-permute-done | bytes 589856 | tf_op jit(solution)/shard_map/ppermute | solution.py:29
  283.1 4.6 %shard_map.289.refs_2_ = f32[768,3072]{1,0:T(8,128)} custom-call(s32[20]{0:T(128)} %concatenate.45.places, bf16[4,192,384]{2,1,0:T(8,128)(2,1)} %copy-done.6, bf16[4,192,384]{2,1,0:T(8,128)(2,1)} %copy-done.4, bf16[4,192,384]{2,1,0:T(8,128)(2,1)} %collective-permute-done.65.refs_2_, bf16[4,192,384]{2,1,0:T(8,128)(2,1)} %copy-done.33), custom_call_target="tpu_custom_call" | custom-call | tf_op jit(solution)/shard_map/pallas_call | solution.py:652
  287.7 4.7 %shard_map.288 = f32[3072,768]{1,0:T(8,128)} custom-call(s32[20]{0:T(128)} %concatenate.45.places, bf16[4,96,768]{2,1,0:T(8,128)(2,1)} %collective-permute-done.55.refs_0_, bf16[4,96,768]{2,1,0:T(8,128)(2,1)} %collective-permute-done.59.refs_1_, bf16[4,96,768]{2,1,0:T(8,128)(2,1)} %collective-permute-done.60.refs_2_, ...), custom_call_target="tpu_custom_call", output_to_operand_aliasing={{}: (5, {})} | custom-call | tf_op jit(solution)/shard_map/pallas_call | solution.py:652
  297.1 5.6 %collective-permute-done.67 = bf16[1,192,384]{2,1,0:T(8,128)(2,1)S(1)} collective-permute-done((bf16[1,192,384]{2,1,0:T(8,128)(2,1)S(1)}, bf16[1,192,384]{2,1,0:T(8,128)(2,1)S(1)}, u32[]{:S(2)}, u32[]{:S(2)}) %collective-permute-start.67) | collective-permute-done | bytes 147488 | tf_op jit(solution)/shard_map/ppermute | solution.py:29
  303.8 7.8 %shard_map.291 = (f32[768,2304]{1,0:T(8,128)}, f32[768,768]{1,0:T(8,128)}, f32[16,768]{1,0:T(8,128)}, f32[8,768]{1,0:T(8,128)}) custom-call(s32[20]{0:T(128)} %concatenate.45.places, bf16[4,112,768]{2,1,0:T(8,128)(2,1)} %copy-done.1, bf16[4,112,768]{2,1,0:T(8,128)(2,1)} %copy-done, bf16[4,112,768]{2,1,0:T(8,128)(2,1)} %copy-done.25, ...), custom_call_target="tpu_custom_call" | custom-call | tf_op jit(solution)/shard_map/pallas_call | solution.py:746
  312.5 3.4 %shard_map.290.refs_2_ = f32[768,3072]{1,0:T(8,128)} custom-call(s32[20]{0:T(128)} %concatenate.45.places, bf16[4,192,384]{2,1,0:T(8,128)(2,1)} %collective-permute-done.63.refs_0_, bf16[4,192,384]{2,1,0:T(8,128)(2,1)} %copy-done.32, f32[768,3072]{1,0:T(8,128)} %shard_map.289.refs_2_), custom_call_target="tpu_custom_call", output_to_operand_aliasing={{}: (3, {})} | custom-call | tf_op jit(solution)/shard_map/pallas_call | solution.py:652
  320.4 3.4 %shard_map.292 = f32[768,3072]{1,0:T(8,128)} custom-call(s32[20]{0:T(128)} %concatenate.45.places, bf16[4,192,384]{2,1,0:T(8,128)(2,1)} %copy-done.18, bf16[4,192,384]{2,1,0:T(8,128)(2,1)} %copy-done.31, f32[768,3072]{1,0:T(8,128)} %shard_map.290.refs_2_), custom_call_target="tpu_custom_call", output_to_operand_aliasing={{}: (3, {})} | custom-call | tf_op jit(solution)/shard_map/pallas_call | solution.py:652
  (368 shorter events, 124.0 us)
Async XLA Ops:
  2.0 14.8 %collective-permute-start.1 = (bf16[256,768]{1,0:T(8,128)(2,1)S(1)}, bf16[256,768]{1,0:T(8,128)(2,1)S(1)}, u32[]{:S(2)}, u32[]{:S(2)}) collective-permute-start(bf16[256,768]{1,0:T(8,128)(2,1)S(1)} %get-tuple-element.372.x0), channel_id=1, source_target_pairs={{0,1},{1,0},{2,3},{3,2},{4,5},{5,4},{6,7},{7,6},{8,9},{9,8},{10,11... | collective-permute-start | bytes 1179656 | tf_op jit(solution)/shard_map/ppermute | solution.py:29
  41.0 13.3 %collective-permute-start.10 = (bf16[192,256]{1,0:T(8,128)(2,1)}, bf16[192,256]{1,0:T(8,128)(2,1)S(1)}, u32[]{:S(2)}, u32[]{:S(2)}) collective-permute-start(bf16[192,256]{1,0:T(8,128)(2,1)} %get-tuple-element.197), channel_id=1, source_target_pairs={{0,2},{1,3},{2,0},{3,1},{4,6},{5,7},{6,4},{7,5},{8,10},{9,11},{10,... | collective-permute-start | bytes 294920 | tf_op jit(solution)/shard_map/ppermute | solution.py:29
  110.1 25.1 %collective-permute-start.25 = (bf16[2,384,768]{2,1,0:T(8,128)(2,1)}, bf16[2,384,768]{2,1,0:T(8,128)(2,1)}, u32[]{:S(2)}, u32[]{:S(2)}) collective-permute-start(bf16[2,384,768]{2,1,0:T(8,128)(2,1)} %get-tuple-element.230), channel_id=1, source_target_pairs={{0,1},{1,0},{2,3},{3,2},{4,5},{5,4},{6,7},{7,6},{8,9},{9,8},{10,11... | collective-permute-start | bytes 3538952 | tf_op jit(solution)/shard_map/ppermute | solution.py:29
  110.6 24.5 %collective-permute-start.24 = (bf16[2,2,192,256]{3,2,1,0:T(8,128)(2,1)}, bf16[2,2,192,256]{3,2,1,0:T(8,128)(2,1)S(1)}, u32[]{:S(2)}, u32[]{:S(2)}) collective-permute-start(bf16[2,2,192,256]{3,2,1,0:T(8,128)(2,1)} %get-tuple-element.227), channel_id=1, source_target_pairs={{0,2},{1,3},{2,0},{3,1},{4,6},{5,7},{6,4},{7,5},{8,10},{9,11},{10,... | collective-permute-start | bytes 1179656 | tf_op jit(solution)/shard_map/ppermute | solution.py:29
  117.6 38.1 %collective-permute-start.26 = (bf16[2,384,768]{2,1,0:T(8,128)(2,1)S(1)}, bf16[2,384,768]{2,1,0:T(8,128)(2,1)}, u32[]{:S(2)}, u32[]{:S(2)}) collective-permute-start(bf16[2,384,768]{2,1,0:T(8,128)(2,1)S(1)} %add_convert_fusion.1), channel_id=1, source_target_pairs={{0,4},{4,0},{8,12},{12,8},{16,20},{20,16},{24,28},{28,24},{1,5},{5... | collective-permute-start | bytes 3538952 | tf_op jit(solution)/shard_map/ppermute | solution.py:29
  119.2 36.5 %collective-permute-start.27 = (bf16[2,768,384]{2,1,0:T(8,128)(2,1)}, bf16[2,768,384]{2,1,0:T(8,128)(2,1)}, u32[]{:S(2)}, u32[]{:S(2)}) collective-permute-start(bf16[2,768,384]{2,1,0:T(8,128)(2,1)} %add_convert_fusion), channel_id=1, source_target_pairs={{0,8},{4,12},{8,0},{12,4},{16,24},{20,28},{24,16},{28,20},{1,9},{5... | collective-permute-start | bytes 3538952 | tf_op jit(solution)/shard_map/ppermute | solution.py:29
  135.2 17.5 %collective-permute-start.31 = (bf16[2,256,768]{2,1,0:T(8,128)(2,1)}, bf16[2,256,768]{2,1,0:T(8,128)(2,1)}, u32[]{:S(2)}, u32[]{:S(2)}) collective-permute-start(bf16[2,256,768]{2,1,0:T(8,128)(2,1)} %get-tuple-element.250), channel_id=1, source_target_pairs={{0,1},{1,0},{2,3},{3,2},{4,5},{5,4},{6,7},{7,6},{8,9},{9,8},{10,11... | collective-permute-start | bytes 2359304 | tf_op jit(solution)/shard_map/ppermute | solution.py:29
  135.9 19.8 %collective-permute-start.28 = (bf16[2,8,96,192]{3,2,1,0:T(8,128)(2,1)}, bf16[2,8,96,192]{3,2,1,0:T(8,128)(2,1)S(1)}, u32[]{:S(2)}, u32[]{:S(2)}) collective-permute-start(bf16[2,8,96,192]{3,2,1,0:T(8,128)(2,1)} %get-tuple-element.235), channel_id=1, source_target_pairs={{0,2},{1,3},{2,0},{3,1},{4,6},{5,7},{6,4},{7,5},{8,10},{9,11},{10,... | collective-permute-start | bytes 1769480 | tf_op jit(solution)/shard_map/ppermute | solution.py:29
  155.9 20.3 %collective-permute-start.35 = (bf16[2,256,768]{2,1,0:T(8,128)(2,1)}, bf16[2,256,768]{2,1,0:T(8,128)(2,1)S(1)}, u32[]{:S(2)}, u32[]{:S(2)}) collective-permute-start(bf16[2,256,768]{2,1,0:T(8,128)(2,1)} %get-tuple-element.262), channel_id=1, source_target_pairs={{0,1},{1,0},{2,3},{3,2},{4,5},{5,4},{6,7},{7,6},{8,9},{9,8},{10,11... | collective-permute-start | bytes 2359304 | tf_op jit(solution)/shard_map/ppermute | solution.py:29
  161.2 16.0 %collective-permute-start.33 = (bf16[384,768]{1,0:T(8,128)(2,1)}, bf16[384,768]{1,0:T(8,128)(2,1)}, u32[]{:S(2)}, u32[]{:S(2)}) collective-permute-start(bf16[384,768]{1,0:T(8,128)(2,1)} %fusion.3), channel_id=1, source_target_pairs={{0,8},{4,12},{8,0},{12,4},{16,24},{20,28},{24,16},{28,20},{1,9},{5... | collective-permute-start | bytes 1769480 | tf_op jit(solution)/shard_map/ppermute | solution.py:29
  161.6 15.5 %collective-permute-start.34 = (bf16[768,384]{1,0:T(8,128)(2,1)}, bf16[768,384]{1,0:T(8,128)(2,1)}, u32[]{:S(2)}, u32[]{:S(2)}) collective-permute-start(bf16[768,384]{1,0:T(8,128)(2,1)} %fusion.4), channel_id=1, source_target_pairs={{0,4},{4,0},{8,12},{12,8},{16,20},{20,16},{24,28},{28,24},{1,5},{5... | collective-permute-start | bytes 1769480 | tf_op jit(solution)/shard_map/ppermute | solution.py:29
  162.1 15.0 %collective-permute-start.36 = (bf16[256,768]{1,0:T(8,128)(2,1)}, bf16[256,768]{1,0:T(8,128)(2,1)S(1)}, u32[]{:S(2)}, u32[]{:S(2)}) collective-permute-start(bf16[256,768]{1,0:T(8,128)(2,1)} %get-tuple-element.260), channel_id=1, source_target_pairs={{0,2},{1,3},{2,0},{3,1},{4,6},{5,7},{6,4},{7,5},{8,10},{9,11},{10,... | collective-permute-start | bytes 1179656 | tf_op jit(solution)/shard_map/ppermute | solution.py:29
  185.3 13.7 %collective-permute-start.38 = (bf16[2,2,112,384]{3,2,1,0:T(8,128)(2,1)S(1)}, bf16[2,2,112,384]{3,2,1,0:T(8,128)(2,1)S(1)}, u32[]{:S(2)}, u32[]{:S(2)}) collective-permute-start(bf16[2,2,112,384]{3,2,1,0:T(8,128)(2,1)S(1)} %slice_bitcast_fusion.3), channel_id=1, source_target_pairs={{0,8},{4,12},{8,0},{12,4},{16,24},{20,28},{24,16},{28,20},{1,9},{5... | collective-permute-start | bytes 1032200 | tf_op jit(solution)/shard_map/ppermute | solution.py:29
  186.9 12.9 %collective-permute-start.40 = (bf16[2,256,768]{2,1,0:T(8,128)(2,1)S(1)}, bf16[2,256,768]{2,1,0:T(8,128)(2,1)S(1)}, u32[]{:S(2)}, u32[]{:S(2)}) collective-permute-start(bf16[2,256,768]{2,1,0:T(8,128)(2,1)S(1)} %copy-done.60), channel_id=1, source_target_pairs={{0,1},{1,0},{2,3},{3,2},{4,5},{5,4},{6,7},{7,6},{8,9},{9,8},{10,11... | collective-permute-start | bytes 2359304 | tf_op jit(solution)/shard_map/ppermute | solution.py:29
  189.3 14.5 %collective-permute-start.44 = (bf16[2,96,768]{2,1,0:T(8,128)(2,1)S(1)}, bf16[2,96,768]{2,1,0:T(8,128)(2,1)}, u32[]{:S(2)}, u32[]{:S(2)}) collective-permute-start(bf16[2,96,768]{2,1,0:T(8,128)(2,1)S(1)} %fusion.10), channel_id=1, source_target_pairs={{0,16},{4,20},{8,24},{12,28},{16,0},{20,4},{24,8},{28,12},{1,17},{... | collective-permute-start | bytes 884744 | tf_op jit(solution)/shard_map/ppermute | solution.py:29
  208.9 15.8 %collective-permute-start.46 = (bf16[2,112,768]{2,1,0:T(8,128)(2,1)S(1)}, bf16[2,112,768]{2,1,0:T(8,128)(2,1)S(1)}, u32[]{:S(2)}, u32[]{:S(2)}) collective-permute-start(bf16[2,112,768]{2,1,0:T(8,128)(2,1)S(1)} %pad_maximum_fusion.5), channel_id=1, source_target_pairs={{0,16},{4,20},{8,24},{12,28},{16,0},{20,4},{24,8},{28,12},{1,17},{... | collective-permute-start | bytes 1032200 | tf_op jit(solution)/shard_map/ppermute | solution.py:29
  237.5 20.6 %collective-permute-start.52 = (bf16[4,112,768]{2,1,0:T(8,128)(2,1)S(1)}, bf16[4,112,768]{2,1,0:T(8,128)(2,1)S(1)}, u32[]{:S(2)}, u32[]{:S(2)}) collective-permute-start(bf16[4,112,768]{2,1,0:T(8,128)(2,1)S(1)} %pad_maximum_fusion), channel_id=1, source_target_pairs={{0,8},{4,12},{8,0},{12,4},{16,24},{20,28},{24,16},{28,20},{1,9},{5... | collective-permute-start | bytes 2064392 | tf_op jit(solution)/shard_map/ppermute | solution.py:29
  258.4 19.7 %collective-permute-start.61 = (bf16[4,112,768]{2,1,0:T(8,128)(2,1)S(1)}, bf16[4,112,768]{2,1,0:T(8,128)(2,1)S(1)}, u32[]{:S(2)}, u32[]{:S(2)}) collective-permute-start(bf16[4,112,768]{2,1,0:T(8,128)(2,1)S(1)} %pad_maximum_fusion.1.refs_0_), channel_id=1, source_target_pairs={{0,1},{1,0},{2,3},{3,2},{4,5},{5,4},{6,7},{7,6},{8,9},{9,8},{10,11... | collective-permute-start | bytes 2064392 | tf_op jit(solution)/shard_map/ppermute | solution.py:29
  259.5 18.6 %collective-permute-start.57 = (bf16[4,112,768]{2,1,0:T(8,128)(2,1)S(1)}, bf16[4,112,768]{2,1,0:T(8,128)(2,1)S(1)}, u32[]{:S(2)}, u32[]{:S(2)}) collective-permute-start(bf16[4,112,768]{2,1,0:T(8,128)(2,1)S(1)} %pad_maximum_fusion.1.refs_0_), channel_id=1, source_target_pairs={{0,2},{1,3},{2,0},{3,1},{4,6},{5,7},{6,4},{7,5},{8,10},{9,11},{10,... | collective-permute-start | bytes 2064392 | tf_op jit(solution)/shard_map/ppermute | solution.py:29
  260.4 14.4 %collective-permute-start.58 = (bf16[4,192,384]{2,1,0:T(8,128)(2,1)S(1)}, bf16[4,192,384]{2,1,0:T(8,128)(2,1)S(1)}, u32[]{:S(2)}, u32[]{:S(2)}) collective-permute-start(bf16[4,192,384]{2,1,0:T(8,128)(2,1)S(1)} %pad_maximum_fusion.4.refs_0_), channel_id=1, source_target_pairs={{0,8},{4,12},{8,0},{12,4},{16,24},{20,28},{24,16},{28,20},{1,9},{5... | collective-permute-start | bytes 1769480 | tf_op jit(solution)/shard_map/ppermute | solution.py:29
  262.0 16.1 %collective-permute-start.59 = (bf16[4,96,768]{2,1,0:T(8,128)(2,1)}, bf16[4,96,768]{2,1,0:T(8,128)(2,1)}, u32[]{:S(2)}, u32[]{:S(2)}) collective-permute-start(bf16[4,96,768]{2,1,0:T(8,128)(2,1)} %collective-permute-done.50.refs_1_), channel_id=1, source_target_pairs={{0,4},{4,0},{8,12},{12,8},{16,20},{20,16},{24,28},{28,24},{1,5},{5... | collective-permute-start | bytes 1769480 | tf_op jit(solution)/shard_map/ppermute | solution.py:29
  278.1 17.7 %collective-permute-start.62 = (bf16[4,112,768]{2,1,0:T(8,128)(2,1)S(1)}, bf16[4,112,768]{2,1,0:T(8,128)(2,1)}, u32[]{:S(2)}, u32[]{:S(2)}) collective-permute-start(bf16[4,112,768]{2,1,0:T(8,128)(2,1)S(1)} %pad_maximum_fusion.2.refs_1_), channel_id=1, source_target_pairs={{0,2},{1,3},{2,0},{3,1},{4,6},{5,7},{6,4},{7,5},{8,10},{9,11},{10,... | collective-permute-start | bytes 2064392 | tf_op jit(solution)/shard_map/ppermute | solution.py:29
  280.0 15.8 %collective-permute-start.63 = (bf16[4,192,384]{2,1,0:T(8,128)(2,1)S(1)}, bf16[4,192,384]{2,1,0:T(8,128)(2,1)}, u32[]{:S(2)}, u32[]{:S(2)}) collective-permute-start(bf16[4,192,384]{2,1,0:T(8,128)(2,1)S(1)} %pad_maximum_fusion.4.refs_0_), channel_id=1, source_target_pairs={{0,4},{4,0},{8,12},{12,8},{16,20},{20,16},{24,28},{28,24},{1,5},{5... | collective-permute-start | bytes 1769480 | tf_op jit(solution)/shard_map/ppermute | solution.py:29
  302.9 13.1 %collective-permute-start.71 = (bf16[3,192,384]{2,1,0:T(8,128)(2,1)S(1)}, bf16[3,192,384]{2,1,0:T(8,128)(2,1)S(1)}, u32[]{:S(2)}, u32[]{:S(2)}) collective-permute-start(bf16[3,192,384]{2,1,0:T(8,128)(2,1)S(1)} %slice.238), channel_id=1, source_target_pairs={{0,4},{4,0},{8,12},{12,8},{16,20},{20,16},{24,28},{28,24},{1,5},{5... | collective-permute-start | bytes 1327112 | tf_op jit(solution)/shard_map/ppermute | solution.py:29
  (126 other events, 936.6 us)
